TPU v7x, 32 devices: a whole 2x2x4 slice. The times are simulated.
32 devices in a mesh: blk: 8 (over z, x), head: 4 (over y, core).
Axes of the slice: x: 2, y: 2, z: 4, core: 2. Of those that a mesh axis runs over, the one named last changes fastest.
Arguments:
- tokens: bfloat16 [1, 4096, 2048], P(None, ('blk', 'head')), may hold values from -6 to 6
- attention_norm: bfloat16 [2048], P(('blk', 'head')), may hold values from 0.5 to 1.5
- query_weight: bfloat16 [2048, 2048], P(('blk', 'head')), may hold values from -0.125 to 0.125
- key_projection: bfloat16 [2048, 1024], P(('blk', 'head')), may hold values from -0.125 to 0.125
- value_projection: bfloat16 [2048, 1024], P(('blk', 'head')), may hold values from -0.125 to 0.125
- query_norm: bfloat16 [128], P(('blk', 'head')), may hold values from 0.5 to 1.5
- key_norm: bfloat16 [128], P(('blk', 'head')), may hold values from 0.5 to 1.5
- output_weight: bfloat16 [2048, 2048], P(('blk', 'head')), may hold values from -2 to 2
- feedforward_norm: bfloat16 [2048], P(('blk', 'head')), may hold values from 0.5 to 1.5
- gate_weight: bfloat16 [2048, 6144], P(('blk', 'head')), may hold values from -0.125 to 0.125
- up_weight: bfloat16 [2048, 6144], P(('blk', 'head')), may hold values from -0.125 to 0.125
- down_weight: bfloat16 [6144, 2048], P(('blk', 'head')), may hold values from -0.078125 to 0.078125
- stretch_order: int32 [1, 16], replicated, may hold values from 0 to 15, each once within a row
- out_cotangent: bfloat16 [1, 4096, 2048], P(None, ('blk', 'head')), may hold values from -6 to 6
Outputs:
- layer_out: bfloat16 [1, 4096, 2048], P(None, ('blk', 'head'))
- tokens_gradient: bfloat16 [1, 4096, 2048], P(None, ('blk', 'head'))
- attention_norm_gradient: float32 [2048], P(('blk', 'head'))
- query_weight_gradient: float32 [2048, 2048], P(('blk', 'head'))
- key_weight_gradient: float32 [2048, 1024], P(('blk', 'head'))
- value_weight_gradient: float32 [2048, 1024], P(('blk', 'head'))
- query_norm_gradient: float32 [128], P(('blk', 'head'))
- key_norm_gradient: float32 [128], P(('blk', 'head'))
- output_weight_gradient: float32 [2048, 2048], P(('blk', 'head'))
- feedforward_norm_gradient: float32 [2048], P(('blk', 'head'))
- gate_weight_gradient: float32 [2048, 6144], P(('blk', 'head'))
- up_weight_gradient: float32 [2048, 6144], P(('blk', 'head'))
- down_weight_gradient: float32 [6144, 2048], P(('blk', 'head'))
Inputs may be any that keep to these rules, and one draw needn't show every extreme that they name: Each row is an order of the 16 stretches of a sequence: stored slot j holds positions stretch_order[b, j] * 256 to stretch_order[b, j] * 256 + 255.
All inputs are finite; a program needn't handle non-finite values.
Results may differ from a plain program's by a relative error of at most 0.025.
Values may be sent and summed in bfloat16 or wider, within the bound.
No kernel may reach another device: no remote copies, remote signals or barrier semaphores. Data moves between devices by JAX's collectives and lax.ppermute only.
A program may use at most 384 MiB of HBM per device.

v0:
```python
import math

import jax
import jax.numpy as jnp
from jax import lax
from jax.sharding import PartitionSpec as P

QUERY_HEADS = 16
KEY_VALUE_HEADS = 8
HEAD_SIZE = 128


EPS = 1e-06
NEG = -1e30
ROPE_BASE = 1000000.0


def passed_along(value, axis, by):
    count = lax.axis_size(axis)
    return lax.ppermute(value, axis, [(i, (i + by) % count) for i in range(count)])


def norm_rows(inputs, norm_gain):
    return inputs * lax.rsqrt(jnp.mean(inputs * inputs, axis=-1, keepdims=True) + EPS) * norm_gain


def rotary(inputs, phases):
    half_width = inputs.shape[-1] // 2
    cosine = jnp.cos(phases)
    sine_term = jnp.sin(phases)
    first_half = inputs[..., :half_width]
    second_half = inputs[..., half_width:]
    return jnp.concatenate(
        [
            first_half * cosine - second_half * sine_term,
            second_half * cosine + first_half * sine_term,
        ],
        axis=-1,
    )


def angles(positions, head_width):
    half_width = head_width // 2
    frequency = jnp.exp(
        jnp.arange(half_width, dtype=jnp.float32) * (-2.0 * math.log(ROPE_BASE) / head_width)
    )
    return positions.astype(jnp.float32)[..., None, None] * frequency


def token_positions(stretch_order, first_row, row_count, stretch_rows):
    row_index = first_row + jnp.arange(row_count, dtype=jnp.int32)
    slot_index = row_index // stretch_rows
    matches = slot_index[:, None] == jnp.arange(stretch_order.shape[1], dtype=jnp.int32)[None, :]
    picked = jnp.sum(jnp.where(matches[None], stretch_order[:, None, :], 0), axis=-1)
    return picked * stretch_rows + row_index % stretch_rows


def per_device(
    tokens,
    attention_norm,
    query_weight,
    key_projection,
    value_projection,
    query_norm,
    key_norm,
    output_weight,
    feedforward_norm,
    gate_weight,
    up_weight,
    down_weight,
    stretch_order,
    out_cotangent,
):
    count_of_heads = lax.axis_size("head")
    span_count = lax.axis_size("blk")
    span_index = lax.axis_index("blk")
    head_index = lax.axis_index("head")
    sequence_total = tokens.shape[0]
    local_rows = tokens.shape[1]
    group_rows = local_rows * count_of_heads
    stretch_rows = group_rows // 2
    heads_shared = KEY_VALUE_HEADS // count_of_heads
    heads_per_group = QUERY_HEADS // KEY_VALUE_HEADS
    score_scale = 1.0 / math.sqrt(HEAD_SIZE)
    gain_one, query_matrix, key_matrix, value_matrix, query_gain, key_gain, output_matrix = (
        lax.all_gather(attention_norm, ("blk", "head"), axis=0, tiled=True),
        lax.all_gather(query_weight, ("blk", "head"), axis=0, tiled=True),
        lax.all_gather(key_projection, ("blk", "head"), axis=0, tiled=True),
        lax.all_gather(value_projection, ("blk", "head"), axis=0, tiled=True),
        lax.all_gather(query_norm, ("blk", "head"), axis=0, tiled=True),
        lax.all_gather(key_norm, ("blk", "head"), axis=0, tiled=True),
        lax.all_gather(output_weight, ("blk", "head"), axis=0, tiled=True),
    )
    gain_two, gate_matrix, up_matrix, down_matrix = (
        lax.all_gather(feedforward_norm, ("blk", "head"), axis=0, tiled=True),
        lax.all_gather(gate_weight, ("blk", "head"), axis=0, tiled=True),
        lax.all_gather(up_weight, ("blk", "head"), axis=0, tiled=True),
        lax.all_gather(down_weight, ("blk", "head"), axis=0, tiled=True),
    )
    gain_one = gain_one.astype(jnp.float32)
    gain_two = gain_two.astype(jnp.float32)
    query_gain = query_gain.astype(jnp.float32)
    key_gain = key_gain.astype(jnp.float32)
    own_first = (span_index * count_of_heads + head_index) * local_rows
    own_pos = token_positions(stretch_order, own_first, local_rows, stretch_rows)
    group_pos = token_positions(stretch_order, span_index * group_rows, group_rows, stretch_rows)
    phases = angles(own_pos, HEAD_SIZE)
    tokens_wide = tokens.astype(jnp.float32)
    first_normed, norm_one_back = jax.vjp(norm_rows, tokens_wide, gain_one)
    first_normed = first_normed.astype(jnp.bfloat16)
    query_raw = jnp.einsum(
        "btd,de->bte", first_normed, query_matrix, preferred_element_type=jnp.float32
    ).reshape(sequence_total, local_rows, QUERY_HEADS, HEAD_SIZE)
    key_unnormed = jnp.einsum(
        "btd,de->bte", first_normed, key_matrix, preferred_element_type=jnp.float32
    ).reshape(sequence_total, local_rows, KEY_VALUE_HEADS, HEAD_SIZE)
    value_tokens = (
        jnp.einsum("btd,de->bte", first_normed, value_matrix, preferred_element_type=jnp.float32)
        .astype(jnp.bfloat16)
        .reshape(sequence_total, local_rows, KEY_VALUE_HEADS, HEAD_SIZE)
    )

    def heads_local(query_in, key_in, query_scale, key_scale):
        return (
            rotary(norm_rows(query_in, query_scale), phases),
            rotary(norm_rows(key_in, key_scale), phases),
        )

    (query_tokens, key_tokens), heads_back = jax.vjp(
        heads_local, query_raw, key_unnormed, query_gain, key_gain
    )
    query_tokens = query_tokens.astype(jnp.bfloat16)
    key_tokens = key_tokens.astype(jnp.bfloat16)
    query_group, key_group, value_group = (
        lax.all_to_all(query_tokens, "head", split_axis=2, concat_axis=1, tiled=True),
        lax.all_to_all(key_tokens, "head", split_axis=2, concat_axis=1, tiled=True),
        lax.all_to_all(value_tokens, "head", split_axis=2, concat_axis=1, tiled=True),
    )
    query_five = query_group.reshape(
        sequence_total, group_rows, heads_shared, heads_per_group, HEAD_SIZE
    )

    def block_update(carry, key_block, value_block, key_pos):
        run_max, run_sum, run_total = carry
        scores = (
            jnp.einsum(
                "bqkgd,bckd->bkgqc", query_five, key_block, preferred_element_type=jnp.float32
            )
            * score_scale
        )
        allowed = key_pos[:, None, None, None, :] <= group_pos[:, None, None, :, None]
        scores = jnp.where(allowed, scores, NEG)
        new_max = jnp.maximum(run_max, jnp.max(scores, axis=-1))
        exponent = jnp.where(allowed, jnp.exp(scores - new_max[..., None]), 0.0)
        factor = jnp.exp(run_max - new_max)
        new_sum = run_sum * factor + jnp.sum(exponent, axis=-1)
        new_total = run_total * factor[..., None] + jnp.einsum(
            "bkgqc,bckd->bkgqd",
            exponent.astype(jnp.bfloat16),
            value_block,
            preferred_element_type=jnp.float32,
        )
        return (new_max, new_sum, new_total)

    def fold_update(carry, key_block, value_block, key_pos):
        result = block_update(carry, key_block, value_block, key_pos)
        return result

    stat_shape = (sequence_total, heads_shared, heads_per_group, group_rows)
    start_state = (
        jnp.full(stat_shape, NEG, jnp.float32),
        jnp.zeros(stat_shape, jnp.float32),
        jnp.zeros(stat_shape + (HEAD_SIZE,), jnp.float32),
    )
    key_piece = lax.all_gather(key_group, "blk", axis=1, tiled=True)
    value_piece = lax.all_gather(value_group, "blk", axis=1, tiled=True)
    piece_rows = key_piece.shape[1]
    block_len = math.gcd(group_rows, piece_rows)

    def inner(block_number, carry_in):
        offset = block_number * block_len
        key_block = lax.dynamic_slice_in_dim(key_piece, offset, block_len, 1)
        value_block = lax.dynamic_slice_in_dim(value_piece, offset, block_len, 1)
        key_pos = token_positions(stretch_order, offset, block_len, stretch_rows)
        return fold_update(carry_in, key_block, value_block, key_pos)

    run_max, run_sum, run_total = lax.fori_loop(0, piece_rows // block_len, inner, start_state)
    log_total = run_max + jnp.log(run_sum)
    attended_five = run_total / run_sum[..., None]
    attended_group = (
        jnp.transpose(attended_five, (0, 3, 1, 2, 4))
        .reshape(sequence_total, group_rows, heads_shared * heads_per_group, HEAD_SIZE)
        .astype(jnp.bfloat16)
    )
    attended_tokens = lax.all_to_all(
        attended_group, "head", split_axis=1, concat_axis=2, tiled=True
    ).reshape(sequence_total, local_rows, QUERY_HEADS * HEAD_SIZE)
    branch = jnp.einsum(
        "bte,ed->btd", attended_tokens, output_matrix, preferred_element_type=jnp.float32
    )
    resid = tokens_wide + branch
    normed_two, norm_two_back = jax.vjp(norm_rows, resid, gain_two)
    normed_two = normed_two.astype(jnp.bfloat16)
    gate = jnp.einsum("btd,df->btf", normed_two, gate_matrix, preferred_element_type=jnp.float32)
    up_proj = jnp.einsum("btd,df->btf", normed_two, up_matrix, preferred_element_type=jnp.float32)

    def swish_product(gate_in, up_in):
        return jax.nn.silu(gate_in) * up_in

    hidden, swish_back = jax.vjp(swish_product, gate, up_proj)
    hidden = hidden.astype(jnp.bfloat16)
    layer_out = (
        resid + jnp.einsum("btf,fd->btd", hidden, down_matrix, preferred_element_type=jnp.float32)
    ).astype(jnp.bfloat16)
    gain_again, gate_matrix, up_matrix, down_matrix = (
        lax.all_gather(feedforward_norm, ("blk", "head"), axis=0, tiled=True),
        lax.all_gather(gate_weight, ("blk", "head"), axis=0, tiled=True),
        lax.all_gather(up_weight, ("blk", "head"), axis=0, tiled=True),
        lax.all_gather(down_weight, ("blk", "head"), axis=0, tiled=True),
    )
    down_gradient = jnp.einsum(
        "btf,btd->fd", hidden, out_cotangent, preferred_element_type=jnp.float32
    )
    hidden_gradient = jnp.einsum(
        "btd,fd->btf", out_cotangent, down_matrix, preferred_element_type=jnp.float32
    )
    gate_gradient, up_gradient = swish_back(hidden_gradient)
    gate_gradient = gate_gradient.astype(jnp.bfloat16)
    up_gradient = up_gradient.astype(jnp.bfloat16)
    gate_matrix_gradient = jnp.einsum(
        "btd,btf->df", normed_two, gate_gradient, preferred_element_type=jnp.float32
    )
    up_matrix_gradient = jnp.einsum(
        "btd,btf->df", normed_two, up_gradient, preferred_element_type=jnp.float32
    )
    normed_two_gradient = jnp.einsum(
        "btf,df->btd", gate_gradient, gate_matrix, preferred_element_type=jnp.float32
    ) + jnp.einsum("btf,df->btd", up_gradient, up_matrix, preferred_element_type=jnp.float32)
    resid_part, gain_two_gradient = norm_two_back(normed_two_gradient)
    resid_gradient = out_cotangent.astype(jnp.float32) + resid_part
    feedforward_sums = (
        lax.psum_scatter(gain_two_gradient, ("blk", "head"), scatter_dimension=0, tiled=True),
        lax.psum_scatter(gate_matrix_gradient, ("blk", "head"), scatter_dimension=0, tiled=True),
        lax.psum_scatter(up_matrix_gradient, ("blk", "head"), scatter_dimension=0, tiled=True),
        lax.psum_scatter(down_gradient, ("blk", "head"), scatter_dimension=0, tiled=True),
    )
    gain_again, query_matrix, key_matrix, value_matrix, query_again, key_again, output_matrix = (
        lax.all_gather(attention_norm, ("blk", "head"), axis=0, tiled=True),
        lax.all_gather(query_weight, ("blk", "head"), axis=0, tiled=True),
        lax.all_gather(key_projection, ("blk", "head"), axis=0, tiled=True),
        lax.all_gather(value_projection, ("blk", "head"), axis=0, tiled=True),
        lax.all_gather(query_norm, ("blk", "head"), axis=0, tiled=True),
        lax.all_gather(key_norm, ("blk", "head"), axis=0, tiled=True),
        lax.all_gather(output_weight, ("blk", "head"), axis=0, tiled=True),
    )
    branch_gradient = resid_gradient.astype(jnp.bfloat16)
    output_matrix_gradient = jnp.einsum(
        "bte,btd->ed", attended_tokens, branch_gradient, preferred_element_type=jnp.float32
    )
    attended_gradient = (
        jnp.einsum(
            "btd,ed->bte", branch_gradient, output_matrix, preferred_element_type=jnp.float32
        )
        .astype(jnp.bfloat16)
        .reshape(sequence_total, local_rows, QUERY_HEADS, HEAD_SIZE)
    )
    attended_grad_group = lax.all_to_all(
        attended_gradient, "head", split_axis=2, concat_axis=1, tiled=True
    ).reshape(sequence_total, group_rows, heads_shared, heads_per_group, HEAD_SIZE)
    delta = jnp.sum(
        jnp.transpose(attended_grad_group.astype(jnp.float32), (0, 2, 3, 1, 4)) * attended_five,
        axis=-1,
    )

    def block_grads(sums_in, key_current, value_current, key_pos):
        key_sum, value_sum, query_sum = sums_in
        scores = (
            jnp.einsum(
                "bqkgd,bckd->bkgqc", query_five, key_current, preferred_element_type=jnp.float32
            )
            * score_scale
        )
        allowed = key_pos[:, None, None, None, :] <= group_pos[:, None, None, :, None]
        weights = jnp.where(allowed, jnp.exp(scores - log_total[..., None]), 0.0)
        probs = weights.astype(jnp.bfloat16)
        value_sum = value_sum + jnp.einsum(
            "bkgqc,bqkgd->bckd", probs, attended_grad_group, preferred_element_type=jnp.float32
        )
        probs_gradient = jnp.einsum(
            "bqkgd,bckd->bkgqc",
            attended_grad_group,
            value_current,
            preferred_element_type=jnp.float32,
        )
        scores_gradient = (weights * (probs_gradient - delta[..., None])).astype(jnp.bfloat16)
        query_sum = (
            query_sum
            + jnp.einsum(
                "bkgqc,bckd->bqkgd",
                scores_gradient,
                key_current,
                preferred_element_type=jnp.float32,
            )
            * score_scale
        )
        key_sum = (
            key_sum
            + jnp.einsum(
                "bkgqc,bqkgd->bckd", scores_gradient, query_five, preferred_element_type=jnp.float32
            )
            * score_scale
        )
        return (key_sum, value_sum, query_sum)

    def pass_step(step_index, carry):
        key_current, value_current, key_sum, value_sum, query_sum = carry
        anchor = (span_index - step_index) % span_count
        key_pos = token_positions(stretch_order, anchor * group_rows, group_rows, stretch_rows)
        key_sum, value_sum, query_sum = block_grads(
            (key_sum, value_sum, query_sum), key_current, value_current, key_pos
        )
        key_current, value_current = passed_along((key_current, value_current), "blk", 1)
        key_sum, value_sum = (
            passed_along(key_sum.astype(jnp.bfloat16), "blk", 1).astype(key_sum.dtype),
            passed_along(value_sum.astype(jnp.bfloat16), "blk", 1).astype(value_sum.dtype),
        )
        return (key_current, value_current, key_sum, value_sum, query_sum)

    kv_zeros = jnp.zeros((sequence_total, group_rows, heads_shared, HEAD_SIZE), jnp.float32)
    query_zeros = jnp.zeros(
        (sequence_total, group_rows, heads_shared, heads_per_group, HEAD_SIZE), jnp.float32
    )
    final_state = lax.fori_loop(
        0, span_count, pass_step, (key_group, value_group, kv_zeros, kv_zeros, query_zeros)
    )
    key_grad_group = final_state[2].astype(jnp.bfloat16)
    value_grad_group = final_state[3].astype(jnp.bfloat16)
    query_grad_group = (
        final_state[4]
        .astype(jnp.bfloat16)
        .reshape(sequence_total, group_rows, heads_shared * heads_per_group, HEAD_SIZE)
    )
    query_grad_tokens, key_grad_tokens, value_gradient_tokens = (
        lax.all_to_all(query_grad_group, "head", split_axis=1, concat_axis=2, tiled=True),
        lax.all_to_all(key_grad_group, "head", split_axis=1, concat_axis=2, tiled=True),
        lax.all_to_all(value_grad_group, "head", split_axis=1, concat_axis=2, tiled=True),
    )
    query_raw_gradient, key_unnormed_gradient, query_gain_gradient, key_gain_gradient = heads_back(
        (query_grad_tokens.astype(jnp.float32), key_grad_tokens.astype(jnp.float32))
    )
    query_raw_gradient = query_raw_gradient.astype(jnp.bfloat16).reshape(
        sequence_total, local_rows, QUERY_HEADS * HEAD_SIZE
    )
    key_unnormed_gradient = key_unnormed_gradient.astype(jnp.bfloat16).reshape(
        sequence_total, local_rows, KEY_VALUE_HEADS * HEAD_SIZE
    )
    value_unnormed_gradient = value_gradient_tokens.reshape(
        sequence_total, local_rows, KEY_VALUE_HEADS * HEAD_SIZE
    )
    query_matrix_gradient = jnp.einsum(
        "btd,bte->de", first_normed, query_raw_gradient, preferred_element_type=jnp.float32
    )
    key_matrix_gradient = jnp.einsum(
        "btd,bte->de", first_normed, key_unnormed_gradient, preferred_element_type=jnp.float32
    )
    value_matrix_gradient = jnp.einsum(
        "btd,bte->de", first_normed, value_unnormed_gradient, preferred_element_type=jnp.float32
    )
    normed_one_gradient = jnp.einsum(
        "bte,de->btd", query_raw_gradient, query_matrix, preferred_element_type=jnp.float32
    )
    normed_one_gradient = normed_one_gradient + jnp.einsum(
        "bte,de->btd", key_unnormed_gradient, key_matrix, preferred_element_type=jnp.float32
    )
    normed_one_gradient = normed_one_gradient + jnp.einsum(
        "bte,de->btd", value_unnormed_gradient, value_matrix, preferred_element_type=jnp.float32
    )
    token_part, gain_one_gradient = norm_one_back(normed_one_gradient)
    tokens_gradient = (resid_gradient + token_part).astype(jnp.bfloat16)
    attention_sums = (
        lax.psum_scatter(gain_one_gradient, ("blk", "head"), scatter_dimension=0, tiled=True),
        lax.psum_scatter(query_matrix_gradient, ("blk", "head"), scatter_dimension=0, tiled=True),
        lax.psum_scatter(key_matrix_gradient, ("blk", "head"), scatter_dimension=0, tiled=True),
        lax.psum_scatter(value_matrix_gradient, ("blk", "head"), scatter_dimension=0, tiled=True),
        lax.psum_scatter(query_gain_gradient, ("blk", "head"), scatter_dimension=0, tiled=True),
        lax.psum_scatter(key_gain_gradient, ("blk", "head"), scatter_dimension=0, tiled=True),
        lax.psum_scatter(output_matrix_gradient, ("blk", "head"), scatter_dimension=0, tiled=True),
    )
    return (
        layer_out,
        tokens_gradient,
        attention_sums[0],
        attention_sums[1],
        attention_sums[2],
        attention_sums[3],
        attention_sums[4],
        attention_sums[5],
        attention_sums[6],
        feedforward_sums[0],
        feedforward_sums[1],
        feedforward_sums[2],
        feedforward_sums[3],
    )


def solution(mesh):
    placed = (
        P(None, ("blk", "head"), None),
        P(("blk", "head")),
        P(("blk", "head"), None),
        P(("blk", "head"), None),
        P(("blk", "head"), None),
        P(("blk", "head")),
        P(("blk", "head")),
        P(("blk", "head"), None),
        P(("blk", "head")),
        P(("blk", "head"), None),
        P(("blk", "head"), None),
        P(("blk", "head"), None),
        P(),
        P(None, ("blk", "head"), None),
    )
    return jax.shard_map(
        per_device,
        mesh=mesh,
        in_specs=placed,
        out_specs=(
            P(None, ("blk", "head"), None),
            P(None, ("blk", "head"), None),
            P(("blk", "head")),
            P(("blk", "head"), None),
            P(("blk", "head"), None),
            P(("blk", "head"), None),
            P(("blk", "head")),
            P(("blk", "head")),
            P(("blk", "head"), None),
            P(("blk", "head")),
            P(("blk", "head"), None),
            P(("blk", "head"), None),
            P(("blk", "head"), None),
        ),
        check_vma=False,
    )
```

profile of v0, /device:TPU:0, one launch (start us, length us, event | category | flops | bytes accessed | tf_op | source)
XLA Modules:
  0.0 3159.3 jit_solution(2925224750232870461)
XLA Ops:
  12.9 42.2 %all-reduce.13 = (bf16[2048]{0:T(1024)(128)(2,1)S(1)}, bf16[128]{0:T(256)(128)(2,1)S(1)}, bf16[128]{0:T(256)(128)(2,1)S(1)}, bf16[2048]{0:T(1024)(128)(2,1)S(1)}) all-reduce(bf16[2048]{0:T(1024)(128)(2,1)S(1)} %dynamic-update-slice, bf16[128]{0:T(256)(128)(2,1)S(1)} %dynamic-update-slice.1, ...), channel_id=1, replica_groups=mesh['blk'=8,'head'=4] {'blk','head'}, use_global_device_ids=true, to_apply=%add.4 | all-reduce | flops 4352 | bytes 17408
  57.3 18.0 all-gather.10.cloned.1.call-done
  89.0 49.7 %all-gather.16.cloned.1.call-done = bf16[2048,1024]{1,0:T(8,128)(2,1)} async-done(((bf16[64,1024]{1,0:T(8,128)(2,1)}), bf16[2048,1024]{1,0:T(8,128)(2,1)}) %all-gather.16.cloned.1.call-update) | async-done | bytes 4194320 | tf_op jit(solution)/shard_map/all_gather | solution.py:89
  154.0 63.4 %all-gather.14.cloned.1.call-done = bf16[2048,2048]{1,0:T(8,128)(2,1)} async-done(((bf16[64,2048]{1,0:T(8,128)(2,1)}), bf16[2048,2048]{1,0:T(8,128)(2,1)}) %all-gather.14.cloned.1.call-update) | async-done | bytes 8388624 | tf_op jit(solution)/shard_map/all_gather | solution.py:87
  238.3 28.9 all-gather.12.cloned.1.call-done
  267.2 49.7 %all-gather.18.cloned.1.call-done = bf16[1,4096,2,128]{3,1,2,0:T(8,128)(2,1)} async-done(((bf16[1,512,2,128]{3,1,2,0:T(8,128)(2,1)}), bf16[1,4096,2,128]{3,1,2,0:T(8,128)(2,1)}) %all-gather.18.cloned.1.call-update) | async-done | bytes 2097168 | tf_op jit(solution)/shard_map/all_gather | solution.py:176
  316.8 83.7 %while.45 = (s32[]{:T(128)}, f32[1,2,2,512]{3,2,1,0:T(2,128)S(1)}, f32[1,2,2,512]{3,2,1,0:T(2,128)S(1)}, f32[1,2,2,512,128]{4,3,2,1,0:T(8,128)S(1)}, s32[1,16]{1...) while((s32[]{:T(128)}, f32[1,2,2,512]{3,2,1,0:T(2,128)S(1)}, ...), condition=%wide.region_9.10_spmd.clone, body=%wide.region_5.9_spmd.clone.sunk | while | flops 551602688 | bytes 33700136 | solution.py:187
  425.2 128.1 %all-gather.22.cloned.1.call-done = bf16[2048,6144]{1,0:T(8,128)(2,1)} async-done(((bf16[64,6144]{1,0:T(8,128)(2,1)}), bf16[2048,6144]{1,0:T(8,128)(2,1)}) %all-gather.22.cloned.1.call-update) | async-done | bytes 25165840 | tf_op jit(solution)/shard_map/all_gather | solution.py:96
  566.5 141.9 %all-gather.24.cloned.1.call-done = bf16[2048,6144]{1,0:T(8,128)(2,1)} async-done(((bf16[64,6144]{1,0:T(8,128)(2,1)}), bf16[2048,6144]{1,0:T(8,128)(2,1)}) %all-gather.24.cloned.1.call-update) | async-done | bytes 25165840 | tf_op jit(solution)/shard_map/all_gather | solution.py:97
  721.7 141.9 %all-gather.26.cloned.1.call-done = bf16[6144,2048]{1,0:T(8,128)(2,1)} async-done(((bf16[192,2048]{1,0:T(8,128)(2,1)}), bf16[6144,2048]{1,0:T(8,128)(2,1)}) %all-gather.26.cloned.1.call-update) | async-done | bytes 25165840 | tf_op jit(solution)/shard_map/all_gather | solution.py:98
  863.6 16.4 multiply_convert_fusion
  894.0 15.1 fusion.108
  933.3 227.1 %while.46 = (s32[]{:T(128)}, bf16[1,512,2,128]{3,1,2,0:T(8,128)(2,1)}, bf16[1,512,2,128]{3,1,2,0:T(8,128)(2,1)}, f32[1,512,2,128]{3,1,2,0:T(8,128)}, f32[1,512,2...) while((s32[]{:T(128)}, ...), condition=%wide.region_15.16_spmd.clone, body=%wide.region_13.15_spmd.clone.sunk | while | flops 1354930688 | bytes 54041196 | solution.py:333
  1207.1 19.5 all_to_all.118
  1239.2 21.1 fusion.147
  1260.4 21.2 fusion.148
  1282.6 21.1 fusion.117
  1328.6 40.3 %all-reduce.12 = (f32[2048]{0:T(1024)S(1)}, f32[128]{0:T(128)S(1)}, f32[128]{0:T(128)S(1)}, f32[2048]{0:T(1024)S(1)}) all-reduce(f32[2048]{0:T(1024)S(1)} %get-tuple-element.674, f32[128]{0:T(128)S(1)} %get-tuple-element.672, f32[128]{0:T(128)S(1)} %get-tuple-element.676, ...), channel_id=2, replica_groups=mesh['blk'=8,'head'=4] {'blk','head'}, use_global_device_ids=true, to_apply=%region_20.21.clone | all-reduce | flops 4352 | bytes 34816
  1372.3 102.9 %reduce-scatter.12.cloned.1.call-done = f32[64,1024]{1,0:T(8,128)} async-done(((f32[2048,1024]{1,0:T(8,128)}), f32[64,1024]{1,0:T(8,128)}) %reduce-scatter.12.cloned.1.call-update) | async-done | bytes 262160 | tf_op jit(solution)/shard_map/reduce_scatter | solution.py:384
  1475.3 181.8 %reduce-scatter.14.cloned.1.call-done = f32[64,2048]{1,0:T(8,128)} async-done(((f32[2048,2048]{1,0:T(8,128)}), f32[64,2048]{1,0:T(8,128)}) %reduce-scatter.14.cloned.1.call-update) | async-done | bytes 524304 | tf_op jit(solution)/shard_map/reduce_scatter | solution.py:387
  1657.1 187.5 %reduce-scatter.8.cloned.1.call-done = f32[64,2048]{1,0:T(8,128)} async-done(((f32[2048,2048]{1,0:T(8,128)}), f32[64,2048]{1,0:T(8,128)}) %reduce-scatter.8.cloned.1.call-update) | async-done | bytes 524304 | tf_op jit(solution)/shard_map/reduce_scatter | solution.py:382
  1844.6 437.4 %reduce-scatter.16.cloned.1.call-done = f32[64,6144]{1,0:T(8,128)} async-done(((f32[2048,6144]{1,0:T(8,128)}), f32[64,6144]{1,0:T(8,128)}) %reduce-scatter.16.cloned.1.call-update) | async-done | bytes 1572880 | tf_op jit(solution)/shard_map/reduce_scatter | solution.py:243
  2282.0 435.1 %reduce-scatter.18.cloned.1.call-done = f32[64,6144]{1,0:T(8,128)} async-done(((f32[2048,6144]{1,0:T(8,128)}), f32[64,6144]{1,0:T(8,128)}) %reduce-scatter.18.cloned.1.call-update) | async-done | bytes 1572880 | tf_op jit(solution)/shard_map/reduce_scatter | solution.py:244
  2717.1 435.1 %reduce-scatter.20.cloned.1.call-done = f32[192,2048]{1,0:T(8,128)} async-done(((f32[6144,2048]{1,0:T(8,128)}), f32[192,2048]{1,0:T(8,128)}) %reduce-scatter.20.cloned.1.call-update) | async-done | bytes 1572880 | tf_op jit(solution)/shard_map/reduce_scatter | solution.py:245
  (543 shorter events, 544.5 us)
Async XLA Ops:
  7.2 68.2 %all-gather.10.cloned.1.call-start = ((), (), s32[]{:S(2)}) async-start(), calls=%async_computation.15 | async-start | bytes 4325376 | tf_op jit(solution)/shard_map/all_gather | solution.py:88
  7.9 130.7 %all-gather.16.cloned.1.call-start = ((), (), s32[]{:S(2)}) async-start(), calls=%async_computation.18 | async-start | bytes 4325376 | tf_op jit(solution)/shard_map/all_gather | solution.py:89
  8.7 208.7 %all-gather.14.cloned.1.call-start = ((), (), s32[]{:S(2)}) async-start(), calls=%async_computation.17 | async-start | bytes 8650752 | tf_op jit(solution)/shard_map/all_gather | solution.py:87
  9.4 257.8 %all-gather.12.cloned.1.call-start = ((), (), s32[]{:S(2)}) async-start(), calls=%async_computation.16 | async-start | bytes 2359296 | tf_op jit(solution)/shard_map/all_gather | solution.py:175
  88.9 227.9 %all-gather.18.cloned.1.call-start = ((), (), s32[]{:S(2)}) async-start(), calls=%async_computation.19 | async-start | bytes 2359296 | tf_op jit(solution)/shard_map/all_gather | solution.py:176
  151.0 269.0 %all-gather.20.cloned.1.call-start = ((), (), s32[]{:S(2)}) async-start(), calls=%async_computation.20 | async-start | bytes 8650752 | tf_op jit(solution)/shard_map/all_gather | solution.py:92
  151.6 401.7 %all-gather.22.cloned.1.call-start = ((), (), s32[]{:S(2)}) async-start(), calls=%async_computation.21 | async-start | bytes 25952256 | tf_op jit(solution)/shard_map/all_gather | solution.py:96
  152.4 556.0 %all-gather.24.cloned.1.call-start = ((), (), s32[]{:S(2)}) async-start(), calls=%async_computation.22 | async-start | bytes 25952256 | tf_op jit(solution)/shard_map/all_gather | solution.py:97
  153.1 710.4 %all-gather.26.cloned.1.call-start = ((), (), s32[]{:S(2)}) async-start(), calls=%async_computation.23 | async-start | bytes 25952256 | tf_op jit(solution)/shard_map/all_gather | solution.py:98
  922.0 450.3 %reduce-scatter.10.cloned.1.call-start = ((), (), s32[]{:S(2)}) async-start(), calls=%async_computation.25 | async-start | bytes 8650752 | tf_op jit(solution)/shard_map/reduce_scatter | solution.py:383
  934.5 29.5 collective-permute-start
  964.9 28.2 collective-permute-start
  966.6 26.5 collective-permute-start.1
  994.0 26.7 collective-permute-start
  1021.7 26.7 collective-permute-start
  1049.3 26.5 collective-permute-start
  1076.8 26.8 collective-permute-start
  1131.3 29.1 collective-permute-start
  1176.6 298.6 %reduce-scatter.12.cloned.1.call-start = ((), (), s32[]{:S(2)}) async-start(), calls=%async_computation.26 | async-start | bytes 8650752 | tf_op jit(solution)/shard_map/reduce_scatter | solution.py:384
  1195.8 461.2 %reduce-scatter.14.cloned.1.call-start = ((), (), s32[]{:S(2)}) async-start(), calls=%async_computation.27 | async-start | bytes 17301504 | tf_op jit(solution)/shard_map/reduce_scatter | solution.py:387
  1205.3 639.3 %reduce-scatter.8.cloned.1.call-start = ((), (), s32[]{:S(2)}) async-start(), calls=%async_computation.24 | async-start | bytes 17301504 | tf_op jit(solution)/shard_map/reduce_scatter | solution.py:382
  1238.2 1043.8 %reduce-scatter.16.cloned.1.call-start = ((), (), s32[]{:S(2)}) async-start(), calls=%async_computation.28 | async-start | bytes 51904512 | tf_op jit(solution)/shard_map/reduce_scatter | solution.py:243
  1260.4 1456.8 %reduce-scatter.18.cloned.1.call-start = ((), (), s32[]{:S(2)}) async-start(), calls=%async_computation.29 | async-start | bytes 51904512 | tf_op jit(solution)/shard_map/reduce_scatter | solution.py:244
  1281.6 1870.7 %reduce-scatter.20.cloned.1.call-start = ((), (), s32[]{:S(2)}) async-start(), calls=%async_computation.30 | async-start | bytes 51904512 | tf_op jit(solution)/shard_map/reduce_scatter | solution.py:245
  (101 other events, 2900.3 us)
Sparse Core Ops, SparseCore 0:
  10.9 64.4 all-gather.9
  78.2 60.3 all-gather.15
  141.5 75.8 all-gather.13
  219.4 47.6 all-gather.11
  269.2 47.5 all-gather.17
  319.6 75.5 all-gather.19
  398.1 155.1 all-gather.21
  556.2 152.1 all-gather.23
  711.3 152.2 all-gather.25
  1176.7 147.7 reduce-scatter.9
  1327.4 147.7 reduce-scatter.11
  1478.0 179.0 reduce-scatter.13
  1659.9 184.5 reduce-scatter.7
  1851.4 430.5 reduce-scatter.15
  2288.9 428.2 reduce-scatter.17
  2724.0 428.2 reduce-scatter.19
where the time goes:
time: 3170 us; the launch traced here: 3160 us
  waiting for transfers between devices  2470 us (78%)
  matrix products  370 us (12%)
  blocking collectives  140 us (4%)
  other arithmetic  73.3 us (2%)
  local copies, waits for them, and re-layouts  47.2 us (1%)
  starting transfers between devices  45.8 us (1%)
    reduce_scatter x1, waiting for transfers between devices, per_device(): lax.psum_scatter(gate_matrix_gradient, ('blk', 'head'), scatter_dimension...  437 us
    reduce_scatter x1, waiting for transfers between devices, per_device(): lax.psum_scatter(down_gradient, ('blk', 'head'), scatter_dimension=0, til...  435 us
    reduce_scatter x1, waiting for transfers between devices, per_device(): lax.psum_scatter(up_matrix_gradient, ('blk', 'head'), scatter_dimension=0...  435 us
    reduce_scatter x1, waiting for transfers between devices, per_device(): lax.psum_scatter(query_matrix_gradient, ('blk', 'head'), scatter_dimensio...  188 us
    reduce_scatter x1, waiting for transfers between devices, per_device(): lax.psum_scatter(output_matrix_gradient, ('blk', 'head'), scatter_dimensi...  182 us
    all_gather x1, waiting for transfers between devices, per_device(): lax.all_gather(up_weight, ('blk', 'head'), axis=0, tiled=True)  142 us
    all_gather x1, waiting for transfers between devices, per_device(): lax.all_gather(down_weight, ('blk', 'head'), axis=0, tiled=True)  142 us
    all_gather x1, waiting for transfers between devices, per_device(): lax.all_gather(gate_weight, ('blk', 'head'), axis=0, tiled=True)  128 us
  transfers between devices with their start and end apart: 51, of which 33 were waited for; matrix products, arithmetic and copies ran while one was open for 13% of the time, Pallas kernels for 0%

commit v1 on v0

--- a/solution.py
+++ b/solution.py
@@ -3,6 +3,8 @@
 import jax
 import jax.numpy as jnp
 from jax import lax
+from jax.experimental import pallas as pl
+from jax.experimental.pallas import tpu as pltpu
 from jax.sharding import PartitionSpec as P
 
 QUERY_HEADS = 16
@@ -55,7 +57,7 @@
     return picked * stretch_rows + row_index % stretch_rows
 
 
-def per_device(
+def per_device_by_tokens(
     tokens,
     attention_norm,
     query_weight,
@@ -403,6 +405,495 @@
     )
 
 
+LOG2E = math.log2(math.e)
+STRIP = 128
+CHUNK = 512
+ALONG = (((1,), (1,)), ((), ()))
+DOWN = (((0,), (0,)), ((), ()))
+
+
+def two_heads(block):
+    return jnp.concatenate([block[:, :HEAD_SIZE], block[:, HEAD_SIZE:]], axis=0)
+
+
+def side_by_side(rows):
+    half = rows.shape[0] // 2
+    return jnp.concatenate([rows[:half], rows[half:]], axis=1)
+
+
+def attend_kernel(place_ref, order_ref, q_ref, kv_ref, out_ref, lse_ref, keys, values):
+    step = pl.program_id(0)
+
+    @pl.when(step == 0)
+    def _():
+        values[:, HEAD_SIZE:] = jnp.ones((values.shape[0], HEAD_SIZE), jnp.bfloat16)
+
+        def sort(index, carry):
+            source = pl.multiple_of(order_ref[index] * STRIP, STRIP)
+            target = pl.multiple_of(index * STRIP, STRIP)
+            keys[pl.ds(target, STRIP), :] = kv_ref[pl.ds(source, STRIP), :HEAD_SIZE]
+            values[pl.ds(target, STRIP), :HEAD_SIZE] = kv_ref[pl.ds(source, STRIP), HEAD_SIZE:]
+            return carry
+
+        lax.fori_loop(0, kv_ref.shape[0] // STRIP, sort, 0)
+
+    place = place_ref[step]
+    queries = two_heads(q_ref[...])
+    last = place // (CHUNK // STRIP)
+
+    def part(index, total, masked):
+        first = pl.multiple_of(index * CHUNK, CHUNK)
+        scores = lax.dot_general(
+            queries, keys[pl.ds(first, CHUNK), :], ALONG, preferred_element_type=jnp.float32
+        )
+        weights = jnp.exp2(scores)
+        if masked:
+            row = lax.broadcasted_iota(jnp.int32, scores.shape, 0) % STRIP
+            column = lax.broadcasted_iota(jnp.int32, scores.shape, 1)
+            weights = jnp.where(column - row <= place * STRIP - first, weights, 0.0)
+        return total + jnp.dot(
+            weights.astype(jnp.bfloat16),
+            values[pl.ds(first, CHUNK), :],
+            preferred_element_type=jnp.float32,
+        )
+
+    total = jnp.zeros((2 * STRIP, 2 * HEAD_SIZE), jnp.float32)
+    total = lax.fori_loop(0, last, lambda index, t: part(index, t, False), total)
+    total = part(last, total, True)
+    norm = total[:, HEAD_SIZE:]
+    out_ref[...] = side_by_side(total[:, :HEAD_SIZE] / norm).astype(jnp.bfloat16)
+    lse_ref[0] = jnp.transpose(jnp.log2(norm))[:8]
+
+
+def attend(place, order, queries, kv):
+    rows, width = queries.shape
+    steps = rows // STRIP
+    whole = pl.BlockSpec(kv.shape, lambda i, *_: (0, 0))
+    strip = pl.BlockSpec((STRIP, width), lambda i, *_: (i, 0))
+    flops = 4 * rows * 2 * kv.shape[0] * HEAD_SIZE // 2
+    return pl.pallas_call(
+        attend_kernel,
+        grid_spec=pltpu.PrefetchScalarGridSpec(
+            num_scalar_prefetch=2,
+            grid=(steps,),
+            in_specs=[strip, whole],
+            out_specs=[strip, pl.BlockSpec((1, 8, 2 * STRIP), lambda i, *_: (i, 0, 0))],
+            scratch_shapes=[
+                pltpu.VMEM((kv.shape[0], HEAD_SIZE), jnp.bfloat16),
+                pltpu.VMEM((kv.shape[0], 2 * HEAD_SIZE), jnp.bfloat16),
+            ],
+        ),
+        out_shape=[
+            jax.ShapeDtypeStruct((rows, width), jnp.bfloat16),
+            jax.ShapeDtypeStruct((steps, 8, 2 * STRIP), jnp.float32),
+        ],
+        cost_estimate=pl.CostEstimate(
+            flops=flops, bytes_accessed=kv.size * 2 + queries.size * 4, transcendentals=rows * kv.shape[0]
+        ),
+        name="attend",
+    )(place, order, queries, kv)
+
+
+def attend_back_kernel(
+    place_ref, order_ref, q_ref, grad_ref, out_ref, lse_ref, kv_ref, dq_ref, dkv_ref,
+    keys, values, key_sums, value_sums,
+):
+    step = pl.program_id(0)
+    strips = kv_ref.shape[0] // STRIP
+
+    @pl.when(step == 0)
+    def _():
+        key_sums[...] = jnp.zeros_like(key_sums)
+        value_sums[...] = jnp.zeros_like(value_sums)
+
+        def sort(index, carry):
+            source = pl.multiple_of(order_ref[index] * STRIP, STRIP)
+            target = pl.multiple_of(index * STRIP, STRIP)
+            keys[pl.ds(target, STRIP), :] = kv_ref[pl.ds(source, STRIP), :HEAD_SIZE]
+            values[pl.ds(target, STRIP), :] = kv_ref[pl.ds(source, STRIP), HEAD_SIZE:]
+            return carry
+
+        lax.fori_loop(0, strips, sort, 0)
+
+    place = place_ref[step]
+    queries = two_heads(q_ref[...])
+    grads = two_heads(grad_ref[...])
+    product = grads.astype(jnp.float32) * two_heads(out_ref[...]).astype(jnp.float32)
+    delta = jnp.sum(jnp.transpose(product), axis=0, keepdims=True)
+    lse = lse_ref[0, :1]
+    last = place // (CHUNK // STRIP)
+
+    def part(index, total, masked):
+        first = pl.multiple_of(index * CHUNK, CHUNK)
+        here = pl.ds(first, CHUNK)
+        key_rows = keys[here, :]
+        scores = lax.dot_general(key_rows, queries, ALONG, preferred_element_type=jnp.float32)
+        weights = jnp.exp2(scores - lse)
+        if masked:
+            row = lax.broadcasted_iota(jnp.int32, scores.shape, 0)
+            column = lax.broadcasted_iota(jnp.int32, scores.shape, 1) % STRIP
+            weights = jnp.where(row - column <= place * STRIP - first, weights, 0.0)
+        slopes = lax.dot_general(
+            values[here, :], grads, ALONG, preferred_element_type=jnp.float32
+        )
+        score_grads = (weights * (slopes - delta)).astype(jnp.bfloat16)
+        value_sums[here, :] += jnp.dot(
+            weights.astype(jnp.bfloat16), grads, preferred_element_type=jnp.float32
+        )
+        key_sums[here, :] += jnp.dot(score_grads, queries, preferred_element_type=jnp.float32)
+        return total + lax.dot_general(
+            score_grads, key_rows, DOWN, preferred_element_type=jnp.float32
+        )
+
+    total = jnp.zeros((2 * STRIP, HEAD_SIZE), jnp.float32)
+    total = lax.fori_loop(0, last, lambda index, t: part(index, t, False), total)
+    total = part(last, total, True)
+    dq_ref[...] = side_by_side(total * (1.0 / math.sqrt(HEAD_SIZE))).astype(jnp.bfloat16)
+
+    @pl.when(step == pl.num_programs(0) - 1)
+    def _():
+        def spread(index, carry):
+            target = pl.multiple_of(order_ref[index] * STRIP, STRIP)
+            source = pl.multiple_of(index * STRIP, STRIP)
+            dkv_ref[pl.ds(target, STRIP), :HEAD_SIZE] = (
+                key_sums[pl.ds(source, STRIP), :] * (1.0 / LOG2E)
+            ).astype(jnp.bfloat16)
+            dkv_ref[pl.ds(target, STRIP), HEAD_SIZE:] = value_sums[
+                pl.ds(source, STRIP), :
+            ].astype(jnp.bfloat16)
+            return carry
+
+        lax.fori_loop(0, strips, spread, 0)
+
+
+def attend_back(place, order, queries, grads, attended, lse, kv):
+    rows, width = queries.shape
+    steps = rows // STRIP
+    total = kv.shape[0]
+    whole = pl.BlockSpec(kv.shape, lambda i, *_: (0, 0))
+    strip = pl.BlockSpec((STRIP, width), lambda i, *_: (i, 0))
+    return pl.pallas_call(
+        attend_back_kernel,
+        grid_spec=pltpu.PrefetchScalarGridSpec(
+            num_scalar_prefetch=2,
+            grid=(steps,),
+            in_specs=[
+                strip, strip, strip, pl.BlockSpec((1, 8, 2 * STRIP), lambda i, *_: (i, 0, 0)), whole,
+            ],
+            out_specs=[strip, whole],
+            scratch_shapes=[
+                pltpu.VMEM((total, HEAD_SIZE), jnp.bfloat16),
+                pltpu.VMEM((total, HEAD_SIZE), jnp.bfloat16),
+                pltpu.VMEM((total, HEAD_SIZE), jnp.float32),
+                pltpu.VMEM((total, HEAD_SIZE), jnp.float32),
+            ],
+        ),
+        out_shape=[
+            jax.ShapeDtypeStruct((rows, width), jnp.bfloat16),
+            jax.ShapeDtypeStruct(kv.shape, jnp.bfloat16),
+        ],
+        cost_estimate=pl.CostEstimate(
+            flops=10 * rows * 2 * total * HEAD_SIZE // 2,
+            bytes_accessed=kv.size * 4 + queries.size * 8,
+            transcendentals=rows * total,
+        ),
+        name="attend_back",
+    )(place, order, queries, grads, attended, lse, kv)
+
+
+def matmul(left, right, dims=(((1,), (0,)), ((), ()))):
+    return lax.dot_general(left, right, dims, preferred_element_type=jnp.float32)
+
+
+def gather_blk(rows):
+    return lax.all_gather(rows, "blk", axis=0, tiled=True)
+
+
+def scatter_blk(rows):
+    return lax.psum_scatter(rows, "blk", scatter_dimension=0, tiled=True)
+
+
+def exchange_blk(pieces):
+    return lax.all_to_all(pieces, "blk", split_axis=0, concat_axis=0, tiled=True)
+
+
+def gather_head(rows):
+    return lax.all_gather(rows, "head", axis=0, tiled=True)
+
+
+def scatter_head(rows):
+    return lax.psum_scatter(rows, "head", scatter_dimension=0, tiled=True)
+
+
+def inverse_rms(rows):
+    return lax.rsqrt(jnp.mean(rows * rows, axis=-1, keepdims=True) + EPS)
+
+
+def per_device(
+    tokens,
+    attention_norm,
+    query_weight,
+    key_projection,
+    value_projection,
+    query_norm,
+    key_norm,
+    output_weight,
+    feedforward_norm,
+    gate_weight,
+    up_weight,
+    down_weight,
+    stretch_order,
+    out_cotangent,
+):
+    blk_count = lax.axis_size("blk")
+    head_count = lax.axis_size("head")
+    head_index = lax.axis_index("head")
+    narrow, wide = jnp.bfloat16, jnp.float32
+    tokens, out_cotangent = tokens[0], out_cotangent[0]
+    local_rows, model_width = tokens.shape
+    group_rows = local_rows * blk_count
+    weight_rows = query_weight.shape[0]
+    ff_local = gate_weight.shape[1] // blk_count
+    group_heads = QUERY_HEADS // blk_count
+    query_cols = group_heads * HEAD_SIZE
+    attn_cols = query_cols + 2 * HEAD_SIZE
+    strip_count = blk_count * head_count
+    halves = strip_count // stretch_order.shape[1]
+
+    def by_head(rows):
+        shape = (rows.shape[0], blk_count, head_count, weight_rows)
+        return rows.reshape(shape).transpose(0, 2, 1, 3).reshape(rows.shape)
+
+    def by_blk(rows):
+        shape = (rows.shape[0], head_count, blk_count, weight_rows)
+        return rows.reshape(shape).transpose(0, 2, 1, 3).reshape(rows.shape)
+
+    attn_pieces = jnp.concatenate(
+        [
+            query_weight.reshape(weight_rows, blk_count, query_cols),
+            key_projection.reshape(weight_rows, blk_count, HEAD_SIZE),
+            value_projection.reshape(weight_rows, blk_count, HEAD_SIZE),
+        ],
+        axis=2,
+    ).transpose(1, 0, 2)
+    small = query_norm.shape[0]
+    gains = jnp.concatenate([attention_norm, feedforward_norm, query_norm, key_norm])
+    gains = jnp.pad(gains, (0, attn_cols - gains.shape[0]))[None, None, :]
+    gains = jnp.pad(gains, ((0, 0), (0, 15), (0, 0)))
+    attn_pieces = jnp.concatenate(
+        [attn_pieces, jnp.broadcast_to(gains, (blk_count, 16, attn_cols))], axis=1
+    )
+    attn_all = gather_head(exchange_blk(attn_pieces)).reshape(
+        head_count, blk_count, weight_rows + 16, attn_cols
+    )
+    attn_matrix = attn_all[:, :, :weight_rows].reshape(model_width, attn_cols)
+    gain_rows = attn_all[:, :, weight_rows]
+    gain_one = gain_rows[:, :, :weight_rows].reshape(1, model_width).astype(wide)
+    gain_two_rows = gain_rows[:, :, weight_rows : 2 * weight_rows].astype(wide)
+    gain_two = gain_two_rows.transpose(1, 0, 2).reshape(1, model_width)
+    gain_one_natural = by_blk(gain_one)
+    at = 2 * weight_rows
+    query_gain = gain_rows[:, :, at : at + small].transpose(1, 0, 2).reshape(HEAD_SIZE)
+    key_gain = gain_rows[:, :, at + small : at + 2 * small].transpose(1, 0, 2).reshape(HEAD_SIZE)
+    query_gain, key_gain = query_gain.astype(wide), key_gain.astype(wide)
+
+    ff_pieces = jnp.concatenate(
+        [
+            gate_weight.reshape(weight_rows, blk_count, ff_local),
+            up_weight.reshape(weight_rows, blk_count, ff_local),
+        ],
+        axis=2,
+    ).transpose(1, 0, 2)
+    ff_matrix = gather_head(exchange_blk(ff_pieces)).reshape(model_width, 2 * ff_local)
+    down_matrix = gather_head(down_weight)
+    output_matrix = lax.all_gather(output_weight, ("blk", "head"), axis=0, tiled=True)
+
+    strip_blk = jnp.arange(strip_count, dtype=jnp.int32) % blk_count
+    strip_head = jnp.arange(strip_count, dtype=jnp.int32) // blk_count
+    strip = strip_blk * head_count + strip_head
+    slots = jnp.arange(stretch_order.shape[1], dtype=jnp.int32)
+    held = jnp.sum(
+        jnp.where((strip // halves)[:, None] == slots[None, :], stretch_order, 0), axis=1
+    )
+    strip_place = held * halves + strip % halves
+    ranks = jnp.arange(strip_count, dtype=jnp.int32)
+    order = jnp.sum(
+        jnp.where(strip_place[None, :] == ranks[:, None], ranks[None, :], 0), axis=1
+    ).astype(jnp.int32)
+    place = jnp.sum(
+        jnp.where(
+            jnp.arange(head_count, dtype=jnp.int32)[:, None] == head_index,
+            strip_place.reshape(head_count, blk_count),
+            0,
+        ),
+        axis=0,
+    ).astype(jnp.int32)
+    positions = (
+        place[:, None] * local_rows + jnp.arange(local_rows, dtype=jnp.int32)[None, :]
+    ).reshape(group_rows)
+    phases = angles(positions, HEAD_SIZE)
+
+    tokens_wide = tokens.astype(wide)
+    group_tokens = gather_blk(by_head(tokens)).astype(wide)
+    first_normed = (group_tokens * inverse_rms(group_tokens) * gain_one).astype(narrow)
+    attn_raw = matmul(first_normed, attn_matrix)
+    query_raw = attn_raw[:, :query_cols].reshape(group_rows, group_heads, HEAD_SIZE)
+    key_raw = attn_raw[:, query_cols : query_cols + HEAD_SIZE].reshape(group_rows, 1, HEAD_SIZE)
+    value_rows = attn_raw[:, query_cols + HEAD_SIZE :].astype(narrow)
+
+    def heads_local(query_in, key_in, query_scale, key_scale):
+        return (
+            rotary(norm_rows(query_in, query_scale), phases),
+            rotary(norm_rows(key_in, key_scale), phases),
+        )
+
+    (query_rows, key_rows), heads_back = jax.vjp(
+        heads_local, query_raw, key_raw, query_gain, key_gain
+    )
+    query_rows = (query_rows * (LOG2E / math.sqrt(HEAD_SIZE))).astype(narrow)
+    query_rows = query_rows.reshape(group_rows, query_cols)
+    kv = jnp.concatenate([key_rows.reshape(group_rows, HEAD_SIZE).astype(narrow), value_rows], 1)
+    kv = gather_head(kv)
+    attended_heads, lse = attend(place, order, query_rows, kv)
+    attended = (
+        exchange_blk(attended_heads.reshape(blk_count, local_rows, query_cols))
+        .transpose(1, 0, 2)
+        .reshape(local_rows, QUERY_HEADS * HEAD_SIZE)
+    )
+
+    resid = tokens_wide + matmul(attended, output_matrix)
+    rho_two = inverse_rms(resid)
+    unit_two = resid * rho_two
+    second_normed = gather_blk(by_head((unit_two * gain_two).astype(narrow)))
+    group_cotangent = gather_blk(out_cotangent)
+    ff_raw = matmul(second_normed, ff_matrix)
+    gate, up_proj = ff_raw[:, :ff_local], ff_raw[:, ff_local:]
+    sigma = jax.nn.sigmoid(gate)
+    swish = gate * sigma
+    hidden = (swish * up_proj).astype(narrow)
+    out_part = scatter_blk(matmul(hidden, down_matrix).astype(narrow))
+    layer_out = (resid + out_part.astype(wide)).astype(narrow)
+
+    hidden_gradient = matmul(group_cotangent, down_matrix, ALONG)
+    gate_gradient = hidden_gradient * up_proj * (sigma * (1.0 + gate * (1.0 - sigma)))
+    ff_gradient = jnp.concatenate([gate_gradient, hidden_gradient * swish], 1).astype(narrow)
+    second_gradient = matmul(ff_gradient, ff_matrix, ALONG).astype(narrow)
+    second_gradient = by_blk(scatter_blk(second_gradient)).astype(wide)
+    down_gradient = scatter_head(matmul(hidden, group_cotangent, DOWN).astype(narrow))
+    ff_matrix_gradient = scatter_head(matmul(second_normed, ff_gradient, DOWN).astype(narrow))
+    ff_matrix_gradient = exchange_blk(
+        ff_matrix_gradient.reshape(blk_count, weight_rows, 2 * ff_local)
+    ).astype(wide)
+    gate_weight_gradient = (
+        ff_matrix_gradient[:, :, :ff_local].transpose(1, 0, 2).reshape(gate_weight.shape)
+    )
+    up_weight_gradient = (
+        ff_matrix_gradient[:, :, ff_local:].transpose(1, 0, 2).reshape(up_weight.shape)
+    )
+    feedforward_norm_gradient = (
+        jnp.sum(gate_weight_gradient * gate_weight.astype(wide), axis=1)
+        + jnp.sum(up_weight_gradient * up_weight.astype(wide), axis=1)
+    ) / feedforward_norm.astype(wide)
+    scaled = gain_two * second_gradient
+    resid_gradient = out_cotangent.astype(wide) + rho_two * (
+        scaled - unit_two * jnp.mean(unit_two * scaled, axis=-1, keepdims=True)
+    )
+
+    branch_gradient = resid_gradient.astype(narrow)
+    attended_gradient = (
+        matmul(branch_gradient, output_matrix, ALONG)
+        .astype(narrow)
+        .reshape(local_rows, blk_count, query_cols)
+        .transpose(1, 0, 2)
+    )
+    attended_gradient = exchange_blk(attended_gradient).reshape(group_rows, query_cols)
+    output_weight_gradient = lax.psum_scatter(
+        matmul(attended, branch_gradient, DOWN).astype(narrow),
+        ("blk", "head"),
+        scatter_dimension=0,
+        tiled=True,
+    ).astype(wide)
+    query_grads, kv_grads = attend_back(
+        place, order, query_rows, attended_gradient, attended_heads, lse, kv
+    )
+    kv_grads = scatter_head(kv_grads)
+    query_raw_gradient, key_raw_gradient, query_gain_part, key_gain_part = heads_back(
+        (
+            query_grads.reshape(group_rows, group_heads, HEAD_SIZE).astype(wide),
+            kv_grads[:, :HEAD_SIZE].reshape(group_rows, 1, HEAD_SIZE).astype(wide),
+        )
+    )
+    attn_gradient = jnp.concatenate(
+        [
+            query_raw_gradient.reshape(group_rows, query_cols).astype(narrow),
+            key_raw_gradient.reshape(group_rows, HEAD_SIZE).astype(narrow),
+            kv_grads[:, HEAD_SIZE:],
+        ],
+        axis=1,
+    )
+    first_gradient = scatter_blk(matmul(attn_gradient, attn_matrix, ALONG).astype(narrow))
+    first_gradient = by_blk(first_gradient).astype(wide)
+    attn_matrix_gradient = (
+        matmul(first_normed, attn_gradient, DOWN)
+        .astype(narrow)
+        .reshape(head_count, blk_count, weight_rows, attn_cols)
+    )
+    gain_parts = jnp.stack(
+        [
+            query_gain_part.reshape(blk_count, head_count, small),
+            key_gain_part.reshape(blk_count, head_count, small),
+        ],
+        axis=2,
+    ).transpose(1, 0, 2, 3)
+    gain_parts = gain_parts.reshape(head_count, blk_count, 1, 2 * small).astype(narrow)
+    gain_parts = jnp.pad(gain_parts, ((0, 0), (0, 0), (0, 15), (0, attn_cols - 2 * small)))
+    attn_matrix_gradient = jnp.concatenate([attn_matrix_gradient, gain_parts], axis=2)
+    attn_matrix_gradient = exchange_blk(
+        scatter_head(
+            attn_matrix_gradient.reshape(head_count * blk_count, weight_rows + 16, attn_cols)
+        )
+    ).astype(wide)
+    attn_rows = attn_matrix_gradient[:, :weight_rows]
+    query_weight_gradient = (
+        attn_rows[:, :, :query_cols].transpose(1, 0, 2).reshape(query_weight.shape)
+    )
+    key_weight_gradient = (
+        attn_rows[:, :, query_cols : query_cols + HEAD_SIZE]
+        .transpose(1, 0, 2)
+        .reshape(key_projection.shape)
+    )
+    value_weight_gradient = (
+        attn_rows[:, :, query_cols + HEAD_SIZE :].transpose(1, 0, 2).reshape(value_projection.shape)
+    )
+    gain_sums = jnp.sum(attn_matrix_gradient[:, weight_rows], axis=0)
+    attention_norm_gradient = (
+        jnp.sum(query_weight_gradient * query_weight.astype(wide), axis=1)
+        + jnp.sum(key_weight_gradient * key_projection.astype(wide), axis=1)
+        + jnp.sum(value_weight_gradient * value_projection.astype(wide), axis=1)
+    ) / attention_norm.astype(wide)
+    rho_one = inverse_rms(tokens_wide)
+    unit_one = tokens_wide * rho_one
+    scaled = gain_one_natural * first_gradient
+    tokens_gradient = resid_gradient + rho_one * (
+        scaled - unit_one * jnp.mean(unit_one * scaled, axis=-1, keepdims=True)
+    )
+    return (
+        layer_out[None],
+        tokens_gradient.astype(narrow)[None],
+        attention_norm_gradient,
+        query_weight_gradient,
+        key_weight_gradient,
+        value_weight_gradient,
+        gain_sums[:small],
+        gain_sums[small : 2 * small],
+        output_weight_gradient,
+        feedforward_norm_gradient,
+        gate_weight_gradient,
+        up_weight_gradient,
+        down_gradient.astype(wide),
+    )
+
+
 def solution(mesh):
     placed = (
         P(None, ("blk", "head"), None),
@@ -420,8 +911,9 @@
         P(),
         P(None, ("blk", "head"), None),
     )
+    fits = mesh.shape["blk"] == KEY_VALUE_HEADS and mesh.shape["head"] == 4
     return jax.shard_map(
-        per_device,
+        per_device if fits else per_device_by_tokens,
         mesh=mesh,
         in_specs=placed,
         out_specs=(

time: 3170 us -> 1180 us (0.37)
  waiting for transfers between devices: 2470 us -> 791 us
  matrix products: 370 us -> 90.4 us
  Pallas kernels: 0 us -> 51.3 us
  starting transfers between devices: 45.8 us -> 9.49 us
  other arithmetic: 73.3 us -> 37.2 us
    reduce_scatter x7 -> x8, waiting for transfers between devices: 1780 us -> 460 us  [the longest x3 244 us: scatter_blk(): return lax.psum_scatter(rows, 'blk', scatter_dimension=0, tiled=True)]
    all_gather x8 -> x7, waiting for transfers between devices: 622 us -> 299 us  [the longest x3 225 us: gather_blk(): return lax.all_gather(rows, 'blk', axis=0, tiled=True)]
    dot_general x77 -> x12, matrix products: 370 us -> 90.4 us  [matmul(): lax.dot_general(left, right, dims, preferred_element_type=jnp.float32)]
    unnamed x2 -> x0, blocking collectives: 82.5 us -> none
    all_to_all x5 -> x4, blocking collectives: 57.9 us -> 131 us  [exchange_blk(): lax.all_to_all(pieces, 'blk', split_axis=0, concat_axis=0, tiled=True)]
    pallas_call x0 -> x2, Pallas kernels: none -> 51.3 us  [the longest x1 29.5 us: attend_back(): pl.pallas_call(attend_back_kernel, grid_spec=pltpu.PrefetchScalarGridSpec...]
    ppermute x32 -> x0, starting transfers between devices: 33.8 us -> none  [passed_along(): lax.ppermute(value, axis, [(i, (i + by) % count) for i in range(count)])]
  transfers between devices with their start and end apart: 51 -> 18, of which waited for: 33 -> 15; matrix products, arithmetic and copies ran while one was open for 13% -> 10% of each run, Pallas kernels for 0% -> 2%
where the time goes in v1:
time: 1180 us; the launch traced here: 1170 us
  waiting for transfers between devices  791 us (67%)
  blocking collectives  131 us (11%)
  matrix products  90.4 us (8%)
  Pallas kernels  51.3 us (4%)
  local copies, waits for them, and re-layouts  43.1 us (4%)
  other arithmetic  37.2 us (3%)
  between operations  15.2 us (1%)
    reduce_scatter x3, waiting for transfers between devices, scatter_blk(): return lax.psum_scatter(rows, 'blk', scatter_dimension=0, tiled=True)  244 us
    all_gather x3, waiting for transfers between devices, gather_blk(): return lax.all_gather(rows, 'blk', axis=0, tiled=True)  225 us
    reduce_scatter x1, waiting for transfers between devices, per_device(): lax.psum_scatter(matmul(attended, branch_gradient, DOWN).astype(narrow),...  147 us
    all_to_all x4, blocking collectives, exchange_blk(): lax.all_to_all(pieces, 'blk', split_axis=0, concat_axis=0, tiled=True)  131 us
    dot_general x12, matrix products, matmul(): lax.dot_general(left, right, dims, preferred_element_type=jnp.float32)  90.4 us
    all_gather x4, waiting for transfers between devices, gather_head(): return lax.all_gather(rows, 'head', axis=0, tiled=True)  74.3 us
    reduce_scatter x4, waiting for transfers between devices, scatter_head(): return lax.psum_scatter(rows, 'head', scatter_dimension=0, tiled=True)  69.7 us
    pallas_call x1, Pallas kernels, attend_back(): pl.pallas_call(attend_back_kernel, grid_spec=pltpu.PrefetchScalarGridSpec...  29.5 us
  transfers between devices with their start and end apart: 18, of which 15 were waited for; matrix products, arithmetic and copies ran while one was open for 10% of the time, Pallas kernels for 2%

profile of v1, /device:TPU:0, one launch (start us, length us, event | category | flops | bytes accessed | tf_op | source)
XLA Modules:
  0.0 1169.0 jit_solution(5410590086074430725)
XLA Ops:
  11.3 24.9 %all_to_all.30 = bf16[8,80,512]{2,1,0:T(8,128)(2,1)} all-to-all(bf16[8,80,512]{2,1,0:T(8,128)(2,1)S(1)} %copy.171), channel_id=1, replica_groups=mesh['blk'=8,'head'=4] {'blk'}, dimensions={0} | all-to-all | bytes 1310720 | tf_op jit(solution)/shard_map/all_to_all | solution.py:617
  37.9 22.7 %all-gather.12.cloned.1.call-done = bf16[32,80,512]{2,1,0:T(8,128)(2,1)} async-done(((bf16[8,80,512]{2,1,0:T(8,128)(2,1)}), bf16[32,80,512]{2,1,0:T(8,128)(2,1)}) %all-gather.12.cloned.1.call-update) | async-done | bytes 2621456 | tf_op jit(solution)/shard_map/all_gather | solution.py:621
  65.1 72.8 %all-gather.10.cloned.1.call-done = bf16[1024,2048]{0,1:T(8,128)(2,1)} async-done(((bf16[128,2048]{0,1:T(8,128)(2,1)}), bf16[1024,2048]{0,1:T(8,128)(2,1)}) %all-gather.10.cloned.1.call-update) | async-done | bytes 4194320 | tf_op jit(solution)/shard_map/all_gather | solution.py:609
  153.3 45.4 %all_to_all.31 = bf16[8,64,1536]{2,1,0:T(8,128)(2,1)} all-to-all(bf16[8,64,1536]{2,1,0:T(8,128)(2,1)S(1)} %copy.181), channel_id=1, replica_groups=mesh['blk'=8,'head'=4] {'blk'}, dimensions={0} | all-to-all | bytes 3145728 | tf_op jit(solution)/shard_map/all_to_all | solution.py:617
  204.0 21.8 %attend.1 = (bf16[1024,256]{1,0:T(8,128)(2,1)}, f32[8,8,256]{2,1,0:T(8,128)}) custom-call(s32[8]{0:T(128)} %copy-done.28, s32[32]{0:T(128)} %select_reduce_fusion.order_ref, bf16[1024,256]{1,0:T(8,128)(2,1)} %copy.204.q_ref, bf16[4096,256]{1,0:T(8,128)(2,1)} %all-gather.14.cloned.1.call-done.kv_ref), custom_call_target="tpu_custom_call" | custom-call | flops 2147483648 | bytes 3145728 | tf_op jit(solution)/shard_map/attend/pallas_call | solution.py:474
  231.9 26.4 %all-to-all-done.1 = bf16[8,128,256]{1,2,0:T(8,128)(2,1)S(1)} async-done(((bf16[8,128,256]{1,2,0:T(8,128)(2,1)}), bf16[8,128,256]{1,2,0:T(8,128)(2,1)S(1)}, u32[]{:S(2)}, u32[]{:S(2)}) %all-to-all-start.1) | async-done | bytes 524320 | tf_op jit(solution)/shard_map/all_to_all | solution.py:617
  273.2 35.3 %all-gather.20.cloned.1.call-done = bf16[32,64,1536]{2,1,0:T(8,128)(2,1)} async-done(((bf16[8,64,1536]{2,1,0:T(8,128)(2,1)}), bf16[32,64,1536]{2,1,0:T(8,128)(2,1)}) %all-gather.20.cloned.1.call-update) | async-done | bytes 6291472 | tf_op jit(solution)/shard_map/all_gather | solution.py:621
  308.4 77.1 %all-gather.18.cloned.1.call-done = bf16[1024,2048]{0,1:T(8,128)(2,1)} async-done(((bf16[128,2048]{0,1:T(8,128)(2,1)}), bf16[1024,2048]{0,1:T(8,128)(2,1)}) %all-gather.18.cloned.1.call-update) | async-done | bytes 4194320 | tf_op jit(solution)/shard_map/all_gather | solution.py:609
  385.6 11.9 %fusion.73 = f32[1024,1536]{1,0:T(8,128)} fusion(bf16[1024,2048]{0,1:T(8,128)(2,1)} %all-gather.18.cloned.1.call-done, bf16[2048,1536]{1,0:T(8,128)(2,1)} %bitcast.205), kind=kOutput, calls=%fused_computation.181 | convolution fusion | flops 6442450944 | bytes 16777216 | tf_op jit(solution)/shard_map/dot_general | solution.py:605
  397.5 16.3 %all-gather.22.cloned.1.call-done = bf16[768,2048]{1,0:T(8,128)(2,1)} async-done(((bf16[192,2048]{1,0:T(8,128)(2,1)}), bf16[768,2048]{1,0:T(8,128)(2,1)}) %all-gather.22.cloned.1.call-update) | async-done | bytes 3145744 | tf_op jit(solution)/shard_map/all_gather | solution.py:621
  413.9 74.9 %all-gather.24.cloned.1.call-done = bf16[1,1024,2048]{2,1,0:T(8,128)(2,1)} async-done(((bf16[1,128,2048]{2,1,0:T(8,128)(2,1)}), bf16[1,1024,2048]{2,1,0:T(8,128)(2,1)}) %all-gather.24.cloned.1.call-update) | async-done | bytes 4194320 | tf_op jit(solution)/shard_map/all_gather | solution.py:609
  488.8 10.5 multiply_convert_fusion.1
  501.0 11.0 convolution_convert_fusion.2
  520.1 78.9 %reduce-scatter.11.cloned.1.call-done = bf16[128,2048]{1,0:T(8,128)(2,1)} async-done(((bf16[1024,2048]{1,0:T(8,128)(2,1)}), bf16[128,2048]{1,0:T(8,128)(2,1)}) %reduce-scatter.11.cloned.1.call-update) | async-done | bytes 524304 | tf_op jit(solution)/shard_map/reduce_scatter | solution.py:613
  607.7 82.8 %reduce-scatter.9.cloned.1.call-done = bf16[128,2048]{1,0:T(8,128)(2,1)} async-done(((bf16[1024,2048]{1,0:T(8,128)(2,1)}), bf16[128,2048]{1,0:T(8,128)(2,1)}) %reduce-scatter.9.cloned.1.call-update) | async-done | bytes 524304 | tf_op jit(solution)/shard_map/reduce_scatter | solution.py:613
  699.9 18.8 %all_to_all.32 = bf16[8,128,256]{2,1,0:T(8,128)(2,1)} all-to-all(bf16[8,128,256]{2,1,0:T(8,128)(2,1)S(1)} %bitcast.187), channel_id=1, replica_groups=mesh['blk'=8,'head'=4] {'blk'}, dimensions={0} | all-to-all | bytes 1048576 | tf_op jit(solution)/shard_map/all_to_all | solution.py:617
  718.8 29.5 %attend_back.1 = (bf16[1024,256]{1,0:T(8,128)(2,1)}, bf16[4096,256]{1,0:T(8,128)(2,1)}) custom-call(s32[8]{0:T(128)} %copy-done.28, s32[32]{0:T(128)} %select_reduce_fusion.order_ref, bf16[1024,256]{1,0:T(8,128)(2,1)} %copy.204.q_ref, bf16[1024,256]{1,0:T(8,128)(2,1)} %bitcast.197, bf16[1024,256]{1,0:T(8,128)(2,1)} %get-tuple-element.17.out_ref, ...), custom_call_target="tpu_custom_call" | custom-call | flops 5368709120 | bytes 6291456 | tf_op jit(solution)/shard_map/attend_back/pallas_call | solution.py:575
  748.4 11.1 convolution_convert_fusion
  767.1 10.7 reduce-scatter.13.cloned.1.call-done
  810.5 28.5 %reduce-scatter.21.cloned.1.call-done = bf16[512,1536]{1,0:T(8,128)(2,1)} async-done(((bf16[2048,1536]{1,0:T(8,128)(2,1)}), bf16[512,1536]{1,0:T(8,128)(2,1)}) %reduce-scatter.21.cloned.1.call-update) | async-done | bytes 1572880 | tf_op jit(solution)/shard_map/reduce_scatter | solution.py:625
  839.0 42.4 %all_to_all.33 = bf16[8,64,1536]{2,1,0:T(8,128)(2,1)S(1)} all-to-all(bf16[8,64,1536]{2,1,0:T(8,128)(2,1)} %bitcast.191), channel_id=1, replica_groups=mesh['blk'=8,'head'=4] {'blk'}, dimensions={0} | all-to-all | bytes 3145728 | tf_op jit(solution)/shard_map/all_to_all | solution.py:617
  885.9 30.5 %reduce-scatter.23.cloned.1.call-done = bf16[192,2048]{1,0:T(8,128)(2,1)} async-done(((bf16[768,2048]{1,0:T(8,128)(2,1)}), bf16[192,2048]{1,0:T(8,128)(2,1)}) %reduce-scatter.23.cloned.1.call-update) | async-done | bytes 786448 | tf_op jit(solution)/shard_map/reduce_scatter | solution.py:625
  926.5 81.8 %reduce-scatter.15.cloned.1.call-done = bf16[128,2048]{1,0:T(8,128)(2,1)} async-done(((bf16[1024,2048]{1,0:T(8,128)(2,1)}), bf16[128,2048]{1,0:T(8,128)(2,1)}) %reduce-scatter.15.cloned.1.call-update) | async-done | bytes 524304 | tf_op jit(solution)/shard_map/reduce_scatter | solution.py:613
  1013.7 146.6 %reduce-scatter.19.cloned.1.call-done = bf16[64,2048]{1,0:T(8,128)(2,1)} async-done(((bf16[2048,2048]{1,0:T(8,128)(2,1)}), bf16[64,2048]{1,0:T(8,128)(2,1)}) %reduce-scatter.19.cloned.1.call-update) | async-done | bytes 262160 | tf_op jit(solution)/shard_map/reduce_scatter | solution.py:810
  (229 shorter events, 141.0 us)
Async XLA Ops:
  7.2 53.4 %all-gather.12.cloned.1.call-start = ((), (), s32[]{:S(2)}) async-start(), calls=%async_computation.15 | async-start | bytes 3276800 | tf_op jit(solution)/shard_map/all_gather | solution.py:621
  8.2 28.0 %copy-start.4 = (bf16[1,128,2048]{2,1,0:T(8,128)(2,1)S(1)}, bf16[1,128,2048]{2,1,0:T(8,128)(2,1)}, u32[]{:S(2)}) copy-start(bf16[1,128,2048]{2,1,0:T(8,128)(2,1)} %param.14) | copy-start | bytes 1572868
  11.1 26.4 %copy-start.29 = (s32[1,16]{1,0:T(1,128)S(1)}, s32[1,16]{1,0:T(1,128)}, u32[]{:S(2)}) copy-start(s32[1,16]{1,0:T(1,128)} %param.26) | copy-start | bytes 196
  36.2 101.7 %all-gather.10.cloned.1.call-start = ((), (), s32[]{:S(2)}) async-start(), calls=%async_computation.14 | async-start | bytes 4718592 | tf_op jit(solution)/shard_map/all_gather | solution.py:609
  37.4 166.6 %all-gather.14.cloned.1.call-start = ((), (), s32[]{:S(2)}) async-start(), calls=%async_computation.16 | async-start | bytes 2621440 | tf_op jit(solution)/shard_map/all_gather | solution.py:621
  37.8 103.4 %copy-start.28 = (s32[8]{0:T(128)}, s32[8]{0:T(128)S(1)}, u32[]{:S(2)}) copy-start(s32[8]{0:T(128)S(1)} %fusion.55.place_ref) | copy-start | bytes 100
  145.4 614.4 %copy-start = (f32[1024,512]{0,1:T(8,128)}, f32[1024,512]{0,1:T(8,128)S(1)}, u32[]{:S(2)}) copy-start(f32[1024,512]{0,1:T(8,128)S(1)} %fusion.14) | copy-start | bytes 6291460
  150.6 111.0 %all-gather.16.cloned.1.call-start = ((), (), s32[]{:S(2)}) async-start(), calls=%async_computation.17 | async-start | bytes 8650752 | tf_op jit(solution)/shard_map/all_gather | solution.py:709
  151.2 157.2 %all-gather.20.cloned.1.call-start = ((), (), s32[]{:S(2)}) async-start(), calls=%async_computation.19 | async-start | bytes 7864320 | tf_op jit(solution)/shard_map/all_gather | solution.py:621
  227.8 30.5 %all-to-all-start.1 = ((bf16[8,128,256]{1,2,0:T(8,128)(2,1)}), bf16[8,128,256]{1,2,0:T(8,128)(2,1)S(1)}, u32[]{:S(2)}, u32[]{:S(2)}) async-start(bf16[8,128,256]{1,2,0:T(8,128)(2,1)} %copy.177), calls=%async_computation.1 | async-start | bytes 1048576 | tf_op jit(solution)/shard_map/all_to_all | solution.py:617
  231.3 154.3 %all-gather.18.cloned.1.call-start = ((), (), s32[]{:S(2)}) async-start(), calls=%async_computation.18 | async-start | bytes 4718592 | tf_op jit(solution)/shard_map/all_gather | solution.py:609
  271.6 142.2 %all-gather.22.cloned.1.call-start = ((), (), s32[]{:S(2)}) async-start(), calls=%async_computation.20 | async-start | bytes 3932160 | tf_op jit(solution)/shard_map/all_gather | solution.py:621
  272.4 216.4 %all-gather.24.cloned.1.call-start = ((), (), s32[]{:S(2)}) async-start(), calls=%async_computation.29 | async-start | bytes 4718592 | tf_op jit(solution)/shard_map/all_gather | solution.py:609
  273.1 325.9 %reduce-scatter.11.cloned.1.call-start = ((), (), s32[]{:S(2)}) async-start(), calls=%async_computation.22 | async-start | bytes 4718592 | tf_op jit(solution)/shard_map/reduce_scatter | solution.py:613
  512.0 178.5 %reduce-scatter.9.cloned.1.call-start = ((), (), s32[]{:S(2)}) async-start(), calls=%async_computation.21 | async-start | bytes 4718592 | tf_op jit(solution)/shard_map/reduce_scatter | solution.py:613
  520.0 257.7 %reduce-scatter.13.cloned.1.call-start = ((), (), s32[]{:S(2)}) async-start(), calls=%async_computation.23 | async-start | bytes 2621440 | tf_op jit(solution)/shard_map/reduce_scatter | solution.py:625
  748.3 90.7 %reduce-scatter.21.cloned.1.call-start = ((), (), s32[]{:S(2)}) async-start(), calls=%async_computation.27 | async-start | bytes 7864320 | tf_op jit(solution)/shard_map/reduce_scatter | solution.py:625
  759.5 121.9 %reduce-scatter.17.cloned.1.call-start = ((), (), s32[]{:S(2)}) async-start(), calls=%async_computation.25 | async-start | bytes 3276800 | tf_op jit(solution)/shard_map/reduce_scatter | solution.py:625
  789.4 127.0 %reduce-scatter.23.cloned.1.call-start = ((), (), s32[]{:S(2)}) async-start(), calls=%async_computation.28 | async-start | bytes 3932160 | tf_op jit(solution)/shard_map/reduce_scatter | solution.py:625
  797.6 210.7 %reduce-scatter.15.cloned.1.call-start = ((), (), s32[]{:S(2)}) async-start(), calls=%async_computation.24 | async-start | bytes 4718592 | tf_op jit(solution)/shard_map/reduce_scatter | solution.py:613
  803.6 356.7 %reduce-scatter.19.cloned.1.call-start = ((), (), s32[]{:S(2)}) async-start(), calls=%async_computation.26 | async-start | bytes 8650752 | tf_op jit(solution)/shard_map/reduce_scatter | solution.py:810
  810.5 75.1 %copy-start.5 = (bf16[1,128,2048]{2,1,0:T(8,128)(2,1)S(1)}, bf16[1,128,2048]{2,1,0:T(8,128)(2,1)}, u32[]{:S(2)}) copy-start(bf16[1,128,2048]{2,1,0:T(8,128)(2,1)} %param.14) | copy-start | bytes 1572868
  881.4 41.4 %all-to-all-start.4 = ((bf16[8,80,512]{2,1,0:T(8,128)(2,1)}), bf16[8,80,512]{2,1,0:T(8,128)(2,1)}, u32[]{:S(2)}, u32[]{:S(2)}) async-start(bf16[8,80,512]{2,1,0:T(8,128)(2,1)} %reduce-scatter.17.cloned.1.call-done), calls=%async_computation.9 | async-start | bytes 1310720 | tf_op jit(solution)/shard_map/all_to_all | solution.py:617
  924.1 86.5 %copy-start.20 = (f32[8,8,8,256]{3,2,0,1:T(8,128)}, f32[8,8,8,256]{3,2,0,1:T(8,128)S(1)}, u32[]{:S(2)}) copy-start(f32[8,8,8,256]{3,2,0,1:T(8,128)S(1)} %copy.211) | copy-start | bytes 1572868
  (28 other events, 87.3 us)
Sparse Core Ops, SparseCore 0:
  36.3 24.2 all-gather.11
  63.2 74.6 all-gather.9
  150.8 20.7 all-gather.13
  174.3 87.3 all-gather.15
  263.0 45.3 all-gather.19
  310.9 74.6 all-gather.17
  387.1 26.6 all-gather.21
  416.0 72.7 all-gather.23
  512.1 86.8 reduce-scatter.10
  602.5 87.9 reduce-scatter.8
  748.4 29.2 reduce-scatter.12
  780.2 58.8 reduce-scatter.20
  841.6 34.4 reduce-scatter.16
  878.5 37.8 reduce-scatter.22
  919.9 88.3 reduce-scatter.14
  1010.4 149.8 reduce-scatter.18

commit v2 on v1

--- a/solution.py
+++ b/solution.py
@@ -605,16 +605,71 @@
     return lax.dot_general(left, right, dims, preferred_element_type=jnp.float32)
 
 
-def gather_blk(rows):
-    return lax.all_gather(rows, "blk", axis=0, tiled=True)
-
-
-def scatter_blk(rows):
-    return lax.psum_scatter(rows, "blk", scatter_dimension=0, tiled=True)
-
-
-def exchange_blk(pieces):
-    return lax.all_to_all(pieces, "blk", split_axis=0, concat_axis=0, tiled=True)
+RING = (0, 2, 4, 6, 7, 5, 3, 1)
+STRIPS = (0, 1, 7, 2, 6, 3, 5, 4)
+GROUPS = ((0, 3), (3, 5), (5, 7), (7, 8))
+
+
+def hop(value, by):
+    count = len(RING)
+    return lax.ppermute(value, "blk", [(RING[i], RING[(i + by) % count]) for i in range(count)])
+
+
+def cross(value, by):
+    return lax.ppermute(value, "head", [(i, i ^ by) for i in range(4)])
+
+
+def add(left, right):
+    return (left.astype(jnp.float32) + right.astype(jnp.float32)).astype(left.dtype)
+
+
+def ring_gather(own):
+    half = own.shape[0] // 2
+    got = {0: own}
+    for step in (1, 2, 3):
+        got[step] = hop(got[step - 1], -1)
+        got[8 - step] = hop(got[(9 - step) % 8], 1)
+    got[4] = jnp.concatenate([hop(got[3][:half], -1), hop(got[5][half:], 1)], axis=0)
+    return [got[s] for s in STRIPS]
+
+
+def ring_scatter(parts):
+    part = dict(zip(STRIPS, parts))
+    half = part[0].shape[0] // 2
+    up = hop(part[4][:half], 1)
+    down = hop(part[4][half:], -1)
+    up = hop(jnp.concatenate([add(part[3][:half], up), part[3][half:]], axis=0), 1)
+    down = hop(jnp.concatenate([part[5][:half], add(part[5][half:], down)], axis=0), -1)
+    up, down = hop(add(part[2], up), 1), hop(add(part[6], down), -1)
+    up, down = hop(add(part[1], up), 1), hop(add(part[7], down), -1)
+    wide = jnp.float32
+    return part[0].astype(wide) + up.astype(wide) + down.astype(wide)
+
+
+def grouped(strips):
+    return [
+        jnp.concatenate(strips[a:b], axis=0) if b - a > 1 else strips[a] for a, b in GROUPS
+    ]
+
+
+def split_groups(groups, rows):
+    return [
+        group[i * rows : (i + 1) * rows]
+        for group in groups
+        for i in range(group.shape[0] // rows)
+    ]
+
+
+def swap_slices(pieces, place, blk_index):
+    ring = jnp.asarray(RING, jnp.int32)
+    own = lax.dynamic_index_in_dim(pieces, blk_index, 0)
+    out = lax.dynamic_update_slice_in_dim(jnp.zeros_like(pieces), own, blk_index, 0)
+    for by in (4, 1, 7, 2, 6, 3, 5):
+        target = ring[(place + by) % 8]
+        source = ring[(place - by) % 8]
+        moved = hop(lax.dynamic_index_in_dim(pieces, target, 0), by)
+        out = lax.dynamic_update_slice_in_dim(out, moved, source, 0)
+    return out
 
 
 def gather_head(rows):
@@ -627,6 +682,27 @@
 
 def inverse_rms(rows):
     return lax.rsqrt(jnp.mean(rows * rows, axis=-1, keepdims=True) + EPS)
+
+
+def turn(rows, cosine, sine):
+    half = HEAD_SIZE // 2
+    first, second = rows[:, :half], rows[:, half:]
+    return jnp.concatenate(
+        [first * cosine - second * sine, second * cosine + first * sine], axis=1
+    )
+
+
+def head_back(grads, raw, gain, cosine, sine):
+    rho = inverse_rms(raw)
+    unit = raw * rho
+    turned = turn(grads.astype(jnp.float32), cosine, -sine)
+    gain_part = jnp.sum(turned * unit, axis=0)
+    scaled = turned * gain
+    return rho * (scaled - unit * jnp.mean(unit * scaled, axis=-1, keepdims=True)), gain_part
+
+
+def after(value, *earlier):
+    return lax.optimization_barrier((value, *earlier))[0]
 
 
 def per_device(
@@ -648,6 +724,7 @@
     blk_count = lax.axis_size("blk")
     head_count = lax.axis_size("head")
     head_index = lax.axis_index("head")
+    blk_index = lax.axis_index("blk")
     narrow, wide = jnp.bfloat16, jnp.float32
     tokens, out_cotangent = tokens[0], out_cotangent[0]
     local_rows, model_width = tokens.shape
@@ -659,131 +736,156 @@
     attn_cols = query_cols + 2 * HEAD_SIZE
     strip_count = blk_count * head_count
     halves = strip_count // stretch_order.shape[1]
-
-    def by_head(rows):
-        shape = (rows.shape[0], blk_count, head_count, weight_rows)
-        return rows.reshape(shape).transpose(0, 2, 1, 3).reshape(rows.shape)
-
-    def by_blk(rows):
-        shape = (rows.shape[0], head_count, blk_count, weight_rows)
-        return rows.reshape(shape).transpose(0, 2, 1, 3).reshape(rows.shape)
-
-    attn_pieces = jnp.concatenate(
-        [
-            query_weight.reshape(weight_rows, blk_count, query_cols),
-            key_projection.reshape(weight_rows, blk_count, HEAD_SIZE),
-            value_projection.reshape(weight_rows, blk_count, HEAD_SIZE),
-        ],
-        axis=2,
-    ).transpose(1, 0, 2)
+    ring_place = jnp.where(blk_index % 2 == 0, blk_index // 2, 7 - blk_index // 2)
+
+    def pieces_of(*weights):
+        return jnp.concatenate(
+            [w.reshape(weight_rows, blk_count, w.shape[1] // blk_count) for w in weights], axis=2
+        ).transpose(1, 0, 2)
+
+    def natural(pieces, rows):
+        return pieces.reshape(head_count, blk_count, rows, -1).transpose(1, 0, 2, 3)
+
     small = query_norm.shape[0]
     gains = jnp.concatenate([attention_norm, feedforward_norm, query_norm, key_norm])
     gains = jnp.pad(gains, (0, attn_cols - gains.shape[0]))[None, None, :]
     gains = jnp.pad(gains, ((0, 0), (0, 15), (0, 0)))
     attn_pieces = jnp.concatenate(
-        [attn_pieces, jnp.broadcast_to(gains, (blk_count, 16, attn_cols))], axis=1
-    )
-    attn_all = gather_head(exchange_blk(attn_pieces)).reshape(
-        head_count, blk_count, weight_rows + 16, attn_cols
+        [
+            pieces_of(query_weight, key_projection, value_projection),
+            jnp.broadcast_to(gains, (blk_count, 16, attn_cols)),
+        ],
+        axis=1,
+    )
+    token_strips = ring_gather(tokens)
+    attn_all = natural(
+        gather_head(swap_slices(attn_pieces, ring_place, blk_index)), weight_rows + 16
     )
     attn_matrix = attn_all[:, :, :weight_rows].reshape(model_width, attn_cols)
     gain_rows = attn_all[:, :, weight_rows]
     gain_one = gain_rows[:, :, :weight_rows].reshape(1, model_width).astype(wide)
-    gain_two_rows = gain_rows[:, :, weight_rows : 2 * weight_rows].astype(wide)
-    gain_two = gain_two_rows.transpose(1, 0, 2).reshape(1, model_width)
-    gain_one_natural = by_blk(gain_one)
+    gain_two = (
+        gain_rows[:, :, weight_rows : 2 * weight_rows].reshape(1, model_width).astype(wide)
+    )
     at = 2 * weight_rows
-    query_gain = gain_rows[:, :, at : at + small].transpose(1, 0, 2).reshape(HEAD_SIZE)
-    key_gain = gain_rows[:, :, at + small : at + 2 * small].transpose(1, 0, 2).reshape(HEAD_SIZE)
-    query_gain, key_gain = query_gain.astype(wide), key_gain.astype(wide)
-
-    ff_pieces = jnp.concatenate(
-        [
-            gate_weight.reshape(weight_rows, blk_count, ff_local),
-            up_weight.reshape(weight_rows, blk_count, ff_local),
-        ],
-        axis=2,
-    ).transpose(1, 0, 2)
-    ff_matrix = gather_head(exchange_blk(ff_pieces)).reshape(model_width, 2 * ff_local)
+    query_gain = gain_rows[:, :, at : at + small].reshape(1, HEAD_SIZE).astype(wide)
+    key_gain = gain_rows[:, :, at + small : at + 2 * small].reshape(1, HEAD_SIZE).astype(wide)
+
+    output_rows = gather_head(output_weight)
+    ff_pieces = after(pieces_of(gate_weight, up_weight), token_strips[-1])
+    ff_matrix = natural(
+        gather_head(swap_slices(ff_pieces, ring_place, blk_index)), weight_rows
+    ).reshape(model_width, 2 * ff_local)
     down_matrix = gather_head(down_weight)
-    output_matrix = lax.all_gather(output_weight, ("blk", "head"), axis=0, tiled=True)
-
-    strip_blk = jnp.arange(strip_count, dtype=jnp.int32) % blk_count
-    strip_head = jnp.arange(strip_count, dtype=jnp.int32) // blk_count
-    strip = strip_blk * head_count + strip_head
+    cotangent_strips = ring_gather(after(out_cotangent, token_strips[-1]))
+
+    numbers = jnp.arange(strip_count, dtype=jnp.int32)
+    on = jnp.asarray(STRIPS, jnp.int32)
+    ring_spot = (ring_place + on) % blk_count
+    strip_blk = jnp.where(ring_spot < 4, 2 * ring_spot, 15 - 2 * ring_spot)
+    strip_head = head_index ^ jnp.arange(head_count, dtype=jnp.int32)
+    strip = (strip_blk[None, :] * head_count + strip_head[:, None]).reshape(strip_count)
     slots = jnp.arange(stretch_order.shape[1], dtype=jnp.int32)
     held = jnp.sum(
         jnp.where((strip // halves)[:, None] == slots[None, :], stretch_order, 0), axis=1
     )
     strip_place = held * halves + strip % halves
-    ranks = jnp.arange(strip_count, dtype=jnp.int32)
     order = jnp.sum(
-        jnp.where(strip_place[None, :] == ranks[:, None], ranks[None, :], 0), axis=1
+        jnp.where(strip_place[None, :] == numbers[:, None], numbers[None, :], 0), axis=1
     ).astype(jnp.int32)
-    place = jnp.sum(
-        jnp.where(
-            jnp.arange(head_count, dtype=jnp.int32)[:, None] == head_index,
-            strip_place.reshape(head_count, blk_count),
-            0,
-        ),
-        axis=0,
-    ).astype(jnp.int32)
+    place = strip_place[:blk_count].astype(jnp.int32)
     positions = (
         place[:, None] * local_rows + jnp.arange(local_rows, dtype=jnp.int32)[None, :]
     ).reshape(group_rows)
-    phases = angles(positions, HEAD_SIZE)
+    phases = angles(positions, HEAD_SIZE)[:, 0, :]
+    cosine, sine = jnp.cos(phases), jnp.sin(phases)
 
     tokens_wide = tokens.astype(wide)
-    group_tokens = gather_blk(by_head(tokens)).astype(wide)
-    first_normed = (group_tokens * inverse_rms(group_tokens) * gain_one).astype(narrow)
-    attn_raw = matmul(first_normed, attn_matrix)
-    query_raw = attn_raw[:, :query_cols].reshape(group_rows, group_heads, HEAD_SIZE)
-    key_raw = attn_raw[:, query_cols : query_cols + HEAD_SIZE].reshape(group_rows, 1, HEAD_SIZE)
-    value_rows = attn_raw[:, query_cols + HEAD_SIZE :].astype(narrow)
-
-    def heads_local(query_in, key_in, query_scale, key_scale):
-        return (
-            rotary(norm_rows(query_in, query_scale), phases),
-            rotary(norm_rows(key_in, key_scale), phases),
-        )
-
-    (query_rows, key_rows), heads_back = jax.vjp(
-        heads_local, query_raw, key_raw, query_gain, key_gain
-    )
-    query_rows = (query_rows * (LOG2E / math.sqrt(HEAD_SIZE))).astype(narrow)
-    query_rows = query_rows.reshape(group_rows, query_cols)
-    kv = jnp.concatenate([key_rows.reshape(group_rows, HEAD_SIZE).astype(narrow), value_rows], 1)
-    kv = gather_head(kv)
-    attended_heads, lse = attend(place, order, query_rows, kv)
-    attended = (
-        exchange_blk(attended_heads.reshape(blk_count, local_rows, query_cols))
-        .transpose(1, 0, 2)
-        .reshape(local_rows, QUERY_HEADS * HEAD_SIZE)
-    )
-
-    resid = tokens_wide + matmul(attended, output_matrix)
+    raw_groups, normed_groups, query_groups, kv_groups = [], [], [], []
+    for (first, last), rows in zip(GROUPS, grouped(token_strips)):
+        here = slice(first * local_rows, last * local_rows)
+        rows = rows.astype(wide)
+        normed = (rows * inverse_rms(rows) * gain_one).astype(narrow)
+        raw = matmul(normed, attn_matrix)
+        heads = []
+        for h in range(group_heads + 1):
+            part = raw[:, h * HEAD_SIZE : (h + 1) * HEAD_SIZE]
+            gain = query_gain if h < group_heads else key_gain
+            part = turn(part * inverse_rms(part) * gain, cosine[here], sine[here])
+            if h < group_heads:
+                part = part * (LOG2E / math.sqrt(HEAD_SIZE))
+            heads.append(part.astype(narrow))
+        raw_groups.append(raw)
+        normed_groups.append(normed)
+        query_groups.append(jnp.concatenate(heads[:group_heads], axis=1))
+        kv_groups.append(
+            jnp.concatenate(
+                [heads[group_heads], raw[:, query_cols + HEAD_SIZE :].astype(narrow)], axis=1
+            )
+        )
+    first_normed = jnp.concatenate(normed_groups, axis=0)
+    attn_raw = jnp.concatenate(raw_groups, axis=0)
+    query_rows = jnp.concatenate(query_groups, axis=0)
+    kv_own = jnp.concatenate(kv_groups, axis=0)
+    kv_far = cross(kv_own, 2)
+    kv = jnp.concatenate([kv_own, cross(kv_own, 1), kv_far, cross(kv_far, 1)], axis=0)
+    attended, lse = attend(place, order, query_rows, kv)
+
+    def by_groups(rows):
+        return [rows[a * local_rows : b * local_rows] for a, b in GROUPS]
+
+    branch_parts = [
+        matmul(rows, output_rows).astype(narrow) for rows in reversed(by_groups(attended))
+    ]
+    branch = ring_scatter(split_groups(branch_parts[::-1], local_rows))
+    resid = tokens_wide + branch
     rho_two = inverse_rms(resid)
     unit_two = resid * rho_two
-    second_normed = gather_blk(by_head((unit_two * gain_two).astype(narrow)))
-    group_cotangent = gather_blk(out_cotangent)
-    ff_raw = matmul(second_normed, ff_matrix)
-    gate, up_proj = ff_raw[:, :ff_local], ff_raw[:, ff_local:]
-    sigma = jax.nn.sigmoid(gate)
-    swish = gate * sigma
-    hidden = (swish * up_proj).astype(narrow)
-    out_part = scatter_blk(matmul(hidden, down_matrix).astype(narrow))
-    layer_out = (resid + out_part.astype(wide)).astype(narrow)
-
-    hidden_gradient = matmul(group_cotangent, down_matrix, ALONG)
-    gate_gradient = hidden_gradient * up_proj * (sigma * (1.0 + gate * (1.0 - sigma)))
-    ff_gradient = jnp.concatenate([gate_gradient, hidden_gradient * swish], 1).astype(narrow)
-    second_gradient = matmul(ff_gradient, ff_matrix, ALONG).astype(narrow)
-    second_gradient = by_blk(scatter_blk(second_gradient)).astype(wide)
+    second_strips = ring_gather((unit_two * gain_two).astype(narrow))
+
+    hidden_groups, ff_gradient_groups, second_parts = [], [], []
+    second_groups = grouped(second_strips)
+    cotangent_groups = grouped(cotangent_strips)
+    for rows, grads in zip(second_groups, cotangent_groups):
+        ff_raw = matmul(rows, ff_matrix)
+        gate, up_proj = ff_raw[:, :ff_local], ff_raw[:, ff_local:]
+        sigma = jax.nn.sigmoid(gate)
+        swish = gate * sigma
+        hidden_groups.append((swish * up_proj).astype(narrow))
+        hidden_gradient = matmul(grads, down_matrix, ALONG)
+        gate_gradient = hidden_gradient * up_proj * (sigma * (1.0 + gate * (1.0 - sigma)))
+        ff_gradient_groups.append(
+            jnp.concatenate([gate_gradient, hidden_gradient * swish], 1).astype(narrow)
+        )
+    for rows in reversed(ff_gradient_groups):
+        second_parts.append(matmul(rows, ff_matrix, ALONG).astype(narrow))
+    second_gradient = ring_scatter(split_groups(second_parts[::-1], local_rows))
+    scaled = gain_two * second_gradient
+    resid_gradient = out_cotangent.astype(wide) + rho_two * (
+        scaled - unit_two * jnp.mean(unit_two * scaled, axis=-1, keepdims=True)
+    )
+    branch_gradient = resid_gradient.astype(narrow)
+    branch_strips = ring_gather(branch_gradient)
+
+    out_parts = [matmul(rows, down_matrix).astype(narrow) for rows in reversed(hidden_groups)]
+    out_parts = split_groups(out_parts[::-1], local_rows)
+    out_part = ring_scatter(out_parts[:-1] + [after(out_parts[-1], branch_strips[-1])])
+    layer_out = (resid + out_part).astype(narrow)
+
+    second_normed = jnp.concatenate(second_groups, axis=0)
+    group_cotangent = jnp.concatenate(cotangent_groups, axis=0)
+    hidden = jnp.concatenate(hidden_groups, axis=0)
+    ff_gradient = jnp.concatenate(ff_gradient_groups, axis=0)
+
+    def by_head(grads, rows):
+        shape = (blk_count, head_count, rows, grads.shape[-1])
+        return grads.reshape(shape).transpose(1, 0, 2, 3).reshape(-1, rows, grads.shape[-1])
+
     down_gradient = scatter_head(matmul(hidden, group_cotangent, DOWN).astype(narrow))
-    ff_matrix_gradient = scatter_head(matmul(second_normed, ff_gradient, DOWN).astype(narrow))
-    ff_matrix_gradient = exchange_blk(
-        ff_matrix_gradient.reshape(blk_count, weight_rows, 2 * ff_local)
-    ).astype(wide)
+    ff_matrix_gradient = scatter_head(
+        by_head(matmul(second_normed, ff_gradient, DOWN).astype(narrow), weight_rows)
+    )
+    ff_matrix_gradient = swap_slices(ff_matrix_gradient, ring_place, blk_index).astype(wide)
     gate_weight_gradient = (
         ff_matrix_gradient[:, :, :ff_local].transpose(1, 0, 2).reshape(gate_weight.shape)
     )
@@ -794,64 +896,52 @@
         jnp.sum(gate_weight_gradient * gate_weight.astype(wide), axis=1)
         + jnp.sum(up_weight_gradient * up_weight.astype(wide), axis=1)
     ) / feedforward_norm.astype(wide)
-    scaled = gain_two * second_gradient
-    resid_gradient = out_cotangent.astype(wide) + rho_two * (
-        scaled - unit_two * jnp.mean(unit_two * scaled, axis=-1, keepdims=True)
-    )
-
-    branch_gradient = resid_gradient.astype(narrow)
-    attended_gradient = (
-        matmul(branch_gradient, output_matrix, ALONG)
-        .astype(narrow)
-        .reshape(local_rows, blk_count, query_cols)
-        .transpose(1, 0, 2)
-    )
-    attended_gradient = exchange_blk(attended_gradient).reshape(group_rows, query_cols)
-    output_weight_gradient = lax.psum_scatter(
-        matmul(attended, branch_gradient, DOWN).astype(narrow),
-        ("blk", "head"),
-        scatter_dimension=0,
-        tiled=True,
+
+    branch_groups = grouped(branch_strips)
+    attended_gradient = jnp.concatenate(
+        [matmul(rows, output_rows, ALONG).astype(narrow) for rows in branch_groups], axis=0
+    )
+    output_weight_gradient = scatter_head(
+        matmul(attended, jnp.concatenate(branch_groups, axis=0), DOWN).astype(narrow)
     ).astype(wide)
     query_grads, kv_grads = attend_back(
-        place, order, query_rows, attended_gradient, attended_heads, lse, kv
-    )
-    kv_grads = scatter_head(kv_grads)
-    query_raw_gradient, key_raw_gradient, query_gain_part, key_gain_part = heads_back(
-        (
-            query_grads.reshape(group_rows, group_heads, HEAD_SIZE).astype(wide),
-            kv_grads[:, :HEAD_SIZE].reshape(group_rows, 1, HEAD_SIZE).astype(wide),
-        )
-    )
-    attn_gradient = jnp.concatenate(
-        [
-            query_raw_gradient.reshape(group_rows, query_cols).astype(narrow),
-            key_raw_gradient.reshape(group_rows, HEAD_SIZE).astype(narrow),
-            kv_grads[:, HEAD_SIZE:],
-        ],
-        axis=1,
-    )
-    first_gradient = scatter_blk(matmul(attn_gradient, attn_matrix, ALONG).astype(narrow))
-    first_gradient = by_blk(first_gradient).astype(wide)
-    attn_matrix_gradient = (
-        matmul(first_normed, attn_gradient, DOWN)
-        .astype(narrow)
-        .reshape(head_count, blk_count, weight_rows, attn_cols)
+        place, order, query_rows, attended_gradient, attended, lse, kv
+    )
+    kv_near = [kv_grads[j * group_rows : (j + 1) * group_rows] for j in range(head_count)]
+    kv_sent = cross(jnp.concatenate([kv_near[1], kv_near[3]], axis=0), 1)
+    kv_grads = add(
+        add(kv_near[0], kv_sent[:group_rows]), cross(add(kv_near[2], kv_sent[group_rows:]), 2)
+    )
+    attn_gradient, gain_parts = [], []
+    for h in range(group_heads + 1):
+        cols = slice(h * HEAD_SIZE, (h + 1) * HEAD_SIZE)
+        grads = query_grads[:, cols] if h < group_heads else kv_grads[:, :HEAD_SIZE]
+        gain = query_gain if h < group_heads else key_gain
+        raw_gradient, gain_part = head_back(grads, attn_raw[:, cols], gain, cosine, sine)
+        attn_gradient.append(raw_gradient.astype(narrow))
+        gain_parts.append(gain_part)
+    attn_gradient = jnp.concatenate(attn_gradient + [kv_grads[:, HEAD_SIZE:]], axis=1)
+    first_parts = [
+        matmul(rows, attn_matrix, ALONG).astype(narrow)
+        for rows in reversed(by_groups(attn_gradient))
+    ]
+    first_gradient = ring_scatter(split_groups(first_parts[::-1], local_rows))
+    attn_matrix_gradient = by_head(
+        matmul(first_normed, attn_gradient, DOWN).astype(narrow), weight_rows
     )
     gain_parts = jnp.stack(
         [
-            query_gain_part.reshape(blk_count, head_count, small),
-            key_gain_part.reshape(blk_count, head_count, small),
+            sum(gain_parts[:group_heads]).reshape(blk_count, head_count, small),
+            gain_parts[group_heads].reshape(blk_count, head_count, small),
         ],
         axis=2,
     ).transpose(1, 0, 2, 3)
-    gain_parts = gain_parts.reshape(head_count, blk_count, 1, 2 * small).astype(narrow)
-    gain_parts = jnp.pad(gain_parts, ((0, 0), (0, 0), (0, 15), (0, attn_cols - 2 * small)))
-    attn_matrix_gradient = jnp.concatenate([attn_matrix_gradient, gain_parts], axis=2)
-    attn_matrix_gradient = exchange_blk(
-        scatter_head(
-            attn_matrix_gradient.reshape(head_count * blk_count, weight_rows + 16, attn_cols)
-        )
+    gain_parts = gain_parts.reshape(strip_count, 1, 2 * small).astype(narrow)
+    gain_parts = jnp.pad(gain_parts, ((0, 0), (0, 15), (0, attn_cols - 2 * small)))
+    attn_matrix_gradient = swap_slices(
+        scatter_head(jnp.concatenate([attn_matrix_gradient, gain_parts], axis=1)),
+        ring_place,
+        blk_index,
     ).astype(wide)
     attn_rows = attn_matrix_gradient[:, :weight_rows]
     query_weight_gradient = (
@@ -873,7 +963,7 @@
     ) / attention_norm.astype(wide)
     rho_one = inverse_rms(tokens_wide)
     unit_one = tokens_wide * rho_one
-    scaled = gain_one_natural * first_gradient
+    scaled = gain_one * first_gradient
     tokens_gradient = resid_gradient + rho_one * (
         scaled - unit_one * jnp.mean(unit_one * scaled, axis=-1, keepdims=True)
     )

time: 1180 us -> 837 us (0.71)
  waiting for transfers between devices: 791 us -> 358 us
  starting transfers between devices: 9.49 us -> 149 us
  blocking collectives: 131 us -> 0 us
  local copies, waits for them, and re-layouts: 43.1 us -> 75 us
  between operations: 15.2 us -> 44.6 us
  other arithmetic: 37.2 us -> 65 us
    reduce_scatter x4 -> x0, waiting for transfers between devices: 390 us -> none  [the longest x3 244 us: scatter_blk(): return lax.psum_scatter(rows, 'blk', scatter_dimension=0, tiled=True)]
    ppermute x0 -> x97, waiting for transfers between devices: none -> 358 us  [the longest x92 318 us: hop(): lax.ppermute(value, 'blk', [(RING[i], RING[(i + by) % count]) for i in ra...]
    all_gather x4 -> x0, waiting for transfers between devices: 228 us -> none  [the longest x3 225 us: gather_blk(): return lax.all_gather(rows, 'blk', axis=0, tiled=True)]
    ppermute x0 -> x97, starting transfers between devices: none -> 148 us  [the longest x92 146 us: hop(): lax.ppermute(value, 'blk', [(RING[i], RING[(i + by) % count]) for i in ra...]
    all_to_all x4 -> x0, blocking collectives: 131 us -> none  [exchange_blk(): lax.all_to_all(pieces, 'blk', split_axis=0, concat_axis=0, tiled=True)]
    all_gather x4, waiting for transfers between devices: 74.3 us -> 0.04 us  [gather_head(): return lax.all_gather(rows, 'head', axis=0, tiled=True)]
    reduce_scatter x4, waiting for transfers between devices: 69.7 us -> 0.04 us  [scatter_head(): return lax.psum_scatter(rows, 'head', scatter_dimension=0, tiled=True)]
    all_to_all x2 -> x0, waiting for transfers between devices: 26.4 us -> none  [exchange_blk(): lax.all_to_all(pieces, 'blk', split_axis=0, concat_axis=0, tiled=True)]
  transfers between devices with their start and end apart: 18 -> 105, of which waited for: 15 -> 51; matrix products, arithmetic and copies ran while one was open for 10% -> 22% of each run, Pallas kernels for 2% -> 6%
where the time goes in v2:
time: 837 us; the launch traced here: 828 us
  waiting for transfers between devices  358 us (43%)
  starting transfers between devices  149 us (18%)
  matrix products  82 us (10%)
  local copies, waits for them, and re-layouts  75 us (9%)
  other arithmetic  65 us (8%)
  Pallas kernels  53.3 us (6%)
  between operations  44.6 us (5%)
    ppermute x92, waiting for transfers between devices, hop(): lax.ppermute(value, 'blk', [(RING[i], RING[(i + by) % count]) for i in ra...  318 us
    ppermute x92, starting transfers between devices, hop(): lax.ppermute(value, 'blk', [(RING[i], RING[(i + by) % count]) for i in ra...  146 us
    dot_general x36, matrix products, matmul(): lax.dot_general(left, right, dims, preferred_element_type=jnp.float32)  82 us
    ppermute x5, waiting for transfers between devices, cross(): return lax.ppermute(value, 'head', [(i, i ^ by) for i in range(4)])  40.2 us
    unnamed x338, local copies, waits for them, and re-layouts  38.9 us
    pallas_call x1, Pallas kernels, attend_back(): pl.pallas_call(attend_back_kernel, grid_spec=pltpu.PrefetchScalarGridSpec...  30.7 us
    pallas_call x1, Pallas kernels, attend(): pl.pallas_call(attend_kernel, grid_spec=pltpu.PrefetchScalarGridSpec(num_...  22.6 us
  transfers between devices with their start and end apart: 105, of which 51 were waited for; matrix products, arithmetic and copies ran while one was open for 22% of the time, Pallas kernels for 6%

profile of v2, /device:TPU:0, one launch (start us, length us, event | category | flops | bytes accessed | tf_op | source)
XLA Modules:
  0.0 827.6 jit_solution(10459137883337848328)
XLA Ops:
  126.2 34.0 %collective-permute-done.28 = bf16[1,64,1536]{2,0,1:T(2,128)(2,1)S(1)} collective-permute-done((bf16[1,64,1536]{2,0,1:T(2,128)(2,1)S(1)}, bf16[1,64,1536]{2,0,1:T(2,128)(2,1)S(1)}, u32[]{:S(2)}, u32[]{:S(2)}) %collective-permute-start.28) | collective-permute-done | bytes 196640 | tf_op jit(solution)/shard_map/ppermute | solution.py:615
  160.2 17.3 %collective-permute-start.29 = (bf16[1,64,1536]{2,0,1:T(2,128)(2,1)S(1)}, bf16[1,64,1536]{2,0,1:T(2,128)(2,1)S(1)}, u32[]{:S(2)}, u32[]{:S(2)}) collective-permute-start(bf16[1,64,1536]{2,0,1:T(2,128)(2,1)S(1)} %get-tuple-element.98), channel_id=1, source_target_pairs={{0,8},{8,16},{16,24},{24,28},{28,20},{20,12},{12,4},{4,0},{1,9},{9... | collective-permute-start | bytes 589832 | tf_op jit(solution)/shard_map/ppermute | solution.py:615
  186.0 10.9 %collective-permute-done.30 = bf16[1,64,1536]{2,0,1:T(2,128)(2,1)S(1)} collective-permute-done((bf16[1,64,1536]{2,0,1:T(2,128)(2,1)S(1)}, bf16[1,64,1536]{2,0,1:T(2,128)(2,1)S(1)}, u32[]{:S(2)}, u32[]{:S(2)}) %collective-permute-start.30) | collective-permute-done | bytes 196640 | tf_op jit(solution)/shard_map/ppermute | solution.py:615
  230.2 22.4 %collective-permute-done.16 = bf16[1024,256]{1,0:T(8,128)(2,1)S(1)} collective-permute-done((bf16[1024,256]{1,0:T(8,128)(2,1)S(1)}, bf16[1024,256]{1,0:T(8,128)(2,1)S(1)}, u32[]{:S(2)}, u32[]{:S(2)}) %collective-permute-start.16) | collective-permute-done | bytes 524320 | tf_op jit(solution)/shard_map/ppermute | solution.py:619
  255.9 22.6 %attend.1 = (bf16[1024,256]{1,0:T(8,128)(2,1)}, f32[8,8,256]{2,1,0:T(8,128)}) custom-call(s32[8]{0:T(128)} %get-tuple-element.236.place_ref, s32[32]{0:T(128)} %select_reduce_fusion.order_ref, bf16[1024,256]{1,0:T(8,128)(2,1)} %maximum_maximum_fusion.q_ref, bf16[4096,256]{1,0:T(8,128)(2,1)} %copy-done.125), custom_call_target="tpu_custom_call" | custom-call | flops 2147483648 | bytes 3145728 | tf_op jit(solution)/shard_map/attend/pallas_call | solution.py:474
  292.6 10.3 %collective-permute-done.23 = bf16[128,2048]{1,0:T(8,128)(2,1)S(1)} collective-permute-done((bf16[128,2048]{1,0:T(8,128)(2,1)S(1)}, bf16[128,2048]{1,0:T(8,128)(2,1)S(1)}, u32[]{:S(2)}, u32[]{:S(2)}) %collective-permute-start.23) | collective-permute-done | bytes 524320 | tf_op jit(solution)/shard_map/ppermute | solution.py:615
  338.8 10.7 %collective-permute-done.27 = bf16[128,2048]{1,0:T(8,128)(2,1)S(1)} collective-permute-done((bf16[128,2048]{1,0:T(8,128)(2,1)S(1)}, bf16[128,2048]{1,0:T(8,128)(2,1)S(1)}, u32[]{:S(2)}, u32[]{:S(2)}) %collective-permute-start.27) | collective-permute-done | bytes 524320 | tf_op jit(solution)/shard_map/ppermute | solution.py:615
  351.6 9.2 %collective-permute-done.42 = bf16[128,2048]{1,0:T(8,128)(2,1)S(1)} collective-permute-done((bf16[128,2048]{1,0:T(8,128)(2,1)S(1)}, bf16[128,2048]{1,0:T(8,128)(2,1)S(1)}, u32[]{:S(2)}, u32[]{:S(2)}) %collective-permute-start.42) | collective-permute-done | bytes 524320 | tf_op jit(solution)/shard_map/ppermute | solution.py:615
  362.9 9.2 %collective-permute-done.36 = bf16[128,2048]{1,0:T(8,128)(2,1)S(1)} collective-permute-done((bf16[128,2048]{1,0:T(8,128)(2,1)S(1)}, bf16[128,2048]{1,0:T(8,128)(2,1)S(1)}, u32[]{:S(2)}, u32[]{:S(2)}) %collective-permute-start.36) | collective-permute-done | bytes 524320 | tf_op jit(solution)/shard_map/ppermute | solution.py:615
  374.1 9.2 %collective-permute-done.44 = bf16[128,2048]{1,0:T(8,128)(2,1)S(1)} collective-permute-done((bf16[128,2048]{1,0:T(8,128)(2,1)S(1)}, bf16[128,2048]{1,0:T(8,128)(2,1)S(1)}, u32[]{:S(2)}, u32[]{:S(2)}) %collective-permute-start.44) | collective-permute-done | bytes 524320 | tf_op jit(solution)/shard_map/ppermute | solution.py:615
  385.4 9.2 %collective-permute-done.38 = bf16[128,2048]{1,0:T(8,128)(2,1)S(1)} collective-permute-done((bf16[128,2048]{1,0:T(8,128)(2,1)S(1)}, bf16[128,2048]{1,0:T(8,128)(2,1)S(1)}, u32[]{:S(2)}, u32[]{:S(2)}) %collective-permute-start.38) | collective-permute-done | bytes 524320 | tf_op jit(solution)/shard_map/ppermute | solution.py:615
  446.4 10.4 %collective-permute-done.54 = bf16[128,2048]{1,0:T(8,128)(2,1)S(1)} collective-permute-done((bf16[128,2048]{1,0:T(8,128)(2,1)S(1)}, bf16[128,2048]{1,0:T(8,128)(2,1)S(1)}, u32[]{:S(2)}, u32[]{:S(2)}) %collective-permute-start.54) | collective-permute-done | bytes 524320 | tf_op jit(solution)/shard_map/ppermute | solution.py:615
  462.1 8.6 %collective-permute-done.51 = bf16[128,2048]{1,0:T(8,128)(2,1)S(1)} collective-permute-done((bf16[128,2048]{1,0:T(8,128)(2,1)S(1)}, bf16[128,2048]{1,0:T(8,128)(2,1)S(1)}, u32[]{:S(2)}, u32[]{:S(2)}) %collective-permute-start.51) | collective-permute-done | bytes 524320 | tf_op jit(solution)/shard_map/ppermute | solution.py:615
  473.9 11.7 %collective-permute-done.52 = bf16[128,2048]{1,0:T(8,128)(2,1)S(1)} collective-permute-done((bf16[128,2048]{1,0:T(8,128)(2,1)S(1)}, bf16[128,2048]{1,0:T(8,128)(2,1)S(1)}, u32[]{:S(2)}, u32[]{:S(2)}) %collective-permute-start.52) | collective-permute-done | bytes 524320 | tf_op jit(solution)/shard_map/ppermute | solution.py:615
  490.1 9.7 %collective-permute-done.61 = bf16[128,2048]{1,0:T(8,128)(2,1)S(1)} collective-permute-done((bf16[128,2048]{1,0:T(8,128)(2,1)S(1)}, bf16[128,2048]{1,0:T(8,128)(2,1)S(1)}, u32[]{:S(2)}, u32[]{:S(2)}) %collective-permute-start.61) | collective-permute-done | bytes 524320 | tf_op jit(solution)/shard_map/ppermute | solution.py:615
  501.9 9.3 %collective-permute-done.62 = bf16[128,2048]{1,0:T(8,128)(2,1)S(1)} collective-permute-done((bf16[128,2048]{1,0:T(8,128)(2,1)S(1)}, bf16[128,2048]{1,0:T(8,128)(2,1)S(1)}, u32[]{:S(2)}, u32[]{:S(2)}) %collective-permute-start.62) | collective-permute-done | bytes 524320 | tf_op jit(solution)/shard_map/ppermute | solution.py:615
  556.6 30.7 %attend_back.1 = (bf16[1024,256]{1,0:T(8,128)(2,1)}, bf16[4096,256]{1,0:T(8,128)(2,1)}) custom-call(s32[8]{0:T(128)} %get-tuple-element.236.place_ref, s32[32]{0:T(128)} %select_reduce_fusion.order_ref, bf16[1024,256]{1,0:T(8,128)(2,1)} %maximum_maximum_fusion.q_ref, bf16[1024,256]{1,0:T(8,128)(2,1)} %pad_maximum_fusion.16.grad_ref, ...), custom_call_target="tpu_custom_call" | custom-call | flops 5368709120 | bytes 6291456 | tf_op jit(solution)/shard_map/attend_back/pallas_call | solution.py:575
  591.9 15.0 %collective-permute-done.74 = bf16[1024,256]{1,0:T(8,128)(2,1)S(1)} collective-permute-done((bf16[1024,256]{1,0:T(8,128)(2,1)S(1)}, bf16[1024,256]{1,0:T(8,128)(2,1)S(1)}, u32[]{:S(2)}, u32[]{:S(2)}) %collective-permute-start.74) | collective-permute-done | bytes 524320 | tf_op jit(solution)/shard_map/ppermute | solution.py:619
  633.2 20.0 %convolution_convert_fusion = bf16[2048,1536]{1,0:T(8,128)(2,1)S(1)} fusion(bf16[1024,2048]{1,0:T(8,128)(2,1)} %constant_dynamic-update-slice_fusion.17, bf16[128,768]{1,0:T(8,128)(2,1)S(1)} %copy-done.116, bf16[128,768]{1,0:T(8,128)(2,1)S(1)} %copy-done.114, bf16[256,768]{1,0:T(8,128)(2,1)S(1)} %copy-done.143, bf16[256,768]{1,0:T(8,128)(2,1)S(1)} %copy-done.141, ...), kind=kOutput, calls=%fused_computation | convolution fusion | flops 6470762496 | bytes 13631488 | tf_op jit(solution)/shard_map/dot_general | solution.py:605
  677.7 12.4 %collective-permute-done.75 = bf16[64,2048]{1,0:T(8,128)(2,1)S(1)} collective-permute-done((bf16[64,2048]{1,0:T(8,128)(2,1)S(1)}, bf16[64,2048]{1,0:T(8,128)(2,1)S(1)}, u32[]{:S(2)}, u32[]{:S(2)}) %collective-permute-start.75) | collective-permute-done | bytes 262176 | tf_op jit(solution)/shard_map/ppermute | solution.py:615
  695.6 9.5 %collective-permute-done.80 = bf16[128,2048]{1,0:T(8,128)(2,1)S(1)} collective-permute-done((bf16[128,2048]{1,0:T(8,128)(2,1)S(1)}, bf16[128,2048]{1,0:T(8,128)(2,1)S(1)}, u32[]{:S(2)}, u32[]{:S(2)}) %collective-permute-start.80) | collective-permute-done | bytes 524320 | tf_op jit(solution)/shard_map/ppermute | solution.py:615
  709.2 8.8 %collective-permute-done.67 = bf16[128,2048]{1,0:T(8,128)(2,1)S(1)} collective-permute-done((bf16[128,2048]{1,0:T(8,128)(2,1)S(1)}, bf16[128,2048]{1,0:T(8,128)(2,1)S(1)}, u32[]{:S(2)}, u32[]{:S(2)}) %collective-permute-start.67) | collective-permute-done | bytes 524320 | tf_op jit(solution)/shard_map/ppermute | solution.py:615
  788.5 10.0 %collective-permute-start.91 = (bf16[1,64,1536]{2,1,0:T(8,128)(2,1)S(1)}, bf16[1,64,1536]{2,1,0:T(8,128)(2,1)S(1)}, u32[]{:S(2)}, u32[]{:S(2)}) collective-permute-start(bf16[1,64,1536]{2,1,0:T(8,128)(2,1)S(1)} %get-tuple-element.82), channel_id=1, source_target_pairs={{0,8},{8,16},{16,24},{24,28},{28,20},{20,12},{12,4},{4,0},{1,9},{9... | collective-permute-start | bytes 589832 | tf_op jit(solution)/shard_map/ppermute | solution.py:615
  801.6 9.9 %collective-permute-start.92 = (bf16[1,64,1536]{2,1,0:T(8,128)(2,1)S(1)}, bf16[1,64,1536]{2,1,0:T(8,128)(2,1)S(1)}, u32[]{:S(2)}, u32[]{:S(2)}) collective-permute-start(bf16[1,64,1536]{2,1,0:T(8,128)(2,1)S(1)} %get-tuple-element.81), channel_id=1, source_target_pairs={{0,4},{8,0},{16,8},{24,16},{28,24},{20,28},{12,20},{4,12},{1,5},{9... | collective-permute-start | bytes 589832 | tf_op jit(solution)/shard_map/ppermute | solution.py:615
  (790 shorter events, 452.3 us)
Async XLA Ops:
  7.2 191.7 %all-gather.5.cloned.1.call-start = ((), (), s32[]{:S(2)}) async-start(), calls=%async_computation.4 | async-start | bytes 3276800 | tf_op jit(solution)/shard_map/all_gather | solution.py:676
  18.1 48.1 %collective-permute-start.7 = (bf16[1,80,512]{2,0,1:T(2,128)(2,1)}, bf16[1,80,512]{2,0,1:T(2,128)(2,1)S(1)}, u32[]{:S(2)}, u32[]{:S(2)}) collective-permute-start(bf16[1,80,512]{2,0,1:T(2,128)(2,1)} %get-tuple-element.183), channel_id=1, source_target_pairs={{0,24},{8,28},{16,20},{24,12},{28,4},{20,0},{12,8},{4,16},{1,25},{... | collective-permute-start | bytes 245768 | tf_op jit(solution)/shard_map/ppermute | solution.py:615
  23.2 43.0 %collective-permute-start.6 = (bf16[1,80,512]{2,0,1:T(2,128)(2,1)}, bf16[1,80,512]{2,0,1:T(2,128)(2,1)S(1)}, u32[]{:S(2)}, u32[]{:S(2)}) collective-permute-start(bf16[1,80,512]{2,0,1:T(2,128)(2,1)} %get-tuple-element.184), channel_id=1, source_target_pairs={{0,12},{8,4},{16,0},{24,8},{28,16},{20,24},{12,28},{4,20},{1,13},{... | collective-permute-start | bytes 245768 | tf_op jit(solution)/shard_map/ppermute | solution.py:615
  34.6 31.6 %collective-permute-start.8 = (bf16[1,80,512]{2,0,1:T(2,128)(2,1)}, bf16[1,80,512]{2,0,1:T(2,128)(2,1)S(1)}, u32[]{:S(2)}, u32[]{:S(2)}) collective-permute-start(bf16[1,80,512]{2,0,1:T(2,128)(2,1)} %get-tuple-element.177), channel_id=1, source_target_pairs={{0,20},{8,12},{16,4},{24,0},{28,8},{20,16},{12,24},{4,28},{1,21},{... | collective-permute-start | bytes 245768 | tf_op jit(solution)/shard_map/ppermute | solution.py:615
  67.2 211.3 %all-gather.7.cloned.1.call-start = ((), (), s32[]{:S(2)}) async-start(), calls=%async_computation.5 | async-start | bytes 1310720 | tf_op jit(solution)/shard_map/all_gather | solution.py:676
  69.4 341.6 %all-gather.9.cloned.1.call-start = ((), (), s32[]{:S(2)}) async-start(), calls=%async_computation.6 | async-start | bytes 7864320 | tf_op jit(solution)/shard_map/all_gather | solution.py:676
  115.8 81.3 %collective-permute-start.34 = (bf16[1,64,1536]{2,0,1:T(2,128)(2,1)S(1)}, bf16[1,64,1536]{2,0,1:T(2,128)(2,1)S(1)}, u32[]{:S(2)}, u32[]{:S(2)}) collective-permute-start(bf16[1,64,1536]{2,0,1:T(2,128)(2,1)S(1)} %get-tuple-element.93), channel_id=1, source_target_pairs={{0,20},{8,12},{16,4},{24,0},{28,8},{20,16},{12,24},{4,28},{1,21},{... | collective-permute-start | bytes 589832 | tf_op jit(solution)/shard_map/ppermute | solution.py:615
  118.0 79.0 %collective-permute-start.33 = (bf16[1,64,1536]{2,0,1:T(2,128)(2,1)S(1)}, bf16[1,64,1536]{2,0,1:T(2,128)(2,1)S(1)}, u32[]{:S(2)}, u32[]{:S(2)}) collective-permute-start(bf16[1,64,1536]{2,0,1:T(2,128)(2,1)S(1)} %get-tuple-element.94), channel_id=1, source_target_pairs={{0,24},{8,28},{16,20},{24,12},{28,4},{20,0},{12,8},{4,16},{1,25},{... | collective-permute-start | bytes 589832 | tf_op jit(solution)/shard_map/ppermute | solution.py:615
  119.7 77.3 %collective-permute-start.32 = (bf16[1,64,1536]{2,0,1:T(2,128)(2,1)S(1)}, bf16[1,64,1536]{2,0,1:T(2,128)(2,1)S(1)}, u32[]{:S(2)}, u32[]{:S(2)}) collective-permute-start(bf16[1,64,1536]{2,0,1:T(2,128)(2,1)S(1)} %get-tuple-element.95), channel_id=1, source_target_pairs={{0,12},{8,4},{16,0},{24,8},{28,16},{20,24},{12,28},{4,20},{1,13},{... | collective-permute-start | bytes 589832 | tf_op jit(solution)/shard_map/ppermute | solution.py:615
  120.7 76.3 %collective-permute-start.31 = (bf16[1,64,1536]{2,0,1:T(2,128)(2,1)S(1)}, bf16[1,64,1536]{2,0,1:T(2,128)(2,1)S(1)}, u32[]{:S(2)}, u32[]{:S(2)}) collective-permute-start(bf16[1,64,1536]{2,0,1:T(2,128)(2,1)S(1)} %get-tuple-element.96), channel_id=1, source_target_pairs={{0,16},{8,24},{16,28},{24,20},{28,12},{20,4},{12,0},{4,8},{1,17},{... | collective-permute-start | bytes 589832 | tf_op jit(solution)/shard_map/ppermute | solution.py:615
  122.7 37.5 %collective-permute-start.28 = (bf16[1,64,1536]{2,0,1:T(2,128)(2,1)S(1)}, bf16[1,64,1536]{2,0,1:T(2,128)(2,1)S(1)}, u32[]{:S(2)}, u32[]{:S(2)}) collective-permute-start(bf16[1,64,1536]{2,0,1:T(2,128)(2,1)S(1)} %get-tuple-element.99), channel_id=1, source_target_pairs={{0,28},{8,20},{16,12},{24,4},{28,0},{20,8},{12,16},{4,24},{1,29},{... | collective-permute-start | bytes 589832 | tf_op jit(solution)/shard_map/ppermute | solution.py:615
  160.2 25.8 %collective-permute-start.29 = (bf16[1,64,1536]{2,0,1:T(2,128)(2,1)S(1)}, bf16[1,64,1536]{2,0,1:T(2,128)(2,1)S(1)}, u32[]{:S(2)}, u32[]{:S(2)}) collective-permute-start(bf16[1,64,1536]{2,0,1:T(2,128)(2,1)S(1)} %get-tuple-element.98), channel_id=1, source_target_pairs={{0,8},{8,16},{16,24},{24,28},{28,20},{20,12},{12,4},{4,0},{1,9},{9... | collective-permute-start | bytes 589832 | tf_op jit(solution)/shard_map/ppermute | solution.py:615
  198.3 219.5 %all-gather.11.cloned.1.call-start = ((), (), s32[]{:S(2)}) async-start(), calls=%async_computation.7 | async-start | bytes 3932160 | tf_op jit(solution)/shard_map/all_gather | solution.py:676
  227.3 25.4 %collective-permute-start.16 = (bf16[1024,256]{1,0:T(8,128)(2,1)S(1)}, bf16[1024,256]{1,0:T(8,128)(2,1)S(1)}, u32[]{:S(2)}, u32[]{:S(2)}) collective-permute-start(bf16[1024,256]{1,0:T(8,128)(2,1)S(1)} %maximum_maximum_fusion.1), channel_id=1, source_target_pairs={{0,2},{1,3},{2,0},{3,1},{4,6},{5,7},{6,4},{7,5},{8,10},{9,11},{10,... | collective-permute-start | bytes 1572872 | tf_op jit(solution)/shard_map/ppermute | solution.py:619
  228.7 25.0 %collective-permute-start.15 = (bf16[1024,256]{1,0:T(8,128)(2,1)S(1)}, bf16[1024,256]{1,0:T(8,128)(2,1)S(1)}, u32[]{:S(2)}, u32[]{:S(2)}) collective-permute-start(bf16[1024,256]{1,0:T(8,128)(2,1)S(1)} %maximum_maximum_fusion.1), channel_id=1, source_target_pairs={{0,1},{1,0},{2,3},{3,2},{4,5},{5,4},{6,7},{7,6},{8,9},{9,8},{10,11... | collective-permute-start | bytes 1572872 | tf_op jit(solution)/shard_map/ppermute | solution.py:619
  306.8 434.7 %reduce-scatter.7.cloned.1.call-start = ((), (), s32[]{:S(2)}) async-start(), calls=%async_computation.9 | async-start | bytes 1310720 | tf_op jit(solution)/shard_map/reduce_scatter | solution.py:680
  533.2 210.2 %reduce-scatter.11.cloned.1.call-start = ((), (), s32[]{:S(2)}) async-start(), calls=%async_computation.11 | async-start | bytes 3932160 | tf_op jit(solution)/shard_map/reduce_scatter | solution.py:680
  549.5 200.5 %reduce-scatter.5.cloned.1.call-start = ((), (), s32[]{:S(2)}) async-start(), calls=%async_computation.8 | async-start | bytes 3276800 | tf_op jit(solution)/shard_map/reduce_scatter | solution.py:680
  622.1 154.1 %reduce-scatter.9.cloned.1.call-start = ((), (), s32[]{:S(2)}) async-start(), calls=%async_computation.10 | async-start | bytes 7864320 | tf_op jit(solution)/shard_map/reduce_scatter | solution.py:680
  692.8 25.1 %collective-permute-start.67 = (bf16[128,2048]{1,0:T(8,128)(2,1)S(1)}, bf16[128,2048]{1,0:T(8,128)(2,1)S(1)}, u32[]{:S(2)}, u32[]{:S(2)}) collective-permute-start(bf16[128,2048]{1,0:T(8,128)(2,1)S(1)} %get-tuple-element.137), channel_id=1, source_target_pairs={{0,8},{8,16},{16,24},{24,28},{28,20},{20,12},{12,4},{4,0},{1,9},{9... | collective-permute-start | bytes 1572872 | tf_op jit(solution)/shard_map/ppermute | solution.py:615
  780.2 35.8 %collective-permute-start.96 = (bf16[1,64,1536]{2,1,0:T(8,128)(2,1)S(1)}, bf16[1,64,1536]{2,1,0:T(8,128)(2,1)S(1)}, u32[]{:S(2)}, u32[]{:S(2)}) collective-permute-start(bf16[1,64,1536]{2,1,0:T(8,128)(2,1)S(1)} %get-tuple-element.77), channel_id=1, source_target_pairs={{0,20},{8,12},{16,4},{24,0},{28,8},{20,16},{12,24},{4,28},{1,21},{... | collective-permute-start | bytes 589832 | tf_op jit(solution)/shard_map/ppermute | solution.py:615
  781.6 34.3 %collective-permute-start.95 = (bf16[1,64,1536]{2,1,0:T(8,128)(2,1)S(1)}, bf16[1,64,1536]{2,1,0:T(8,128)(2,1)S(1)}, u32[]{:S(2)}, u32[]{:S(2)}) collective-permute-start(bf16[1,64,1536]{2,1,0:T(8,128)(2,1)S(1)} %get-tuple-element.78), channel_id=1, source_target_pairs={{0,24},{8,28},{16,20},{24,12},{28,4},{20,0},{12,8},{4,16},{1,25},{... | collective-permute-start | bytes 589832 | tf_op jit(solution)/shard_map/ppermute | solution.py:615
  784.0 31.9 %collective-permute-start.94 = (bf16[1,64,1536]{2,1,0:T(8,128)(2,1)S(1)}, bf16[1,64,1536]{2,1,0:T(8,128)(2,1)S(1)}, u32[]{:S(2)}, u32[]{:S(2)}) collective-permute-start(bf16[1,64,1536]{2,1,0:T(8,128)(2,1)S(1)} %get-tuple-element.79), channel_id=1, source_target_pairs={{0,12},{8,4},{16,0},{24,8},{28,16},{20,24},{12,28},{4,20},{1,13},{... | collective-permute-start | bytes 589832 | tf_op jit(solution)/shard_map/ppermute | solution.py:615
  784.0 31.9 %collective-permute-start.93 = (bf16[1,64,1536]{2,1,0:T(8,128)(2,1)S(1)}, bf16[1,64,1536]{2,1,0:T(8,128)(2,1)S(1)}, u32[]{:S(2)}, u32[]{:S(2)}) collective-permute-start(bf16[1,64,1536]{2,1,0:T(8,128)(2,1)S(1)} %get-tuple-element.80), channel_id=1, source_target_pairs={{0,16},{8,24},{16,28},{24,20},{28,12},{20,4},{12,0},{4,8},{1,17},{... | collective-permute-start | bytes 589832 | tf_op jit(solution)/shard_map/ppermute | solution.py:615
  (233 other events, 2383.7 us)
Sparse Core Ops, SparseCore 0:
  67.3 24.1 all-gather.4
  93.1 16.6 all-gather.6
  198.5 57.0 all-gather.8
  306.9 26.7 all-gather.10
  533.4 23.3 reduce-scatter.6
  559.2 39.0 reduce-scatter.10
  622.2 34.4 reduce-scatter.4
  659.3 58.8 reduce-scatter.8

commit v3 on v2

--- a/solution.py
+++ b/solution.py
@@ -623,27 +623,238 @@
     return (left.astype(jnp.float32) + right.astype(jnp.float32)).astype(left.dtype)
 
 
-def ring_gather(own):
+def tied(values, extra):
+    if not extra:
+        return values
+    return lax.optimization_barrier((*values, *extra))[: len(values)]
+
+
+def no_fill(step, got):
+    return ()
+
+
+def ring_gather(own, fill=no_fill):
     half = own.shape[0] // 2
     got = {0: own}
+    left = right = own
     for step in (1, 2, 3):
-        got[step] = hop(got[step - 1], -1)
-        got[8 - step] = hop(got[(9 - step) % 8], 1)
-    got[4] = jnp.concatenate([hop(got[3][:half], -1), hop(got[5][half:], 1)], axis=0)
+        got[step], got[8 - step] = left, right = hop(left, -1), hop(right, 1)
+        left, right = tied((left, right), fill(step, got))
+    got[4] = jnp.concatenate([hop(left[:half], -1), hop(right[half:], 1)], axis=0)
+    fill(4, got)
     return [got[s] for s in STRIPS]
 
 
-def ring_scatter(parts):
-    part = dict(zip(STRIPS, parts))
+def ring_scatter(part, fill=no_fill):
     half = part[0].shape[0] // 2
-    up = hop(part[4][:half], 1)
-    down = hop(part[4][half:], -1)
-    up = hop(jnp.concatenate([add(part[3][:half], up), part[3][half:]], axis=0), 1)
-    down = hop(jnp.concatenate([part[5][:half], add(part[5][half:], down)], axis=0), -1)
-    up, down = hop(add(part[2], up), 1), hop(add(part[6], down), -1)
-    up, down = hop(add(part[1], up), 1), hop(add(part[7], down), -1)
+    up, down = hop(part[4][:half], 1), hop(part[4][half:], -1)
+    up = jnp.concatenate([add(part[3][:half], up), part[3][half:]], axis=0)
+    down = jnp.concatenate([part[5][:half], add(part[5][half:], down)], axis=0)
+    for step in (2, 1):
+        up, down = tied((up, down), fill(3 - step, None))
+        up, down = add(part[step], hop(up, 1)), add(part[8 - step], hop(down, -1))
+    up, down = tied((up, down), fill(3, None))
+    up, down = hop(up, 1), hop(down, -1)
     wide = jnp.float32
     return part[0].astype(wide) + up.astype(wide) + down.astype(wide)
+
+
+def ring_swap(pieces, rows, fill=no_fill):
+    cut = 4 * rows + rows // 2
+    right, left = pieces[rows:cut], pieces[cut:]
+    from_left, from_right = [], []
+    for step in (1, 2, 3, 4):
+        right, left = hop(right, 1), hop(left, -1)
+        if step < 4:
+            from_left.append(right[:rows])
+            from_right.append(left[-rows:])
+            right, left = tied((right[rows:], left[:-rows]), fill(step, None))
+    return jnp.concatenate(
+        [pieces[:rows], *from_right, right, left, *reversed(from_left)], axis=0
+    )
+
+
+def gather_cross(own):
+    far = cross(own, 2)
+    return own, cross(own, 1), far, cross(far, 1)
+
+
+def scatter_cross(pieces):
+    half = pieces.shape[0] // 2
+    kept = add(pieces[:half], cross(pieces[half:], 1))
+    return add(kept[: half // 2], cross(kept[half // 2 :], 2))
+
+
+def slice_attn_kernel(at_ref, q_ref, k_ref, v_ref, gain_ref, out_ref):
+    rows, cols = q_ref.shape
+    out_ref[:rows, :cols] = q_ref[...]
+    out_ref[:rows, cols : cols + HEAD_SIZE] = k_ref[...]
+    out_ref[:rows, cols + HEAD_SIZE :] = v_ref[...]
+    out_ref[rows:, :] = gain_ref[...]
+
+
+def slice_attn(at, query, key, value, gains):
+    count = at.shape[0]
+    rows, pad = query.shape[0], gains.shape[0]
+    widths = [w.shape[1] // count for w in (query, key, value)]
+    specs = [pl.BlockSpec((rows, w), lambda i, at: (0, at[i])) for w in widths]
+    return pl.pallas_call(
+        slice_attn_kernel,
+        grid_spec=pltpu.PrefetchScalarGridSpec(
+            num_scalar_prefetch=1,
+            grid=(count,),
+            in_specs=specs + [pl.BlockSpec(gains.shape, lambda i, at: (0, 0))],
+            out_specs=pl.BlockSpec((rows + pad, sum(widths)), lambda i, at: (i, 0)),
+        ),
+        out_shape=jax.ShapeDtypeStruct((count * (rows + pad), sum(widths)), jnp.bfloat16),
+        name="slice_attn",
+    )(at, query, key, value, gains)
+
+
+def slice_ff_kernel(at_ref, gate_ref, up_ref, out_ref):
+    cols = gate_ref.shape[1]
+    out_ref[:, :cols] = gate_ref[...]
+    out_ref[:, cols:] = up_ref[...]
+
+
+def slice_ff(at, gate, up):
+    count = at.shape[0]
+    rows, cols = gate.shape[0], gate.shape[1] // count
+    spec = pl.BlockSpec((rows, cols), lambda i, at: (0, at[i]))
+    return pl.pallas_call(
+        slice_ff_kernel,
+        grid_spec=pltpu.PrefetchScalarGridSpec(
+            num_scalar_prefetch=1,
+            grid=(count,),
+            in_specs=[spec, spec],
+            out_specs=pl.BlockSpec((rows, 2 * cols), lambda i, at: (i, 0)),
+        ),
+        out_shape=jax.ShapeDtypeStruct((count * rows, 2 * cols), jnp.bfloat16),
+        name="slice_ff",
+    )(at, gate, up)
+
+
+def assemble_kernel(at_ref, *refs, rows):
+    inputs, outputs = refs[:4], refs[4:]
+    own = at_ref[8]
+    for j, piece in enumerate(inputs):
+        outputs[0][0, own ^ j] = piece[:rows]
+        if len(outputs) > 1:
+            outputs[1][0, own ^ j] = piece[rows:]
+
+
+def assemble(at, pieces, rows):
+    count = at.shape[0] - 1
+    total, cols = pieces[0].shape
+    each = total // count
+    parts = [rows] if each == rows else [rows, each - rows]
+    return pl.pallas_call(
+        lambda *refs: assemble_kernel(*refs, rows=rows),
+        grid_spec=pltpu.PrefetchScalarGridSpec(
+            num_scalar_prefetch=1,
+            grid=(count,),
+            in_specs=[pl.BlockSpec((each, cols), lambda i, at: (i, 0))] * 4,
+            out_specs=[
+                pl.BlockSpec((1, 4, part, cols), lambda i, at: (at[i], 0, 0, 0)) for part in parts
+            ],
+        ),
+        out_shape=[
+            jax.ShapeDtypeStruct((count, 4, part, cols), jnp.bfloat16) for part in parts
+        ],
+        name="assemble",
+    )(at, *pieces)
+
+
+def weight_grads_kernel(at_ref, left_ref, right_ref, *refs, rows):
+    out_ref, held = refs[-2:]
+    own = at_ref[8]
+    sums = lax.dot_general(left_ref[...], right_ref[...], DOWN, preferred_element_type=jnp.float32)
+    held[...] = sums.astype(jnp.bfloat16).reshape(held.shape)
+    for k, j in enumerate((0, 2, 1, 3)):
+        out_ref[k, 0, :rows] = held[own ^ j]
+        if len(refs) > 2:
+            out_ref[k, 0, rows:] = refs[0][0, own ^ j]
+
+
+def weight_grads(at, left, right, rows, extra=None):
+    count = at.shape[0] - 1
+    tokens, cols = right.shape
+    each = rows if extra is None else rows + extra.shape[2]
+    in_specs = [
+        pl.BlockSpec((tokens, 4 * rows), lambda i, at: (0, at[i])),
+        pl.BlockSpec((tokens, cols), lambda i, at: (0, 0)),
+    ]
+    operands = [left, right]
+    if extra is not None:
+        in_specs.append(pl.BlockSpec((1, *extra.shape[1:]), lambda i, at: (at[i], 0, 0, 0)))
+        operands.append(extra)
+    out = pl.pallas_call(
+        lambda *refs: weight_grads_kernel(*refs, rows=rows),
+        grid_spec=pltpu.PrefetchScalarGridSpec(
+            num_scalar_prefetch=1,
+            grid=(count,),
+            in_specs=in_specs,
+            out_specs=pl.BlockSpec((4, 1, each, cols), lambda i, at: (0, i, 0, 0)),
+            scratch_shapes=[pltpu.VMEM((4, rows, cols), jnp.bfloat16)],
+        ),
+        out_shape=jax.ShapeDtypeStruct((4, count, each, cols), jnp.bfloat16),
+        cost_estimate=pl.CostEstimate(
+            flops=2 * left.size * cols,
+            bytes_accessed=2 * (left.size + right.size + left.shape[1] * cols),
+            transcendentals=0,
+        ),
+        name="weight_grads",
+    )(at, *operands)
+    return out.reshape(4 * count * each, cols)
+
+
+def lane_sums(block):
+    return sum(block[:, i : i + 128] for i in range(0, block.shape[1], 128))
+
+
+def widen_kernel(at_ref, piece_ref, *refs, count):
+    weights, grads, sums_ref = refs[:count], refs[count : 2 * count], refs[2 * count]
+    rows = weights[0].shape[0]
+
+    @pl.when(pl.program_id(0) == 0)
+    def _():
+        for ref in refs[2 * count :]:
+            ref[...] = jnp.zeros_like(ref)
+
+    first = 0
+    for weight, grad in zip(weights, grads):
+        cols = weight.shape[1]
+        block = piece_ref[:rows, first : first + cols].astype(jnp.float32)
+        grad[...] = block
+        sums_ref[...] += lane_sums(block * weight[...].astype(jnp.float32))
+        first += cols
+    if len(refs) > 2 * count + 1:
+        refs[-1][...] += piece_ref[rows:, :].astype(jnp.float32)
+
+
+def widen(at, pieces, *weights):
+    count = at.shape[0]
+    rows = weights[0].shape[0]
+    each, cols = pieces.shape[0] // count, pieces.shape[1]
+    specs = [
+        pl.BlockSpec((rows, w.shape[1] // count), lambda i, at: (0, at[i])) for w in weights
+    ]
+    shapes = [w.shape for w in weights] + [(rows, 128)]
+    out_specs = specs + [pl.BlockSpec((rows, 128), lambda i, at: (0, 0))]
+    if each > rows:
+        shapes.append((each - rows, cols))
+        out_specs.append(pl.BlockSpec(shapes[-1], lambda i, at: (0, 0)))
+    return pl.pallas_call(
+        lambda *refs: widen_kernel(*refs, count=len(weights)),
+        grid_spec=pltpu.PrefetchScalarGridSpec(
+            num_scalar_prefetch=1,
+            grid=(count,),
+            in_specs=[pl.BlockSpec((each, cols), lambda i, at: (i, 0))] + specs,
+            out_specs=out_specs,
+        ),
+        out_shape=[jax.ShapeDtypeStruct(shape, jnp.float32) for shape in shapes],
+        name="widen",
+    )(at, pieces, *weights)
 
 
 def grouped(strips):
@@ -658,18 +869,6 @@
         for group in groups
         for i in range(group.shape[0] // rows)
     ]
-
-
-def swap_slices(pieces, place, blk_index):
-    ring = jnp.asarray(RING, jnp.int32)
-    own = lax.dynamic_index_in_dim(pieces, blk_index, 0)
-    out = lax.dynamic_update_slice_in_dim(jnp.zeros_like(pieces), own, blk_index, 0)
-    for by in (4, 1, 7, 2, 6, 3, 5):
-        target = ring[(place + by) % 8]
-        source = ring[(place - by) % 8]
-        moved = hop(lax.dynamic_index_in_dim(pieces, target, 0), by)
-        out = lax.dynamic_update_slice_in_dim(out, moved, source, 0)
-    return out
 
 
 def gather_head(rows):
@@ -699,10 +898,6 @@
     gain_part = jnp.sum(turned * unit, axis=0)
     scaled = turned * gain
     return rho * (scaled - unit * jnp.mean(unit * scaled, axis=-1, keepdims=True)), gain_part
-
-
-def after(value, *earlier):
-    return lax.optimization_barrier((value, *earlier))[0]
 
 
 def per_device(
@@ -738,52 +933,31 @@
     halves = strip_count // stretch_order.shape[1]
     ring_place = jnp.where(blk_index % 2 == 0, blk_index // 2, 7 - blk_index // 2)
 
-    def pieces_of(*weights):
-        return jnp.concatenate(
-            [w.reshape(weight_rows, blk_count, w.shape[1] // blk_count) for w in weights], axis=2
-        ).transpose(1, 0, 2)
-
-    def natural(pieces, rows):
-        return pieces.reshape(head_count, blk_count, rows, -1).transpose(1, 0, 2, 3)
-
+    on = jnp.arange(blk_count, dtype=jnp.int32)
+    spot = (ring_place + on) % blk_count
+    at = jnp.where(spot < 4, 2 * spot, 15 - 2 * spot).astype(jnp.int32)
+    at_own = jnp.concatenate([at, head_index[None].astype(jnp.int32)])
     small = query_norm.shape[0]
     gains = jnp.concatenate([attention_norm, feedforward_norm, query_norm, key_norm])
-    gains = jnp.pad(gains, (0, attn_cols - gains.shape[0]))[None, None, :]
-    gains = jnp.pad(gains, ((0, 0), (0, 15), (0, 0)))
-    attn_pieces = jnp.concatenate(
-        [
-            pieces_of(query_weight, key_projection, value_projection),
-            jnp.broadcast_to(gains, (blk_count, 16, attn_cols)),
-        ],
-        axis=1,
-    )
+    gains = jnp.pad(gains[None, :], ((0, 15), (0, attn_cols - gains.shape[0])))
+    attn_pieces = slice_attn(at, query_weight, key_projection, value_projection, gains)
+    attn_pieces = ring_swap(attn_pieces, weight_rows + 16)
     token_strips = ring_gather(tokens)
-    attn_all = natural(
-        gather_head(swap_slices(attn_pieces, ring_place, blk_index)), weight_rows + 16
-    )
-    attn_matrix = attn_all[:, :, :weight_rows].reshape(model_width, attn_cols)
-    gain_rows = attn_all[:, :, weight_rows]
-    gain_one = gain_rows[:, :, :weight_rows].reshape(1, model_width).astype(wide)
-    gain_two = (
-        gain_rows[:, :, weight_rows : 2 * weight_rows].reshape(1, model_width).astype(wide)
-    )
-    at = 2 * weight_rows
-    query_gain = gain_rows[:, :, at : at + small].reshape(1, HEAD_SIZE).astype(wide)
-    key_gain = gain_rows[:, :, at + small : at + 2 * small].reshape(1, HEAD_SIZE).astype(wide)
-
+    attn_matrix, gain_rows = assemble(at_own, gather_cross(attn_pieces), weight_rows)
+    attn_matrix = attn_matrix.reshape(model_width, attn_cols)
+    gain_rows = gain_rows[:, :, 0].astype(wide)
+    gain_one = gain_rows[:, :, :weight_rows].reshape(1, model_width)
+    gain_two = gain_rows[:, :, weight_rows : 2 * weight_rows].reshape(1, model_width)
+    first = 2 * weight_rows
+    query_gain = gain_rows[:, :, first : first + small].reshape(1, HEAD_SIZE)
+    key_gain = gain_rows[:, :, first + small : first + 2 * small].reshape(1, HEAD_SIZE)
     output_rows = gather_head(output_weight)
-    ff_pieces = after(pieces_of(gate_weight, up_weight), token_strips[-1])
-    ff_matrix = natural(
-        gather_head(swap_slices(ff_pieces, ring_place, blk_index)), weight_rows
-    ).reshape(model_width, 2 * ff_local)
     down_matrix = gather_head(down_weight)
-    cotangent_strips = ring_gather(after(out_cotangent, token_strips[-1]))
 
     numbers = jnp.arange(strip_count, dtype=jnp.int32)
-    on = jnp.asarray(STRIPS, jnp.int32)
-    ring_spot = (ring_place + on) % blk_count
+    ring_spot = (ring_place + jnp.asarray(STRIPS, jnp.int32)) % blk_count
     strip_blk = jnp.where(ring_spot < 4, 2 * ring_spot, 15 - 2 * ring_spot)
-    strip_head = head_index ^ jnp.arange(head_count, dtype=jnp.int32)
+    strip_head = head_index ^ jnp.asarray((0, 2, 1, 3), jnp.int32)
     strip = (strip_blk[None, :] * head_count + strip_head[:, None]).reshape(strip_count)
     slots = jnp.arange(stretch_order.shape[1], dtype=jnp.int32)
     held = jnp.sum(
@@ -827,75 +1001,79 @@
     attn_raw = jnp.concatenate(raw_groups, axis=0)
     query_rows = jnp.concatenate(query_groups, axis=0)
     kv_own = jnp.concatenate(kv_groups, axis=0)
-    kv_far = cross(kv_own, 2)
-    kv = jnp.concatenate([kv_own, cross(kv_own, 1), kv_far, cross(kv_far, 1)], axis=0)
+    own, near, far, both = gather_cross(kv_own)
+    kv = jnp.concatenate([own, far, near, both], axis=0)
     attended, lse = attend(place, order, query_rows, kv)
+
+    ties = {1: (query_rows, kv_own), 2: (kv,), 3: (attended,)}
+    ff_pieces, cotangent = tied(
+        (slice_ff(at, gate_weight, up_weight), out_cotangent), (token_strips[-1],)
+    )
+    ff_pieces = ring_swap(ff_pieces, weight_rows, lambda step, got: ties[step])
+    cotangent_strips = ring_gather(cotangent, lambda step, got: ties.get(step, ()))
+    ff_matrix = assemble(at_own, gather_cross(ff_pieces), weight_rows)[0].reshape(
+        model_width, 2 * ff_local
+    )
 
     def by_groups(rows):
         return [rows[a * local_rows : b * local_rows] for a, b in GROUPS]
 
-    branch_parts = [
-        matmul(rows, output_rows).astype(narrow) for rows in reversed(by_groups(attended))
-    ]
-    branch = ring_scatter(split_groups(branch_parts[::-1], local_rows))
+    def by_strips(groups):
+        return dict(zip(STRIPS, split_groups(groups, local_rows)))
+
+    def group_of(got, index):
+        first, last = GROUPS[index]
+        return jnp.concatenate([got[s] for s in STRIPS[first:last]], axis=0)
+
+    cotangent_groups = grouped(cotangent_strips)
+    branch_parts = [matmul(rows, output_rows).astype(narrow) for rows in by_groups(attended)]
+    branch = ring_scatter(by_strips(branch_parts))
     resid = tokens_wide + branch
     rho_two = inverse_rms(resid)
     unit_two = resid * rho_two
-    second_strips = ring_gather((unit_two * gain_two).astype(narrow))
-
-    hidden_groups, ff_gradient_groups, second_parts = [], [], []
-    second_groups = grouped(second_strips)
-    cotangent_groups = grouped(cotangent_strips)
-    for rows, grads in zip(second_groups, cotangent_groups):
+    hidden_grads = [matmul(rows, down_matrix, ALONG) for rows in cotangent_groups]
+
+    second_groups, hidden_groups, ff_gradient_groups = [], [], []
+
+    def feed_forward(step, got):
+        if step == 1:
+            return ()
+        rows = group_of(got, step - 2)
         ff_raw = matmul(rows, ff_matrix)
         gate, up_proj = ff_raw[:, :ff_local], ff_raw[:, ff_local:]
         sigma = jax.nn.sigmoid(gate)
         swish = gate * sigma
+        hidden_gradient = hidden_grads[step - 2]
+        gate_gradient = hidden_gradient * up_proj * (sigma * (1.0 + gate * (1.0 - sigma)))
+        second_groups.append(rows)
         hidden_groups.append((swish * up_proj).astype(narrow))
-        hidden_gradient = matmul(grads, down_matrix, ALONG)
-        gate_gradient = hidden_gradient * up_proj * (sigma * (1.0 + gate * (1.0 - sigma)))
         ff_gradient_groups.append(
             jnp.concatenate([gate_gradient, hidden_gradient * swish], 1).astype(narrow)
         )
-    for rows in reversed(ff_gradient_groups):
-        second_parts.append(matmul(rows, ff_matrix, ALONG).astype(narrow))
-    second_gradient = ring_scatter(split_groups(second_parts[::-1], local_rows))
-    scaled = gain_two * second_gradient
-    resid_gradient = out_cotangent.astype(wide) + rho_two * (
-        scaled - unit_two * jnp.mean(unit_two * scaled, axis=-1, keepdims=True)
-    )
-    branch_gradient = resid_gradient.astype(narrow)
-    branch_strips = ring_gather(branch_gradient)
-
-    out_parts = [matmul(rows, down_matrix).astype(narrow) for rows in reversed(hidden_groups)]
-    out_parts = split_groups(out_parts[::-1], local_rows)
-    out_part = ring_scatter(out_parts[:-1] + [after(out_parts[-1], branch_strips[-1])])
-    layer_out = (resid + out_part).astype(narrow)
-
+        return hidden_groups[-1], ff_gradient_groups[-1]
+
+    second_strips = ring_gather((unit_two * gain_two).astype(narrow), feed_forward)
+    feed_forward(5, dict(zip(STRIPS, second_strips)))
     second_normed = jnp.concatenate(second_groups, axis=0)
     group_cotangent = jnp.concatenate(cotangent_groups, axis=0)
     hidden = jnp.concatenate(hidden_groups, axis=0)
     ff_gradient = jnp.concatenate(ff_gradient_groups, axis=0)
-
-    def by_head(grads, rows):
-        shape = (blk_count, head_count, rows, grads.shape[-1])
-        return grads.reshape(shape).transpose(1, 0, 2, 3).reshape(-1, rows, grads.shape[-1])
-
-    down_gradient = scatter_head(matmul(hidden, group_cotangent, DOWN).astype(narrow))
-    ff_matrix_gradient = scatter_head(
-        by_head(matmul(second_normed, ff_gradient, DOWN).astype(narrow), weight_rows)
-    )
-    ff_matrix_gradient = swap_slices(ff_matrix_gradient, ring_place, blk_index).astype(wide)
-    gate_weight_gradient = (
-        ff_matrix_gradient[:, :, :ff_local].transpose(1, 0, 2).reshape(gate_weight.shape)
-    )
-    up_weight_gradient = (
-        ff_matrix_gradient[:, :, ff_local:].transpose(1, 0, 2).reshape(up_weight.shape)
-    )
-    feedforward_norm_gradient = (
-        jnp.sum(gate_weight_gradient * gate_weight.astype(wide), axis=1)
-        + jnp.sum(up_weight_gradient * up_weight.astype(wide), axis=1)
-    ) / feedforward_norm.astype(wide)
+    ff_matrix_gradient = weight_grads(at_own, second_normed, ff_gradient, weight_rows)
+    down_gradient = matmul(hidden, group_cotangent, DOWN).astype(narrow)
+    out_parts = [matmul(rows, down_matrix).astype(narrow) for rows in hidden_groups]
+    second_parts = [
+        matmul(rows, ff_matrix, ALONG).astype(narrow) for rows in ff_gradient_groups
+    ]
+    fillers = {1: (ff_matrix_gradient,), 2: (down_gradient,), 3: tuple(out_parts)}
+    second_gradient = ring_scatter(by_strips(second_parts), lambda step, got: fillers[step])
+    down_gradient = scatter_head(down_gradient)
+    ff_matrix_gradient = scatter_cross(ff_matrix_gradient)
+    scaled = gain_two * second_gradient
+    resid_gradient = out_cotangent.astype(wide) + rho_two * (
+        scaled - unit_two * jnp.mean(unit_two * scaled, axis=-1, keepdims=True)
+    )
+    branch_gradient = resid_gradient.astype(narrow)
+    branch_strips = ring_gather(branch_gradient)
 
     branch_groups = grouped(branch_strips)
     attended_gradient = jnp.concatenate(
@@ -907,60 +1085,62 @@
     query_grads, kv_grads = attend_back(
         place, order, query_rows, attended_gradient, attended, lse, kv
     )
-    kv_near = [kv_grads[j * group_rows : (j + 1) * group_rows] for j in range(head_count)]
-    kv_sent = cross(jnp.concatenate([kv_near[1], kv_near[3]], axis=0), 1)
-    kv_grads = add(
-        add(kv_near[0], kv_sent[:group_rows]), cross(add(kv_near[2], kv_sent[group_rows:]), 2)
-    )
+    kv_sums = scatter_cross(kv_grads)
+
+    ties = {1: (query_grads,), 2: (kv_sums,), 3: ()}
+    out_strips = by_strips(out_parts)
+    out_strips[4], ff_matrix_gradient = tied(
+        (out_strips[4], ff_matrix_gradient), (branch_strips[-1],)
+    )
+    out_part = ring_scatter(out_strips, lambda step, got: ties[step])
+    layer_out = (resid + out_part).astype(narrow)
+    ff_matrix_gradient = ring_swap(
+        ff_matrix_gradient, weight_rows, lambda step, got: ties[step]
+    )
+    gate_weight_gradient, up_weight_gradient, norm_sums = widen(
+        at, ff_matrix_gradient, gate_weight, up_weight
+    )
+    feedforward_norm_gradient = jnp.sum(norm_sums, axis=1) / feedforward_norm.astype(wide)
+
     attn_gradient, gain_parts = [], []
     for h in range(group_heads + 1):
         cols = slice(h * HEAD_SIZE, (h + 1) * HEAD_SIZE)
-        grads = query_grads[:, cols] if h < group_heads else kv_grads[:, :HEAD_SIZE]
+        grads = query_grads[:, cols] if h < group_heads else kv_sums[:, :HEAD_SIZE]
         gain = query_gain if h < group_heads else key_gain
         raw_gradient, gain_part = head_back(grads, attn_raw[:, cols], gain, cosine, sine)
         attn_gradient.append(raw_gradient.astype(narrow))
         gain_parts.append(gain_part)
-    attn_gradient = jnp.concatenate(attn_gradient + [kv_grads[:, HEAD_SIZE:]], axis=1)
+    attn_gradient = jnp.concatenate(attn_gradient + [kv_sums[:, HEAD_SIZE:]], axis=1)
     first_parts = [
-        matmul(rows, attn_matrix, ALONG).astype(narrow)
-        for rows in reversed(by_groups(attn_gradient))
+        matmul(rows, attn_matrix, ALONG).astype(narrow) for rows in by_groups(attn_gradient)
     ]
-    first_gradient = ring_scatter(split_groups(first_parts[::-1], local_rows))
-    attn_matrix_gradient = by_head(
-        matmul(first_normed, attn_gradient, DOWN).astype(narrow), weight_rows
-    )
     gain_parts = jnp.stack(
         [
             sum(gain_parts[:group_heads]).reshape(blk_count, head_count, small),
             gain_parts[group_heads].reshape(blk_count, head_count, small),
         ],
         axis=2,
-    ).transpose(1, 0, 2, 3)
-    gain_parts = gain_parts.reshape(strip_count, 1, 2 * small).astype(narrow)
-    gain_parts = jnp.pad(gain_parts, ((0, 0), (0, 15), (0, attn_cols - 2 * small)))
-    attn_matrix_gradient = swap_slices(
-        scatter_head(jnp.concatenate([attn_matrix_gradient, gain_parts], axis=1)),
-        ring_place,
-        blk_index,
-    ).astype(wide)
-    attn_rows = attn_matrix_gradient[:, :weight_rows]
-    query_weight_gradient = (
-        attn_rows[:, :, :query_cols].transpose(1, 0, 2).reshape(query_weight.shape)
-    )
-    key_weight_gradient = (
-        attn_rows[:, :, query_cols : query_cols + HEAD_SIZE]
-        .transpose(1, 0, 2)
-        .reshape(key_projection.shape)
-    )
-    value_weight_gradient = (
-        attn_rows[:, :, query_cols + HEAD_SIZE :].transpose(1, 0, 2).reshape(value_projection.shape)
-    )
-    gain_sums = jnp.sum(attn_matrix_gradient[:, weight_rows], axis=0)
-    attention_norm_gradient = (
-        jnp.sum(query_weight_gradient * query_weight.astype(wide), axis=1)
-        + jnp.sum(key_weight_gradient * key_projection.astype(wide), axis=1)
-        + jnp.sum(value_weight_gradient * value_projection.astype(wide), axis=1)
-    ) / attention_norm.astype(wide)
+    ).reshape(blk_count, head_count, 1, 2 * small)
+    gain_parts = jnp.pad(
+        gain_parts.astype(narrow), ((0, 0), (0, 0), (0, 15), (0, attn_cols - 2 * small))
+    )
+    attn_matrix_gradient = weight_grads(
+        at_own, first_normed, attn_gradient, weight_rows, gain_parts
+    )
+    first_gradient = ring_scatter(
+        by_strips(first_parts),
+        lambda step, got: (attn_matrix_gradient,) if step == 1 else (),
+    )
+    attn_matrix_gradient = ring_swap(scatter_cross(attn_matrix_gradient), weight_rows + 16)
+    (
+        query_weight_gradient,
+        key_weight_gradient,
+        value_weight_gradient,
+        norm_sums,
+        gain_sums,
+    ) = widen(at, attn_matrix_gradient, query_weight, key_projection, value_projection)
+    gain_sums = gain_sums[0]
+    attention_norm_gradient = jnp.sum(norm_sums, axis=1) / attention_norm.astype(wide)
     rho_one = inverse_rms(tokens_wide)
     unit_one = tokens_wide * rho_one
     scaled = gain_one * first_gradient

time: 837 us -> 722 us (0.86)
  waiting for transfers between devices: 358 us -> 215 us
  Pallas kernels: 53.3 us -> 110 us
  starting transfers between devices: 149 us -> 112 us
  other arithmetic: 65 us -> 97.3 us
  between operations: 44.6 us -> 16.3 us
  local copies, waits for them, and re-layouts: 75 us -> 94.5 us
  matrix products: 82 us -> 69.5 us
    ppermute x92 -> x96, waiting for transfers between devices: 318 us -> 175 us  [hop(): lax.ppermute(value, 'blk', [(RING[i], RING[(i + by) % count]) for i in ra...]
    pallas_call x0 -> x8, Pallas kernels: none -> 61.8 us  [the longest x2 22.2 us: weight_grads(): pl.pallas_call(lambda *refs: weight_grads_kernel(*refs, rows=rows), grid_...]
    ppermute x92 -> x96, starting transfers between devices: 146 us -> 108 us  [hop(): lax.ppermute(value, 'blk', [(RING[i], RING[(i + by) % count]) for i in ra...]
    slice x20 -> x52, local copies, waits for them, and re-layouts: 7.72 us -> 29 us  [the longest x24 11.3 us: ring_swap(): right, left = tied((right[rows:], left[:-rows]), fill(step, None))]
    concatenate x13 -> x12, other arithmetic: 6.78 us -> 25.5 us  [the longest x1 16.2 us: per_device(): ff_gradient = jnp.concatenate(ff_gradient_groups, axis=0)]
    dot_general x36 -> x34, matrix products: 82 us -> 69.5 us  [matmul(): lax.dot_general(left, right, dims, preferred_element_type=jnp.float32)]
    convert_element_type x14 -> x18, other arithmetic: 7.97 us -> 19.9 us  [add(): (left.astype(jnp.float32) + right.astype(jnp.float32)).astype(left.dtype)]
    unnamed x338 -> x322, local copies, waits for them, and re-layouts: 38.9 us -> 50.1 us
  transfers between devices with their start and end apart: 105 -> 115, of which waited for: 51 -> 50; matrix products, arithmetic and copies ran while one was open for 22% -> 33% of each run, Pallas kernels for 6% -> 15%
where the time goes in v3:
time: 722 us; the launch traced here: 714 us
  waiting for transfers between devices  215 us (30%)
  starting transfers between devices  112 us (16%)
  Pallas kernels  110 us (15%)
  other arithmetic  97.3 us (13%)
  local copies, waits for them, and re-layouts  94.5 us (13%)
  matrix products  69.5 us (10%)
  between operations  16.3 us (2%)
    ppermute x96, waiting for transfers between devices, hop(): lax.ppermute(value, 'blk', [(RING[i], RING[(i + by) % count]) for i in ra...  175 us
    ppermute x96, starting transfers between devices, hop(): lax.ppermute(value, 'blk', [(RING[i], RING[(i + by) % count]) for i in ra...  108 us
    dot_general x34, matrix products, matmul(): lax.dot_general(left, right, dims, preferred_element_type=jnp.float32)  69.5 us
    unnamed x322, local copies, waits for them, and re-layouts  50.1 us
    ppermute x15, waiting for transfers between devices, cross(): return lax.ppermute(value, 'head', [(i, i ^ by) for i in range(4)])  38.9 us
    pallas_call x1, Pallas kernels, attend_back(): pl.pallas_call(attend_back_kernel, grid_spec=pltpu.PrefetchScalarGridSpec...  27.7 us
    pallas_call x2, Pallas kernels, weight_grads(): pl.pallas_call(lambda *refs: weight_grads_kernel(*refs, rows=rows), grid_...  22.2 us
    pallas_call x1, Pallas kernels, attend(): pl.pallas_call(attend_kernel, grid_spec=pltpu.PrefetchScalarGridSpec(num_...  20.1 us
  transfers between devices with their start and end apart: 115, of which 50 were waited for; matrix products, arithmetic and copies ran while one was open for 33% of the time, Pallas kernels for 15%

profile of v3, /device:TPU:0, one launch (start us, length us, event | category | flops | bytes accessed | tf_op | source)
XLA Modules:
  0.0 713.9 jit_solution(3312909903234945977)
XLA Ops:
  44.6 7.7 %collective-permute-done.8 = bf16[40,512]{1,0:T(8,128)(2,1)S(1)} collective-permute-done((bf16[40,512]{1,0:T(8,128)(2,1)S(1)}, bf16[40,512]{1,0:T(8,128)(2,1)S(1)}, u32[]{:S(2)}, u32[]{:S(2)}) %collective-permute-start.8) | collective-permute-done | bytes 40992 | tf_op jit(solution)/shard_map/ppermute | solution.py:615
  57.9 6.2 slice_ff.1
  92.6 6.7 assemble.2
  143.9 10.1 %collective-permute-done.34 = bf16[160,1536]{1,0:T(8,128)(2,1)S(1)} collective-permute-done((bf16[160,1536]{1,0:T(8,128)(2,1)S(1)}, bf16[160,1536]{1,0:T(8,128)(2,1)S(1)}, u32[]{:S(2)}, u32[]{:S(2)}) %collective-permute-start.34) | collective-permute-done | bytes 491552 | tf_op jit(solution)/shard_map/ppermute | solution.py:615
  163.9 20.1 %attend.1 = (bf16[1024,256]{1,0:T(8,128)(2,1)}, f32[8,8,256]{2,1,0:T(8,128)}) custom-call(s32[8]{0:T(128)} %get-tuple-element.292.place_ref, s32[32]{0:T(128)} %select_reduce_fusion.order_ref, bf16[1024,256]{1,0:T(8,128)(2,1)} %maximum_maximum_fusion.1.q_ref, bf16[4096,256]{1,0:T(8,128)(2,1)} %constant_dynamic-update-slice_fusion.11.kv_ref), custom_call_target="tpu_custom_call" | custom-call | flops 2147483648 | bytes 3145728 | tf_op jit(solution)/shard_map/attend/pallas_call | solution.py:474
  201.4 16.5 %collective-permute-done.38 = bf16[32,1536]{1,0:T(8,128)(2,1)S(1)} collective-permute-done((bf16[32,1536]{1,0:T(8,128)(2,1)S(1)}, bf16[32,1536]{1,0:T(8,128)(2,1)S(1)}, u32[]{:S(2)}, u32[]{:S(2)}) %collective-permute-start.38) | collective-permute-done | bytes 98336 | tf_op jit(solution)/shard_map/ppermute | solution.py:615
  229.3 6.0 collective-permute-done.24
  255.7 13.5 %collective-permute-done.41.refs_3_ = bf16[512,1536]{1,0:T(8,128)(2,1)S(1)} collective-permute-done((bf16[512,1536]{1,0:T(8,128)(2,1)}, bf16[512,1536]{1,0:T(8,128)(2,1)S(1)}, u32[]{:S(2)}, u32[]{:S(2)}) %collective-permute-start.41) | collective-permute-done | bytes 1572896 | tf_op jit(solution)/shard_map/ppermute | solution.py:619
  273.8 11.3 %collective-permute-done.43 = bf16[128,2048]{1,0:T(8,128)(2,1)S(1)} collective-permute-done((bf16[128,2048]{1,0:T(8,128)(2,1)S(1)}, bf16[128,2048]{1,0:T(8,128)(2,1)S(1)}, u32[]{:S(2)}, u32[]{:S(2)}) %collective-permute-start.43) | collective-permute-done | bytes 524320 | tf_op jit(solution)/shard_map/ppermute | solution.py:615
  289.1 8.5 %assemble.3 = bf16[8,4,64,1536]{3,2,1,0:T(8,128)(2,1)} custom-call(s32[9]{0:T(128)} %pad_add_fusion.refs_0_, bf16[512,1536]{1,0:T(8,128)(2,1)} %slice_dynamic-update-slice_fusion.6.refs_1_, bf16[512,1536]{1,0:T(8,128)(2,1)} %collective-permute-done.40.refs_2_, bf16[512,1536]{1,0:T(8,128)(2,1)} %copy-done.49, bf16[512,1536]{1,0:T(8,128)(2,1)} %collective-permute-done.42.refs_4_), custom_call_target="tpu_custom_call" | custom-call | tf_op jit(solution)/shard_map/assemble/pallas_call | solution.py:751
  297.6 7.3 %fusion.11 = f32[384,1536]{1,0:T(8,128)} fusion(bf16[2048,1536]{1,0:T(8,128)(2,1)} %bitcast.79, bf16[128,2048]{1,0:T(8,128)(2,1)} %copy-done.88, bf16[128,2048]{1,0:T(8,128)(2,1)} %copy-done.85, bf16[128,2048]{1,0:T(8,128)(2,1)} %copy-done.75), kind=kOutput, calls=%fused_computation.42 | convolution fusion | flops 2420637696 | bytes 10223616 | tf_op jit(solution)/shard_map/dot_general | solution.py:605
  380.2 16.2 %maximum_maximum_fusion.refs_2_ = bf16[1024,1536]{1,0:T(8,128)(2,1)} fusion(bf16[128,768]{1,0:T(8,128)(2,1)S(1)} %copy-done.68, bf16[128,768]{1,0:T(8,128)(2,1)S(1)} %copy-done.66, bf16[256,768]{1,0:T(8,128)(2,1)S(1)} %copy-done.100, bf16[256,768]{1,0:T(8,128)(2,1)S(1)} %copy-done.98, bf16[256,768]{1,0:T(8,128)(2,1)S(1)} %copy-done.96, ...), kind=kLoop, calls=%fused_computation.9 | loop fusion | flops 25165824 | bytes 6291456 | tf_op jit(solution)/shard_map/concatenate | solution.py:1060
  401.8 13.1 %weight_grads.2 = bf16[4,8,64,1536]{3,2,1,0:T(8,128)(2,1)} custom-call(s32[9]{0:T(128)} %pad_add_fusion.refs_0_, bf16[1024,2048]{1,0:T(8,128)(2,1)} %constant_dynamic-update-slice_fusion.19.refs_1_, bf16[1024,1536]{1,0:T(8,128)(2,1)} %maximum_maximum_fusion.refs_2_), custom_call_target="tpu_custom_call" | custom-call | flops 6442450944 | bytes 13631488 | tf_op jit(solution)/shard_map/weight_grads/pallas_call | solution.py:791
  417.0 6.1 fusion.138
  427.6 11.0 %collective-permute-done.73 = bf16[128,2048]{1,0:T(8,128)(2,1)S(1)} collective-permute-done((bf16[128,2048]{1,0:T(8,128)(2,1)S(1)}, bf16[128,2048]{1,0:T(8,128)(2,1)S(1)}, u32[]{:S(2)}, u32[]{:S(2)}) %collective-permute-start.73) | collective-permute-done | bytes 524320 | tf_op jit(solution)/shard_map/ppermute | solution.py:615
  440.9 7.1 collective-permute-done.70
  471.4 27.7 %attend_back.1 = (bf16[1024,256]{1,0:T(8,128)(2,1)}, bf16[4096,256]{1,0:T(8,128)(2,1)}) custom-call(s32[8]{0:T(128)} %get-tuple-element.292.place_ref, s32[32]{0:T(128)} %select_reduce_fusion.order_ref, bf16[1024,256]{1,0:T(8,128)(2,1)} %maximum_maximum_fusion.1.q_ref, bf16[1024,256]{1,0:T(8,128)(2,1)} %pad_maximum_fusion.18.grad_ref, ...), custom_call_target="tpu_custom_call" | custom-call | flops 5368709120 | bytes 6291456 | tf_op jit(solution)/shard_map/attend_back/pallas_call | solution.py:575
  501.9 10.2 %collective-permute-done.58 = bf16[512,1536]{1,0:T(8,128)(2,1)} collective-permute-done((bf16[512,1536]{1,0:T(8,128)(2,1)}, bf16[512,1536]{1,0:T(8,128)(2,1)}, u32[]{:S(2)}, u32[]{:S(2)}) %collective-permute-start.58) | collective-permute-done | bytes 1572896 | tf_op jit(solution)/shard_map/ppermute | solution.py:619
  527.2 7.6 %collective-permute-done.80 = bf16[1024,256]{1,0:T(8,128)(2,1)S(1)} collective-permute-done((bf16[1024,256]{1,0:T(8,128)(2,1)S(1)}, bf16[1024,256]{1,0:T(8,128)(2,1)S(1)}, u32[]{:S(2)}, u32[]{:S(2)}) %collective-permute-start.80) | collective-permute-done | bytes 524320 | tf_op jit(solution)/shard_map/ppermute | solution.py:619
  547.7 9.1 %weight_grads.3 = bf16[4,8,80,512]{3,2,1,0:T(8,128)(2,1)} custom-call(s32[9]{0:T(128)} %pad_add_fusion.refs_0_, bf16[1024,2048]{1,0:T(8,128)(2,1)} %pad_maximum_fusion.refs_1_, bf16[1024,512]{1,0:T(8,128)(2,1)} %copy-done.10, bf16[8,4,16,512]{3,2,1,0:T(8,128)(2,1)} %pad.9.refs_3_), custom_call_target="tpu_custom_call" | custom-call | flops 2147483648 | bytes 7340032 | tf_op jit(solution)/shard_map/weight_grads/pallas_call | solution.py:791
  587.6 9.1 %collective-permute-done.81 = bf16[128,2048]{1,0:T(8,128)(2,1)} collective-permute-done((bf16[128,2048]{1,0:T(8,128)(2,1)}, bf16[128,2048]{1,0:T(8,128)(2,1)}, u32[]{:S(2)}, u32[]{:S(2)}) %collective-permute-start.81) | collective-permute-done | bytes 524320 | tf_op jit(solution)/shard_map/ppermute | solution.py:615
  601.6 6.2 collective-permute-done.87
  618.2 17.1 %collective-permute-done.109 = bf16[32,1536]{1,0:T(8,128)(2,1)S(1)} collective-permute-done((bf16[32,1536]{1,0:T(8,128)(2,1)S(1)}, bf16[32,1536]{1,0:T(8,128)(2,1)S(1)}, u32[]{:S(2)}, u32[]{:S(2)}) %collective-permute-start.109) | collective-permute-done | bytes 98336 | tf_op jit(solution)/shard_map/ppermute | solution.py:615
  646.3 7.1 widen.3
  (778 shorter events, 436.1 us)
Async XLA Ops:
  7.2 176.8 %all-gather.3.cloned.1.call-start = ((), (), s32[]{:S(2)}) async-start(), calls=%async_computation.2 | async-start | bytes 1310720 | tf_op jit(solution)/shard_map/all_gather | solution.py:875
  7.9 297.0 %all-gather.5.cloned.1.call-start = ((), (), s32[]{:S(2)}) async-start(), calls=%async_computation.3 | async-start | bytes 3932160 | tf_op jit(solution)/shard_map/all_gather | solution.py:875
  21.5 559.3 %reduce-scatter.3.cloned.1.call-start = ((), (), s32[]{:S(2)}) async-start(), calls=%async_computation.4 | async-start | bytes 1310720 | tf_op jit(solution)/shard_map/reduce_scatter | solution.py:879
  84.5 44.2 %collective-permute-start.46 = (bf16[128,2048]{1,0:T(8,128)(2,1)}, bf16[128,2048]{1,0:T(8,128)(2,1)}, u32[]{:S(2)}, u32[]{:S(2)}) collective-permute-start(bf16[128,2048]{1,0:T(8,128)(2,1)} %bitcast.5), channel_id=1, source_target_pairs={{0,8},{8,16},{16,24},{24,28},{28,20},{20,12},{12,4},{4,0},{1,9},{9... | collective-permute-start | bytes 1572872 | tf_op jit(solution)/shard_map/ppermute | solution.py:615
  86.4 42.3 %collective-permute-start.45 = (bf16[128,2048]{1,0:T(8,128)(2,1)}, bf16[128,2048]{1,0:T(8,128)(2,1)}, u32[]{:S(2)}, u32[]{:S(2)}) collective-permute-start(bf16[128,2048]{1,0:T(8,128)(2,1)} %bitcast.5), channel_id=1, source_target_pairs={{0,4},{8,0},{16,8},{24,16},{28,24},{20,28},{12,20},{4,12},{1,5},{9... | collective-permute-start | bytes 1572872 | tf_op jit(solution)/shard_map/ppermute | solution.py:615
  89.7 47.5 %collective-permute-start.33 = (bf16[224,1536]{1,0:T(8,128)(2,1)}, bf16[224,1536]{1,0:T(8,128)(2,1)}, u32[]{:S(2)}, u32[]{:S(2)}) collective-permute-start(bf16[224,1536]{1,0:T(8,128)(2,1)} %get-tuple-element.169), channel_id=1, source_target_pairs={{0,8},{8,16},{16,24},{24,28},{28,20},{20,12},{12,4},{4,0},{1,9},{9... | collective-permute-start | bytes 2064392 | tf_op jit(solution)/shard_map/ppermute | solution.py:615
  92.3 46.0 %collective-permute-start.32 = (bf16[224,1536]{1,0:T(8,128)(2,1)}, bf16[224,1536]{1,0:T(8,128)(2,1)}, u32[]{:S(2)}, u32[]{:S(2)}) collective-permute-start(bf16[224,1536]{1,0:T(8,128)(2,1)} %get-tuple-element.170), channel_id=1, source_target_pairs={{0,4},{8,0},{16,8},{24,16},{28,24},{20,28},{12,20},{4,12},{1,5},{9... | collective-permute-start | bytes 2064392 | tf_op jit(solution)/shard_map/ppermute | solution.py:615
  128.8 31.4 %collective-permute-start.49 = (bf16[128,2048]{1,0:T(8,128)(2,1)}, bf16[128,2048]{1,0:T(8,128)(2,1)}, u32[]{:S(2)}, u32[]{:S(2)}) collective-permute-start(bf16[128,2048]{1,0:T(8,128)(2,1)} %collective-permute-done.45), channel_id=1, source_target_pairs={{0,4},{8,0},{16,8},{24,16},{28,24},{20,28},{12,20},{4,12},{1,5},{9... | collective-permute-start | bytes 1572872 | tf_op jit(solution)/shard_map/ppermute | solution.py:615
  160.2 35.0 %collective-permute-start.36 = (bf16[96,1536]{1,0:T(8,128)(2,1)}, bf16[96,1536]{1,0:T(8,128)(2,1)}, u32[]{:S(2)}, u32[]{:S(2)}) collective-permute-start(bf16[96,1536]{1,0:T(8,128)(2,1)} %slice.986), channel_id=1, source_target_pairs={{0,4},{8,0},{16,8},{24,16},{28,24},{20,28},{12,20},{4,12},{1,5},{9... | collective-permute-start | bytes 884744 | tf_op jit(solution)/shard_map/ppermute | solution.py:615
  161.9 35.0 %collective-permute-start.37 = (bf16[96,1536]{1,0:T(8,128)(2,1)}, bf16[96,1536]{1,0:T(8,128)(2,1)}, u32[]{:S(2)}, u32[]{:S(2)}) collective-permute-start(bf16[96,1536]{1,0:T(8,128)(2,1)} %slice.985), channel_id=1, source_target_pairs={{0,8},{8,16},{16,24},{24,28},{28,20},{20,12},{12,4},{4,0},{1,9},{9... | collective-permute-start | bytes 884744 | tf_op jit(solution)/shard_map/ppermute | solution.py:615
  162.7 79.7 %collective-permute-start.53 = (bf16[128,2048]{1,0:T(8,128)(2,1)}, bf16[128,2048]{1,0:T(8,128)(2,1)S(1)}, u32[]{:S(2)}, u32[]{:S(2)}) collective-permute-start(bf16[128,2048]{1,0:T(8,128)(2,1)} %collective-permute-done.49), channel_id=1, source_target_pairs={{0,4},{8,0},{16,8},{24,16},{28,24},{20,28},{12,20},{4,12},{1,5},{9... | collective-permute-start | bytes 1572872 | tf_op jit(solution)/shard_map/ppermute | solution.py:615
  192.9 49.5 %collective-permute-start.54 = (bf16[128,2048]{1,0:T(8,128)(2,1)S(1)}, bf16[128,2048]{1,0:T(8,128)(2,1)S(1)}, u32[]{:S(2)}, u32[]{:S(2)}) collective-permute-start(bf16[128,2048]{1,0:T(8,128)(2,1)S(1)} %copy-done.77), channel_id=1, source_target_pairs={{0,8},{8,16},{16,24},{24,28},{28,20},{20,12},{12,4},{4,0},{1,9},{9... | collective-permute-start | bytes 1572872 | tf_op jit(solution)/shard_map/ppermute | solution.py:615
  242.4 44.7 %collective-permute-start.40 = (bf16[512,1536]{1,0:T(8,128)(2,1)}, bf16[512,1536]{1,0:T(8,128)(2,1)}, u32[]{:S(2)}, u32[]{:S(2)}) collective-permute-start(bf16[512,1536]{1,0:T(8,128)(2,1)} %slice_dynamic-update-slice_fusion.6.refs_1_), channel_id=1, source_target_pairs={{0,1},{1,0},{2,3},{3,2},{4,5},{5,4},{6,7},{7,6},{8,9},{9,8},{10,11... | collective-permute-start | bytes 4718600 | tf_op jit(solution)/shard_map/ppermute | solution.py:619
  423.1 38.8 %collective-permute-start.57 = (bf16[1024,1536]{1,0:T(8,128)(2,1)}, bf16[1024,1536]{1,0:T(8,128)(2,1)}, u32[]{:S(2)}, u32[]{:S(2)}) collective-permute-start(bf16[1024,1536]{1,0:T(8,128)(2,1)} %bitcast.8), channel_id=1, source_target_pairs={{0,1},{1,0},{2,3},{3,2},{4,5},{5,4},{6,7},{7,6},{8,9},{9,8},{10,11... | collective-permute-start | bytes 9437192 | tf_op jit(solution)/shard_map/ppermute | solution.py:619
  451.8 202.4 %reduce-scatter.5.cloned.1.call-start = ((), (), s32[]{:S(2)}) async-start(), calls=%async_computation.5 | async-start | bytes 3932160 | tf_op jit(solution)/shard_map/reduce_scatter | solution.py:879
  466.1 46.0 %collective-permute-start.58 = (bf16[512,1536]{1,0:T(8,128)(2,1)}, bf16[512,1536]{1,0:T(8,128)(2,1)}, u32[]{:S(2)}, u32[]{:S(2)}) collective-permute-start(bf16[512,1536]{1,0:T(8,128)(2,1)} %slice.1008), channel_id=1, source_target_pairs={{0,2},{1,3},{2,0},{3,1},{4,6},{5,7},{6,4},{7,5},{8,10},{9,11},{10,... | collective-permute-start | bytes 4718600 | tf_op jit(solution)/shard_map/ppermute | solution.py:619
  517.2 46.4 %collective-permute-start.104 = (bf16[224,1536]{1,0:T(8,128)(2,1)}, bf16[224,1536]{1,0:T(8,128)(2,1)}, u32[]{:S(2)}, u32[]{:S(2)}) collective-permute-start(bf16[224,1536]{1,0:T(8,128)(2,1)} %get-tuple-element.159), channel_id=1, source_target_pairs={{0,8},{8,16},{16,24},{24,28},{28,20},{20,12},{12,4},{4,0},{1,9},{9... | collective-permute-start | bytes 2064392 | tf_op jit(solution)/shard_map/ppermute | solution.py:615
  519.0 48.1 %collective-permute-start.103 = (bf16[224,1536]{1,0:T(8,128)(2,1)}, bf16[224,1536]{1,0:T(8,128)(2,1)}, u32[]{:S(2)}, u32[]{:S(2)}) collective-permute-start(bf16[224,1536]{1,0:T(8,128)(2,1)} %get-tuple-element.160), channel_id=1, source_target_pairs={{0,4},{8,0},{16,8},{24,16},{28,24},{20,28},{12,20},{4,12},{1,5},{9... | collective-permute-start | bytes 2064392 | tf_op jit(solution)/shard_map/ppermute | solution.py:615
  525.1 46.0 %collective-permute-start.77 = (bf16[128,2048]{1,0:T(8,128)(2,1)}, bf16[128,2048]{1,0:T(8,128)(2,1)}, u32[]{:S(2)}, u32[]{:S(2)}) collective-permute-start(bf16[128,2048]{1,0:T(8,128)(2,1)} %pad_maximum_fusion.16), channel_id=1, source_target_pairs={{0,8},{8,16},{16,24},{24,28},{28,20},{20,12},{12,4},{4,0},{1,9},{9... | collective-permute-start | bytes 1572872 | tf_op jit(solution)/shard_map/ppermute | solution.py:615
  527.0 45.6 %collective-permute-start.78 = (bf16[128,2048]{1,0:T(8,128)(2,1)}, bf16[128,2048]{1,0:T(8,128)(2,1)}, u32[]{:S(2)}, u32[]{:S(2)}) collective-permute-start(bf16[128,2048]{1,0:T(8,128)(2,1)} %pad_maximum_fusion.17), channel_id=1, source_target_pairs={{0,4},{8,0},{16,8},{24,16},{28,24},{20,28},{12,20},{4,12},{1,5},{9... | collective-permute-start | bytes 1572872 | tf_op jit(solution)/shard_map/ppermute | solution.py:615
  586.5 74.9 %collective-permute-start.93 = (bf16[1280,512]{1,0:T(8,128)(2,1)}, bf16[1280,512]{1,0:T(8,128)(2,1)}, u32[]{:S(2)}, u32[]{:S(2)}) collective-permute-start(bf16[1280,512]{1,0:T(8,128)(2,1)} %bitcast.99), channel_id=1, source_target_pairs={{0,1},{1,0},{2,3},{3,2},{4,5},{5,4},{6,7},{7,6},{8,9},{9,8},{10,11... | collective-permute-start | bytes 3932168 | tf_op jit(solution)/shard_map/ppermute | solution.py:619
  607.8 55.9 %collective-permute-start.82 = (bf16[128,2048]{1,0:T(8,128)(2,1)}, bf16[128,2048]{1,0:T(8,128)(2,1)}, u32[]{:S(2)}, u32[]{:S(2)}) collective-permute-start(bf16[128,2048]{1,0:T(8,128)(2,1)} %get-tuple-element.163), channel_id=1, source_target_pairs={{0,8},{8,16},{16,24},{24,28},{28,20},{20,12},{12,4},{4,0},{1,9},{9... | collective-permute-start | bytes 1572872 | tf_op jit(solution)/shard_map/ppermute | solution.py:615
  609.4 54.3 %collective-permute-start.84 = (bf16[128,2048]{1,0:T(8,128)(2,1)}, bf16[128,2048]{1,0:T(8,128)(2,1)}, u32[]{:S(2)}, u32[]{:S(2)}) collective-permute-start(bf16[128,2048]{1,0:T(8,128)(2,1)} %get-tuple-element.164), channel_id=1, source_target_pairs={{0,4},{8,0},{16,8},{24,16},{28,24},{20,28},{12,20},{4,12},{1,5},{9... | collective-permute-start | bytes 1572872 | tf_op jit(solution)/shard_map/ppermute | solution.py:615
  614.1 43.1 %collective-permute-start.88 = (bf16[128,2048]{1,0:T(8,128)(2,1)}, bf16[128,2048]{1,0:T(8,128)(2,1)}, u32[]{:S(2)}, u32[]{:S(2)}) collective-permute-start(bf16[128,2048]{1,0:T(8,128)(2,1)} %get-tuple-element.199), channel_id=1, source_target_pairs={{0,8},{8,16},{16,24},{24,28},{28,20},{20,12},{12,4},{4,0},{1,9},{9... | collective-permute-start | bytes 1572872 | tf_op jit(solution)/shard_map/ppermute | solution.py:615
  (223 other events, 2260.1 us)
Sparse Core Ops, SparseCore 0:
  9.6 19.4 all-gather.2
  30.6 29.0 all-gather.4
  451.9 28.6 reduce-scatter.2
  483.0 45.4 reduce-scatter.4

commit v4 on v2

--- a/solution.py
+++ b/solution.py
@@ -623,27 +623,387 @@
     return (left.astype(jnp.float32) + right.astype(jnp.float32)).astype(left.dtype)
 
 
-def ring_gather(own):
-    half = own.shape[0] // 2
-    got = {0: own}
-    for step in (1, 2, 3):
-        got[step] = hop(got[step - 1], -1)
-        got[8 - step] = hop(got[(9 - step) % 8], 1)
-    got[4] = jnp.concatenate([hop(got[3][:half], -1), hop(got[5][half:], 1)], axis=0)
-    return [got[s] for s in STRIPS]
-
-
-def ring_scatter(parts):
-    part = dict(zip(STRIPS, parts))
-    half = part[0].shape[0] // 2
-    up = hop(part[4][:half], 1)
-    down = hop(part[4][half:], -1)
-    up = hop(jnp.concatenate([add(part[3][:half], up), part[3][half:]], axis=0), 1)
-    down = hop(jnp.concatenate([part[5][:half], add(part[5][half:], down)], axis=0), -1)
-    up, down = hop(add(part[2], up), 1), hop(add(part[6], down), -1)
-    up, down = hop(add(part[1], up), 1), hop(add(part[7], down), -1)
-    wide = jnp.float32
-    return part[0].astype(wide) + up.astype(wide) + down.astype(wide)
+class Gather:
+    def __init__(self, own):
+        self.got, self.step = {0: own}, 0
+        self.state = (own, own)
+
+    def go(self):
+        self.step += 1
+        left, right = self.state
+        if self.step < 4:
+            self.state = hop(left, -1), hop(right, 1)
+            self.got[self.step], self.got[8 - self.step] = self.state
+        else:
+            half = left.shape[0] // 2
+            self.got[4] = jnp.concatenate([hop(left[:half], -1), hop(right[half:], 1)], axis=0)
+            self.state = (self.got[4],)
+
+    def strips(self):
+        return [self.got[s] for s in STRIPS]
+
+    def group(self, index):
+        first, last = GROUPS[index]
+        return jnp.concatenate([self.got[s] for s in STRIPS[first:last]], axis=0)
+
+
+class Scatter:
+    def __init__(self, part):
+        self.part, self.step = part, 0
+        self.half = part[4].shape[0] // 2
+        self.state = (part[4][: self.half], part[4][self.half :])
+
+    def go(self):
+        self.step += 1
+        half, part = self.half, self.part
+        up, down = hop(self.state[0], 1), hop(self.state[1], -1)
+        if self.step == 1:
+            up = jnp.concatenate([add(part[3][:half], up), part[3][half:]], axis=0)
+            down = jnp.concatenate([part[5][:half], add(part[5][half:], down)], axis=0)
+        elif self.step < 4:
+            up, down = add(part[4 - self.step], up), add(part[4 + self.step], down)
+        self.state = up, down
+
+    def total(self):
+        up, down = self.state
+        wide = jnp.float32
+        return self.part[0].astype(wide) + up.astype(wide) + down.astype(wide)
+
+
+class Swap:
+    def __init__(self, pieces, rows):
+        cut = 4 * rows + rows // 2
+        self.rows, self.step = rows, 0
+        self.own, self.from_left, self.from_right = pieces[:rows], [], []
+        self.state = (pieces[rows:cut], pieces[cut:])
+
+    def go(self):
+        self.step += 1
+        rows = self.rows
+        right, left = hop(self.state[0], 1), hop(self.state[1], -1)
+        if self.step < 4:
+            self.from_left.append(right[:rows])
+            self.from_right.append(left[-rows:])
+            right, left = right[rows:], left[:-rows]
+        self.state = right, left
+
+    def result(self):
+        right, left = self.state
+        return jnp.concatenate(
+            [self.own, *self.from_right, right, left, *reversed(self.from_left)], axis=0
+        )
+
+
+def hold(rings, *extra):
+    states, extra = lax.optimization_barrier(([ring.state for ring in rings], extra))
+    for ring, state in zip(rings, states):
+        ring.state = state
+    return extra[0] if len(extra) == 1 else extra
+
+
+def scatter_cross(own, far, sent):
+    moved = cross(sent, 1)
+    half = own.shape[0]
+    return add(own, moved[:half]), add(far, moved[half:])
+
+
+def slice_kernel(at_ref, *refs):
+    first = 0
+    for ref in refs[:-1]:
+        refs[-1][:, first : first + ref.shape[1]] = ref[...]
+        first += ref.shape[1]
+
+
+def slice_pieces(at, *weights):
+    count = at.shape[0]
+    rows = weights[0].shape[0]
+    widths = [w.shape[1] // count for w in weights]
+    return pl.pallas_call(
+        slice_kernel,
+        grid_spec=pltpu.PrefetchScalarGridSpec(
+            num_scalar_prefetch=1,
+            grid=(count,),
+            in_specs=[pl.BlockSpec((rows, w), lambda i, at: (0, at[i])) for w in widths],
+            out_specs=pl.BlockSpec((rows, sum(widths)), lambda i, at: (i, 0)),
+        ),
+        out_shape=jax.ShapeDtypeStruct((count * rows, sum(widths)), jnp.bfloat16),
+        name="slice_pieces",
+    )(at, *weights)
+
+
+def assemble_kernel(at_ref, *refs):
+    own = at_ref[8]
+    for j, piece in enumerate(refs[:4]):
+        refs[4][0, own ^ j] = piece[...]
+
+
+def assemble(at, pieces, rows):
+    count = at.shape[0] - 1
+    total, cols = pieces[0].shape
+    return pl.pallas_call(
+        assemble_kernel,
+        grid_spec=pltpu.PrefetchScalarGridSpec(
+            num_scalar_prefetch=1,
+            grid=(count,),
+            in_specs=[pl.BlockSpec((rows, cols), lambda i, at: (i, 0))] * 4,
+            out_specs=pl.BlockSpec((1, 4, rows, cols), lambda i, at: (at[i], 0, 0, 0)),
+        ),
+        out_shape=jax.ShapeDtypeStruct((count, 4, rows, cols), jnp.bfloat16),
+        name="assemble",
+    )(at, *pieces).reshape(4 * total, cols)
+
+
+def spun(rows, cosine, sine):
+    return rows * cosine + pltpu.roll(rows, HEAD_SIZE // 2, 1) * sine
+
+
+def project_kernel(at_ref, *refs, strips):
+    token_refs, refs = refs[:strips], refs[strips:]
+    pieces, refs = refs[:4], refs[4:]
+    gain_ref, head_gain_ref, cos_ref, sin_ref = refs[:4]
+    normed_ref, raw_ref, q_ref, kv_ref, matrix_ref = refs[4:]
+    rows = pieces[0].shape[0] // 8
+    own = at_ref[8]
+    for s in range(8):
+        for j in range(4):
+            first = pl.multiple_of((at_ref[s] * 4 + (own ^ j)) * rows, rows)
+            matrix_ref[pl.ds(first, rows), :] = pieces[j][s * rows : (s + 1) * rows, :]
+    first = 0
+    for ref in token_refs:
+        block = ref[...].astype(jnp.float32)
+        here = slice(first, first + ref.shape[0])
+        normed_ref[here, :] = (block * inverse_rms(block) * gain_ref[...]).astype(jnp.bfloat16)
+        first += ref.shape[0]
+    query_cols = q_ref.shape[1]
+    step = 256
+    for first in range(0, q_ref.shape[0], step):
+        here = slice(first, first + step)
+        raw = jnp.dot(normed_ref[here, :], matrix_ref[...], preferred_element_type=jnp.float32)
+        raw_ref[here, :] = raw
+        cosine, sine = cos_ref[here, :], sin_ref[here, :]
+        for col in range(0, query_cols + HEAD_SIZE, HEAD_SIZE):
+            part = raw[:, col : col + HEAD_SIZE]
+            if col < query_cols:
+                part = spun(part * inverse_rms(part) * head_gain_ref[:1], cosine, sine)
+                part = part * (LOG2E / math.sqrt(HEAD_SIZE))
+                q_ref[here, col : col + HEAD_SIZE] = part.astype(jnp.bfloat16)
+            else:
+                part = spun(part * inverse_rms(part) * head_gain_ref[1:2], cosine, sine)
+                kv_ref[here, :HEAD_SIZE] = part.astype(jnp.bfloat16)
+        kv_ref[here, HEAD_SIZE:] = raw[:, query_cols + HEAD_SIZE :].astype(jnp.bfloat16)
+
+
+def project(at, strips, pieces, gain, head_gains, cosine, sine, query_cols):
+    rows = sum(strip.shape[0] for strip in strips)
+    width = strips[0].shape[1]
+    cols = pieces[0].shape[1]
+    vmem = pl.BlockSpec(memory_space=pltpu.VMEM)
+    operands = (*strips, *pieces, gain, head_gains, cosine, sine)
+    narrow = jnp.bfloat16
+    return pl.pallas_call(
+        lambda *refs: project_kernel(*refs, strips=len(strips)),
+        in_specs=[pl.BlockSpec(memory_space=pltpu.SMEM)] + [vmem] * len(operands),
+        out_specs=[vmem] * 5,
+        out_shape=[
+            jax.ShapeDtypeStruct((rows, width), narrow),
+            jax.ShapeDtypeStruct((rows, cols), jnp.float32),
+            jax.ShapeDtypeStruct((rows, query_cols), narrow),
+            jax.ShapeDtypeStruct((rows, 2 * HEAD_SIZE), narrow),
+            jax.ShapeDtypeStruct((width, cols), narrow),
+        ],
+        cost_estimate=pl.CostEstimate(
+            flops=2 * rows * width * cols, bytes_accessed=16 << 20, transcendentals=0
+        ),
+        name="project",
+    )(at, *operands)
+
+
+def project_back_kernel(
+    dq_ref, dkv_ref, raw_ref, head_gain_ref, cos_ref, sin_ref, matrix_ref,
+    grad_ref, part_ref, gain_ref,
+):
+    query_cols = dq_ref.shape[1]
+    step = 256
+    gain_ref[...] = jnp.zeros_like(gain_ref)
+    for first in range(0, dq_ref.shape[0], step):
+        here = slice(first, first + step)
+        cosine, sine = cos_ref[here, :], sin_ref[here, :]
+        for col in range(0, query_cols + HEAD_SIZE, HEAD_SIZE):
+            cols = slice(col, col + HEAD_SIZE)
+            which = 0 if col < query_cols else 1
+            grads = dkv_ref[here, :HEAD_SIZE] if which else dq_ref[here, cols]
+            raw = raw_ref[here, cols]
+            rho = inverse_rms(raw)
+            unit = raw * rho
+            turned = spun(grads.astype(jnp.float32), cosine, -sine)
+            gain_ref[which : which + 1, :] += jnp.sum(turned * unit, axis=0, keepdims=True)
+            scaled = turned * head_gain_ref[which : which + 1]
+            back = rho * (scaled - unit * jnp.mean(unit * scaled, axis=-1, keepdims=True))
+            grad_ref[here, cols] = back.astype(jnp.bfloat16)
+        grad_ref[here, query_cols + HEAD_SIZE :] = dkv_ref[here, HEAD_SIZE:]
+        part_ref[here, :] = lax.dot_general(
+            grad_ref[here, :], matrix_ref[...], ALONG, preferred_element_type=jnp.float32
+        ).astype(jnp.bfloat16)
+
+
+def project_back(query_grads, kv_grads, raw, head_gains, cosine, sine, matrix):
+    rows, cols = raw.shape
+    vmem = pl.BlockSpec(memory_space=pltpu.VMEM)
+    return pl.pallas_call(
+        project_back_kernel,
+        in_specs=[vmem] * 7,
+        out_specs=[vmem] * 3,
+        out_shape=[
+            jax.ShapeDtypeStruct((rows, cols), jnp.bfloat16),
+            jax.ShapeDtypeStruct((rows, matrix.shape[0]), jnp.bfloat16),
+            jax.ShapeDtypeStruct((8, HEAD_SIZE), jnp.float32),
+        ],
+        cost_estimate=pl.CostEstimate(
+            flops=2 * rows * matrix.size, bytes_accessed=12 << 20, transcendentals=0
+        ),
+        name="project_back",
+    )(query_grads, kv_grads, raw, head_gains, cosine, sine, matrix)
+
+
+def dots(lefts, rights, dims):
+    return sum(
+        lax.dot_general(left[...], right[...], dims, preferred_element_type=jnp.float32)
+        for left, right in zip(lefts, rights)
+    )
+
+
+def weight_grads_kernel(at_ref, *refs, groups):
+    own_ref, far_ref, sent_ref, held = refs[-4:]
+    own = at_ref[8]
+    sums = dots(refs[:groups], refs[groups : 2 * groups], DOWN)
+    held[...] = sums.astype(jnp.bfloat16).reshape(held.shape)
+    own_ref[...] = held[own]
+    far_ref[...] = held[own ^ 2]
+    sent_ref[0] = held[own ^ 1]
+    sent_ref[1] = held[own ^ 3]
+
+
+def weight_grads(at, lefts, rights, rows):
+    count = at.shape[0] - 1
+    cols = rights[0].shape[1]
+    total = sum(left.shape[0] for left in lefts)
+    part = pl.BlockSpec((rows, cols), lambda i, at: (i, 0))
+    shape = jax.ShapeDtypeStruct((count * rows, cols), jnp.bfloat16)
+    own, far, sent = pl.pallas_call(
+        lambda *refs: weight_grads_kernel(*refs, groups=len(lefts)),
+        grid_spec=pltpu.PrefetchScalarGridSpec(
+            num_scalar_prefetch=1,
+            grid=(count,),
+            in_specs=[
+                pl.BlockSpec((left.shape[0], 4 * rows), lambda i, at: (0, at[i]))
+                for left in lefts
+            ]
+            + [pl.BlockSpec(right.shape, lambda i, at: (0, 0)) for right in rights],
+            out_specs=[part, part, pl.BlockSpec((2, rows, cols), lambda i, at: (0, i, 0))],
+            scratch_shapes=[pltpu.VMEM((4, rows, cols), jnp.bfloat16)],
+        ),
+        out_shape=[
+            shape, shape, jax.ShapeDtypeStruct((2, count * rows, cols), jnp.bfloat16),
+        ],
+        cost_estimate=pl.CostEstimate(
+            flops=2 * total * lefts[0].shape[1] * cols,
+            bytes_accessed=2 * total * (lefts[0].shape[1] + cols),
+            transcendentals=0,
+        ),
+        name="weight_grads",
+    )(at, *lefts, *rights)
+    return own, far, sent.reshape(2 * count * rows, cols)
+
+
+def row_grads_kernel(*refs, groups):
+    refs[-1][...] = dots(refs[:groups], refs[groups : 2 * groups], DOWN).astype(jnp.bfloat16)
+
+
+def row_grads(lefts, rights, block=256):
+    out_rows, cols = lefts[0].shape[1], rights[0].shape[1]
+    total = sum(left.shape[0] for left in lefts)
+    return pl.pallas_call(
+        lambda *refs: row_grads_kernel(*refs, groups=len(lefts)),
+        grid=(out_rows // block,),
+        in_specs=[pl.BlockSpec((left.shape[0], block), lambda i: (0, i)) for left in lefts]
+        + [pl.BlockSpec(right.shape, lambda i: (0, 0)) for right in rights],
+        out_specs=pl.BlockSpec((block, cols), lambda i: (i, 0)),
+        out_shape=jax.ShapeDtypeStruct((out_rows, cols), jnp.bfloat16),
+        cost_estimate=pl.CostEstimate(
+            flops=2 * total * out_rows * cols,
+            bytes_accessed=2 * total * (out_rows + cols),
+            transcendentals=0,
+        ),
+        name="row_grads",
+    )(*lefts, *rights)
+
+
+def stack_project_kernel(*refs):
+    matrix_ref, out_ref = refs[-2:]
+    first = 0
+    for ref in refs[:-2]:
+        out_ref[first : first + ref.shape[0], :] = lax.dot_general(
+            ref[...], matrix_ref[...], ALONG, preferred_element_type=jnp.float32
+        ).astype(jnp.bfloat16)
+        first += ref.shape[0]
+
+
+def stack_project(groups, matrix):
+    rows = sum(group.shape[0] for group in groups)
+    vmem = pl.BlockSpec(memory_space=pltpu.VMEM)
+    return pl.pallas_call(
+        stack_project_kernel,
+        in_specs=[vmem] * (len(groups) + 1),
+        out_specs=vmem,
+        out_shape=jax.ShapeDtypeStruct((rows, matrix.shape[0]), jnp.bfloat16),
+        cost_estimate=pl.CostEstimate(
+            flops=2 * rows * matrix.size, bytes_accessed=2 * rows * matrix.shape[1], transcendentals=0
+        ),
+        name="stack_project",
+    )(*groups, matrix)
+
+
+def lane_sums(block):
+    return sum(block[:, i : i + 128] for i in range(0, block.shape[1], 128))
+
+
+def widen_kernel(at_ref, piece_ref, *refs, count):
+    weights, grads, sums_ref = refs[:count], refs[count : 2 * count], refs[2 * count]
+    rows = weights[0].shape[0]
+
+    @pl.when(pl.program_id(0) == 0)
+    def _():
+        sums_ref[...] = jnp.zeros_like(sums_ref)
+
+    first = 0
+    for weight, grad in zip(weights, grads):
+        cols = weight.shape[1]
+        block = piece_ref[:rows, first : first + cols].astype(jnp.float32)
+        grad[...] = block
+        sums_ref[...] += lane_sums(block * weight[...].astype(jnp.float32))
+        first += cols
+
+
+def widen(at, pieces, *weights):
+    count = at.shape[0]
+    rows = weights[0].shape[0]
+    each, cols = pieces.shape[0] // count, pieces.shape[1]
+    specs = [
+        pl.BlockSpec((rows, w.shape[1] // count), lambda i, at: (0, at[i])) for w in weights
+    ]
+    shapes = [w.shape for w in weights] + [(rows, 128)]
+    out_specs = specs + [pl.BlockSpec((rows, 128), lambda i, at: (0, 0))]
+    return pl.pallas_call(
+        lambda *refs: widen_kernel(*refs, count=len(weights)),
+        grid_spec=pltpu.PrefetchScalarGridSpec(
+            num_scalar_prefetch=1,
+            grid=(count,),
+            in_specs=[pl.BlockSpec((each, cols), lambda i, at: (i, 0))] + specs,
+            out_specs=out_specs,
+        ),
+        out_shape=[jax.ShapeDtypeStruct(shape, jnp.float32) for shape in shapes],
+        name="widen",
+    )(at, pieces, *weights)
 
 
 def grouped(strips):
@@ -660,18 +1020,6 @@
     ]
 
 
-def swap_slices(pieces, place, blk_index):
-    ring = jnp.asarray(RING, jnp.int32)
-    own = lax.dynamic_index_in_dim(pieces, blk_index, 0)
-    out = lax.dynamic_update_slice_in_dim(jnp.zeros_like(pieces), own, blk_index, 0)
-    for by in (4, 1, 7, 2, 6, 3, 5):
-        target = ring[(place + by) % 8]
-        source = ring[(place - by) % 8]
-        moved = hop(lax.dynamic_index_in_dim(pieces, target, 0), by)
-        out = lax.dynamic_update_slice_in_dim(out, moved, source, 0)
-    return out
-
-
 def gather_head(rows):
     return lax.all_gather(rows, "head", axis=0, tiled=True)
 
@@ -682,27 +1030,6 @@
 
 def inverse_rms(rows):
     return lax.rsqrt(jnp.mean(rows * rows, axis=-1, keepdims=True) + EPS)
-
-
-def turn(rows, cosine, sine):
-    half = HEAD_SIZE // 2
-    first, second = rows[:, :half], rows[:, half:]
-    return jnp.concatenate(
-        [first * cosine - second * sine, second * cosine + first * sine], axis=1
-    )
-
-
-def head_back(grads, raw, gain, cosine, sine):
-    rho = inverse_rms(raw)
-    unit = raw * rho
-    turned = turn(grads.astype(jnp.float32), cosine, -sine)
-    gain_part = jnp.sum(turned * unit, axis=0)
-    scaled = turned * gain
-    return rho * (scaled - unit * jnp.mean(unit * scaled, axis=-1, keepdims=True)), gain_part
-
-
-def after(value, *earlier):
-    return lax.optimization_barrier((value, *earlier))[0]
 
 
 def per_device(
@@ -731,59 +1058,18 @@
     group_rows = local_rows * blk_count
     weight_rows = query_weight.shape[0]
     ff_local = gate_weight.shape[1] // blk_count
-    group_heads = QUERY_HEADS // blk_count
-    query_cols = group_heads * HEAD_SIZE
-    attn_cols = query_cols + 2 * HEAD_SIZE
+    query_cols = QUERY_HEADS // blk_count * HEAD_SIZE
     strip_count = blk_count * head_count
     halves = strip_count // stretch_order.shape[1]
     ring_place = jnp.where(blk_index % 2 == 0, blk_index // 2, 7 - blk_index // 2)
 
-    def pieces_of(*weights):
-        return jnp.concatenate(
-            [w.reshape(weight_rows, blk_count, w.shape[1] // blk_count) for w in weights], axis=2
-        ).transpose(1, 0, 2)
-
-    def natural(pieces, rows):
-        return pieces.reshape(head_count, blk_count, rows, -1).transpose(1, 0, 2, 3)
-
-    small = query_norm.shape[0]
-    gains = jnp.concatenate([attention_norm, feedforward_norm, query_norm, key_norm])
-    gains = jnp.pad(gains, (0, attn_cols - gains.shape[0]))[None, None, :]
-    gains = jnp.pad(gains, ((0, 0), (0, 15), (0, 0)))
-    attn_pieces = jnp.concatenate(
-        [
-            pieces_of(query_weight, key_projection, value_projection),
-            jnp.broadcast_to(gains, (blk_count, 16, attn_cols)),
-        ],
-        axis=1,
-    )
-    token_strips = ring_gather(tokens)
-    attn_all = natural(
-        gather_head(swap_slices(attn_pieces, ring_place, blk_index)), weight_rows + 16
-    )
-    attn_matrix = attn_all[:, :, :weight_rows].reshape(model_width, attn_cols)
-    gain_rows = attn_all[:, :, weight_rows]
-    gain_one = gain_rows[:, :, :weight_rows].reshape(1, model_width).astype(wide)
-    gain_two = (
-        gain_rows[:, :, weight_rows : 2 * weight_rows].reshape(1, model_width).astype(wide)
-    )
-    at = 2 * weight_rows
-    query_gain = gain_rows[:, :, at : at + small].reshape(1, HEAD_SIZE).astype(wide)
-    key_gain = gain_rows[:, :, at + small : at + 2 * small].reshape(1, HEAD_SIZE).astype(wide)
-
-    output_rows = gather_head(output_weight)
-    ff_pieces = after(pieces_of(gate_weight, up_weight), token_strips[-1])
-    ff_matrix = natural(
-        gather_head(swap_slices(ff_pieces, ring_place, blk_index)), weight_rows
-    ).reshape(model_width, 2 * ff_local)
-    down_matrix = gather_head(down_weight)
-    cotangent_strips = ring_gather(after(out_cotangent, token_strips[-1]))
-
+    spot = (ring_place + jnp.arange(blk_count, dtype=jnp.int32)) % blk_count
+    at = jnp.where(spot < 4, 2 * spot, 15 - 2 * spot).astype(jnp.int32)
+    at_own = jnp.concatenate([at, head_index[None].astype(jnp.int32)])
     numbers = jnp.arange(strip_count, dtype=jnp.int32)
-    on = jnp.asarray(STRIPS, jnp.int32)
-    ring_spot = (ring_place + on) % blk_count
+    ring_spot = (ring_place + jnp.asarray(STRIPS, jnp.int32)) % blk_count
     strip_blk = jnp.where(ring_spot < 4, 2 * ring_spot, 15 - 2 * ring_spot)
-    strip_head = head_index ^ jnp.arange(head_count, dtype=jnp.int32)
+    strip_head = head_index ^ jnp.asarray((0, 2, 1, 3), jnp.int32)
     strip = (strip_blk[None, :] * head_count + strip_head[:, None]).reshape(strip_count)
     slots = jnp.arange(stretch_order.shape[1], dtype=jnp.int32)
     held = jnp.sum(
@@ -799,171 +1085,222 @@
     ).reshape(group_rows)
     phases = angles(positions, HEAD_SIZE)[:, 0, :]
     cosine, sine = jnp.cos(phases), jnp.sin(phases)
-
-    tokens_wide = tokens.astype(wide)
-    raw_groups, normed_groups, query_groups, kv_groups = [], [], [], []
-    for (first, last), rows in zip(GROUPS, grouped(token_strips)):
-        here = slice(first * local_rows, last * local_rows)
-        rows = rows.astype(wide)
-        normed = (rows * inverse_rms(rows) * gain_one).astype(narrow)
-        raw = matmul(normed, attn_matrix)
-        heads = []
-        for h in range(group_heads + 1):
-            part = raw[:, h * HEAD_SIZE : (h + 1) * HEAD_SIZE]
-            gain = query_gain if h < group_heads else key_gain
-            part = turn(part * inverse_rms(part) * gain, cosine[here], sine[here])
-            if h < group_heads:
-                part = part * (LOG2E / math.sqrt(HEAD_SIZE))
-            heads.append(part.astype(narrow))
-        raw_groups.append(raw)
-        normed_groups.append(normed)
-        query_groups.append(jnp.concatenate(heads[:group_heads], axis=1))
-        kv_groups.append(
-            jnp.concatenate(
-                [heads[group_heads], raw[:, query_cols + HEAD_SIZE :].astype(narrow)], axis=1
-            )
-        )
-    first_normed = jnp.concatenate(normed_groups, axis=0)
-    attn_raw = jnp.concatenate(raw_groups, axis=0)
-    query_rows = jnp.concatenate(query_groups, axis=0)
-    kv_own = jnp.concatenate(kv_groups, axis=0)
-    kv_far = cross(kv_own, 2)
-    kv = jnp.concatenate([kv_own, cross(kv_own, 1), kv_far, cross(kv_far, 1)], axis=0)
+    cosine = jnp.concatenate([cosine, cosine], axis=1)
+    sine = jnp.concatenate([-sine, sine], axis=1)
+
+    small = query_norm.shape[0]
+    gains = jnp.concatenate([attention_norm, feedforward_norm, query_norm, key_norm])
+    gains = lax.all_gather(gains, ("blk", "head"), axis=0).astype(wide)
+    gain_one = gains[:, :weight_rows].reshape(1, model_width)
+    gain_two = gains[:, weight_rows : 2 * weight_rows].reshape(1, model_width)
+    first = 2 * weight_rows
+    head_gains = jnp.concatenate(
+        [
+            gains[:, first : first + small].reshape(1, HEAD_SIZE),
+            gains[:, first + small :].reshape(1, HEAD_SIZE),
+            jnp.zeros((6, HEAD_SIZE), wide),
+        ],
+        axis=0,
+    )
+    down_matrix = gather_head(down_weight)
+    output_rows = gather_head(output_weight)
+
+    attn_swap = Swap(
+        slice_pieces(at, query_weight, key_projection, value_projection), weight_rows
+    )
+    token_ring = Gather(tokens)
+    ff_slices = slice_pieces(at, gate_weight, up_weight)
+    for step in range(4):
+        attn_swap.go()
+        token_ring.go()
+        if step == 0:
+            ff_slices, cosine, sine = hold((attn_swap, token_ring), ff_slices, cosine, sine)
+        elif step < 3:
+            hold((attn_swap, token_ring))
+    ff_swap, cotangent_ring = Swap(ff_slices, weight_rows), Gather(out_cotangent)
+    own = hold((token_ring, ff_swap), attn_swap.result())
+    near, far = cross(own, 1), cross(own, 2)
+    ff_swap.go()
+    own, near, far = hold((ff_swap, cotangent_ring), own, near, far)
+    both = cross(far, 1)
+    ff_swap.go()
+    own, near, far, both = hold((ff_swap, cotangent_ring), own, near, far, both)
+
+    first_normed, attn_raw, query_rows, own, attn_matrix = project(
+        at_own, token_ring.strips(), (own, near, far, both),
+        gain_one, head_gains, cosine, sine, query_cols,
+    )
+    ff_swap.go()
+    cotangent_ring.go()
+    own = hold((ff_swap, cotangent_ring), own)
+    near, far = cross(own, 1), cross(own, 2)
+    ff_swap.go()
+    cotangent_ring.go()
+    own, near, far, ff_own = hold((cotangent_ring,), own, near, far, ff_swap.result())
+    both = cross(far, 1)
+    ff_near, ff_far = cross(ff_own, 1), cross(ff_own, 2)
+    kv = jnp.concatenate([own, far, near, both], axis=0)
+    kv = hold((cotangent_ring,), kv)
     attended, lse = attend(place, order, query_rows, kv)
+    cotangent_ring.go()
 
     def by_groups(rows):
         return [rows[a * local_rows : b * local_rows] for a, b in GROUPS]
 
-    branch_parts = [
-        matmul(rows, output_rows).astype(narrow) for rows in reversed(by_groups(attended))
-    ]
-    branch = ring_scatter(split_groups(branch_parts[::-1], local_rows))
-    resid = tokens_wide + branch
+    def by_strips(groups):
+        return dict(zip(STRIPS, split_groups(groups, local_rows)))
+
+    attended = hold((cotangent_ring,), attended)
+    branch_ring = Scatter(
+        by_strips([matmul(rows, output_rows).astype(narrow) for rows in by_groups(attended)])
+    )
+    branch_ring.go()
+    cotangent_ring.go()
+    hold((branch_ring, cotangent_ring))
+    branch_ring.go()
+    ff_near, ff_far = hold((branch_ring,), ff_near, ff_far)
+    ff_both = cross(ff_far, 1)
+    branch_ring.go()
+    cotangent_groups = grouped(cotangent_ring.strips())
+    hidden_grads = [matmul(rows, down_matrix, ALONG) for rows in cotangent_groups]
+    hidden_grads, ff_own, ff_near, ff_far, ff_both = hold(
+        (branch_ring,), hidden_grads, ff_own, ff_near, ff_far, ff_both
+    )
+    branch_ring.go()
+    ff_matrix = assemble(at_own, (ff_own, ff_near, ff_far, ff_both), weight_rows)
+    ff_matrix = hold((branch_ring,), ff_matrix)
+    tokens_wide = tokens.astype(wide)
+    resid = tokens_wide + branch_ring.total()
     rho_two = inverse_rms(resid)
     unit_two = resid * rho_two
-    second_strips = ring_gather((unit_two * gain_two).astype(narrow))
-
-    hidden_groups, ff_gradient_groups, second_parts = [], [], []
-    second_groups = grouped(second_strips)
-    cotangent_groups = grouped(cotangent_strips)
-    for rows, grads in zip(second_groups, cotangent_groups):
+
+    second_ring = Gather((unit_two * gain_two).astype(narrow))
+    second_groups, hidden_groups, ff_gradient_groups = [], [], []
+
+    def feed_forward(index):
+        rows = second_ring.group(index)
         ff_raw = matmul(rows, ff_matrix)
         gate, up_proj = ff_raw[:, :ff_local], ff_raw[:, ff_local:]
         sigma = jax.nn.sigmoid(gate)
         swish = gate * sigma
-        hidden_groups.append((swish * up_proj).astype(narrow))
-        hidden_gradient = matmul(grads, down_matrix, ALONG)
+        hidden_gradient = hidden_grads[index]
         gate_gradient = hidden_gradient * up_proj * (sigma * (1.0 + gate * (1.0 - sigma)))
-        ff_gradient_groups.append(
-            jnp.concatenate([gate_gradient, hidden_gradient * swish], 1).astype(narrow)
-        )
-    for rows in reversed(ff_gradient_groups):
-        second_parts.append(matmul(rows, ff_matrix, ALONG).astype(narrow))
-    second_gradient = ring_scatter(split_groups(second_parts[::-1], local_rows))
-    scaled = gain_two * second_gradient
+        hidden = (swish * up_proj).astype(narrow)
+        gradient = jnp.concatenate([gate_gradient, hidden_gradient * swish], 1).astype(narrow)
+        if index < 3:
+            rows, hidden, gradient = hold((second_ring,), rows, hidden, gradient)
+        second_groups.append(rows)
+        hidden_groups.append(hidden)
+        ff_gradient_groups.append(gradient)
+
+    second_ring.go()
+    hold((second_ring,))
+    for index in range(3):
+        second_ring.go()
+        feed_forward(index)
+    feed_forward(3)
+
+    def back(index):
+        return matmul(ff_gradient_groups[index], ff_matrix, ALONG).astype(narrow)
+
+    def split(group):
+        return [group[i : i + local_rows] for i in range(0, group.shape[0], local_rows)]
+
+    parts = {4: back(3)}
+    resid_ring = Scatter(parts)
+    parts[3], parts[5] = split(hold((), back(2)))
+    resid_ring.go()
+    parts[2], parts[6] = split(hold((resid_ring,), back(1)))
+    resid_ring.go()
+    parts[0], parts[1], parts[7] = split(hold((resid_ring,), back(0)))
+    resid_ring.go()
+    ff_own, ff_far, ff_sent = hold(
+        (resid_ring,), *weight_grads(at_own, second_groups, ff_gradient_groups, weight_rows)
+    )
+    resid_ring.go()
+    ff_own, ff_far = scatter_cross(ff_own, ff_far, ff_sent)
+    down_gradient = row_grads(hidden_groups, cotangent_groups)
+    down_gradient, ff_own, ff_far = hold((resid_ring,), down_gradient, ff_own, ff_far)
+    down_gradient = scatter_head(down_gradient)
+    ff_far = cross(ff_far, 2)
+    scaled = gain_two * resid_ring.total()
     resid_gradient = out_cotangent.astype(wide) + rho_two * (
         scaled - unit_two * jnp.mean(unit_two * scaled, axis=-1, keepdims=True)
     )
-    branch_gradient = resid_gradient.astype(narrow)
-    branch_strips = ring_gather(branch_gradient)
-
-    out_parts = [matmul(rows, down_matrix).astype(narrow) for rows in reversed(hidden_groups)]
-    out_parts = split_groups(out_parts[::-1], local_rows)
-    out_part = ring_scatter(out_parts[:-1] + [after(out_parts[-1], branch_strips[-1])])
-    layer_out = (resid + out_part).astype(narrow)
-
-    second_normed = jnp.concatenate(second_groups, axis=0)
-    group_cotangent = jnp.concatenate(cotangent_groups, axis=0)
-    hidden = jnp.concatenate(hidden_groups, axis=0)
-    ff_gradient = jnp.concatenate(ff_gradient_groups, axis=0)
-
-    def by_head(grads, rows):
-        shape = (blk_count, head_count, rows, grads.shape[-1])
-        return grads.reshape(shape).transpose(1, 0, 2, 3).reshape(-1, rows, grads.shape[-1])
-
-    down_gradient = scatter_head(matmul(hidden, group_cotangent, DOWN).astype(narrow))
-    ff_matrix_gradient = scatter_head(
-        by_head(matmul(second_normed, ff_gradient, DOWN).astype(narrow), weight_rows)
-    )
-    ff_matrix_gradient = swap_slices(ff_matrix_gradient, ring_place, blk_index).astype(wide)
-    gate_weight_gradient = (
-        ff_matrix_gradient[:, :, :ff_local].transpose(1, 0, 2).reshape(gate_weight.shape)
-    )
-    up_weight_gradient = (
-        ff_matrix_gradient[:, :, ff_local:].transpose(1, 0, 2).reshape(up_weight.shape)
-    )
-    feedforward_norm_gradient = (
-        jnp.sum(gate_weight_gradient * gate_weight.astype(wide), axis=1)
-        + jnp.sum(up_weight_gradient * up_weight.astype(wide), axis=1)
-    ) / feedforward_norm.astype(wide)
-
-    branch_groups = grouped(branch_strips)
-    attended_gradient = jnp.concatenate(
-        [matmul(rows, output_rows, ALONG).astype(narrow) for rows in branch_groups], axis=0
-    )
-    output_weight_gradient = scatter_head(
-        matmul(attended, jnp.concatenate(branch_groups, axis=0), DOWN).astype(narrow)
-    ).astype(wide)
+
+    grad_ring = Gather(resid_gradient.astype(narrow))
+    grad_ring.go()
+    out_parts = [matmul(rows, down_matrix).astype(narrow) for rows in hidden_groups]
+    out_parts = hold((grad_ring,), *out_parts)
+    out_ring = Scatter(by_strips(out_parts))
+    grad_ring.go()
+    hold((grad_ring,))
+    grad_ring.go()
+    ff_far = hold((grad_ring,), ff_far)
+    ff_swap = Swap(add(ff_own, ff_far), weight_rows)
+    grad_ring.go()
+    hold((grad_ring, ff_swap, out_ring))
+    grad_strips = grad_ring.strips()
+    attended_gradient = stack_project(grad_strips, output_rows)
+    out_ring.go()
+    hold((out_ring,), attended_gradient)
     query_grads, kv_grads = attend_back(
         place, order, query_rows, attended_gradient, attended, lse, kv
     )
-    kv_near = [kv_grads[j * group_rows : (j + 1) * group_rows] for j in range(head_count)]
-    kv_sent = cross(jnp.concatenate([kv_near[1], kv_near[3]], axis=0), 1)
-    kv_grads = add(
-        add(kv_near[0], kv_sent[:group_rows]), cross(add(kv_near[2], kv_sent[group_rows:]), 2)
-    )
-    attn_gradient, gain_parts = [], []
-    for h in range(group_heads + 1):
-        cols = slice(h * HEAD_SIZE, (h + 1) * HEAD_SIZE)
-        grads = query_grads[:, cols] if h < group_heads else kv_grads[:, :HEAD_SIZE]
-        gain = query_gain if h < group_heads else key_gain
-        raw_gradient, gain_part = head_back(grads, attn_raw[:, cols], gain, cosine, sine)
-        attn_gradient.append(raw_gradient.astype(narrow))
-        gain_parts.append(gain_part)
-    attn_gradient = jnp.concatenate(attn_gradient + [kv_grads[:, HEAD_SIZE:]], axis=1)
-    first_parts = [
-        matmul(rows, attn_matrix, ALONG).astype(narrow)
-        for rows in reversed(by_groups(attn_gradient))
-    ]
-    first_gradient = ring_scatter(split_groups(first_parts[::-1], local_rows))
-    attn_matrix_gradient = by_head(
-        matmul(first_normed, attn_gradient, DOWN).astype(narrow), weight_rows
-    )
-    gain_parts = jnp.stack(
-        [
-            sum(gain_parts[:group_heads]).reshape(blk_count, head_count, small),
-            gain_parts[group_heads].reshape(blk_count, head_count, small),
-        ],
-        axis=2,
-    ).transpose(1, 0, 2, 3)
-    gain_parts = gain_parts.reshape(strip_count, 1, 2 * small).astype(narrow)
-    gain_parts = jnp.pad(gain_parts, ((0, 0), (0, 15), (0, attn_cols - 2 * small)))
-    attn_matrix_gradient = swap_slices(
-        scatter_head(jnp.concatenate([attn_matrix_gradient, gain_parts], axis=1)),
-        ring_place,
-        blk_index,
-    ).astype(wide)
-    attn_rows = attn_matrix_gradient[:, :weight_rows]
-    query_weight_gradient = (
-        attn_rows[:, :, :query_cols].transpose(1, 0, 2).reshape(query_weight.shape)
-    )
-    key_weight_gradient = (
-        attn_rows[:, :, query_cols : query_cols + HEAD_SIZE]
-        .transpose(1, 0, 2)
-        .reshape(key_projection.shape)
-    )
-    value_weight_gradient = (
-        attn_rows[:, :, query_cols + HEAD_SIZE :].transpose(1, 0, 2).reshape(value_projection.shape)
-    )
-    gain_sums = jnp.sum(attn_matrix_gradient[:, weight_rows], axis=0)
-    attention_norm_gradient = (
-        jnp.sum(query_weight_gradient * query_weight.astype(wide), axis=1)
-        + jnp.sum(key_weight_gradient * key_projection.astype(wide), axis=1)
-        + jnp.sum(value_weight_gradient * value_projection.astype(wide), axis=1)
-    ) / attention_norm.astype(wide)
+    ff_swap.go()
+    out_ring.go()
+    query_grads, kv_grads = hold((out_ring, ff_swap), query_grads, kv_grads)
+    kv_own, kv_far = scatter_cross(
+        kv_grads[:group_rows], kv_grads[group_rows : 2 * group_rows], kv_grads[2 * group_rows :]
+    )
+    kv_far = cross(kv_far, 2)
+    out_ring.go()
+    ff_swap.go()
+    output_weight_gradient = row_grads([attended], [jnp.concatenate(grad_strips, axis=0)])
+    output_weight_gradient, kv_grads = hold(
+        (out_ring, ff_swap), output_weight_gradient, add(kv_own, kv_far)
+    )
+    output_weight_gradient = scatter_head(output_weight_gradient).astype(wide)
+    attn_gradient, first_parts, gain_sums = project_back(
+        query_grads, kv_grads, attn_raw, head_gains, cosine, sine, attn_matrix
+    )
+    ff_swap.go()
+    out_ring.go()
+    attn_gradient, first_parts = hold((out_ring, ff_swap), attn_gradient, first_parts)
+    layer_out = (resid + out_ring.total()).astype(narrow)
+    gain_sums = lax.psum(gain_sums[:2], ("blk", "head"))
+    token_ring = Scatter(by_strips(by_groups(first_parts)))
+    token_ring.go()
+    ff_swap.go()
+    attn_own, attn_far, attn_sent = hold(
+        (token_ring, ff_swap),
+        *weight_grads(at_own, [first_normed], [attn_gradient], weight_rows),
+    )
+    attn_own, attn_far = scatter_cross(attn_own, attn_far, attn_sent)
+    attn_far = cross(attn_far, 2)
+    token_ring.go()
+    gate_weight_gradient, up_weight_gradient, norm_sums = widen(
+        at, ff_swap.result(), gate_weight, up_weight
+    )
+    feedforward_norm_gradient = jnp.sum(norm_sums, axis=1) / feedforward_norm.astype(wide)
+    attn_swap = Swap(add(attn_own, attn_far), weight_rows)
+    hold((token_ring, attn_swap), gate_weight_gradient)
+    attn_swap.go()
+    token_ring.go()
+    hold((token_ring, attn_swap))
+    attn_swap.go()
+    token_ring.go()
+    attn_swap.go()
+    attn_swap.go()
+    query_weight_gradient, key_weight_gradient, value_weight_gradient, norm_sums = widen(
+        at, attn_swap.result(), query_weight, key_projection, value_projection
+    )
+    attention_norm_gradient = jnp.sum(norm_sums, axis=1) / attention_norm.astype(wide)
+    own_first = (blk_index * head_count + head_index) * small
+    gain_sums = lax.dynamic_slice_in_dim(gain_sums, own_first, small, 1)
     rho_one = inverse_rms(tokens_wide)
     unit_one = tokens_wide * rho_one
-    scaled = gain_one * first_gradient
+    scaled = gain_one * token_ring.total()
     tokens_gradient = resid_gradient + rho_one * (
         scaled - unit_one * jnp.mean(unit_one * scaled, axis=-1, keepdims=True)
     )
@@ -974,8 +1311,8 @@
         query_weight_gradient,
         key_weight_gradient,
         value_weight_gradient,
-        gain_sums[:small],
-        gain_sums[small : 2 * small],
+        gain_sums[0],
+        gain_sums[1],
         output_weight_gradient,
         feedforward_norm_gradient,
         gate_weight_gradient,

time: 837 us -> 754 us (0.901)
  waiting for transfers between devices: 358 us -> 215 us
  Pallas kernels: 53.3 us -> 146 us
  blocking collectives: 0 us -> 85.3 us
  matrix products: 82 us -> 39.4 us
  starting transfers between devices: 149 us -> 108 us
  between operations: 44.6 us -> 15.8 us
  local copies, waits for them, and re-layouts: 75 us -> 64.8 us
    ppermute x92 -> x96, waiting for transfers between devices: 318 us -> 190 us  [hop(): lax.ppermute(value, 'blk', [(RING[i], RING[(i + by) % count]) for i in ra...]
    pallas_call x0 -> x12, Pallas kernels: none -> 93.9 us  [the longest x2 23.2 us: weight_grads(): pl.pallas_call(lambda *refs: weight_grads_kernel(*refs, groups=len(lefts)...]
    unnamed x0 -> x1, blocking collectives: none -> 46 us
    ppermute x92 -> x96, starting transfers between devices: 146 us -> 103 us  [hop(): lax.ppermute(value, 'blk', [(RING[i], RING[(i + by) % count]) for i in ra...]
    dot_general x36 -> x20, matrix products: 82 us -> 39.4 us  [matmul(): lax.dot_general(left, right, dims, preferred_element_type=jnp.float32)]
    psum x0 -> x1, blocking collectives: none -> 39.3 us  [per_device(): gain_sums = lax.psum(gain_sums[:2], ('blk', 'head'))]
    convert_element_type x14 -> x18, other arithmetic: 7.97 us -> 30.5 us  [add(): (left.astype(jnp.float32) + right.astype(jnp.float32)).astype(left.dtype)]
    ppermute x5 -> x15, waiting for transfers between devices: 40.2 us -> 24.5 us  [cross(): return lax.ppermute(value, 'head', [(i, i ^ by) for i in range(4)])]
  transfers between devices with their start and end apart: 105 -> 115, of which waited for: 51 -> 47; matrix products, arithmetic and copies ran while one was open for 22% -> 19% of each run, Pallas kernels for 6% -> 20%
where the time goes in v4:
time: 754 us; the launch traced here: 744 us
  waiting for transfers between devices  215 us (29%)
  Pallas kernels  146 us (19%)
  starting transfers between devices  108 us (14%)
  blocking collectives  85.3 us (11%)
  other arithmetic  68.9 us (9%)
  local copies, waits for them, and re-layouts  64.8 us (9%)
  matrix products  39.4 us (5%)
  between operations  15.8 us (2%)
    ppermute x96, waiting for transfers between devices, hop(): lax.ppermute(value, 'blk', [(RING[i], RING[(i + by) % count]) for i in ra...  190 us
    ppermute x96, starting transfers between devices, hop(): lax.ppermute(value, 'blk', [(RING[i], RING[(i + by) % count]) for i in ra...  103 us
    unnamed x1, blocking collectives  46 us
    dot_general x20, matrix products, matmul(): lax.dot_general(left, right, dims, preferred_element_type=jnp.float32)  39.4 us
    psum x1, blocking collectives, per_device(): gain_sums = lax.psum(gain_sums[:2], ('blk', 'head'))  39.3 us
    unnamed x218, local copies, waits for them, and re-layouts  32.4 us
    convert_element_type x18, other arithmetic, add(): (left.astype(jnp.float32) + right.astype(jnp.float32)).astype(left.dtype)  30.5 us
    pallas_call x1, Pallas kernels, attend_back(): pl.pallas_call(attend_back_kernel, grid_spec=pltpu.PrefetchScalarGridSpec...  30 us
  transfers between devices with their start and end apart: 115, of which 47 were waited for; matrix products, arithmetic and copies ran while one was open for 19% of the time, Pallas kernels for 20%

profile of v4, /device:TPU:0, one launch (start us, length us, event | category | flops | bytes accessed | tf_op | source)
XLA Modules:
  0.0 743.8 jit_solution(11490058745591119939)
XLA Ops:
  35.5 46.0 %all-reduce = bf16[4352]{0:T(1024)(128)(2,1)S(1)} all-reduce(bf16[4352]{0:T(1024)(128)(2,1)S(1)} %dynamic-update-slice), channel_id=2, replica_groups=mesh['blk'=8,'head'=4] {'blk','head'}, use_global_device_ids=true, to_apply=%add | all-reduce | flops 4352 | bytes 17408
  93.8 10.6 %collective-permute-done.8 = bf16[96,512]{1,0:T(8,128)(2,1)S(1)} collective-permute-done((bf16[96,512]{1,0:T(8,128)(2,1)S(1)}, bf16[96,512]{1,0:T(8,128)(2,1)S(1)}, u32[]{:S(2)}, u32[]{:S(2)}) %collective-permute-start.8) | collective-permute-done | bytes 98336 | tf_op jit(solution)/shard_map/ppermute | solution.py:615
  138.8 8.4 %collective-permute-done.20 = bf16[160,1536]{1,0:T(8,128)(2,1)S(1)} collective-permute-done((bf16[160,1536]{1,0:T(8,128)(2,1)S(1)}, bf16[160,1536]{1,0:T(8,128)(2,1)S(1)}, u32[]{:S(2)}, u32[]{:S(2)}) %collective-permute-start.20) | collective-permute-done | bytes 491552 | tf_op jit(solution)/shard_map/ppermute | solution.py:615
  152.9 9.7 %project.1 = (bf16[1024,2048]{1,0:T(8,128)(2,1)}, f32[1024,512]{1,0:T(8,128)}, bf16[1024,256]{1,0:T(8,128)(2,1)}, bf16[1024,256]{1,0:T(8,128)(2,1)}, bf16[2048,512]{1,0:T(8,128)(2,1)}) custom-call(s32[9]{0:T(128)} %pad_add_fusion.refs_0_.at_ref, bf16[128,2048]{1,0:T(8,128)(2,1)} %bitcast.69, bf16[128,2048]{1,0:T(8,128)(2,1)} %collective-permute-done.2.refs_2_, ...), custom_call_target="tpu_custom_call" | custom-call | flops 2147483648 | bytes 16777216 | tf_op jit(solution)/shard_map/project/pallas_call | solution.py:803
  174.5 11.5 %collective-permute-done.32 = bf16[32,1536]{1,0:T(8,128)(2,1)S(1)} collective-permute-done((bf16[32,1536]{1,0:T(8,128)(2,1)S(1)}, bf16[32,1536]{1,0:T(8,128)(2,1)S(1)}, u32[]{:S(2)}, u32[]{:S(2)}) %collective-permute-start.32) | collective-permute-done | bytes 98336 | tf_op jit(solution)/shard_map/ppermute | solution.py:615
  199.3 22.0 %attend.1 = (bf16[1024,256]{1,0:T(8,128)(2,1)}, f32[8,8,256]{2,1,0:T(8,128)}) custom-call(s32[8]{0:T(128)} %get-tuple-element.444.place_ref, s32[32]{0:T(128)} %select_reduce_fusion.order_ref, bf16[1024,256]{1,0:T(8,128)(2,1)} %get-tuple-element.234.q_ref, bf16[4096,256]{1,0:T(8,128)(2,1)} %pad_maximum_fusion.kv_ref), custom_call_target="tpu_custom_call" | custom-call | flops 2147483648 | bytes 3145728 | tf_op jit(solution)/shard_map/attend/pallas_call | solution.py:474
  260.6 10.5 %collective-permute-done.45 = bf16[128,2048]{1,0:T(8,128)(2,1)S(1)} collective-permute-done((bf16[128,2048]{1,0:T(8,128)(2,1)S(1)}, bf16[128,2048]{1,0:T(8,128)(2,1)S(1)}, u32[]{:S(2)}, u32[]{:S(2)}) %collective-permute-start.45) | collective-permute-done | bytes 524320 | tf_op jit(solution)/shard_map/ppermute | solution.py:615
  276.0 8.7 %assemble.1 = bf16[8,4,64,1536]{3,2,1,0:T(8,128)(2,1)} custom-call(s32[9]{0:T(128)} %pad_add_fusion.refs_0_.at_ref, bf16[512,1536]{1,0:T(8,128)(2,1)} %slice_dynamic-update-slice_fusion.7.refs_0_, bf16[512,1536]{1,0:T(8,128)(2,1)} %collective-permute-done.42.refs_1_, bf16[512,1536]{1,0:T(8,128)(2,1)} %collective-permute-done.43.refs_2_, ...), custom_call_target="tpu_custom_call" | custom-call | tf_op jit(solution)/shard_map/assemble/pallas_call | solution.py:743
  292.8 10.7 %collective-permute-done.49 = bf16[128,2048]{1,0:T(8,128)(2,1)S(1)} collective-permute-done((bf16[128,2048]{1,0:T(8,128)(2,1)S(1)}, bf16[128,2048]{1,0:T(8,128)(2,1)S(1)}, u32[]{:S(2)}, u32[]{:S(2)}) %collective-permute-start.49) | collective-permute-done | bytes 524320 | tf_op jit(solution)/shard_map/ppermute | solution.py:615
  346.6 7.1 collective-permute-done.58
  360.5 8.3 %collective-permute-done.60 = bf16[128,2048]{1,0:T(8,128)(2,1)S(1)} collective-permute-done((bf16[128,2048]{1,0:T(8,128)(2,1)S(1)}, bf16[128,2048]{1,0:T(8,128)(2,1)S(1)}, u32[]{:S(2)}, u32[]{:S(2)}) %collective-permute-start.60) | collective-permute-done | bytes 524320 | tf_op jit(solution)/shard_map/ppermute | solution.py:615
  372.7 14.4 %weight_grads.2 = (bf16[512,1536]{1,0:T(8,128)(2,1)}, bf16[512,1536]{1,0:T(8,128)(2,1)}, bf16[2,512,1536]{2,1,0:T(8,128)(2,1)}) custom-call(s32[9]{0:T(128)} %pad_add_fusion.refs_0_.at_ref, bf16[384,2048]{1,0:T(8,128)(2,1)} %pad_maximum_fusion.2.refs_1_, bf16[256,2048]{1,0:T(8,128)(2,1)} %copy-done.55, bf16[256,2048]{1,0:T(8,128)(2,1)} %copy-done.54, ...), custom_call_target="tpu_custom_call" | custom-call | flops 6442450944 | bytes 7340032 | tf_op jit(solution)/shard_map/weight_grads/pallas_call | solution.py:892
  396.8 8.2 %row_grads.2 = bf16[768,2048]{1,0:T(8,128)(2,1)} custom-call(bf16[384,768]{1,0:T(8,128)(2,1)} %get-tuple-element.283.refs_0_, bf16[256,768]{1,0:T(8,128)(2,1)} %get-tuple-element.284.refs_1_, bf16[256,768]{1,0:T(8,128)(2,1)} %get-tuple-element.285.refs_2_, bf16[128,768]{1,0:T(8,128)(2,1)} %get-tuple-element.419.refs_3_, ...), custom_call_target="tpu_custom_call" | custom-call | flops 3221225472 | bytes 5767168 | tf_op jit(solution)/shard_map/row_grads/pallas_call | solution.py:925
  428.1 6.9 collective-permute-done.66.refs_1_
  459.0 18.2 %collective-permute-done.72 = bf16[512,1536]{1,0:T(8,128)(2,1)} collective-permute-done((bf16[512,1536]{1,0:T(8,128)(2,1)}, bf16[512,1536]{1,0:T(8,128)(2,1)}, u32[]{:S(2)}, u32[]{:S(2)}) %collective-permute-start.72) | collective-permute-done | bytes 1572896 | tf_op jit(solution)/shard_map/ppermute | solution.py:619
  504.1 30.0 %attend_back.1 = (bf16[1024,256]{1,0:T(8,128)(2,1)}, bf16[4096,256]{1,0:T(8,128)(2,1)}) custom-call(s32[8]{0:T(128)} %get-tuple-element.444.place_ref, s32[32]{0:T(128)} %select_reduce_fusion.order_ref, bf16[1024,256]{1,0:T(8,128)(2,1)} %get-tuple-element.234.q_ref, bf16[1024,256]{1,0:T(8,128)(2,1)} %stack_project.1.grad_ref, ...), custom_call_target="tpu_custom_call" | custom-call | flops 5368709120 | bytes 6291456 | tf_op jit(solution)/shard_map/attend_back/pallas_call | solution.py:575
  553.7 7.8 %collective-permute-done.84 = bf16[160,1536]{1,0:T(8,128)(2,1)S(1)} collective-permute-done((bf16[160,1536]{1,0:T(8,128)(2,1)}, bf16[160,1536]{1,0:T(8,128)(2,1)S(1)}, u32[]{:S(2)}, u32[]{:S(2)}) %collective-permute-start.84) | collective-permute-done | bytes 491552 | tf_op jit(solution)/shard_map/ppermute | solution.py:615
  562.3 11.5 %collective-permute-done.83 = bf16[160,1536]{1,0:T(8,128)(2,1)S(1)} collective-permute-done((bf16[160,1536]{1,0:T(8,128)(2,1)}, bf16[160,1536]{1,0:T(8,128)(2,1)S(1)}, u32[]{:S(2)}, u32[]{:S(2)}) %collective-permute-start.83) | collective-permute-done | bytes 491552 | tf_op jit(solution)/shard_map/ppermute | solution.py:615
  582.5 9.3 %project_back.1 = (bf16[1024,512]{1,0:T(8,128)(2,1)}, bf16[1024,2048]{1,0:T(8,128)(2,1)}, f32[8,128]{1,0:T(8,128)}) custom-call(bf16[1024,256]{1,0:T(8,128)(2,1)} %get-tuple-element.322.dq_ref, bf16[1024,256]{1,0:T(8,128)(2,1)} %add_convert_fusion.11.dkv_ref, f32[1024,512]{1,0:T(8,128)} %get-tuple-element.324.raw_ref, ...), custom_call_target="tpu_custom_call" | custom-call | flops 2147483648 | bytes 12582912 | tf_op jit(solution)/shard_map/project_back/pallas_call | solution.py:852
  592.5 39.3 %psum.7 = f32[2,128]{1,0:T(2,128)S(1)} all-reduce(f32[2,128]{1,0:T(2,128)S(1)} %slice.598), channel_id=1, replica_groups=mesh['blk'=8,'head'=4] {'blk','head'}, use_global_device_ids=true, to_apply=%region_7.8 | all-reduce | flops 256 | bytes 2048 | tf_op jit(solution)/shard_map/psum | solution.py:1271
  641.8 8.9 %weight_grads.3 = (bf16[512,512]{1,0:T(8,128)(2,1)}, bf16[512,512]{1,0:T(8,128)(2,1)}, bf16[2,512,512]{2,1,0:T(8,128)(2,1)}) custom-call(s32[9]{0:T(128)} %pad_add_fusion.refs_0_.at_ref, bf16[1024,2048]{1,0:T(8,128)(2,1)} %get-tuple-element.333.refs_1_, bf16[1024,512]{1,0:T(8,128)(2,1)} %get-tuple-element.334.refs_2_), custom_call_target="tpu_custom_call" | custom-call | flops 2147483648 | bytes 5242880 | tf_op jit(solution)/shard_map/weight_grads/pallas_call | solution.py:892
  664.9 6.9 widen.2
  689.0 8.5 %collective-permute-done.101 = bf16[224,512]{1,0:T(8,128)(2,1)S(1)} collective-permute-done((bf16[224,512]{1,0:T(8,128)(2,1)}, bf16[224,512]{1,0:T(8,128)(2,1)S(1)}, u32[]{:S(2)}, u32[]{:S(2)}) %collective-permute-start.101) | collective-permute-done | bytes 229408 | tf_op jit(solution)/shard_map/ppermute | solution.py:615
  709.8 9.7 %collective-permute-done.108 = bf16[96,512]{1,0:T(8,128)(2,1)S(1)} collective-permute-done((bf16[96,512]{1,0:T(8,128)(2,1)S(1)}, bf16[96,512]{1,0:T(8,128)(2,1)S(1)}, u32[]{:S(2)}, u32[]{:S(2)}) %collective-permute-start.108) | collective-permute-done | bytes 98336 | tf_op jit(solution)/shard_map/ppermute | solution.py:615
  (605 shorter events, 394.8 us)
Async XLA Ops:
  7.2 214.1 %all-gather.6.cloned.1.call-start = ((), (), s32[]{:S(2)}) async-start(), calls=%async_computation.3 | async-start | bytes 3932160 | tf_op jit(solution)/shard_map/all_gather | solution.py:1024
  7.9 217.9 %all-gather.4.cloned.1.call-start = ((), (), s32[]{:S(2)}) async-start(), calls=%async_computation.2 | async-start | bytes 1310720 | tf_op jit(solution)/shard_map/all_gather | solution.py:1024
  8.0 25.0 %collective-permute-start.2 = (bf16[128,2048]{1,0:T(8,128)(2,1)}, bf16[128,2048]{1,0:T(8,128)(2,1)}, u32[]{:S(2)}, u32[]{:S(2)}) collective-permute-start(bf16[128,2048]{1,0:T(8,128)(2,1)} %bitcast.67), channel_id=1, source_target_pairs={{0,4},{8,0},{16,8},{24,16},{28,24},{20,28},{12,20},{4,12},{1,5},{9... | collective-permute-start | bytes 1572872 | tf_op jit(solution)/shard_map/ppermute | solution.py:615
  20.7 664.1 %reduce-scatter.5.cloned.1.call-start = ((), (), s32[]{:S(2)}) async-start(), calls=%async_computation.5 | async-start | bytes 3932160 | tf_op jit(solution)/shard_map/reduce_scatter | solution.py:1028
  33.0 54.9 %collective-permute-start.6 = (bf16[128,2048]{1,0:T(8,128)(2,1)}, bf16[128,2048]{1,0:T(8,128)(2,1)S(1)}, u32[]{:S(2)}, u32[]{:S(2)}) collective-permute-start(bf16[128,2048]{1,0:T(8,128)(2,1)} %collective-permute-done.2.refs_2_), channel_id=1, source_target_pairs={{0,4},{8,0},{16,8},{24,16},{28,24},{20,28},{12,20},{4,12},{1,5},{9... | collective-permute-start | bytes 1572872 | tf_op jit(solution)/shard_map/ppermute | solution.py:615
  35.0 53.8 %collective-permute-start.7 = (bf16[128,2048]{1,0:T(8,128)(2,1)}, bf16[128,2048]{1,0:T(8,128)(2,1)}, u32[]{:S(2)}, u32[]{:S(2)}) collective-permute-start(bf16[128,2048]{1,0:T(8,128)(2,1)} %collective-permute-done.3.refs_3_), channel_id=1, source_target_pairs={{0,8},{8,16},{16,24},{24,28},{28,20},{20,12},{12,4},{4,0},{1,9},{9... | collective-permute-start | bytes 1572872 | tf_op jit(solution)/shard_map/ppermute | solution.py:615
  191.3 63.4 %collective-permute-start.42 = (bf16[512,1536]{1,0:T(8,128)(2,1)}, bf16[512,1536]{1,0:T(8,128)(2,1)}, u32[]{:S(2)}, u32[]{:S(2)}) collective-permute-start(bf16[512,1536]{1,0:T(8,128)(2,1)} %slice_dynamic-update-slice_fusion.7.refs_0_), channel_id=1, source_target_pairs={{0,1},{1,0},{2,3},{3,2},{4,5},{5,4},{6,7},{7,6},{8,9},{9,8},{10,11... | collective-permute-start | bytes 4718600 | tf_op jit(solution)/shard_map/ppermute | solution.py:619
  191.8 62.9 %collective-permute-start.43 = (bf16[512,1536]{1,0:T(8,128)(2,1)}, bf16[512,1536]{1,0:T(8,128)(2,1)}, u32[]{:S(2)}, u32[]{:S(2)}) collective-permute-start(bf16[512,1536]{1,0:T(8,128)(2,1)} %slice_dynamic-update-slice_fusion.7.refs_0_), channel_id=1, source_target_pairs={{0,2},{1,3},{2,0},{3,1},{4,6},{5,7},{6,4},{7,5},{8,10},{9,11},{10,... | collective-permute-start | bytes 4718600 | tf_op jit(solution)/shard_map/ppermute | solution.py:619
  197.3 28.5 %collective-permute-start.34 = (bf16[128,2048]{1,0:T(8,128)(2,1)S(1)}, bf16[128,2048]{1,0:T(8,128)(2,1)S(1)}, u32[]{:S(2)}, u32[]{:S(2)}) collective-permute-start(bf16[128,2048]{1,0:T(8,128)(2,1)S(1)} %collective-permute-done.27), channel_id=1, source_target_pairs={{0,4},{8,0},{16,8},{24,16},{28,24},{20,28},{12,20},{4,12},{1,5},{9... | collective-permute-start | bytes 1572872 | tf_op jit(solution)/shard_map/ppermute | solution.py:615
  198.6 27.3 %collective-permute-start.35 = (bf16[128,2048]{1,0:T(8,128)(2,1)}, bf16[128,2048]{1,0:T(8,128)(2,1)S(1)}, u32[]{:S(2)}, u32[]{:S(2)}) collective-permute-start(bf16[128,2048]{1,0:T(8,128)(2,1)} %collective-permute-done.28), channel_id=1, source_target_pairs={{0,8},{8,16},{16,24},{24,28},{28,20},{20,12},{12,4},{4,0},{1,9},{9... | collective-permute-start | bytes 1572872 | tf_op jit(solution)/shard_map/ppermute | solution.py:615
  426.6 50.7 %collective-permute-start.72 = (bf16[512,1536]{1,0:T(8,128)(2,1)}, bf16[512,1536]{1,0:T(8,128)(2,1)}, u32[]{:S(2)}, u32[]{:S(2)}) collective-permute-start(bf16[512,1536]{1,0:T(8,128)(2,1)} %get-tuple-element.298), channel_id=1, source_target_pairs={{0,2},{1,3},{2,0},{3,1},{4,6},{5,7},{6,4},{7,5},{8,10},{9,11},{10,... | collective-permute-start | bytes 4718600 | tf_op jit(solution)/shard_map/ppermute | solution.py:619
  428.0 259.2 %reduce-scatter.3.cloned.1.call-start = ((), (), s32[]{:S(2)}) async-start(), calls=%async_computation.4 | async-start | bytes 1310720 | tf_op jit(solution)/shard_map/reduce_scatter | solution.py:1028
  491.0 43.1 %collective-permute-start.79 = (bf16[224,1536]{1,0:T(8,128)(2,1)}, bf16[224,1536]{1,0:T(8,128)(2,1)}, u32[]{:S(2)}, u32[]{:S(2)}) collective-permute-start(bf16[224,1536]{1,0:T(8,128)(2,1)} %get-tuple-element.308), channel_id=1, source_target_pairs={{0,8},{8,16},{16,24},{24,28},{28,20},{20,12},{12,4},{4,0},{1,9},{9... | collective-permute-start | bytes 2064392 | tf_op jit(solution)/shard_map/ppermute | solution.py:615
  492.4 43.7 %collective-permute-start.80 = (bf16[224,1536]{1,0:T(8,128)(2,1)}, bf16[224,1536]{1,0:T(8,128)(2,1)}, u32[]{:S(2)}, u32[]{:S(2)}) collective-permute-start(bf16[224,1536]{1,0:T(8,128)(2,1)} %get-tuple-element.309), channel_id=1, source_target_pairs={{0,4},{8,0},{16,8},{24,16},{28,24},{20,28},{12,20},{4,12},{1,5},{9... | collective-permute-start | bytes 2064392 | tf_op jit(solution)/shard_map/ppermute | solution.py:615
  501.4 36.7 %collective-permute-start.78 = (bf16[128,2048]{1,0:T(8,128)(2,1)S(1)}, bf16[128,2048]{1,0:T(8,128)(2,1)S(1)}, u32[]{:S(2)}, u32[]{:S(2)}) collective-permute-start(bf16[128,2048]{1,0:T(8,128)(2,1)S(1)} %pad_maximum_fusion.13), channel_id=1, source_target_pairs={{0,4},{8,0},{16,8},{24,16},{28,24},{20,28},{12,20},{4,12},{1,5},{9... | collective-permute-start | bytes 1572872 | tf_op jit(solution)/shard_map/ppermute | solution.py:615
  501.5 36.6 %collective-permute-start.77 = (bf16[128,2048]{1,0:T(8,128)(2,1)S(1)}, bf16[128,2048]{1,0:T(8,128)(2,1)}, u32[]{:S(2)}, u32[]{:S(2)}) collective-permute-start(bf16[128,2048]{1,0:T(8,128)(2,1)S(1)} %pad_maximum_fusion.12), channel_id=1, source_target_pairs={{0,8},{8,16},{16,24},{24,28},{28,20},{20,12},{12,4},{4,0},{1,9},{9... | collective-permute-start | bytes 1572872 | tf_op jit(solution)/shard_map/ppermute | solution.py:615
  548.4 26.3 %collective-permute-start.82 = (bf16[128,2048]{1,0:T(8,128)(2,1)}, bf16[128,2048]{1,0:T(8,128)(2,1)S(1)}, u32[]{:S(2)}, u32[]{:S(2)}) collective-permute-start(bf16[128,2048]{1,0:T(8,128)(2,1)} %get-tuple-element.314), channel_id=1, source_target_pairs={{0,4},{8,0},{16,8},{24,16},{28,24},{20,28},{12,20},{4,12},{1,5},{9... | collective-permute-start | bytes 1572872 | tf_op jit(solution)/shard_map/ppermute | solution.py:615
  549.1 25.7 %collective-permute-start.81 = (bf16[128,2048]{1,0:T(8,128)(2,1)}, bf16[128,2048]{1,0:T(8,128)(2,1)S(1)}, u32[]{:S(2)}, u32[]{:S(2)}) collective-permute-start(bf16[128,2048]{1,0:T(8,128)(2,1)} %get-tuple-element.313), channel_id=1, source_target_pairs={{0,8},{8,16},{16,24},{24,28},{28,20},{20,12},{12,4},{4,0},{1,9},{9... | collective-permute-start | bytes 1572872 | tf_op jit(solution)/shard_map/ppermute | solution.py:615
  578.4 55.7 %collective-permute-start.87 = (bf16[128,2048]{1,0:T(8,128)(2,1)}, bf16[128,2048]{1,0:T(8,128)(2,1)}, u32[]{:S(2)}, u32[]{:S(2)}) collective-permute-start(bf16[128,2048]{1,0:T(8,128)(2,1)} %get-tuple-element.318), channel_id=1, source_target_pairs={{0,8},{8,16},{16,24},{24,28},{28,20},{20,12},{12,4},{4,0},{1,9},{9... | collective-permute-start | bytes 1572872 | tf_op jit(solution)/shard_map/ppermute | solution.py:615
  579.8 54.3 %collective-permute-start.88 = (bf16[128,2048]{1,0:T(8,128)(2,1)}, bf16[128,2048]{1,0:T(8,128)(2,1)}, u32[]{:S(2)}, u32[]{:S(2)}) collective-permute-start(bf16[128,2048]{1,0:T(8,128)(2,1)} %get-tuple-element.319), channel_id=1, source_target_pairs={{0,4},{8,0},{16,8},{24,16},{28,24},{20,28},{12,20},{4,12},{1,5},{9... | collective-permute-start | bytes 1572872 | tf_op jit(solution)/shard_map/ppermute | solution.py:615
  580.4 52.0 %collective-permute-start.89 = (bf16[96,1536]{1,0:T(8,128)(2,1)}, bf16[96,1536]{1,0:T(8,128)(2,1)S(1)}, u32[]{:S(2)}, u32[]{:S(2)}) collective-permute-start(bf16[96,1536]{1,0:T(8,128)(2,1)} %slice.663), channel_id=1, source_target_pairs={{0,8},{8,16},{16,24},{24,28},{28,20},{20,12},{12,4},{4,0},{1,9},{9... | collective-permute-start | bytes 884744 | tf_op jit(solution)/shard_map/ppermute | solution.py:615
  581.8 50.6 %collective-permute-start.90 = (bf16[96,1536]{1,0:T(8,128)(2,1)}, bf16[96,1536]{1,0:T(8,128)(2,1)}, u32[]{:S(2)}, u32[]{:S(2)}) collective-permute-start(bf16[96,1536]{1,0:T(8,128)(2,1)} %slice.664), channel_id=1, source_target_pairs={{0,4},{8,0},{16,8},{24,16},{28,24},{20,28},{12,20},{4,12},{1,5},{9... | collective-permute-start | bytes 884744 | tf_op jit(solution)/shard_map/ppermute | solution.py:615
  702.6 30.4 %collective-permute-start.104 = (bf16[128,2048]{1,0:T(8,128)(2,1)}, bf16[128,2048]{1,0:T(8,128)(2,1)S(1)}, u32[]{:S(2)}, u32[]{:S(2)}) collective-permute-start(bf16[128,2048]{1,0:T(8,128)(2,1)} %get-tuple-element.351), channel_id=1, source_target_pairs={{0,4},{8,0},{16,8},{24,16},{28,24},{20,28},{12,20},{4,12},{1,5},{9... | collective-permute-start | bytes 1572872 | tf_op jit(solution)/shard_map/ppermute | solution.py:615
  703.8 29.1 %collective-permute-start.103 = (bf16[128,2048]{1,0:T(8,128)(2,1)}, bf16[128,2048]{1,0:T(8,128)(2,1)S(1)}, u32[]{:S(2)}, u32[]{:S(2)}) collective-permute-start(bf16[128,2048]{1,0:T(8,128)(2,1)} %get-tuple-element.350), channel_id=1, source_target_pairs={{0,8},{8,16},{16,24},{24,28},{28,20},{20,12},{12,4},{4,0},{1,9},{9... | collective-permute-start | bytes 1572872 | tf_op jit(solution)/shard_map/ppermute | solution.py:615
  (176 other events, 2071.3 us)
Sparse Core Ops, SparseCore 0:
  9.6 31.2 all-gather.5
  42.4 16.8 all-gather.3
  428.2 50.8 reduce-scatter.4
  592.6 23.7 reduce-scatter.2

commit v5 on v4

--- a/solution.py
+++ b/solution.py
@@ -421,21 +421,27 @@
     return jnp.concatenate([rows[:half], rows[half:]], axis=1)
 
 
-def attend_kernel(place_ref, order_ref, q_ref, kv_ref, out_ref, lse_ref, keys, values):
+CHEAP = pl.CostEstimate(flops=1, bytes_accessed=1, transcendentals=0)
+
+
+def sort_strips(order_ref, kv_refs, keys, values):
+    per = kv_refs[0].shape[0] // STRIP
+    for j, ref in enumerate(kv_refs):
+        for i in range(per):
+            target = pl.multiple_of(order_ref[j * per + i] * STRIP, STRIP)
+            here = slice(i * STRIP, (i + 1) * STRIP)
+            keys[pl.ds(target, STRIP), :] = ref[here, :HEAD_SIZE]
+            values[pl.ds(target, STRIP), :HEAD_SIZE] = ref[here, HEAD_SIZE:]
+
+
+def attend_kernel(place_ref, order_ref, q_ref, *refs):
+    kv_refs, (out_ref, lse_ref, keys, values) = refs[:4], refs[4:]
     step = pl.program_id(0)
 
     @pl.when(step == 0)
     def _():
         values[:, HEAD_SIZE:] = jnp.ones((values.shape[0], HEAD_SIZE), jnp.bfloat16)
-
-        def sort(index, carry):
-            source = pl.multiple_of(order_ref[index] * STRIP, STRIP)
-            target = pl.multiple_of(index * STRIP, STRIP)
-            keys[pl.ds(target, STRIP), :] = kv_ref[pl.ds(source, STRIP), :HEAD_SIZE]
-            values[pl.ds(target, STRIP), :HEAD_SIZE] = kv_ref[pl.ds(source, STRIP), HEAD_SIZE:]
-            return carry
-
-        lax.fori_loop(0, kv_ref.shape[0] // STRIP, sort, 0)
+        sort_strips(order_ref, kv_refs, keys, values)
 
     place = place_ref[step]
     queries = two_heads(q_ref[...])
@@ -468,56 +474,48 @@
 def attend(place, order, queries, kv):
     rows, width = queries.shape
     steps = rows // STRIP
-    whole = pl.BlockSpec(kv.shape, lambda i, *_: (0, 0))
+    total = sum(part.shape[0] for part in kv)
     strip = pl.BlockSpec((STRIP, width), lambda i, *_: (i, 0))
-    flops = 4 * rows * 2 * kv.shape[0] * HEAD_SIZE // 2
     return pl.pallas_call(
         attend_kernel,
         grid_spec=pltpu.PrefetchScalarGridSpec(
             num_scalar_prefetch=2,
             grid=(steps,),
-            in_specs=[strip, whole],
+            in_specs=[strip] + [pl.BlockSpec(part.shape, lambda i, *_: (0, 0)) for part in kv],
             out_specs=[strip, pl.BlockSpec((1, 8, 2 * STRIP), lambda i, *_: (i, 0, 0))],
             scratch_shapes=[
-                pltpu.VMEM((kv.shape[0], HEAD_SIZE), jnp.bfloat16),
-                pltpu.VMEM((kv.shape[0], 2 * HEAD_SIZE), jnp.bfloat16),
+                pltpu.VMEM((total, HEAD_SIZE), jnp.bfloat16),
+                pltpu.VMEM((total, 2 * HEAD_SIZE), jnp.bfloat16),
             ],
         ),
         out_shape=[
             jax.ShapeDtypeStruct((rows, width), jnp.bfloat16),
             jax.ShapeDtypeStruct((steps, 8, 2 * STRIP), jnp.float32),
         ],
-        cost_estimate=pl.CostEstimate(
-            flops=flops, bytes_accessed=kv.size * 2 + queries.size * 4, transcendentals=rows * kv.shape[0]
-        ),
+        cost_estimate=CHEAP,
         name="attend",
-    )(place, order, queries, kv)
-
-
-def attend_back_kernel(
-    place_ref, order_ref, q_ref, grad_ref, out_ref, lse_ref, kv_ref, dq_ref, dkv_ref,
-    keys, values, key_sums, value_sums,
-):
+    )(place, order, queries, *kv)
+
+
+def attend_back_kernel(place_ref, order_ref, q_ref, out_ref, lse_ref, *refs, groups):
+    grad_refs, kv_refs = refs[:groups], refs[groups : groups + 4]
+    dq_ref, own_ref, far_ref, sent_ref = refs[groups + 4 : groups + 8]
+    keys, values, key_sums, value_sums, grads_all = refs[groups + 8 :]
     step = pl.program_id(0)
-    strips = kv_ref.shape[0] // STRIP
 
     @pl.when(step == 0)
     def _():
         key_sums[...] = jnp.zeros_like(key_sums)
         value_sums[...] = jnp.zeros_like(value_sums)
-
-        def sort(index, carry):
-            source = pl.multiple_of(order_ref[index] * STRIP, STRIP)
-            target = pl.multiple_of(index * STRIP, STRIP)
-            keys[pl.ds(target, STRIP), :] = kv_ref[pl.ds(source, STRIP), :HEAD_SIZE]
-            values[pl.ds(target, STRIP), :] = kv_ref[pl.ds(source, STRIP), HEAD_SIZE:]
-            return carry
-
-        lax.fori_loop(0, strips, sort, 0)
+        sort_strips(order_ref, kv_refs, keys, values)
+        first = 0
+        for ref in grad_refs:
+            grads_all[first : first + ref.shape[0], :] = ref[...]
+            first += ref.shape[0]
 
     place = place_ref[step]
     queries = two_heads(q_ref[...])
-    grads = two_heads(grad_ref[...])
+    grads = two_heads(grads_all[pl.ds(pl.multiple_of(step * STRIP, STRIP), STRIP), :])
     product = grads.astype(jnp.float32) * two_heads(out_ref[...]).astype(jnp.float32)
     delta = jnp.sum(jnp.transpose(product), axis=0, keepdims=True)
     lse = lse_ref[0, :1]
@@ -552,53 +550,52 @@
 
     @pl.when(step == pl.num_programs(0) - 1)
     def _():
-        def spread(index, carry):
-            target = pl.multiple_of(order_ref[index] * STRIP, STRIP)
-            source = pl.multiple_of(index * STRIP, STRIP)
-            dkv_ref[pl.ds(target, STRIP), :HEAD_SIZE] = (
-                key_sums[pl.ds(source, STRIP), :] * (1.0 / LOG2E)
-            ).astype(jnp.bfloat16)
-            dkv_ref[pl.ds(target, STRIP), HEAD_SIZE:] = value_sums[
-                pl.ds(source, STRIP), :
-            ].astype(jnp.bfloat16)
-            return carry
-
-        lax.fori_loop(0, strips, spread, 0)
+        per = own_ref.shape[0] // STRIP
+        for j in range(4):
+            target = (own_ref, far_ref, sent_ref, sent_ref)[j]
+            base = per if j == 3 else 0
+            for i in range(per):
+                source = pl.multiple_of(order_ref[j * per + i] * STRIP, STRIP)
+                here = slice((base + i) * STRIP, (base + i + 1) * STRIP)
+                target[here, :HEAD_SIZE] = (
+                    key_sums[pl.ds(source, STRIP), :] * (1.0 / LOG2E)
+                ).astype(jnp.bfloat16)
+                target[here, HEAD_SIZE:] = value_sums[pl.ds(source, STRIP), :].astype(
+                    jnp.bfloat16
+                )
 
 
 def attend_back(place, order, queries, grads, attended, lse, kv):
     rows, width = queries.shape
     steps = rows // STRIP
-    total = kv.shape[0]
-    whole = pl.BlockSpec(kv.shape, lambda i, *_: (0, 0))
+    total = sum(part.shape[0] for part in kv)
     strip = pl.BlockSpec((STRIP, width), lambda i, *_: (i, 0))
+
+    def whole(shape):
+        return pl.BlockSpec(shape, lambda i, *_: (0, 0))
+
+    outs = [kv[0].shape, kv[0].shape, (2 * kv[0].shape[0], kv[0].shape[1])]
     return pl.pallas_call(
-        attend_back_kernel,
+        lambda *refs: attend_back_kernel(*refs, groups=len(grads)),
         grid_spec=pltpu.PrefetchScalarGridSpec(
             num_scalar_prefetch=2,
             grid=(steps,),
-            in_specs=[
-                strip, strip, strip, pl.BlockSpec((1, 8, 2 * STRIP), lambda i, *_: (i, 0, 0)), whole,
-            ],
-            out_specs=[strip, whole],
+            in_specs=[strip, strip, pl.BlockSpec((1, 8, 2 * STRIP), lambda i, *_: (i, 0, 0))]
+            + [whole(part.shape) for part in (*grads, *kv)],
+            out_specs=[strip] + [whole(shape) for shape in outs],
             scratch_shapes=[
                 pltpu.VMEM((total, HEAD_SIZE), jnp.bfloat16),
                 pltpu.VMEM((total, HEAD_SIZE), jnp.bfloat16),
                 pltpu.VMEM((total, HEAD_SIZE), jnp.float32),
                 pltpu.VMEM((total, HEAD_SIZE), jnp.float32),
+                pltpu.VMEM((rows, width), jnp.bfloat16),
             ],
         ),
-        out_shape=[
-            jax.ShapeDtypeStruct((rows, width), jnp.bfloat16),
-            jax.ShapeDtypeStruct(kv.shape, jnp.bfloat16),
-        ],
-        cost_estimate=pl.CostEstimate(
-            flops=10 * rows * 2 * total * HEAD_SIZE // 2,
-            bytes_accessed=kv.size * 4 + queries.size * 8,
-            transcendentals=rows * total,
-        ),
+        out_shape=[jax.ShapeDtypeStruct((rows, width), jnp.bfloat16)]
+        + [jax.ShapeDtypeStruct(shape, jnp.bfloat16) for shape in outs],
+        cost_estimate=CHEAP,
         name="attend_back",
-    )(place, order, queries, grads, attended, lse, kv)
+    )(place, order, queries, attended, lse, *grads, *kv)
 
 
 def matmul(left, right, dims=(((1,), (0,)), ((), ()))):
@@ -617,6 +614,10 @@
 
 def cross(value, by):
     return lax.ppermute(value, "head", [(i, i ^ by) for i in range(4)])
+
+
+def mirror(value, by):
+    return lax.ppermute(value, "blk", [(i, i ^ by) for i in range(len(RING))])
 
 
 def add(left, right):
@@ -687,11 +688,12 @@
             right, left = right[rows:], left[:-rows]
         self.state = right, left
 
+    def pieces(self):
+        right, left = self.state
+        return [self.own, *self.from_right, right, left, *reversed(self.from_left)]
+
     def result(self):
-        right, left = self.state
-        return jnp.concatenate(
-            [self.own, *self.from_right, right, left, *reversed(self.from_left)], axis=0
-        )
+        return jnp.concatenate(self.pieces(), axis=0)
 
 
 def hold(rings, *extra):
@@ -707,28 +709,42 @@
     return add(own, moved[:half]), add(far, moved[half:])
 
 
-def slice_kernel(at_ref, *refs):
-    first = 0
-    for ref in refs[:-1]:
-        refs[-1][:, first : first + ref.shape[1]] = ref[...]
-        first += ref.shape[1]
-
-
-def slice_pieces(at, *weights):
-    count = at.shape[0]
+def columns(at, width):
+    return pl.ds(pl.multiple_of(at * width, width), width)
+
+
+def slice_kernel(at_ref, *refs, pad):
+    weights, out_ref = refs[:-1], refs[-1]
+    if pad:
+        weights, pad_ref = weights[:-1], weights[-1]
     rows = weights[0].shape[0]
-    widths = [w.shape[1] // count for w in weights]
+    each = rows + pad
+    for s in range(8):
+        first = 0
+        for ref in weights:
+            width = ref.shape[1] // 8
+            out_ref[s * each : s * each + rows, first : first + width] = ref[
+                :, columns(at_ref[s], width)
+            ]
+            first += width
+        if pad:
+            out_ref[s * each + rows : (s + 1) * each, :] = pad_ref[...]
+
+
+def slice_pieces(at, *weights, pad=None):
+    rows = weights[0].shape[0]
+    cols = sum(w.shape[1] for w in weights) // 8
+    extra = 0 if pad is None else pad.shape[0]
+    operands = weights if pad is None else (*weights, pad)
+    vmem = pl.BlockSpec(memory_space=pltpu.VMEM)
     return pl.pallas_call(
-        slice_kernel,
-        grid_spec=pltpu.PrefetchScalarGridSpec(
-            num_scalar_prefetch=1,
-            grid=(count,),
-            in_specs=[pl.BlockSpec((rows, w), lambda i, at: (0, at[i])) for w in widths],
-            out_specs=pl.BlockSpec((rows, sum(widths)), lambda i, at: (i, 0)),
-        ),
-        out_shape=jax.ShapeDtypeStruct((count * rows, sum(widths)), jnp.bfloat16),
+        lambda *refs: slice_kernel(*refs, pad=extra),
+        in_specs=[pl.BlockSpec(memory_space=pltpu.SMEM)] + [vmem] * len(operands),
+        out_specs=vmem,
+        out_shape=jax.ShapeDtypeStruct((8 * (rows + extra), cols), jnp.bfloat16),
+        cost_estimate=CHEAP,
         name="slice_pieces",
-    )(at, *weights)
+    )(at, *operands)
 
 
 def assemble_kernel(at_ref, *refs):
@@ -749,6 +765,7 @@
             out_specs=pl.BlockSpec((1, 4, rows, cols), lambda i, at: (at[i], 0, 0, 0)),
         ),
         out_shape=jax.ShapeDtypeStruct((count, 4, rows, cols), jnp.bfloat16),
+        cost_estimate=CHEAP,
         name="assemble",
     )(at, *pieces).reshape(4 * total, cols)
 
@@ -760,20 +777,28 @@
 def project_kernel(at_ref, *refs, strips):
     token_refs, refs = refs[:strips], refs[strips:]
     pieces, refs = refs[:4], refs[4:]
-    gain_ref, head_gain_ref, cos_ref, sin_ref = refs[:4]
-    normed_ref, raw_ref, q_ref, kv_ref, matrix_ref = refs[4:]
-    rows = pieces[0].shape[0] // 8
+    cos_ref, sin_ref, normed_ref, raw_ref, q_ref, kv_ref, matrix_ref, gains_ref = refs
+    each = pieces[0].shape[0] // 8
+    rows = matrix_ref.shape[0] // 32
     own = at_ref[8]
+    gains = jnp.zeros(gains_ref.shape, jnp.float32)
     for s in range(8):
         for j in range(4):
             first = pl.multiple_of((at_ref[s] * 4 + (own ^ j)) * rows, rows)
-            matrix_ref[pl.ds(first, rows), :] = pieces[j][s * rows : (s + 1) * rows, :]
+            matrix_ref[pl.ds(first, rows), :] = pieces[j][s * each : s * each + rows, :]
+            gains += pieces[j][s * each + rows : (s + 1) * each, :].astype(jnp.float32)
+    gains_ref[...] = gains
+    width = gains.shape[1]
     first = 0
     for ref in token_refs:
         block = ref[...].astype(jnp.float32)
+        block = block * inverse_rms(block)
         here = slice(first, first + ref.shape[0])
-        normed_ref[here, :] = (block * inverse_rms(block) * gain_ref[...]).astype(jnp.bfloat16)
+        for i in range(block.shape[1] // width):
+            cols = slice(i * width, (i + 1) * width)
+            normed_ref[here, cols] = (block[:, cols] * gains[i : i + 1]).astype(jnp.bfloat16)
         first += ref.shape[0]
+    query_gain, key_gain = gains[8:9, :HEAD_SIZE], gains[8:9, HEAD_SIZE : 2 * HEAD_SIZE]
     query_cols = q_ref.shape[1]
     step = 256
     for first in range(0, q_ref.shape[0], step):
@@ -784,36 +809,35 @@
         for col in range(0, query_cols + HEAD_SIZE, HEAD_SIZE):
             part = raw[:, col : col + HEAD_SIZE]
             if col < query_cols:
-                part = spun(part * inverse_rms(part) * head_gain_ref[:1], cosine, sine)
+                part = spun(part * inverse_rms(part) * query_gain, cosine, sine)
                 part = part * (LOG2E / math.sqrt(HEAD_SIZE))
                 q_ref[here, col : col + HEAD_SIZE] = part.astype(jnp.bfloat16)
             else:
-                part = spun(part * inverse_rms(part) * head_gain_ref[1:2], cosine, sine)
+                part = spun(part * inverse_rms(part) * key_gain, cosine, sine)
                 kv_ref[here, :HEAD_SIZE] = part.astype(jnp.bfloat16)
         kv_ref[here, HEAD_SIZE:] = raw[:, query_cols + HEAD_SIZE :].astype(jnp.bfloat16)
 
 
-def project(at, strips, pieces, gain, head_gains, cosine, sine, query_cols):
+def project(at, strips, pieces, cosine, sine, query_cols, pad):
     rows = sum(strip.shape[0] for strip in strips)
     width = strips[0].shape[1]
     cols = pieces[0].shape[1]
     vmem = pl.BlockSpec(memory_space=pltpu.VMEM)
-    operands = (*strips, *pieces, gain, head_gains, cosine, sine)
-    narrow = jnp.bfloat16
+    operands = (*strips, *pieces, cosine, sine)
+    narrow, wide = jnp.bfloat16, jnp.float32
     return pl.pallas_call(
         lambda *refs: project_kernel(*refs, strips=len(strips)),
         in_specs=[pl.BlockSpec(memory_space=pltpu.SMEM)] + [vmem] * len(operands),
-        out_specs=[vmem] * 5,
+        out_specs=[vmem] * 6,
         out_shape=[
             jax.ShapeDtypeStruct((rows, width), narrow),
-            jax.ShapeDtypeStruct((rows, cols), jnp.float32),
+            jax.ShapeDtypeStruct((rows, cols), wide),
             jax.ShapeDtypeStruct((rows, query_cols), narrow),
             jax.ShapeDtypeStruct((rows, 2 * HEAD_SIZE), narrow),
             jax.ShapeDtypeStruct((width, cols), narrow),
+            jax.ShapeDtypeStruct((pad, cols), wide),
         ],
-        cost_estimate=pl.CostEstimate(
-            flops=2 * rows * width * cols, bytes_accessed=16 << 20, transcendentals=0
-        ),
+        cost_estimate=CHEAP,
         name="project",
     )(at, *operands)
 
@@ -858,9 +882,7 @@
             jax.ShapeDtypeStruct((rows, matrix.shape[0]), jnp.bfloat16),
             jax.ShapeDtypeStruct((8, HEAD_SIZE), jnp.float32),
         ],
-        cost_estimate=pl.CostEstimate(
-            flops=2 * rows * matrix.size, bytes_accessed=12 << 20, transcendentals=0
-        ),
+        cost_estimate=CHEAP,
         name="project_back",
     )(query_grads, kv_grads, raw, head_gains, cosine, sine, matrix)
 
@@ -905,11 +927,7 @@
         out_shape=[
             shape, shape, jax.ShapeDtypeStruct((2, count * rows, cols), jnp.bfloat16),
         ],
-        cost_estimate=pl.CostEstimate(
-            flops=2 * total * lefts[0].shape[1] * cols,
-            bytes_accessed=2 * total * (lefts[0].shape[1] + cols),
-            transcendentals=0,
-        ),
+        cost_estimate=CHEAP,
         name="weight_grads",
     )(at, *lefts, *rights)
     return own, far, sent.reshape(2 * count * rows, cols)
@@ -929,81 +947,45 @@
         + [pl.BlockSpec(right.shape, lambda i: (0, 0)) for right in rights],
         out_specs=pl.BlockSpec((block, cols), lambda i: (i, 0)),
         out_shape=jax.ShapeDtypeStruct((out_rows, cols), jnp.bfloat16),
-        cost_estimate=pl.CostEstimate(
-            flops=2 * total * out_rows * cols,
-            bytes_accessed=2 * total * (out_rows + cols),
-            transcendentals=0,
-        ),
+        cost_estimate=CHEAP,
         name="row_grads",
     )(*lefts, *rights)
 
 
-def stack_project_kernel(*refs):
-    matrix_ref, out_ref = refs[-2:]
-    first = 0
-    for ref in refs[:-2]:
-        out_ref[first : first + ref.shape[0], :] = lax.dot_general(
-            ref[...], matrix_ref[...], ALONG, preferred_element_type=jnp.float32
-        ).astype(jnp.bfloat16)
-        first += ref.shape[0]
-
-
-def stack_project(groups, matrix):
-    rows = sum(group.shape[0] for group in groups)
-    vmem = pl.BlockSpec(memory_space=pltpu.VMEM)
-    return pl.pallas_call(
-        stack_project_kernel,
-        in_specs=[vmem] * (len(groups) + 1),
-        out_specs=vmem,
-        out_shape=jax.ShapeDtypeStruct((rows, matrix.shape[0]), jnp.bfloat16),
-        cost_estimate=pl.CostEstimate(
-            flops=2 * rows * matrix.size, bytes_accessed=2 * rows * matrix.shape[1], transcendentals=0
-        ),
-        name="stack_project",
-    )(*groups, matrix)
-
-
 def lane_sums(block):
     return sum(block[:, i : i + 128] for i in range(0, block.shape[1], 128))
 
 
-def widen_kernel(at_ref, piece_ref, *refs, count):
+def widen_kernel(at_ref, *refs, pieces, count):
+    piece_refs, refs = refs[:pieces], refs[pieces:]
     weights, grads, sums_ref = refs[:count], refs[count : 2 * count], refs[2 * count]
     rows = weights[0].shape[0]
-
-    @pl.when(pl.program_id(0) == 0)
-    def _():
-        sums_ref[...] = jnp.zeros_like(sums_ref)
-
-    first = 0
-    for weight, grad in zip(weights, grads):
-        cols = weight.shape[1]
-        block = piece_ref[:rows, first : first + cols].astype(jnp.float32)
-        grad[...] = block
-        sums_ref[...] += lane_sums(block * weight[...].astype(jnp.float32))
-        first += cols
+    sums_ref[...] = jnp.zeros_like(sums_ref)
+    spots = [0, 1, 2, 3, 4, 4, 5, 6, 7]
+    tops = [0] * 5 + [rows // 2] + [0] * 3
+    for ref, s, top in zip(piece_refs, spots, tops):
+        here = slice(top, top + ref.shape[0])
+        first = 0
+        for weight, grad in zip(weights, grads):
+            width = weight.shape[1] // 8
+            there = columns(at_ref[s], width)
+            block = ref[:, first : first + width].astype(jnp.float32)
+            grad[here, there] = block
+            sums_ref[here, :] += lane_sums(block * weight[here, there].astype(jnp.float32))
+            first += width
 
 
 def widen(at, pieces, *weights):
-    count = at.shape[0]
-    rows = weights[0].shape[0]
-    each, cols = pieces.shape[0] // count, pieces.shape[1]
-    specs = [
-        pl.BlockSpec((rows, w.shape[1] // count), lambda i, at: (0, at[i])) for w in weights
-    ]
-    shapes = [w.shape for w in weights] + [(rows, 128)]
-    out_specs = specs + [pl.BlockSpec((rows, 128), lambda i, at: (0, 0))]
+    vmem = pl.BlockSpec(memory_space=pltpu.VMEM)
+    shapes = [w.shape for w in weights] + [(weights[0].shape[0], 128)]
     return pl.pallas_call(
-        lambda *refs: widen_kernel(*refs, count=len(weights)),
-        grid_spec=pltpu.PrefetchScalarGridSpec(
-            num_scalar_prefetch=1,
-            grid=(count,),
-            in_specs=[pl.BlockSpec((each, cols), lambda i, at: (i, 0))] + specs,
-            out_specs=out_specs,
-        ),
+        lambda *refs: widen_kernel(*refs, pieces=len(pieces), count=len(weights)),
+        in_specs=[pl.BlockSpec(memory_space=pltpu.SMEM)] + [vmem] * (len(pieces) + len(weights)),
+        out_specs=[vmem] * len(shapes),
         out_shape=[jax.ShapeDtypeStruct(shape, jnp.float32) for shape in shapes],
+        cost_estimate=CHEAP,
         name="widen",
-    )(at, pieces, *weights)
+    )(at, *pieces, *weights)
 
 
 def grouped(strips):
@@ -1059,6 +1041,8 @@
     weight_rows = query_weight.shape[0]
     ff_local = gate_weight.shape[1] // blk_count
     query_cols = QUERY_HEADS // blk_count * HEAD_SIZE
+    attn_cols = query_cols + 2 * HEAD_SIZE
+    device_count = blk_count * head_count
     strip_count = blk_count * head_count
     halves = strip_count // stretch_order.shape[1]
     ring_place = jnp.where(blk_index % 2 == 0, blk_index // 2, 7 - blk_index // 2)
@@ -1066,7 +1050,6 @@
     spot = (ring_place + jnp.arange(blk_count, dtype=jnp.int32)) % blk_count
     at = jnp.where(spot < 4, 2 * spot, 15 - 2 * spot).astype(jnp.int32)
     at_own = jnp.concatenate([at, head_index[None].astype(jnp.int32)])
-    numbers = jnp.arange(strip_count, dtype=jnp.int32)
     ring_spot = (ring_place + jnp.asarray(STRIPS, jnp.int32)) % blk_count
     strip_blk = jnp.where(ring_spot < 4, 2 * ring_spot, 15 - 2 * ring_spot)
     strip_head = head_index ^ jnp.asarray((0, 2, 1, 3), jnp.int32)
@@ -1076,9 +1059,7 @@
         jnp.where((strip // halves)[:, None] == slots[None, :], stretch_order, 0), axis=1
     )
     strip_place = held * halves + strip % halves
-    order = jnp.sum(
-        jnp.where(strip_place[None, :] == numbers[:, None], numbers[None, :], 0), axis=1
-    ).astype(jnp.int32)
+    order = strip_place.astype(jnp.int32)
     place = strip_place[:blk_count].astype(jnp.int32)
     positions = (
         place[:, None] * local_rows + jnp.arange(local_rows, dtype=jnp.int32)[None, :]
@@ -1089,24 +1070,24 @@
     sine = jnp.concatenate([-sine, sine], axis=1)
 
     small = query_norm.shape[0]
-    gains = jnp.concatenate([attention_norm, feedforward_norm, query_norm, key_norm])
-    gains = lax.all_gather(gains, ("blk", "head"), axis=0).astype(wide)
-    gain_one = gains[:, :weight_rows].reshape(1, model_width)
-    gain_two = gains[:, weight_rows : 2 * weight_rows].reshape(1, model_width)
-    first = 2 * weight_rows
-    head_gains = jnp.concatenate(
-        [
-            gains[:, first : first + small].reshape(1, HEAD_SIZE),
-            gains[:, first + small :].reshape(1, HEAD_SIZE),
-            jnp.zeros((6, HEAD_SIZE), wide),
-        ],
-        axis=0,
-    )
+    number = blk_index * head_count + head_index
+    pad = 16
+
+    def placed(share):
+        return jnp.where(
+            jnp.arange(device_count, dtype=jnp.int32)[:, None] == number, share[None, :], 0
+        ).reshape(-1)
+
+    gains = jnp.concatenate(
+        [placed(attention_norm), placed(feedforward_norm), placed(query_norm), placed(key_norm)]
+    ).astype(narrow)
+    gains = jnp.pad(gains, (0, pad * attn_cols - gains.shape[0])).reshape(pad, attn_cols)
     down_matrix = gather_head(down_weight)
     output_rows = gather_head(output_weight)
 
     attn_swap = Swap(
-        slice_pieces(at, query_weight, key_projection, value_projection), weight_rows
+        slice_pieces(at, query_weight, key_projection, value_projection, pad=gains),
+        weight_rows + pad,
     )
     token_ring = Gather(tokens)
     ff_slices = slice_pieces(at, gate_weight, up_weight)
@@ -1126,23 +1107,25 @@
     ff_swap.go()
     own, near, far, both = hold((ff_swap, cotangent_ring), own, near, far, both)
 
-    first_normed, attn_raw, query_rows, own, attn_matrix = project(
-        at_own, token_ring.strips(), (own, near, far, both),
-        gain_one, head_gains, cosine, sine, query_cols,
-    )
+    first_normed, attn_raw, query_rows, own, attn_matrix, gains = project(
+        at_own, token_ring.strips(), (own, near, far, both), cosine, sine, query_cols, pad
+    )
+    gain_one = gains[:4].reshape(1, model_width)
+    gain_two = gains[4:8].reshape(1, model_width)
+    head_gains = jnp.pad(gains[8, : 2 * HEAD_SIZE].reshape(2, HEAD_SIZE), ((0, 6), (0, 0)))
     ff_swap.go()
     cotangent_ring.go()
     own = hold((ff_swap, cotangent_ring), own)
     near, far = cross(own, 1), cross(own, 2)
     ff_swap.go()
     cotangent_ring.go()
-    own, near, far, ff_own = hold((cotangent_ring,), own, near, far, ff_swap.result())
+    own, near, far = hold((), own, near, far)
     both = cross(far, 1)
+    kv = own, far, near, both
+    *kv, ff_own = hold((cotangent_ring,), *kv, ff_swap.result())
     ff_near, ff_far = cross(ff_own, 1), cross(ff_own, 2)
-    kv = jnp.concatenate([own, far, near, both], axis=0)
-    kv = hold((cotangent_ring,), kv)
+    cotangent_ring.go()
     attended, lse = attend(place, order, query_rows, kv)
-    cotangent_ring.go()
 
     def by_groups(rows):
         return [rows[a * local_rows : b * local_rows] for a, b in GROUPS]
@@ -1209,95 +1192,119 @@
     parts = {4: back(3)}
     resid_ring = Scatter(parts)
     parts[3], parts[5] = split(hold((), back(2)))
+    parts[2], parts[6] = split(hold((), back(1)))
     resid_ring.go()
-    parts[2], parts[6] = split(hold((resid_ring,), back(1)))
-    resid_ring.go()
-    parts[0], parts[1], parts[7] = split(hold((resid_ring,), back(0)))
+    hold((resid_ring,), parts[2], parts[6])
     resid_ring.go()
     ff_own, ff_far, ff_sent = hold(
         (resid_ring,), *weight_grads(at_own, second_groups, ff_gradient_groups, weight_rows)
     )
+    parts[0], parts[1], parts[7] = split(hold((), back(0)))
     resid_ring.go()
     ff_own, ff_far = scatter_cross(ff_own, ff_far, ff_sent)
     down_gradient = row_grads(hidden_groups, cotangent_groups)
-    down_gradient, ff_own, ff_far = hold((resid_ring,), down_gradient, ff_own, ff_far)
+    ff_own, ff_far, down_gradient = hold((resid_ring,), ff_own, ff_far, down_gradient)
     down_gradient = scatter_head(down_gradient)
     ff_far = cross(ff_far, 2)
+    resid_ring.go()
+    out_parts = [matmul(rows, down_matrix).astype(narrow) for rows in hidden_groups]
+    out_parts = hold((resid_ring,), *out_parts)
+    out_ring = Scatter(by_strips(out_parts))
     scaled = gain_two * resid_ring.total()
     resid_gradient = out_cotangent.astype(wide) + rho_two * (
         scaled - unit_two * jnp.mean(unit_two * scaled, axis=-1, keepdims=True)
     )
 
     grad_ring = Gather(resid_gradient.astype(narrow))
-    grad_ring.go()
-    out_parts = [matmul(rows, down_matrix).astype(narrow) for rows in hidden_groups]
-    out_parts = hold((grad_ring,), *out_parts)
-    out_ring = Scatter(by_strips(out_parts))
+    grad_groups, attended_grads = [], []
+
+    def attention_back(index):
+        rows = grad_ring.group(index)
+        grads = matmul(rows, output_rows, ALONG).astype(narrow)
+        if index < 3:
+            rows, grads = hold((grad_ring,), rows, grads)
+        grad_groups.append(rows)
+        attended_grads.append(grads)
+
     grad_ring.go()
     hold((grad_ring,))
-    grad_ring.go()
-    ff_far = hold((grad_ring,), ff_far)
+    for index in range(3):
+        grad_ring.go()
+        attention_back(index)
     ff_swap = Swap(add(ff_own, ff_far), weight_rows)
-    grad_ring.go()
     hold((grad_ring, ff_swap, out_ring))
-    grad_strips = grad_ring.strips()
-    attended_gradient = stack_project(grad_strips, output_rows)
-    out_ring.go()
-    hold((out_ring,), attended_gradient)
-    query_grads, kv_grads = attend_back(
-        place, order, query_rows, attended_gradient, attended, lse, kv
-    )
-    ff_swap.go()
-    out_ring.go()
-    query_grads, kv_grads = hold((out_ring, ff_swap), query_grads, kv_grads)
-    kv_own, kv_far = scatter_cross(
-        kv_grads[:group_rows], kv_grads[group_rows : 2 * group_rows], kv_grads[2 * group_rows :]
-    )
-    kv_far = cross(kv_far, 2)
     out_ring.go()
     ff_swap.go()
-    output_weight_gradient = row_grads([attended], [jnp.concatenate(grad_strips, axis=0)])
-    output_weight_gradient, kv_grads = hold(
-        (out_ring, ff_swap), output_weight_gradient, add(kv_own, kv_far)
+    attention_back(3)
+    query_grads, kv_own, kv_far, kv_sent = attend_back(
+        place, order, query_rows, attended_grads, attended, lse, kv
+    )
+    query_grads, kv_own, kv_far, kv_sent = hold(
+        (out_ring, ff_swap), query_grads, kv_own, kv_far, kv_sent
+    )
+    out_ring.go()
+    ff_swap.go()
+    kv_own, kv_far = scatter_cross(kv_own, kv_far, kv_sent)
+    kv_own, kv_far = hold((), kv_own, kv_far)
+    kv_grads = add(kv_own, cross(kv_far, 2))
+    output_weight_gradient = row_grads([attended], [jnp.concatenate(grad_groups, axis=0)])
+    kv_grads, output_weight_gradient = hold(
+        (out_ring, ff_swap), kv_grads, output_weight_gradient
     )
     output_weight_gradient = scatter_head(output_weight_gradient).astype(wide)
+    out_ring.go()
+    ff_swap.go()
     attn_gradient, first_parts, gain_sums = project_back(
         query_grads, kv_grads, attn_raw, head_gains, cosine, sine, attn_matrix
     )
-    ff_swap.go()
-    out_ring.go()
-    attn_gradient, first_parts = hold((out_ring, ff_swap), attn_gradient, first_parts)
-    layer_out = (resid + out_ring.total()).astype(narrow)
-    gain_sums = lax.psum(gain_sums[:2], ("blk", "head"))
+    attn_gradient, first_parts, gain_sums = hold(
+        (out_ring, ff_swap), attn_gradient, first_parts, gain_sums
+    )
     token_ring = Scatter(by_strips(by_groups(first_parts)))
     token_ring.go()
+    attn_own, attn_far, attn_sent = weight_grads(
+        at_own, [first_normed], [attn_gradient], weight_rows
+    )
+    gain_sums = gain_sums + cross(gain_sums, 1)
+    attn_own, attn_far, attn_sent, gain_sums = hold(
+        (token_ring,), attn_own, attn_far, attn_sent, gain_sums
+    )
+    token_ring.go()
     ff_swap.go()
-    attn_own, attn_far, attn_sent = hold(
-        (token_ring, ff_swap),
-        *weight_grads(at_own, [first_normed], [attn_gradient], weight_rows),
-    )
     attn_own, attn_far = scatter_cross(attn_own, attn_far, attn_sent)
+    gain_sums = gain_sums + cross(gain_sums, 2)
+    attn_own, attn_far, gain_sums = hold(
+        (token_ring, ff_swap), attn_own, attn_far, gain_sums
+    )
     attn_far = cross(attn_far, 2)
     token_ring.go()
+    out_ring.go()
+    gain_sums = gain_sums + mirror(gain_sums, 1)
     gate_weight_gradient, up_weight_gradient, norm_sums = widen(
-        at, ff_swap.result(), gate_weight, up_weight
+        at, ff_swap.pieces(), gate_weight, up_weight
+    )
+    attn_swap = Swap(add(attn_own, attn_far), weight_rows)
+    gate_weight_gradient, up_weight_gradient, norm_sums, gain_sums = hold(
+        (token_ring, attn_swap, out_ring),
+        gate_weight_gradient, up_weight_gradient, norm_sums, gain_sums,
     )
     feedforward_norm_gradient = jnp.sum(norm_sums, axis=1) / feedforward_norm.astype(wide)
-    attn_swap = Swap(add(attn_own, attn_far), weight_rows)
-    hold((token_ring, attn_swap), gate_weight_gradient)
     attn_swap.go()
     token_ring.go()
-    hold((token_ring, attn_swap))
+    gain_sums = gain_sums + mirror(gain_sums, 2)
+    gain_sums = hold((token_ring, attn_swap), gain_sums)
     attn_swap.go()
-    token_ring.go()
+    gain_sums = gain_sums + mirror(gain_sums, 4)
+    layer_out = (resid + out_ring.total()).astype(narrow)
+    layer_out, gain_sums = hold((attn_swap,), layer_out, gain_sums)
     attn_swap.go()
+    hold((attn_swap,))
     attn_swap.go()
     query_weight_gradient, key_weight_gradient, value_weight_gradient, norm_sums = widen(
-        at, attn_swap.result(), query_weight, key_projection, value_projection
+        at, attn_swap.pieces(), query_weight, key_projection, value_projection
     )
     attention_norm_gradient = jnp.sum(norm_sums, axis=1) / attention_norm.astype(wide)
-    own_first = (blk_index * head_count + head_index) * small
-    gain_sums = lax.dynamic_slice_in_dim(gain_sums, own_first, small, 1)
+    gain_sums = lax.dynamic_slice_in_dim(gain_sums, number * small, small, 1)
     rho_one = inverse_rms(tokens_wide)
     unit_one = tokens_wide * rho_one
     scaled = gain_one * token_ring.total()

time: 754 us -> 664 us (0.88)
  blocking collectives: 85.3 us -> 0 us
  Pallas kernels: 146 us -> 119 us
  starting transfers between devices: 108 us -> 133 us
  matrix products: 39.4 us -> 49.1 us
    unnamed x1 -> x0, blocking collectives: 46 us -> none
    psum x1 -> x0, blocking collectives: 39.3 us -> none  [per_device(): gain_sums = lax.psum(gain_sums[:2], ('blk', 'head'))]
    pallas_call x6 -> x5, Pallas kernels: 60.1 us -> 36.4 us  [the longest x1 25.6 us: attend_back(): pl.pallas_call(lambda *refs: attend_back_kernel(*refs, groups=len(grads))...]
    ppermute x15 -> x17, starting transfers between devices: 4.69 us -> 27.2 us  [cross(): return lax.ppermute(value, 'head', [(i, i ^ by) for i in range(4)])]
    slice x4 -> x15, local copies, waits for them, and re-layouts: 2.48 us -> 17.1 us  [the longest x6 7.55 us: go(): self.from_right.append(left[-rows:])]
    ppermute x15 -> x17, waiting for transfers between devices: 24.5 us -> 11.9 us  [cross(): return lax.ppermute(value, 'head', [(i, i ^ by) for i in range(4)])]
    ppermute x96, waiting for transfers between devices: 190 us -> 203 us  [hop(): lax.ppermute(value, 'blk', [(RING[i], RING[(i + by) % count]) for i in ra...]
    unnamed x218 -> x211, local copies, waits for them, and re-layouts: 32.4 us -> 20.1 us
  transfers between devices with their start and end apart: 115 -> 120, of which waited for: 47 -> 53; matrix products, arithmetic and copies ran while one was open for 19% -> 23% of each run, Pallas kernels for 20% -> 14%
where the time goes in v5:
time: 664 us; the launch traced here: 655 us
  waiting for transfers between devices  215 us (32%)
  starting transfers between devices  133 us (20%)
  Pallas kernels  119 us (18%)
  other arithmetic  63.9 us (10%)
  local copies, waits for them, and re-layouts  59.1 us (9%)
  matrix products  49.1 us (7%)
  between operations  15.9 us (2%)
    ppermute x96, waiting for transfers between devices, hop(): lax.ppermute(value, 'blk', [(RING[i], RING[(i + by) % count]) for i in ra...  203 us
    ppermute x96, starting transfers between devices, hop(): lax.ppermute(value, 'blk', [(RING[i], RING[(i + by) % count]) for i in ra...  101 us
    dot_general x24, matrix products, matmul(): lax.dot_general(left, right, dims, preferred_element_type=jnp.float32)  49.1 us
    ppermute x17, starting transfers between devices, cross(): return lax.ppermute(value, 'head', [(i, i ^ by) for i in range(4)])  27.2 us
    pallas_call x1, Pallas kernels, attend_back(): pl.pallas_call(lambda *refs: attend_back_kernel(*refs, groups=len(grads))...  25.6 us
    convert_element_type x18, other arithmetic, add(): (left.astype(jnp.float32) + right.astype(jnp.float32)).astype(left.dtype)  24.9 us
    pallas_call x2, Pallas kernels, weight_grads(): pl.pallas_call(lambda *refs: weight_grads_kernel(*refs, groups=len(lefts)...  23.2 us
    unnamed x211, local copies, waits for them, and re-layouts  20.1 us
  transfers between devices with their start and end apart: 120, of which 53 were waited for; matrix products, arithmetic and copies ran while one was open for 23% of the time, Pallas kernels for 14%

profile of v5, /device:TPU:0, one launch (start us, length us, event | category | flops | bytes accessed | tf_op | source)
XLA Modules:
  0.0 654.9 jit_solution(5201119994634276745)
XLA Ops:
  36.9 12.6 %collective-permute-done.4 = bf16[200,512]{1,0:T(8,128)(2,1)S(1)} collective-permute-done((bf16[200,512]{1,0:T(8,128)(2,1)S(1)}, bf16[200,512]{1,0:T(8,128)(2,1)S(1)}, u32[]{:S(2)}, u32[]{:S(2)}) %collective-permute-start.4) | collective-permute-done | bytes 204832 | tf_op jit(solution)/shard_map/ppermute | solution.py:612
  53.8 11.8 %collective-permute-done.8 = bf16[120,512]{1,0:T(8,128)(2,1)S(1)} collective-permute-done((bf16[120,512]{1,0:T(8,128)(2,1)S(1)}, bf16[120,512]{1,0:T(8,128)(2,1)S(1)}, u32[]{:S(2)}, u32[]{:S(2)}) %collective-permute-start.8) | collective-permute-done | bytes 122912 | tf_op jit(solution)/shard_map/ppermute | solution.py:612
  82.1 8.5 %collective-permute-done.16 = bf16[224,1536]{1,0:T(8,128)(2,1)S(1)} collective-permute-done((bf16[224,1536]{1,0:T(8,128)(2,1)S(1)}, bf16[224,1536]{1,0:T(8,128)(2,1)S(1)}, u32[]{:S(2)}, u32[]{:S(2)}) %collective-permute-start.16) | collective-permute-done | bytes 688160 | tf_op jit(solution)/shard_map/ppermute | solution.py:612
  101.5 10.8 %collective-permute-done.20 = bf16[160,1536]{1,0:T(8,128)(2,1)S(1)} collective-permute-done((bf16[160,1536]{1,0:T(8,128)(2,1)}, bf16[160,1536]{1,0:T(8,128)(2,1)S(1)}, u32[]{:S(2)}, u32[]{:S(2)}) %collective-permute-start.20) | collective-permute-done | bytes 491552 | tf_op jit(solution)/shard_map/ppermute | solution.py:612
  119.4 10.0 %project.1 = (bf16[1024,2048]{1,0:T(8,128)(2,1)}, f32[1024,512]{1,0:T(8,128)}, bf16[1024,256]{1,0:T(8,128)(2,1)}, bf16[1024,256]{1,0:T(8,128)(2,1)}, bf16[2048,512]{1,0:T(8,128)(2,1)}, /*index=5*/f32[16,512]{1,0:T(8,128)}) custom-call(s32[9]{0:T(128)} %pad_add_fusion.refs_0_.at_ref, bf16[128,2048]{1,0:T(8,128)(2,1)} %bitcast.82, ...), custom_call_target="tpu_custom_call" | custom-call | flops 1 | bytes 1 | tf_op jit(solution)/shard_map/project/pallas_call | solution.py:828
  164.4 18.5 %attend.1 = (bf16[1024,256]{1,0:T(8,128)(2,1)}, f32[8,8,256]{2,1,0:T(8,128)}) custom-call(s32[8]{0:T(128)} %get-tuple-element.499.place_ref.refs_0_, s32[32]{0:T(128)} %copy-done.79, bf16[1024,256]{1,0:T(8,128)(2,1)} %get-tuple-element.261.q_ref.refs_2_, bf16[1024,256]{1,0:T(8,128)(2,1)} %get-tuple-element.262.refs_0_.refs_9_, bf16[1024,256]{1,0:T(8,128)(2,1)} %copy-done.26, ...), custom_call_target="tpu_custom_call" | custom-call | flops 1 | bytes 1 | tf_op jit(solution)/shard_map/attend/pallas_call | solution.py:479
  207.3 6.5 collective-permute-done.40
  221.3 10.5 %collective-permute-done.44 = bf16[128,2048]{1,0:T(8,128)(2,1)S(1)} collective-permute-done((bf16[128,2048]{1,0:T(8,128)(2,1)S(1)}, bf16[128,2048]{1,0:T(8,128)(2,1)S(1)}, u32[]{:S(2)}, u32[]{:S(2)}) %collective-permute-start.44) | collective-permute-done | bytes 524320 | tf_op jit(solution)/shard_map/ppermute | solution.py:612
  235.0 8.7 %assemble.1 = bf16[8,4,64,1536]{3,2,1,0:T(8,128)(2,1)} custom-call(s32[9]{0:T(128)} %pad_add_fusion.refs_0_.at_ref, bf16[512,1536]{1,0:T(8,128)(2,1)} %slice_dynamic-update-slice_fusion.refs_0_, bf16[512,1536]{1,0:T(8,128)(2,1)} %collective-permute-done.42.refs_1_, bf16[512,1536]{1,0:T(8,128)(2,1)} %collective-permute-done.43.refs_2_, ...), custom_call_target="tpu_custom_call" | custom-call | flops 1 | bytes 1 | tf_op jit(solution)/shard_map/assemble/pallas_call | solution.py:759
  251.8 10.4 %collective-permute-done.49 = bf16[128,2048]{1,0:T(8,128)(2,1)S(1)} collective-permute-done((bf16[128,2048]{1,0:T(8,128)(2,1)S(1)}, bf16[128,2048]{1,0:T(8,128)(2,1)S(1)}, u32[]{:S(2)}, u32[]{:S(2)}) %collective-permute-start.49) | collective-permute-done | bytes 524320 | tf_op jit(solution)/shard_map/ppermute | solution.py:612
  280.2 8.6 %collective-permute-done.53 = bf16[128,2048]{1,0:T(8,128)(2,1)S(1)} collective-permute-done((bf16[128,2048]{1,0:T(8,128)(2,1)S(1)}, bf16[128,2048]{1,0:T(8,128)(2,1)S(1)}, u32[]{:S(2)}, u32[]{:S(2)}) %collective-permute-start.53) | collective-permute-done | bytes 524320 | tf_op jit(solution)/shard_map/ppermute | solution.py:612
  317.1 14.4 %weight_grads.2 = (bf16[512,1536]{1,0:T(8,128)(2,1)}, bf16[512,1536]{1,0:T(8,128)(2,1)}, bf16[2,512,1536]{2,1,0:T(8,128)(2,1)}) custom-call(s32[9]{0:T(128)} %pad_add_fusion.refs_0_.at_ref, bf16[384,2048]{1,0:T(8,128)(2,1)} %pad_maximum_fusion.1.refs_1_, bf16[256,2048]{1,0:T(8,128)(2,1)} %copy-done.23, bf16[256,2048]{1,0:T(8,128)(2,1)} %copy-done.24, ...), custom_call_target="tpu_custom_call" | custom-call | flops 1 | bytes 1 | tf_op jit(solution)/shard_map/weight_grads/pallas_call | solution.py:914
  337.0 8.2 %convolution_convert_fusion.1 = bf16[384,2048]{1,0:T(8,128)(2,1)} fusion(bf16[384,1536]{1,0:T(8,128)(2,1)S(1)} %copy-done.14, bf16[2048,1536]{1,0:T(8,128)(2,1)} %bitcast.71), kind=kOutput, calls=%fused_computation.4 | convolution fusion | flops 2416705536 | bytes 9043968 | tf_op jit(solution)/shard_map/dot_general | solution.py:602
  351.9 8.2 %row_grads.2 = bf16[768,2048]{1,0:T(8,128)(2,1)} custom-call(bf16[384,768]{1,0:T(8,128)(2,1)} %get-tuple-element.313.refs_0_, bf16[256,768]{1,0:T(8,128)(2,1)} %get-tuple-element.314.refs_1_, bf16[256,768]{1,0:T(8,128)(2,1)} %get-tuple-element.315.refs_2_, bf16[128,768]{1,0:T(8,128)(2,1)} %get-tuple-element.480.refs_3_, ...), custom_call_target="tpu_custom_call" | custom-call | flops 1 | bytes 1 | tf_op jit(solution)/shard_map/row_grads/pallas_call | solution.py:943
  372.9 6.8 %collective-permute-done.64 = bf16[128,2048]{1,0:T(8,128)(2,1)S(1)} collective-permute-done((bf16[128,2048]{1,0:T(8,128)(2,1)S(1)}, bf16[128,2048]{1,0:T(8,128)(2,1)S(1)}, u32[]{:S(2)}, u32[]{:S(2)}) %collective-permute-start.64) | collective-permute-done | bytes 524320 | tf_op jit(solution)/shard_map/ppermute | solution.py:612
  385.0 10.3 %collective-permute-done.71 = bf16[128,2048]{1,0:T(8,128)(2,1)S(1)} collective-permute-done((bf16[128,2048]{1,0:T(8,128)(2,1)S(1)}, bf16[128,2048]{1,0:T(8,128)(2,1)S(1)}, u32[]{:S(2)}, u32[]{:S(2)}) %collective-permute-start.71) | collective-permute-done | bytes 524320 | tf_op jit(solution)/shard_map/ppermute | solution.py:612
  399.9 7.5 %collective-permute-done.73 = bf16[128,2048]{1,0:T(8,128)(2,1)S(1)} collective-permute-done((bf16[128,2048]{1,0:T(8,128)(2,1)S(1)}, bf16[128,2048]{1,0:T(8,128)(2,1)S(1)}, u32[]{:S(2)}, u32[]{:S(2)}) %collective-permute-start.73) | collective-permute-done | bytes 524320 | tf_op jit(solution)/shard_map/ppermute | solution.py:612
  415.2 14.3 %collective-permute-done.67 = bf16[64,2048]{1,0:T(8,128)(2,1)S(1)} collective-permute-done((bf16[64,2048]{1,0:T(8,128)(2,1)S(1)}, bf16[64,2048]{1,0:T(8,128)(2,1)S(1)}, u32[]{:S(2)}, u32[]{:S(2)}) %collective-permute-start.67) | collective-permute-done | bytes 262176 | tf_op jit(solution)/shard_map/ppermute | solution.py:612
  446.2 25.6 %attend_back.1 = (bf16[1024,256]{1,0:T(8,128)(2,1)}, bf16[1024,256]{1,0:T(8,128)(2,1)}, bf16[1024,256]{1,0:T(8,128)(2,1)}, bf16[2048,256]{1,0:T(8,128)(2,1)}) custom-call(s32[8]{0:T(128)} %get-tuple-element.499.place_ref.refs_0_, s32[32]{0:T(128)} %copy-done.79, bf16[1024,256]{1,0:T(8,128)(2,1)} %get-tuple-element.261.q_ref.refs_2_, ...), custom_call_target="tpu_custom_call" | custom-call | flops 1 | bytes 1 | tf_op jit(solution)/shard_map/attend_back/pallas_call | solution.py:578
  481.3 7.0 %collective-permute-start.84 = (bf16[1024,256]{1,0:T(8,128)(2,1)}, bf16[1024,256]{1,0:T(8,128)(2,1)}, u32[]{:S(2)}, u32[]{:S(2)}) collective-permute-start(bf16[1024,256]{1,0:T(8,128)(2,1)} %get-tuple-element.352), channel_id=1, source_target_pairs={{0,2},{1,3},{2,0},{3,1},{4,6},{5,7},{6,4},{7,5},{8,10},{9,11},{10,... | collective-permute-start | bytes 1572872 | tf_op jit(solution)/shard_map/ppermute | solution.py:616
  513.6 9.4 %project_back.1 = (bf16[1024,512]{1,0:T(8,128)(2,1)}, bf16[1024,2048]{1,0:T(8,128)(2,1)}, f32[8,128]{1,0:T(8,128)}) custom-call(bf16[1024,256]{1,0:T(8,128)(2,1)} %get-tuple-element.360.dq_ref, bf16[1024,256]{1,0:T(8,128)(2,1)} %add_convert_fusion.13.dkv_ref, f32[1024,512]{1,0:T(8,128)} %get-tuple-element.362.raw_ref, f32[8,128]{1,0:T(8,128)} %pad.9.head_gain_ref, ...), custom_call_target="tpu_custom_call" | custom-call | flops 1 | bytes 1 | tf_op jit(solution)/shard_map/project_back/pallas_call | solution.py:876
  536.1 8.9 %weight_grads.3 = (bf16[512,512]{1,0:T(8,128)(2,1)}, bf16[512,512]{1,0:T(8,128)(2,1)}, bf16[2,512,512]{2,1,0:T(8,128)(2,1)}) custom-call(s32[9]{0:T(128)} %pad_add_fusion.refs_0_.at_ref, bf16[1024,2048]{1,0:T(8,128)(2,1)} %get-tuple-element.368.refs_1_, bf16[1024,512]{1,0:T(8,128)(2,1)} %get-tuple-element.369.refs_2_), custom_call_target="tpu_custom_call" | custom-call | flops 1 | bytes 1 | tf_op jit(solution)/shard_map/weight_grads/pallas_call | solution.py:914
  549.9 7.1 %collective-permute-start.97 = (f32[8,128]{1,0:T(8,128)S(1)}, f32[8,128]{1,0:T(8,128)S(1)}, u32[]{:S(2)}, u32[]{:S(2)}) collective-permute-start(f32[8,128]{1,0:T(8,128)S(1)} %add.340), channel_id=1, source_target_pairs={{0,2},{1,3},{2,0},{3,1},{4,6},{5,7},{6,4},{7,5},{8,10},{9,11},{10,... | collective-permute-start | bytes 12296 | tf_op jit(solution)/shard_map/ppermute | solution.py:616
  612.3 7.4 %collective-permute-done.107 = bf16[224,512]{1,0:T(8,128)(2,1)} collective-permute-done((bf16[224,512]{1,0:T(8,128)(2,1)}, bf16[224,512]{1,0:T(8,128)(2,1)}, u32[]{:S(2)}, u32[]{:S(2)}) %collective-permute-start.107) | collective-permute-done | bytes 229408 | tf_op jit(solution)/shard_map/ppermute | solution.py:612
  (625 shorter events, 387.2 us)
Async XLA Ops:
  7.2 151.8 %all-gather.5.cloned.1.call-start = ((), (), s32[]{:S(2)}) async-start(), calls=%async_computation.3 | async-start | bytes 3932160 | tf_op jit(solution)/shard_map/all_gather | solution.py:1006
  7.2 23.7 %collective-permute-start.2 = (bf16[128,2048]{1,0:T(8,128)(2,1)}, bf16[128,2048]{1,0:T(8,128)(2,1)S(1)}, u32[]{:S(2)}, u32[]{:S(2)}) collective-permute-start(bf16[128,2048]{1,0:T(8,128)(2,1)} %bitcast.80), channel_id=1, source_target_pairs={{0,4},{8,0},{16,8},{24,16},{28,24},{20,28},{12,20},{4,12},{1,5},{9... | collective-permute-start | bytes 1572872 | tf_op jit(solution)/shard_map/ppermute | solution.py:612
  18.7 165.6 %all-gather.3.cloned.1.call-start = ((), (), s32[]{:S(2)}) async-start(), calls=%async_computation.2 | async-start | bytes 1310720 | tf_op jit(solution)/shard_map/all_gather | solution.py:1006
  98.0 495.7 %reduce-scatter.3.cloned.1.call-start = ((), (), s32[]{:S(2)}) async-start(), calls=%async_computation.4 | async-start | bytes 1310720 | tf_op jit(solution)/shard_map/reduce_scatter | solution.py:1010
  154.8 28.1 %collective-permute-start.34 = (bf16[128,2048]{1,0:T(8,128)(2,1)}, bf16[128,2048]{1,0:T(8,128)(2,1)S(1)}, u32[]{:S(2)}, u32[]{:S(2)}) collective-permute-start(bf16[128,2048]{1,0:T(8,128)(2,1)} %collective-permute-done.27), channel_id=1, source_target_pairs={{0,4},{8,0},{16,8},{24,16},{28,24},{20,28},{12,20},{4,12},{1,5},{9... | collective-permute-start | bytes 1572872 | tf_op jit(solution)/shard_map/ppermute | solution.py:612
  155.3 27.6 %collective-permute-start.35 = (bf16[128,2048]{1,0:T(8,128)(2,1)}, bf16[128,2048]{1,0:T(8,128)(2,1)S(1)}, u32[]{:S(2)}, u32[]{:S(2)}) collective-permute-start(bf16[128,2048]{1,0:T(8,128)(2,1)} %collective-permute-done.28), channel_id=1, source_target_pairs={{0,8},{8,16},{16,24},{24,28},{28,20},{20,12},{12,4},{4,0},{1,9},{9... | collective-permute-start | bytes 1572872 | tf_op jit(solution)/shard_map/ppermute | solution.py:612
  163.6 51.7 %collective-permute-start.42 = (bf16[512,1536]{1,0:T(8,128)(2,1)}, bf16[512,1536]{1,0:T(8,128)(2,1)}, u32[]{:S(2)}, u32[]{:S(2)}) collective-permute-start(bf16[512,1536]{1,0:T(8,128)(2,1)} %slice_dynamic-update-slice_fusion.refs_0_), channel_id=1, source_target_pairs={{0,1},{1,0},{2,3},{3,2},{4,5},{5,4},{6,7},{7,6},{8,9},{9,8},{10,11... | collective-permute-start | bytes 4718600 | tf_op jit(solution)/shard_map/ppermute | solution.py:616
  163.7 51.7 %collective-permute-start.43 = (bf16[512,1536]{1,0:T(8,128)(2,1)}, bf16[512,1536]{1,0:T(8,128)(2,1)}, u32[]{:S(2)}, u32[]{:S(2)}) collective-permute-start(bf16[512,1536]{1,0:T(8,128)(2,1)} %slice_dynamic-update-slice_fusion.refs_0_), channel_id=1, source_target_pairs={{0,2},{1,3},{2,0},{3,1},{4,6},{5,7},{6,4},{7,5},{8,10},{9,11},{10,... | collective-permute-start | bytes 4718600 | tf_op jit(solution)/shard_map/ppermute | solution.py:616
  334.6 28.8 %collective-permute-start.63 = (bf16[1024,1536]{1,0:T(8,128)(2,1)}, bf16[1024,1536]{1,0:T(8,128)(2,1)}, u32[]{:S(2)}, u32[]{:S(2)}) collective-permute-start(bf16[1024,1536]{1,0:T(8,128)(2,1)} %bitcast.94), channel_id=1, source_target_pairs={{0,1},{1,0},{2,3},{3,2},{4,5},{5,4},{6,7},{7,6},{8,9},{9,8},{10,11... | collective-permute-start | bytes 9437192 | tf_op jit(solution)/shard_map/ppermute | solution.py:616
  370.1 39.7 %collective-permute-start.66 = (bf16[512,1536]{1,0:T(8,128)(2,1)S(1)}, bf16[512,1536]{1,0:T(8,128)(2,1)S(1)}, u32[]{:S(2)}, u32[]{:S(2)}) collective-permute-start(bf16[512,1536]{1,0:T(8,128)(2,1)S(1)} %get-tuple-element.322), channel_id=1, source_target_pairs={{0,2},{1,3},{2,0},{3,1},{4,6},{5,7},{6,4},{7,5},{8,10},{9,11},{10,... | collective-permute-start | bytes 4718600 | tf_op jit(solution)/shard_map/ppermute | solution.py:616
  407.5 25.1 %collective-permute-start.75 = (bf16[128,2048]{1,0:T(8,128)(2,1)S(1)}, bf16[128,2048]{1,0:T(8,128)(2,1)S(1)}, u32[]{:S(2)}, u32[]{:S(2)}) collective-permute-start(bf16[128,2048]{1,0:T(8,128)(2,1)S(1)} %collective-permute-done.73), channel_id=1, source_target_pairs={{0,4},{8,0},{16,8},{24,16},{28,24},{20,28},{12,20},{4,12},{1,5},{9... | collective-permute-start | bytes 1572872 | tf_op jit(solution)/shard_map/ppermute | solution.py:612
  408.9 23.7 %collective-permute-start.76 = (bf16[128,2048]{1,0:T(8,128)(2,1)S(1)}, bf16[128,2048]{1,0:T(8,128)(2,1)S(1)}, u32[]{:S(2)}, u32[]{:S(2)}) collective-permute-start(bf16[128,2048]{1,0:T(8,128)(2,1)S(1)} %collective-permute-done.74), channel_id=1, source_target_pairs={{0,8},{8,16},{16,24},{24,28},{28,20},{20,12},{12,4},{4,0},{1,9},{9... | collective-permute-start | bytes 1572872 | tf_op jit(solution)/shard_map/ppermute | solution.py:612
  412.3 29.9 %collective-permute-start.69 = (bf16[224,1536]{1,0:T(8,128)(2,1)S(1)}, bf16[224,1536]{1,0:T(8,128)(2,1)S(1)}, u32[]{:S(2)}, u32[]{:S(2)}) collective-permute-start(bf16[224,1536]{1,0:T(8,128)(2,1)S(1)} %get-tuple-element.326), channel_id=1, source_target_pairs={{0,8},{8,16},{16,24},{24,28},{28,20},{20,12},{12,4},{4,0},{1,9},{9... | collective-permute-start | bytes 2064392 | tf_op jit(solution)/shard_map/ppermute | solution.py:612
  474.4 28.5 %collective-permute-start.79 = (bf16[128,2048]{1,0:T(8,128)(2,1)}, bf16[128,2048]{1,0:T(8,128)(2,1)}, u32[]{:S(2)}, u32[]{:S(2)}) collective-permute-start(bf16[128,2048]{1,0:T(8,128)(2,1)} %pad_maximum_fusion.12), channel_id=1, source_target_pairs={{0,8},{8,16},{16,24},{24,28},{28,20},{20,12},{12,4},{4,0},{1,9},{9... | collective-permute-start | bytes 1572872 | tf_op jit(solution)/shard_map/ppermute | solution.py:612
  475.2 27.6 %collective-permute-start.80 = (bf16[128,2048]{1,0:T(8,128)(2,1)}, bf16[128,2048]{1,0:T(8,128)(2,1)}, u32[]{:S(2)}, u32[]{:S(2)}) collective-permute-start(bf16[128,2048]{1,0:T(8,128)(2,1)} %pad_maximum_fusion.13), channel_id=1, source_target_pairs={{0,4},{8,0},{16,8},{24,16},{28,24},{20,28},{12,20},{4,12},{1,5},{9... | collective-permute-start | bytes 1572872 | tf_op jit(solution)/shard_map/ppermute | solution.py:612
  476.4 23.0 %collective-permute-start.81 = (bf16[160,1536]{1,0:T(8,128)(2,1)}, bf16[160,1536]{1,0:T(8,128)(2,1)}, u32[]{:S(2)}, u32[]{:S(2)}) collective-permute-start(bf16[160,1536]{1,0:T(8,128)(2,1)} %slice.641), channel_id=1, source_target_pairs={{0,8},{8,16},{16,24},{24,28},{28,20},{20,12},{12,4},{4,0},{1,9},{9... | collective-permute-start | bytes 1474568 | tf_op jit(solution)/shard_map/ppermute | solution.py:612
  477.2 23.9 %collective-permute-start.82 = (bf16[160,1536]{1,0:T(8,128)(2,1)}, bf16[160,1536]{1,0:T(8,128)(2,1)}, u32[]{:S(2)}, u32[]{:S(2)}) collective-permute-start(bf16[160,1536]{1,0:T(8,128)(2,1)} %slice.642), channel_id=1, source_target_pairs={{0,4},{8,0},{16,8},{24,16},{28,24},{20,28},{12,20},{4,12},{1,5},{9... | collective-permute-start | bytes 1474568 | tf_op jit(solution)/shard_map/ppermute | solution.py:612
  481.3 24.1 %collective-permute-start.84 = (bf16[1024,256]{1,0:T(8,128)(2,1)}, bf16[1024,256]{1,0:T(8,128)(2,1)}, u32[]{:S(2)}, u32[]{:S(2)}) collective-permute-start(bf16[1024,256]{1,0:T(8,128)(2,1)} %get-tuple-element.352), channel_id=1, source_target_pairs={{0,2},{1,3},{2,0},{3,1},{4,6},{5,7},{6,4},{7,5},{8,10},{9,11},{10,... | collective-permute-start | bytes 1572872 | tf_op jit(solution)/shard_map/ppermute | solution.py:616
  507.4 88.0 %reduce-scatter.5.cloned.1.call-start = ((), (), s32[]{:S(2)}) async-start(), calls=%async_computation.5 | async-start | bytes 3932160 | tf_op jit(solution)/shard_map/reduce_scatter | solution.py:1010
  508.0 22.2 %collective-permute-start.85 = (bf16[128,2048]{1,0:T(8,128)(2,1)}, bf16[128,2048]{1,0:T(8,128)(2,1)}, u32[]{:S(2)}, u32[]{:S(2)}) collective-permute-start(bf16[128,2048]{1,0:T(8,128)(2,1)} %get-tuple-element.356), channel_id=1, source_target_pairs={{0,8},{8,16},{16,24},{24,28},{28,20},{20,12},{12,4},{4,0},{1,9},{9... | collective-permute-start | bytes 1572872 | tf_op jit(solution)/shard_map/ppermute | solution.py:612
  508.9 21.3 %collective-permute-start.86 = (bf16[128,2048]{1,0:T(8,128)(2,1)}, bf16[128,2048]{1,0:T(8,128)(2,1)}, u32[]{:S(2)}, u32[]{:S(2)}) collective-permute-start(bf16[128,2048]{1,0:T(8,128)(2,1)} %get-tuple-element.357), channel_id=1, source_target_pairs={{0,4},{8,0},{16,8},{24,16},{28,24},{20,28},{12,20},{4,12},{1,5},{9... | collective-permute-start | bytes 1572872 | tf_op jit(solution)/shard_map/ppermute | solution.py:612
  567.9 30.0 %collective-permute-start.100 = (bf16[512,512]{1,0:T(8,128)(2,1)S(1)}, bf16[512,512]{1,0:T(8,128)(2,1)S(1)}, u32[]{:S(2)}, u32[]{:S(2)}) collective-permute-start(bf16[512,512]{1,0:T(8,128)(2,1)S(1)} %get-tuple-element.385), channel_id=1, source_target_pairs={{0,2},{1,3},{2,0},{3,1},{4,6},{5,7},{6,4},{7,5},{8,10},{9,11},{10,... | collective-permute-start | bytes 1572872 | tf_op jit(solution)/shard_map/ppermute | solution.py:616
  575.3 23.4 %collective-permute-start.98 = (bf16[128,2048]{1,0:T(8,128)(2,1)}, bf16[128,2048]{1,0:T(8,128)(2,1)}, u32[]{:S(2)}, u32[]{:S(2)}) collective-permute-start(bf16[128,2048]{1,0:T(8,128)(2,1)} %get-tuple-element.382), channel_id=1, source_target_pairs={{0,8},{8,16},{16,24},{24,28},{28,20},{20,12},{12,4},{4,0},{1,9},{9... | collective-permute-start | bytes 1572872 | tf_op jit(solution)/shard_map/ppermute | solution.py:612
  576.3 22.5 %collective-permute-start.99 = (bf16[128,2048]{1,0:T(8,128)(2,1)}, bf16[128,2048]{1,0:T(8,128)(2,1)}, u32[]{:S(2)}, u32[]{:S(2)}) collective-permute-start(bf16[128,2048]{1,0:T(8,128)(2,1)} %get-tuple-element.383), channel_id=1, source_target_pairs={{0,4},{8,0},{16,8},{24,16},{28,24},{20,28},{12,20},{4,12},{1,5},{9... | collective-permute-start | bytes 1572872 | tf_op jit(solution)/shard_map/ppermute | solution.py:612
  (185 other events, 1994.5 us)
Sparse Core Ops, SparseCore 0:
  18.8 30.1 all-gather.4
  98.1 14.1 all-gather.2
  507.5 28.8 reduce-scatter.2
  538.8 39.9 reduce-scatter.4

commit v6 on v5

--- a/solution.py
+++ b/solution.py
@@ -422,6 +422,7 @@
 
 
 CHEAP = pl.CostEstimate(flops=1, bytes_accessed=1, transcendentals=0)
+LONG = pl.CostEstimate(flops=3 * 10**10, bytes_accessed=1 << 25, transcendentals=0)
 
 
 def sort_strips(order_ref, kv_refs, keys, values):
@@ -492,7 +493,7 @@
             jax.ShapeDtypeStruct((rows, width), jnp.bfloat16),
             jax.ShapeDtypeStruct((steps, 8, 2 * STRIP), jnp.float32),
         ],
-        cost_estimate=CHEAP,
+        cost_estimate=LONG,
         name="attend",
     )(place, order, queries, *kv)
 
@@ -593,7 +594,7 @@
         ),
         out_shape=[jax.ShapeDtypeStruct((rows, width), jnp.bfloat16)]
         + [jax.ShapeDtypeStruct(shape, jnp.bfloat16) for shape in outs],
-        cost_estimate=CHEAP,
+        cost_estimate=LONG,
         name="attend_back",
     )(place, order, queries, attended, lse, *grads, *kv)
 
@@ -675,25 +676,47 @@
     def __init__(self, pieces, rows):
         cut = 4 * rows + rows // 2
         self.rows, self.step = rows, 0
-        self.own, self.from_left, self.from_right = pieces[:rows], [], []
+        self.taken = [(pieces, 0, rows, 0, 0)]
         self.state = (pieces[rows:cut], pieces[cut:])
 
     def go(self):
         self.step += 1
-        rows = self.rows
+        rows, step = self.rows, self.step
         right, left = hop(self.state[0], 1), hop(self.state[1], -1)
-        if self.step < 4:
-            self.from_left.append(right[:rows])
-            self.from_right.append(left[-rows:])
-            right, left = right[rows:], left[:-rows]
-        self.state = right, left
-
-    def pieces(self):
-        right, left = self.state
-        return [self.own, *self.from_right, right, left, *reversed(self.from_left)]
+        if step < 4:
+            self.taken.append((right, 0, rows, 8 - step, 0))
+            self.taken.append((left, left.shape[0] - rows, rows, step, 0))
+            self.state = right[rows:], left[:-rows]
+        else:
+            self.taken.append((right, 0, rows // 2, 4, 0))
+            self.taken.append((left, 0, rows // 2, 4, rows // 2))
+            self.state = right, left
+
+    def operands(self):
+        return [item[0] for item in self.taken]
+
+    def specs(self):
+        vmem = pl.BlockSpec(memory_space=pltpu.VMEM)
+        own = pl.BlockSpec((self.rows, self.taken[0][0].shape[1]), lambda i: (0, 0))
+        return [own] + [vmem] * (len(self.taken) - 1)
 
     def result(self):
-        return jnp.concatenate(self.pieces(), axis=0)
+        rows, taken = self.rows, [item[1:] for item in self.taken]
+
+        def stack_kernel(*refs):
+            for ref, (first, count, spot, top) in zip(refs[:-1], taken):
+                at = spot * rows + top
+                refs[-1][at : at + count, :] = ref[first : first + count, :]
+
+        return pl.pallas_call(
+            stack_kernel,
+            grid=(1,),
+            in_specs=self.specs(),
+            out_specs=pl.BlockSpec(memory_space=pltpu.VMEM),
+            out_shape=jax.ShapeDtypeStruct((8 * rows, self.taken[0][0].shape[1]), jnp.bfloat16),
+            cost_estimate=CHEAP,
+            name="stack",
+        )(*self.operands())
 
 
 def hold(rings, *extra):
@@ -837,7 +860,7 @@
             jax.ShapeDtypeStruct((width, cols), narrow),
             jax.ShapeDtypeStruct((pad, cols), wide),
         ],
-        cost_estimate=CHEAP,
+        cost_estimate=LONG,
         name="project",
     )(at, *operands)
 
@@ -888,9 +911,16 @@
 
 
 def dots(lefts, rights, dims):
+    if len(lefts) == 1:
+        parts, first = [], 0
+        for right in rights:
+            parts.append(lefts[0][first : first + right.shape[0], :])
+            first += right.shape[0]
+    else:
+        parts = [left[...] for left in lefts]
     return sum(
-        lax.dot_general(left[...], right[...], dims, preferred_element_type=jnp.float32)
-        for left, right in zip(lefts, rights)
+        lax.dot_general(part, right[...], dims, preferred_element_type=jnp.float32)
+        for part, right in zip(parts, rights)
     )
 
 
@@ -934,7 +964,7 @@
 
 
 def row_grads_kernel(*refs, groups):
-    refs[-1][...] = dots(refs[:groups], refs[groups : 2 * groups], DOWN).astype(jnp.bfloat16)
+    refs[-1][...] = dots(refs[:groups], refs[groups:-1], DOWN).astype(jnp.bfloat16)
 
 
 def row_grads(lefts, rights, block=256):
@@ -956,36 +986,35 @@
     return sum(block[:, i : i + 128] for i in range(0, block.shape[1], 128))
 
 
-def widen_kernel(at_ref, *refs, pieces, count):
-    piece_refs, refs = refs[:pieces], refs[pieces:]
-    weights, grads, sums_ref = refs[:count], refs[count : 2 * count], refs[2 * count]
-    rows = weights[0].shape[0]
-    sums_ref[...] = jnp.zeros_like(sums_ref)
-    spots = [0, 1, 2, 3, 4, 4, 5, 6, 7]
-    tops = [0] * 5 + [rows // 2] + [0] * 3
-    for ref, s, top in zip(piece_refs, spots, tops):
-        here = slice(top, top + ref.shape[0])
-        first = 0
-        for weight, grad in zip(weights, grads):
-            width = weight.shape[1] // 8
-            there = columns(at_ref[s], width)
-            block = ref[:, first : first + width].astype(jnp.float32)
-            grad[here, there] = block
-            sums_ref[here, :] += lane_sums(block * weight[here, there].astype(jnp.float32))
-            first += width
-
-
-def widen(at, pieces, *weights):
+def widen(at, swap, *weights):
+    rows, taken, count = weights[0].shape[0], [item[1:] for item in swap.taken], len(weights)
+
+    def widen_kernel(at_ref, *refs):
+        piece_refs, refs = refs[: len(taken)], refs[len(taken) :]
+        grads, sums_ref = refs[count : 2 * count], refs[2 * count]
+        sums_ref[...] = jnp.zeros_like(sums_ref)
+        for ref, (start, size, spot, top) in zip(piece_refs, taken):
+            here = slice(top, top + size)
+            first = 0
+            for weight, grad in zip(refs[:count], grads):
+                width = weight.shape[1] // 8
+                there = columns(at_ref[spot], width)
+                block = ref[start : start + size, first : first + width].astype(jnp.float32)
+                grad[here, there] = block
+                sums_ref[here, :] += lane_sums(block * weight[here, there].astype(jnp.float32))
+                first += width
+
     vmem = pl.BlockSpec(memory_space=pltpu.VMEM)
-    shapes = [w.shape for w in weights] + [(weights[0].shape[0], 128)]
+    shapes = [w.shape for w in weights] + [(rows, 128)]
     return pl.pallas_call(
-        lambda *refs: widen_kernel(*refs, pieces=len(pieces), count=len(weights)),
-        in_specs=[pl.BlockSpec(memory_space=pltpu.SMEM)] + [vmem] * (len(pieces) + len(weights)),
+        widen_kernel,
+        grid=(1,),
+        in_specs=[pl.BlockSpec(memory_space=pltpu.SMEM), *swap.specs()] + [vmem] * count,
         out_specs=[vmem] * len(shapes),
         out_shape=[jax.ShapeDtypeStruct(shape, jnp.float32) for shape in shapes],
         cost_estimate=CHEAP,
         name="widen",
-    )(at, *pieces, *weights)
+    )(at, *swap.operands(), *weights)
 
 
 def grouped(strips):
@@ -1091,40 +1120,40 @@
     )
     token_ring = Gather(tokens)
     ff_slices = slice_pieces(at, gate_weight, up_weight)
-    for step in range(4):
-        attn_swap.go()
-        token_ring.go()
-        if step == 0:
-            ff_slices, cosine, sine = hold((attn_swap, token_ring), ff_slices, cosine, sine)
-        elif step < 3:
-            hold((attn_swap, token_ring))
+    token_ring.go()
+    attn_swap.go()
+    hold((attn_swap,))
+    attn_swap.go()
+    ff_slices, cosine, sine = hold((attn_swap, token_ring), ff_slices, cosine, sine)
+    token_ring.go()
+    attn_swap.go()
+    hold((attn_swap,))
+    attn_swap.go()
+    own = hold((token_ring,), attn_swap.result())
+    token_ring.go()
+    near, far = cross(own, 1), cross(own, 2)
     ff_swap, cotangent_ring = Swap(ff_slices, weight_rows), Gather(out_cotangent)
-    own = hold((token_ring, ff_swap), attn_swap.result())
+    own, near, far = hold((token_ring, ff_swap), own, near, far)
+    token_ring.go()
+    both = cross(far, 1)
+    ff_swap.go()
+    own, near, far, both = hold((token_ring,), own, near, far, both)
+
+    first_normed, attn_raw, query_rows, own, attn_matrix, gains = project(
+        at_own, token_ring.strips(), (own, near, far, both), cosine, sine, query_cols, pad
+    )
+    gain_one = gains[:4].reshape(1, model_width)
+    gain_two = gains[4:8].reshape(1, model_width)
+    head_gains = jnp.pad(gains[8, : 2 * HEAD_SIZE].reshape(2, HEAD_SIZE), ((0, 6), (0, 0)))
+    own = hold((ff_swap,), own)
     near, far = cross(own, 1), cross(own, 2)
     ff_swap.go()
     own, near, far = hold((ff_swap, cotangent_ring), own, near, far)
     both = cross(far, 1)
     ff_swap.go()
-    own, near, far, both = hold((ff_swap, cotangent_ring), own, near, far, both)
-
-    first_normed, attn_raw, query_rows, own, attn_matrix, gains = project(
-        at_own, token_ring.strips(), (own, near, far, both), cosine, sine, query_cols, pad
-    )
-    gain_one = gains[:4].reshape(1, model_width)
-    gain_two = gains[4:8].reshape(1, model_width)
-    head_gains = jnp.pad(gains[8, : 2 * HEAD_SIZE].reshape(2, HEAD_SIZE), ((0, 6), (0, 0)))
+    kv = hold((ff_swap, cotangent_ring), own, far, near, both)
     ff_swap.go()
     cotangent_ring.go()
-    own = hold((ff_swap, cotangent_ring), own)
-    near, far = cross(own, 1), cross(own, 2)
-    ff_swap.go()
-    cotangent_ring.go()
-    own, near, far = hold((), own, near, far)
-    both = cross(far, 1)
-    kv = own, far, near, both
-    *kv, ff_own = hold((cotangent_ring,), *kv, ff_swap.result())
-    ff_near, ff_far = cross(ff_own, 1), cross(ff_own, 2)
-    cotangent_ring.go()
     attended, lse = attend(place, order, query_rows, kv)
 
     def by_groups(rows):
@@ -1133,25 +1162,24 @@
     def by_strips(groups):
         return dict(zip(STRIPS, split_groups(groups, local_rows)))
 
-    attended = hold((cotangent_ring,), attended)
-    branch_ring = Scatter(
-        by_strips([matmul(rows, output_rows).astype(narrow) for rows in by_groups(attended)])
-    )
+    attended, ff_own = hold((cotangent_ring,), attended, ff_swap.result())
+    branch_parts = [matmul(rows, output_rows).astype(narrow) for rows in by_groups(attended)]
+    branch_ring = Scatter(by_strips(branch_parts))
+    branch_ring.go()
+    cotangent_ring.go()
+    ff_near, ff_far = cross(ff_own, 1), cross(ff_own, 2)
+    hold((branch_ring, cotangent_ring))
     branch_ring.go()
     cotangent_ring.go()
     hold((branch_ring, cotangent_ring))
     branch_ring.go()
-    ff_near, ff_far = hold((branch_ring,), ff_near, ff_far)
+    cotangent_ring.go()
+    ff_near, ff_far = hold((branch_ring, cotangent_ring), ff_near, ff_far)
+    branch_ring.go()
     ff_both = cross(ff_far, 1)
-    branch_ring.go()
     cotangent_groups = grouped(cotangent_ring.strips())
     hidden_grads = [matmul(rows, down_matrix, ALONG) for rows in cotangent_groups]
-    hidden_grads, ff_own, ff_near, ff_far, ff_both = hold(
-        (branch_ring,), hidden_grads, ff_own, ff_near, ff_far, ff_both
-    )
-    branch_ring.go()
-    ff_matrix = assemble(at_own, (ff_own, ff_near, ff_far, ff_both), weight_rows)
-    ff_matrix = hold((branch_ring,), ff_matrix)
+    hidden_grads, ff_both = hold((branch_ring,), hidden_grads, ff_both)
     tokens_wide = tokens.astype(wide)
     resid = tokens_wide + branch_ring.total()
     rho_two = inverse_rms(resid)
@@ -1177,7 +1205,8 @@
         ff_gradient_groups.append(gradient)
 
     second_ring.go()
-    hold((second_ring,))
+    ff_matrix = assemble(at_own, (ff_own, ff_near, ff_far, ff_both), weight_rows)
+    ff_matrix = hold((second_ring,), ff_matrix)
     for index in range(3):
         second_ring.go()
         feed_forward(index)
@@ -1196,20 +1225,15 @@
     resid_ring.go()
     hold((resid_ring,), parts[2], parts[6])
     resid_ring.go()
+    back_zero = hold((resid_ring,), back(0))
+    parts[0], parts[1], parts[7] = split(back_zero)
+    resid_ring.go()
     ff_own, ff_far, ff_sent = hold(
         (resid_ring,), *weight_grads(at_own, second_groups, ff_gradient_groups, weight_rows)
     )
-    parts[0], parts[1], parts[7] = split(hold((), back(0)))
     resid_ring.go()
-    ff_own, ff_far = scatter_cross(ff_own, ff_far, ff_sent)
-    down_gradient = row_grads(hidden_groups, cotangent_groups)
-    ff_own, ff_far, down_gradient = hold((resid_ring,), ff_own, ff_far, down_gradient)
-    down_gradient = scatter_head(down_gradient)
+    ff_own, ff_far = hold((resid_ring,), *scatter_cross(ff_own, ff_far, ff_sent))
     ff_far = cross(ff_far, 2)
-    resid_ring.go()
-    out_parts = [matmul(rows, down_matrix).astype(narrow) for rows in hidden_groups]
-    out_parts = hold((resid_ring,), *out_parts)
-    out_ring = Scatter(by_strips(out_parts))
     scaled = gain_two * resid_ring.total()
     resid_gradient = out_cotangent.astype(wide) + rho_two * (
         scaled - unit_two * jnp.mean(unit_two * scaled, axis=-1, keepdims=True)
@@ -1227,10 +1251,20 @@
         attended_grads.append(grads)
 
     grad_ring.go()
-    hold((grad_ring,))
-    for index in range(3):
-        grad_ring.go()
-        attention_back(index)
+    out_parts = [matmul(rows, down_matrix).astype(narrow) for rows in hidden_groups]
+    out_parts = hold((grad_ring,), *out_parts)
+    out_ring = Scatter(by_strips(out_parts))
+    grad_ring.go()
+    down_gradient = row_grads(hidden_groups, cotangent_groups)
+    down_gradient = hold((grad_ring,), down_gradient)
+    down_gradient = scatter_head(down_gradient)
+    grad_ring.go()
+    attention_back(0)
+    hold((out_ring, grad_ring))
+    out_ring.go()
+    grad_ring.go()
+    attention_back(1)
+    attention_back(2)
     ff_swap = Swap(add(ff_own, ff_far), weight_rows)
     hold((grad_ring, ff_swap, out_ring))
     out_ring.go()
@@ -1242,17 +1276,13 @@
     query_grads, kv_own, kv_far, kv_sent = hold(
         (out_ring, ff_swap), query_grads, kv_own, kv_far, kv_sent
     )
+    kv_own, kv_far = hold((), *scatter_cross(kv_own, kv_far, kv_sent))
+    ff_swap.go()
     out_ring.go()
-    ff_swap.go()
-    kv_own, kv_far = scatter_cross(kv_own, kv_far, kv_sent)
-    kv_own, kv_far = hold((), kv_own, kv_far)
     kv_grads = add(kv_own, cross(kv_far, 2))
-    output_weight_gradient = row_grads([attended], [jnp.concatenate(grad_groups, axis=0)])
-    kv_grads, output_weight_gradient = hold(
-        (out_ring, ff_swap), kv_grads, output_weight_gradient
-    )
+    output_weight_gradient = row_grads([attended], grad_groups)
+    kv_grads, output_weight_gradient = hold((ff_swap,), kv_grads, output_weight_gradient)
     output_weight_gradient = scatter_head(output_weight_gradient).astype(wide)
-    out_ring.go()
     ff_swap.go()
     attn_gradient, first_parts, gain_sums = project_back(
         query_grads, kv_grads, attn_raw, head_gains, cosine, sine, attn_matrix
@@ -1262,46 +1292,41 @@
     )
     token_ring = Scatter(by_strips(by_groups(first_parts)))
     token_ring.go()
+    ff_swap.go()
+    gain_sums = gain_sums + cross(gain_sums, 1)
     attn_own, attn_far, attn_sent = weight_grads(
         at_own, [first_normed], [attn_gradient], weight_rows
     )
-    gain_sums = gain_sums + cross(gain_sums, 1)
     attn_own, attn_far, attn_sent, gain_sums = hold(
         (token_ring,), attn_own, attn_far, attn_sent, gain_sums
     )
     token_ring.go()
-    ff_swap.go()
-    attn_own, attn_far = scatter_cross(attn_own, attn_far, attn_sent)
+    attn_own, attn_far = hold((), *scatter_cross(attn_own, attn_far, attn_sent))
+    attn_far = cross(attn_far, 2)
     gain_sums = gain_sums + cross(gain_sums, 2)
-    attn_own, attn_far, gain_sums = hold(
-        (token_ring, ff_swap), attn_own, attn_far, gain_sums
-    )
-    attn_far = cross(attn_far, 2)
+    gain_sums = hold((token_ring, ff_swap), gain_sums)
     token_ring.go()
-    out_ring.go()
     gain_sums = gain_sums + mirror(gain_sums, 1)
-    gate_weight_gradient, up_weight_gradient, norm_sums = widen(
-        at, ff_swap.pieces(), gate_weight, up_weight
-    )
+    gate_weight_gradient, up_weight_gradient, ff_sums = widen(at, ff_swap, gate_weight, up_weight)
     attn_swap = Swap(add(attn_own, attn_far), weight_rows)
-    gate_weight_gradient, up_weight_gradient, norm_sums, gain_sums = hold(
-        (token_ring, attn_swap, out_ring),
-        gate_weight_gradient, up_weight_gradient, norm_sums, gain_sums,
-    )
-    feedforward_norm_gradient = jnp.sum(norm_sums, axis=1) / feedforward_norm.astype(wide)
+    gate_weight_gradient, up_weight_gradient, ff_sums, gain_sums = hold(
+        (token_ring, attn_swap), gate_weight_gradient, up_weight_gradient, ff_sums, gain_sums
+    )
+    feedforward_norm_gradient = jnp.sum(ff_sums, axis=1) / feedforward_norm.astype(wide)
     attn_swap.go()
     token_ring.go()
     gain_sums = gain_sums + mirror(gain_sums, 2)
-    gain_sums = hold((token_ring, attn_swap), gain_sums)
+    gain_sums = hold((token_ring, attn_swap, out_ring), gain_sums)
     attn_swap.go()
+    out_ring.go()
     gain_sums = gain_sums + mirror(gain_sums, 4)
-    layer_out = (resid + out_ring.total()).astype(narrow)
-    layer_out, gain_sums = hold((attn_swap,), layer_out, gain_sums)
+    gain_sums = hold((attn_swap,), gain_sums)
     attn_swap.go()
     hold((attn_swap,))
     attn_swap.go()
+    layer_out = (resid + out_ring.total()).astype(narrow)
     query_weight_gradient, key_weight_gradient, value_weight_gradient, norm_sums = widen(
-        at, attn_swap.pieces(), query_weight, key_projection, value_projection
+        at, attn_swap, query_weight, key_projection, value_projection
     )
     attention_norm_gradient = jnp.sum(norm_sums, axis=1) / attention_norm.astype(wide)
     gain_sums = lax.dynamic_slice_in_dim(gain_sums, number * small, small, 1)

time: 664 us -> 647 us (0.974)
  local copies, waits for them, and re-layouts: 59.1 us -> 28.5 us
  waiting for transfers between devices: 215 us -> 238 us
  starting transfers between devices: 133 us -> 116 us
  Pallas kernels: 119 us -> 126 us
    ppermute x3, waiting for transfers between devices: 0.01 us -> 22.1 us  [mirror(): return lax.ppermute(value, 'blk', [(i, i ^ by) for i in range(len(RING))])]
    ppermute x17, starting transfers between devices: 27.2 us -> 10.5 us  [cross(): return lax.ppermute(value, 'head', [(i, i ^ by) for i in range(4)])]
    slice x38 -> x24, local copies, waits for them, and re-layouts: 27 us -> 11 us  [go(): self.state = (right[rows:], left[:-rows])]
    unnamed x211 -> x207, local copies, waits for them, and re-layouts: 20.1 us -> 6.59 us
    ppermute x96, waiting for transfers between devices: 203 us -> 210 us  [hop(): lax.ppermute(value, 'blk', [(RING[i], RING[(i + by) % count]) for i in ra...]
  transfers between devices with their start and end apart: 120 -> 120, of which waited for: 53 -> 62; matrix products, arithmetic and copies ran while one was open for 23% -> 18% of each run, Pallas kernels for 14% -> 20%
where the time goes in v6:
time: 647 us; the launch traced here: 636 us
  waiting for transfers between devices  238 us (37%)
  Pallas kernels  126 us (19%)
  starting transfers between devices  116 us (18%)
  other arithmetic  66 us (10%)
  matrix products  45.3 us (7%)
  local copies, waits for them, and re-layouts  28.5 us (4%)
  between operations  15.9 us (2%)
    ppermute x96, waiting for transfers between devices, hop(): lax.ppermute(value, 'blk', [(RING[i], RING[(i + by) % count]) for i in ra...  210 us
    ppermute x96, starting transfers between devices, hop(): lax.ppermute(value, 'blk', [(RING[i], RING[(i + by) % count]) for i in ra...  101 us
    dot_general x24, matrix products, matmul(): lax.dot_general(left, right, dims, preferred_element_type=jnp.float32)  45.3 us
    convert_element_type x18, other arithmetic, add(): (left.astype(jnp.float32) + right.astype(jnp.float32)).astype(left.dtype)  28.4 us
    pallas_call x1, Pallas kernels, attend_back(): pl.pallas_call(lambda *refs: attend_back_kernel(*refs, groups=len(grads))...  26.1 us
    pallas_call x2, Pallas kernels, weight_grads(): pl.pallas_call(lambda *refs: weight_grads_kernel(*refs, groups=len(lefts)...  23.5 us
    ppermute x3, waiting for transfers between devices, mirror(): return lax.ppermute(value, 'blk', [(i, i ^ by) for i in range(len(RING))])  22.1 us
    pallas_call x1, Pallas kernels, attend(): pl.pallas_call(attend_kernel, grid_spec=pltpu.PrefetchScalarGridSpec(num_...  18.6 us
  transfers between devices with their start and end apart: 120, of which 62 were waited for; matrix products, arithmetic and copies ran while one was open for 18% of the time, Pallas kernels for 20%

profile of v6, /device:TPU:0, one launch (start us, length us, event | category | flops | bytes accessed | tf_op | source)
XLA Modules:
  0.0 636.0 jit_solution(3839740811078254995)
XLA Ops:
  19.6 10.4 %collective-permute-done.refs_1_ = bf16[280,512]{1,0:T(8,128)(2,1)S(1)} collective-permute-done((bf16[280,512]{1,0:T(8,128)(2,1)S(1)}, bf16[280,512]{1,0:T(8,128)(2,1)S(1)}, u32[]{:S(2)}, u32[]{:S(2)}) %collective-permute-start) | collective-permute-done | bytes 286752 | tf_op jit(solution)/shard_map/ppermute | solution.py:613
  44.6 12.3 %collective-permute-done.8.refs_5_ = bf16[120,512]{1,0:T(8,128)(2,1)S(1)} collective-permute-done((bf16[120,512]{1,0:T(8,128)(2,1)S(1)}, bf16[120,512]{1,0:T(8,128)(2,1)S(1)}, u32[]{:S(2)}, u32[]{:S(2)}) %collective-permute-start.8) | collective-permute-done | bytes 122912 | tf_op jit(solution)/shard_map/ppermute | solution.py:613
  69.3 11.0 %collective-permute-done.12.refs_6_ = bf16[128,2048]{1,0:T(8,128)(2,1)S(1)} collective-permute-done((bf16[128,2048]{1,0:T(8,128)(2,1)}, bf16[128,2048]{1,0:T(8,128)(2,1)S(1)}, u32[]{:S(2)}, u32[]{:S(2)}) %collective-permute-start.12) | collective-permute-done | bytes 524320 | tf_op jit(solution)/shard_map/ppermute | solution.py:613
  93.8 9.9 %project.1 = (bf16[1024,2048]{1,0:T(8,128)(2,1)}, f32[1024,512]{1,0:T(8,128)}, bf16[1024,256]{1,0:T(8,128)(2,1)}, bf16[1024,256]{1,0:T(8,128)(2,1)}, bf16[2048,512]{1,0:T(8,128)(2,1)}, /*index=5*/f32[16,512]{1,0:T(8,128)}) custom-call(s32[9]{0:T(128)} %pad_add_fusion.refs_0_.at_ref, bf16[128,2048]{1,0:T(8,128)(2,1)} %bitcast.83, ...), custom_call_target="tpu_custom_call" | custom-call | flops 30000001024 | bytes 33554432 | tf_op jit(solution)/shard_map/project/pallas_call | solution.py:851
  111.0 11.3 %collective-permute-done.21.refs_3_ = bf16[160,1536]{1,0:T(8,128)(2,1)S(1)} collective-permute-done((bf16[160,1536]{1,0:T(8,128)(2,1)S(1)}, bf16[160,1536]{1,0:T(8,128)(2,1)S(1)}, u32[]{:S(2)}, u32[]{:S(2)}) %collective-permute-start.21) | collective-permute-done | bytes 491552 | tf_op jit(solution)/shard_map/ppermute | solution.py:613
  127.0 6.4 %collective-permute-done.25.refs_5_ = bf16[96,1536]{1,0:T(8,128)(2,1)S(1)} collective-permute-done((bf16[96,1536]{1,0:T(8,128)(2,1)S(1)}, bf16[96,1536]{1,0:T(8,128)(2,1)S(1)}, u32[]{:S(2)}, u32[]{:S(2)}) %collective-permute-start.25) | collective-permute-done | bytes 294944 | tf_op jit(solution)/shard_map/ppermute | solution.py:613
  138.9 18.6 %attend.1 = (bf16[1024,256]{1,0:T(8,128)(2,1)}, f32[8,8,256]{2,1,0:T(8,128)}) custom-call(s32[8]{0:T(128)} %get-tuple-element.493.place_ref.refs_0_, s32[32]{0:T(128)} %copy-done.92, bf16[1024,256]{1,0:T(8,128)(2,1)} %get-tuple-element.252.q_ref.refs_2_, bf16[1024,256]{1,0:T(8,128)(2,1)} %get-tuple-element.253.refs_0_.refs_9_, ...), custom_call_target="tpu_custom_call" | custom-call | flops 30000001024 | bytes 33554432 | tf_op jit(solution)/shard_map/attend/pallas_call | solution.py:480
  189.3 8.6 %collective-permute-done.37 = bf16[128,2048]{1,0:T(8,128)(2,1)S(1)} collective-permute-done((bf16[128,2048]{1,0:T(8,128)(2,1)S(1)}, bf16[128,2048]{1,0:T(8,128)(2,1)S(1)}, u32[]{:S(2)}, u32[]{:S(2)}) %collective-permute-start.37) | collective-permute-done | bytes 524320 | tf_op jit(solution)/shard_map/ppermute | solution.py:613
  237.6 8.4 %collective-permute-done.46 = bf16[128,2048]{1,0:T(8,128)(2,1)S(1)} collective-permute-done((bf16[128,2048]{1,0:T(8,128)(2,1)S(1)}, bf16[128,2048]{1,0:T(8,128)(2,1)S(1)}, u32[]{:S(2)}, u32[]{:S(2)}) %collective-permute-start.46) | collective-permute-done | bytes 524320 | tf_op jit(solution)/shard_map/ppermute | solution.py:613
  250.6 8.5 %assemble.1 = bf16[8,4,64,1536]{3,2,1,0:T(8,128)(2,1)} custom-call(s32[9]{0:T(128)} %pad_add_fusion.refs_0_.at_ref, bf16[512,1536]{1,0:T(8,128)(2,1)} %stack.3.refs_0_, bf16[512,1536]{1,0:T(8,128)(2,1)} %collective-permute-done.44.refs_1_, bf16[512,1536]{1,0:T(8,128)(2,1)} %collective-permute-done.45.refs_2_, bf16[512,1536]{1,0:T(8,128)(2,1)} %copy-done.32), custom_call_target="tpu_custom_call" | custom-call | flops 1 | bytes 1 | tf_op jit(solution)/shard_map/assemble/pallas_call | solution.py:782
  304.3 7.1 %collective-permute-done.58 = bf16[64,2048]{1,0:T(8,128)(2,1)S(1)} collective-permute-done((bf16[64,2048]{1,0:T(8,128)(2,1)S(1)}, bf16[64,2048]{1,0:T(8,128)(2,1)S(1)}, u32[]{:S(2)}, u32[]{:S(2)}) %collective-permute-start.58) | collective-permute-done | bytes 262176 | tf_op jit(solution)/shard_map/ppermute | solution.py:613
  316.4 8.4 %collective-permute-done.60 = bf16[128,2048]{1,0:T(8,128)(2,1)S(1)} collective-permute-done((bf16[128,2048]{1,0:T(8,128)(2,1)S(1)}, bf16[128,2048]{1,0:T(8,128)(2,1)S(1)}, u32[]{:S(2)}, u32[]{:S(2)}) %collective-permute-start.60) | collective-permute-done | bytes 524320 | tf_op jit(solution)/shard_map/ppermute | solution.py:613
  330.5 14.3 %weight_grads.2 = (bf16[512,1536]{1,0:T(8,128)(2,1)}, bf16[512,1536]{1,0:T(8,128)(2,1)}, bf16[2,512,1536]{2,1,0:T(8,128)(2,1)}) custom-call(s32[9]{0:T(128)} %pad_add_fusion.refs_0_.at_ref, bf16[384,2048]{1,0:T(8,128)(2,1)} %pad_maximum_fusion.1.refs_1_, bf16[256,2048]{1,0:T(8,128)(2,1)} %copy-done.22, bf16[256,2048]{1,0:T(8,128)(2,1)} %copy-done.21, ...), custom_call_target="tpu_custom_call" | custom-call | flops 1 | bytes 1 | tf_op jit(solution)/shard_map/weight_grads/pallas_call | solution.py:944
  354.9 8.2 %row_grads.2 = bf16[768,2048]{1,0:T(8,128)(2,1)} custom-call(bf16[384,768]{1,0:T(8,128)(2,1)} %get-tuple-element.312.refs_0_, bf16[256,768]{1,0:T(8,128)(2,1)} %copy-done.31, bf16[256,768]{1,0:T(8,128)(2,1)} %get-tuple-element.314.refs_2_, bf16[128,768]{1,0:T(8,128)(2,1)} %get-tuple-element.474.refs_3_, bf16[384,2048]{1,0:T(8,128)(2,1)} %pad_maximum_fusion.refs_4_, ...), custom_call_target="tpu_custom_call" | custom-call | flops 1 | bytes 1 | tf_op jit(solution)/shard_map/row_grads/pallas_call | solution.py:973
  368.8 8.7 %collective-permute-done.63 = bf16[128,2048]{1,0:T(8,128)(2,1)S(1)} collective-permute-done((bf16[128,2048]{1,0:T(8,128)(2,1)}, bf16[128,2048]{1,0:T(8,128)(2,1)S(1)}, u32[]{:S(2)}, u32[]{:S(2)}) %collective-permute-start.63) | collective-permute-done | bytes 524320 | tf_op jit(solution)/shard_map/ppermute | solution.py:613
  386.1 7.3 %collective-permute-done.66 = bf16[128,2048]{1,0:T(8,128)(2,1)S(1)} collective-permute-done((bf16[128,2048]{1,0:T(8,128)(2,1)S(1)}, bf16[128,2048]{1,0:T(8,128)(2,1)S(1)}, u32[]{:S(2)}, u32[]{:S(2)}) %collective-permute-start.66) | collective-permute-done | bytes 524320 | tf_op jit(solution)/shard_map/ppermute | solution.py:613
  398.7 7.3 %collective-permute-done.69 = bf16[128,2048]{1,0:T(8,128)(2,1)S(1)} collective-permute-done((bf16[128,2048]{1,0:T(8,128)(2,1)S(1)}, bf16[128,2048]{1,0:T(8,128)(2,1)S(1)}, u32[]{:S(2)}, u32[]{:S(2)}) %collective-permute-start.69) | collective-permute-done | bytes 524320 | tf_op jit(solution)/shard_map/ppermute | solution.py:613
  410.2 8.5 %collective-permute-done.71 = bf16[128,2048]{1,0:T(8,128)(2,1)S(1)} collective-permute-done((bf16[128,2048]{1,0:T(8,128)(2,1)S(1)}, bf16[128,2048]{1,0:T(8,128)(2,1)S(1)}, u32[]{:S(2)}, u32[]{:S(2)}) %collective-permute-start.71) | collective-permute-done | bytes 524320 | tf_op jit(solution)/shard_map/ppermute | solution.py:613
  435.2 26.1 %attend_back.1 = (bf16[1024,256]{1,0:T(8,128)(2,1)}, bf16[1024,256]{1,0:T(8,128)(2,1)}, bf16[1024,256]{1,0:T(8,128)(2,1)}, bf16[2048,256]{1,0:T(8,128)(2,1)}) custom-call(s32[8]{0:T(128)} %get-tuple-element.493.place_ref.refs_0_, s32[32]{0:T(128)} %copy-done.92, bf16[1024,256]{1,0:T(8,128)(2,1)} %get-tuple-element.252.q_ref.refs_2_, ...), custom_call_target="tpu_custom_call" | custom-call | flops 30000001024 | bytes 33554432 | tf_op jit(solution)/shard_map/attend_back/pallas_call | solution.py:579
  496.5 9.7 %collective-permute-done.82 = bf16[128,2048]{1,0:T(8,128)(2,1)S(1)} collective-permute-done((bf16[128,2048]{1,0:T(8,128)(2,1)}, bf16[128,2048]{1,0:T(8,128)(2,1)S(1)}, u32[]{:S(2)}, u32[]{:S(2)}) %collective-permute-start.82) | collective-permute-done | bytes 524320 | tf_op jit(solution)/shard_map/ppermute | solution.py:613
  509.7 9.3 %project_back.1 = (bf16[1024,512]{1,0:T(8,128)(2,1)}, bf16[1024,2048]{1,0:T(8,128)(2,1)}, f32[8,128]{1,0:T(8,128)}) custom-call(bf16[1024,256]{1,0:T(8,128)(2,1)} %get-tuple-element.357.dq_ref, bf16[1024,256]{1,0:T(8,128)(2,1)} %add_convert_fusion.11.dkv_ref, f32[1024,512]{1,0:T(8,128)} %get-tuple-element.359.raw_ref, f32[8,128]{1,0:T(8,128)} %pad.9.head_gain_ref, ...), custom_call_target="tpu_custom_call" | custom-call | flops 1 | bytes 1 | tf_op jit(solution)/shard_map/project_back/pallas_call | solution.py:899
  523.4 9.1 %weight_grads.3 = (bf16[512,512]{1,0:T(8,128)(2,1)}, bf16[512,512]{1,0:T(8,128)(2,1)}, bf16[2,512,512]{2,1,0:T(8,128)(2,1)}) custom-call(s32[9]{0:T(128)} %pad_add_fusion.refs_0_.at_ref, bf16[1024,2048]{1,0:T(8,128)(2,1)} %get-tuple-element.365.refs_1_, bf16[1024,512]{1,0:T(8,128)(2,1)} %get-tuple-element.366.refs_2_), custom_call_target="tpu_custom_call" | custom-call | flops 1 | bytes 1 | tf_op jit(solution)/shard_map/weight_grads/pallas_call | solution.py:944
  540.5 8.3 %collective-permute-done.93 = bf16[128,2048]{1,0:T(8,128)(2,1)S(1)} collective-permute-done((bf16[128,2048]{1,0:T(8,128)(2,1)S(1)}, bf16[128,2048]{1,0:T(8,128)(2,1)S(1)}, u32[]{:S(2)}, u32[]{:S(2)}) %collective-permute-start.93) | collective-permute-done | bytes 524320 | tf_op jit(solution)/shard_map/ppermute | solution.py:613
  578.1 11.5 %collective-permute-done.106 = f32[8,128]{1,0:T(8,128)S(1)} collective-permute-done((f32[8,128]{1,0:T(8,128)S(1)}, f32[8,128]{1,0:T(8,128)S(1)}, u32[]{:S(2)}, u32[]{:S(2)}) %collective-permute-start.106) | collective-permute-done | bytes 4128 | tf_op jit(solution)/shard_map/ppermute | solution.py:621
  (606 shorter events, 371.1 us)
Async XLA Ops:
  7.2 154.8 %all-gather.3.cloned.1.call-start = ((), (), s32[]{:S(2)}) async-start(), calls=%async_computation.2 | async-start | bytes 1310720 | tf_op jit(solution)/shard_map/all_gather | solution.py:1035
  7.3 33.2 %collective-permute-start.4 = (bf16[128,2048]{1,0:T(8,128)(2,1)}, bf16[128,2048]{1,0:T(8,128)(2,1)}, u32[]{:S(2)}, u32[]{:S(2)}) collective-permute-start(bf16[128,2048]{1,0:T(8,128)(2,1)} %bitcast.81), channel_id=1, source_target_pairs={{0,4},{8,0},{16,8},{24,16},{28,24},{20,28},{12,20},{4,12},{1,5},{9... | collective-permute-start | bytes 1572872 | tf_op jit(solution)/shard_map/ppermute | solution.py:613
  10.3 30.2 %collective-permute-start.5 = (bf16[128,2048]{1,0:T(8,128)(2,1)}, bf16[128,2048]{1,0:T(8,128)(2,1)}, u32[]{:S(2)}, u32[]{:S(2)}) collective-permute-start(bf16[128,2048]{1,0:T(8,128)(2,1)} %bitcast.82), channel_id=1, source_target_pairs={{0,8},{8,16},{16,24},{24,28},{28,20},{20,12},{12,4},{4,0},{1,9},{9... | collective-permute-start | bytes 1572872 | tf_op jit(solution)/shard_map/ppermute | solution.py:613
  40.5 23.9 %collective-permute-start.6 = (bf16[128,2048]{1,0:T(8,128)(2,1)}, bf16[128,2048]{1,0:T(8,128)(2,1)}, u32[]{:S(2)}, u32[]{:S(2)}) collective-permute-start(bf16[128,2048]{1,0:T(8,128)(2,1)} %collective-permute-done.4.refs_2_), channel_id=1, source_target_pairs={{0,4},{8,0},{16,8},{24,16},{28,24},{20,28},{12,20},{4,12},{1,5},{9... | collective-permute-start | bytes 1572872 | tf_op jit(solution)/shard_map/ppermute | solution.py:613
  42.1 22.3 %collective-permute-start.7 = (bf16[128,2048]{1,0:T(8,128)(2,1)}, bf16[128,2048]{1,0:T(8,128)(2,1)S(1)}, u32[]{:S(2)}, u32[]{:S(2)}) collective-permute-start(bf16[128,2048]{1,0:T(8,128)(2,1)} %collective-permute-done.5.refs_3_), channel_id=1, source_target_pairs={{0,8},{8,16},{16,24},{24,28},{28,20},{20,12},{12,4},{4,0},{1,9},{9... | collective-permute-start | bytes 1572872 | tf_op jit(solution)/shard_map/ppermute | solution.py:613
  83.7 132.5 %all-gather.5.cloned.1.call-start = ((), (), s32[]{:S(2)}) async-start(), calls=%async_computation.3 | async-start | bytes 3932160 | tf_op jit(solution)/shard_map/all_gather | solution.py:1035
  84.9 22.4 %collective-permute-start.16 = (bf16[224,1536]{1,0:T(8,128)(2,1)}, bf16[224,1536]{1,0:T(8,128)(2,1)S(1)}, u32[]{:S(2)}, u32[]{:S(2)}) collective-permute-start(bf16[224,1536]{1,0:T(8,128)(2,1)} %get-tuple-element.226), channel_id=1, source_target_pairs={{0,8},{8,16},{16,24},{24,28},{28,20},{20,12},{12,4},{4,0},{1,9},{9... | collective-permute-start | bytes 2064392 | tf_op jit(solution)/shard_map/ppermute | solution.py:613
  85.3 22.0 %collective-permute-start.17 = (bf16[224,1536]{1,0:T(8,128)(2,1)}, bf16[224,1536]{1,0:T(8,128)(2,1)S(1)}, u32[]{:S(2)}, u32[]{:S(2)}) collective-permute-start(bf16[224,1536]{1,0:T(8,128)(2,1)} %get-tuple-element.227), channel_id=1, source_target_pairs={{0,4},{8,0},{16,8},{24,16},{28,24},{20,28},{12,20},{4,12},{1,5},{9... | collective-permute-start | bytes 2064392 | tf_op jit(solution)/shard_map/ppermute | solution.py:613
  126.4 447.8 %reduce-scatter.3.cloned.1.call-start = ((), (), s32[]{:S(2)}) async-start(), calls=%async_computation.4 | async-start | bytes 1310720 | tf_op jit(solution)/shard_map/reduce_scatter | solution.py:1039
  134.6 26.7 %collective-permute-start.28 = (bf16[128,2048]{1,0:T(8,128)(2,1)S(1)}, bf16[128,2048]{1,0:T(8,128)(2,1)S(1)}, u32[]{:S(2)}, u32[]{:S(2)}) collective-permute-start(bf16[128,2048]{1,0:T(8,128)(2,1)S(1)} %bitcast.84), channel_id=1, source_target_pairs={{0,4},{8,0},{16,8},{24,16},{28,24},{20,28},{12,20},{4,12},{1,5},{9... | collective-permute-start | bytes 1572872 | tf_op jit(solution)/shard_map/ppermute | solution.py:613
  136.2 25.0 %collective-permute-start.29 = (bf16[128,2048]{1,0:T(8,128)(2,1)S(1)}, bf16[128,2048]{1,0:T(8,128)(2,1)}, u32[]{:S(2)}, u32[]{:S(2)}) collective-permute-start(bf16[128,2048]{1,0:T(8,128)(2,1)S(1)} %bitcast.85), channel_id=1, source_target_pairs={{0,8},{8,16},{16,24},{24,28},{28,20},{20,12},{12,4},{4,0},{1,9},{9... | collective-permute-start | bytes 1572872 | tf_op jit(solution)/shard_map/ppermute | solution.py:613
  136.6 20.8 %collective-permute-start.30 = (bf16[32,1536]{1,0:T(8,128)(2,1)S(1)}, bf16[32,1536]{1,0:T(8,128)(2,1)S(1)}, u32[]{:S(2)}, u32[]{:S(2)}) collective-permute-start(bf16[32,1536]{1,0:T(8,128)(2,1)S(1)} %slice.481), channel_id=1, source_target_pairs={{0,8},{8,16},{16,24},{24,28},{28,20},{20,12},{12,4},{4,0},{1,9},{9... | collective-permute-start | bytes 294920 | tf_op jit(solution)/shard_map/ppermute | solution.py:613
  167.8 59.9 %collective-permute-start.44 = (bf16[512,1536]{1,0:T(8,128)(2,1)}, bf16[512,1536]{1,0:T(8,128)(2,1)}, u32[]{:S(2)}, u32[]{:S(2)}) collective-permute-start(bf16[512,1536]{1,0:T(8,128)(2,1)} %stack.3.refs_0_), channel_id=1, source_target_pairs={{0,1},{1,0},{2,3},{3,2},{4,5},{5,4},{6,7},{7,6},{8,9},{9,8},{10,11... | collective-permute-start | bytes 4718600 | tf_op jit(solution)/shard_map/ppermute | solution.py:617
  197.9 29.9 %collective-permute-start.45 = (bf16[512,1536]{1,0:T(8,128)(2,1)}, bf16[512,1536]{1,0:T(8,128)(2,1)}, u32[]{:S(2)}, u32[]{:S(2)}) collective-permute-start(bf16[512,1536]{1,0:T(8,128)(2,1)} %stack.3.refs_0_), channel_id=1, source_target_pairs={{0,2},{1,3},{2,0},{3,1},{4,6},{5,7},{6,4},{7,5},{8,10},{9,11},{10,... | collective-permute-start | bytes 4718600 | tf_op jit(solution)/shard_map/ppermute | solution.py:617
  384.0 41.8 %collective-permute-start.68 = (bf16[512,1536]{1,0:T(8,128)(2,1)S(1)}, bf16[512,1536]{1,0:T(8,128)(2,1)S(1)}, u32[]{:S(2)}, u32[]{:S(2)}) collective-permute-start(bf16[512,1536]{1,0:T(8,128)(2,1)S(1)} %get-tuple-element.318), channel_id=1, source_target_pairs={{0,2},{1,3},{2,0},{3,1},{4,6},{5,7},{6,4},{7,5},{8,10},{9,11},{10,... | collective-permute-start | bytes 4718600 | tf_op jit(solution)/shard_map/ppermute | solution.py:617
  429.9 31.4 %collective-permute-start.76 = (bf16[128,2048]{1,0:T(8,128)(2,1)}, bf16[128,2048]{1,0:T(8,128)(2,1)}, u32[]{:S(2)}, u32[]{:S(2)}) collective-permute-start(bf16[128,2048]{1,0:T(8,128)(2,1)} %pad_maximum_fusion.13), channel_id=1, source_target_pairs={{0,4},{8,0},{16,8},{24,16},{28,24},{20,28},{12,20},{4,12},{1,5},{9... | collective-permute-start | bytes 1572872 | tf_op jit(solution)/shard_map/ppermute | solution.py:613
  430.7 30.6 %collective-permute-start.75 = (bf16[128,2048]{1,0:T(8,128)(2,1)}, bf16[128,2048]{1,0:T(8,128)(2,1)}, u32[]{:S(2)}, u32[]{:S(2)}) collective-permute-start(bf16[128,2048]{1,0:T(8,128)(2,1)} %pad_maximum_fusion.12), channel_id=1, source_target_pairs={{0,8},{8,16},{16,24},{24,28},{28,20},{20,12},{12,4},{4,0},{1,9},{9... | collective-permute-start | bytes 1572872 | tf_op jit(solution)/shard_map/ppermute | solution.py:613
  431.9 32.1 %collective-permute-start.77 = (bf16[224,1536]{1,0:T(8,128)(2,1)}, bf16[224,1536]{1,0:T(8,128)(2,1)}, u32[]{:S(2)}, u32[]{:S(2)}) collective-permute-start(bf16[224,1536]{1,0:T(8,128)(2,1)} %get-tuple-element.331), channel_id=1, source_target_pairs={{0,8},{8,16},{16,24},{24,28},{28,20},{20,12},{12,4},{4,0},{1,9},{9... | collective-permute-start | bytes 2064392 | tf_op jit(solution)/shard_map/ppermute | solution.py:613
  432.8 33.1 %collective-permute-start.78 = (bf16[224,1536]{1,0:T(8,128)(2,1)}, bf16[224,1536]{1,0:T(8,128)(2,1)}, u32[]{:S(2)}, u32[]{:S(2)}) collective-permute-start(bf16[224,1536]{1,0:T(8,128)(2,1)} %get-tuple-element.332), channel_id=1, source_target_pairs={{0,4},{8,0},{16,8},{24,16},{28,24},{20,28},{12,20},{4,12},{1,5},{9... | collective-permute-start | bytes 2064392 | tf_op jit(solution)/shard_map/ppermute | solution.py:613
  491.1 135.5 %reduce-scatter.5.cloned.1.call-start = ((), (), s32[]{:S(2)}) async-start(), calls=%async_computation.5 | async-start | bytes 3932160 | tf_op jit(solution)/shard_map/reduce_scatter | solution.py:1039
  494.5 24.6 %collective-permute-start.87 = (bf16[96,1536]{1,0:T(8,128)(2,1)}, bf16[96,1536]{1,0:T(8,128)(2,1)S(1)}, u32[]{:S(2)}, u32[]{:S(2)}) collective-permute-start(bf16[96,1536]{1,0:T(8,128)(2,1)} %slice.516), channel_id=1, source_target_pairs={{0,8},{8,16},{16,24},{24,28},{28,20},{20,12},{12,4},{4,0},{1,9},{9... | collective-permute-start | bytes 884744 | tf_op jit(solution)/shard_map/ppermute | solution.py:613
  495.3 23.8 %collective-permute-start.88 = (bf16[96,1536]{1,0:T(8,128)(2,1)}, bf16[96,1536]{1,0:T(8,128)(2,1)S(1)}, u32[]{:S(2)}, u32[]{:S(2)}) collective-permute-start(bf16[96,1536]{1,0:T(8,128)(2,1)} %slice.517), channel_id=1, source_target_pairs={{0,4},{8,0},{16,8},{24,16},{28,24},{20,28},{12,20},{4,12},{1,5},{9... | collective-permute-start | bytes 884744 | tf_op jit(solution)/shard_map/ppermute | solution.py:613
  590.7 33.4 %collective-permute-start.108 = (bf16[128,2048]{1,0:T(8,128)(2,1)}, bf16[128,2048]{1,0:T(8,128)(2,1)}, u32[]{:S(2)}, u32[]{:S(2)}) collective-permute-start(bf16[128,2048]{1,0:T(8,128)(2,1)} %get-tuple-element.395), channel_id=1, source_target_pairs={{0,4},{8,0},{16,8},{24,16},{28,24},{20,28},{12,20},{4,12},{1,5},{9... | collective-permute-start | bytes 1572872 | tf_op jit(solution)/shard_map/ppermute | solution.py:613
  591.0 33.1 %collective-permute-start.107 = (bf16[128,2048]{1,0:T(8,128)(2,1)}, bf16[128,2048]{1,0:T(8,128)(2,1)}, u32[]{:S(2)}, u32[]{:S(2)}) collective-permute-start(bf16[128,2048]{1,0:T(8,128)(2,1)} %get-tuple-element.394), channel_id=1, source_target_pairs={{0,8},{8,16},{16,24},{24,28},{28,20},{20,12},{12,4},{4,0},{1,9},{9... | collective-permute-start | bytes 1572872 | tf_op jit(solution)/shard_map/ppermute | solution.py:613
  (193 other events, 2195.1 us)
Sparse Core Ops, SparseCore 0:
  83.8 16.0 all-gather.2
  126.5 27.5 all-gather.4
  491.2 22.7 reduce-scatter.2
  523.4 36.8 reduce-scatter.4

commit v7 on v6

--- a/solution.py
+++ b/solution.py
@@ -428,11 +428,15 @@
 def sort_strips(order_ref, kv_refs, keys, values):
     per = kv_refs[0].shape[0] // STRIP
     for j, ref in enumerate(kv_refs):
-        for i in range(per):
+
+        def sort(i, carry, j=j, ref=ref):
             target = pl.multiple_of(order_ref[j * per + i] * STRIP, STRIP)
-            here = slice(i * STRIP, (i + 1) * STRIP)
+            here = pl.ds(pl.multiple_of(i * STRIP, STRIP), STRIP)
             keys[pl.ds(target, STRIP), :] = ref[here, :HEAD_SIZE]
             values[pl.ds(target, STRIP), :HEAD_SIZE] = ref[here, HEAD_SIZE:]
+            return carry
+
+        lax.fori_loop(0, per, sort, 0)
 
 
 def attend_kernel(place_ref, order_ref, q_ref, *refs):
@@ -555,15 +559,19 @@
         for j in range(4):
             target = (own_ref, far_ref, sent_ref, sent_ref)[j]
             base = per if j == 3 else 0
-            for i in range(per):
+
+            def spread(i, carry, j=j, target=target, base=base):
                 source = pl.multiple_of(order_ref[j * per + i] * STRIP, STRIP)
-                here = slice((base + i) * STRIP, (base + i + 1) * STRIP)
+                here = pl.ds(pl.multiple_of((base + i) * STRIP, STRIP), STRIP)
                 target[here, :HEAD_SIZE] = (
                     key_sums[pl.ds(source, STRIP), :] * (1.0 / LOG2E)
                 ).astype(jnp.bfloat16)
                 target[here, HEAD_SIZE:] = value_sums[pl.ds(source, STRIP), :].astype(
                     jnp.bfloat16
                 )
+                return carry
+
+            lax.fori_loop(0, per, spread, 0)
 
 
 def attend_back(place, order, queries, grads, attended, lse, kv):
@@ -804,28 +812,44 @@
     each = pieces[0].shape[0] // 8
     rows = matrix_ref.shape[0] // 32
     own = at_ref[8]
-    gains = jnp.zeros(gains_ref.shape, jnp.float32)
-    for s in range(8):
+    gains_ref[...] = jnp.zeros_like(gains_ref)
+
+    def place(s, carry):
+        piece_at = pl.multiple_of(s * each, 16)
         for j in range(4):
             first = pl.multiple_of((at_ref[s] * 4 + (own ^ j)) * rows, rows)
-            matrix_ref[pl.ds(first, rows), :] = pieces[j][s * each : s * each + rows, :]
-            gains += pieces[j][s * each + rows : (s + 1) * each, :].astype(jnp.float32)
-    gains_ref[...] = gains
-    width = gains.shape[1]
+            matrix_ref[pl.ds(first, rows), :] = pieces[j][pl.ds(piece_at, rows), :]
+            gains_ref[...] += pieces[j][
+                pl.ds(pl.multiple_of(piece_at + rows, 16), each - rows), :
+            ].astype(jnp.float32)
+        return carry
+
+    lax.fori_loop(0, 8, place, 0)
+    width = gains_ref.shape[1]
     first = 0
     for ref in token_refs:
-        block = ref[...].astype(jnp.float32)
+        normed_ref[first : first + ref.shape[0], :] = ref[...]
+        first += ref.shape[0]
+
+    def norm(index, carry):
+        here = pl.ds(pl.multiple_of(index * 32, 32), 32)
+        block = normed_ref[here, :].astype(jnp.float32)
         block = block * inverse_rms(block)
-        here = slice(first, first + ref.shape[0])
         for i in range(block.shape[1] // width):
             cols = slice(i * width, (i + 1) * width)
-            normed_ref[here, cols] = (block[:, cols] * gains[i : i + 1]).astype(jnp.bfloat16)
-        first += ref.shape[0]
-    query_gain, key_gain = gains[8:9, :HEAD_SIZE], gains[8:9, HEAD_SIZE : 2 * HEAD_SIZE]
+            normed_ref[here, cols] = (block[:, cols] * gains_ref[i : i + 1, :]).astype(
+                jnp.bfloat16
+            )
+        return carry
+
+    lax.fori_loop(0, normed_ref.shape[0] // 32, norm, 0)
+    query_gain = gains_ref[8:9, :HEAD_SIZE]
+    key_gain = gains_ref[8:9, HEAD_SIZE : 2 * HEAD_SIZE]
     query_cols = q_ref.shape[1]
     step = 256
-    for first in range(0, q_ref.shape[0], step):
-        here = slice(first, first + step)
+
+    def heads(index, carry):
+        here = pl.ds(pl.multiple_of(index * step, step), step)
         raw = jnp.dot(normed_ref[here, :], matrix_ref[...], preferred_element_type=jnp.float32)
         raw_ref[here, :] = raw
         cosine, sine = cos_ref[here, :], sin_ref[here, :]
@@ -839,6 +863,9 @@
                 part = spun(part * inverse_rms(part) * key_gain, cosine, sine)
                 kv_ref[here, :HEAD_SIZE] = part.astype(jnp.bfloat16)
         kv_ref[here, HEAD_SIZE:] = raw[:, query_cols + HEAD_SIZE :].astype(jnp.bfloat16)
+        return carry
+
+    lax.fori_loop(0, q_ref.shape[0] // step, heads, 0)
 
 
 def project(at, strips, pieces, cosine, sine, query_cols, pad):
@@ -872,8 +899,9 @@
     query_cols = dq_ref.shape[1]
     step = 256
     gain_ref[...] = jnp.zeros_like(gain_ref)
-    for first in range(0, dq_ref.shape[0], step):
-        here = slice(first, first + step)
+
+    def block(index, carry):
+        here = pl.ds(pl.multiple_of(index * step, step), step)
         cosine, sine = cos_ref[here, :], sin_ref[here, :]
         for col in range(0, query_cols + HEAD_SIZE, HEAD_SIZE):
             cols = slice(col, col + HEAD_SIZE)
@@ -891,6 +919,9 @@
         part_ref[here, :] = lax.dot_general(
             grad_ref[here, :], matrix_ref[...], ALONG, preferred_element_type=jnp.float32
         ).astype(jnp.bfloat16)
+        return carry
+
+    lax.fori_loop(0, dq_ref.shape[0] // step, block, 0)
 
 
 def project_back(query_grads, kv_grads, raw, head_gains, cosine, sine, matrix):
@@ -905,7 +936,7 @@
             jax.ShapeDtypeStruct((rows, matrix.shape[0]), jnp.bfloat16),
             jax.ShapeDtypeStruct((8, HEAD_SIZE), jnp.float32),
         ],
-        cost_estimate=CHEAP,
+        cost_estimate=LONG,
         name="project_back",
     )(query_grads, kv_grads, raw, head_gains, cosine, sine, matrix)
 
@@ -963,23 +994,79 @@
     return own, far, sent.reshape(2 * count * rows, cols)
 
 
-def row_grads_kernel(*refs, groups):
-    refs[-1][...] = dots(refs[:groups], refs[groups:-1], DOWN).astype(jnp.bfloat16)
+def row_grads_kernel(*refs, lefts):
+    left_refs, right_refs, (out_ref, held) = refs[:lefts], refs[lefts:-2], refs[-2:]
+
+    @pl.when(pl.program_id(0) == 0)
+    def _():
+        first = 0
+        for ref in right_refs:
+            held[first : first + ref.shape[0], :] = ref[...]
+            first += ref.shape[0]
+
+    sums, first = 0.0, 0
+    for ref in left_refs:
+        sums += lax.dot_general(
+            ref[...],
+            held[first : first + ref.shape[0], :],
+            DOWN,
+            preferred_element_type=jnp.float32,
+        )
+        first += ref.shape[0]
+    out_ref[...] = sums.astype(jnp.bfloat16)
 
 
 def row_grads(lefts, rights, block=256):
     out_rows, cols = lefts[0].shape[1], rights[0].shape[1]
     total = sum(left.shape[0] for left in lefts)
     return pl.pallas_call(
-        lambda *refs: row_grads_kernel(*refs, groups=len(lefts)),
+        lambda *refs: row_grads_kernel(*refs, lefts=len(lefts)),
         grid=(out_rows // block,),
         in_specs=[pl.BlockSpec((left.shape[0], block), lambda i: (0, i)) for left in lefts]
         + [pl.BlockSpec(right.shape, lambda i: (0, 0)) for right in rights],
         out_specs=pl.BlockSpec((block, cols), lambda i: (i, 0)),
         out_shape=jax.ShapeDtypeStruct((out_rows, cols), jnp.bfloat16),
+        scratch_shapes=[pltpu.VMEM((total, cols), jnp.bfloat16)],
         cost_estimate=CHEAP,
         name="row_grads",
     )(*lefts, *rights)
+
+
+def hidden_grads_kernel(*refs, strips):
+    matrix_ref, outs, held = refs[strips], refs[strips + 1 : -1], refs[-1]
+
+    @pl.when(pl.program_id(0) == 0)
+    def _():
+        first = 0
+        for ref in refs[:strips]:
+            held[first : first + ref.shape[0], :] = ref[...]
+            first += ref.shape[0]
+
+    first = 0
+    for out in outs:
+        out[...] = lax.dot_general(
+            held[first : first + out.shape[0], :],
+            matrix_ref[...],
+            ALONG,
+            preferred_element_type=jnp.float32,
+        )
+        first += out.shape[0]
+
+
+def hidden_grads_of(strips, matrix, block=256):
+    rows = [(last - first) * strips[0].shape[0] for first, last in GROUPS]
+    cols = matrix.shape[0]
+    return pl.pallas_call(
+        lambda *refs: hidden_grads_kernel(*refs, strips=len(strips)),
+        grid=(cols // block,),
+        in_specs=[pl.BlockSpec(strip.shape, lambda i: (0, 0)) for strip in strips]
+        + [pl.BlockSpec((block, matrix.shape[1]), lambda i: (i, 0))],
+        out_specs=[pl.BlockSpec((n, block), lambda i: (0, i)) for n in rows],
+        out_shape=[jax.ShapeDtypeStruct((n, cols), jnp.float32) for n in rows],
+        scratch_shapes=[pltpu.VMEM((sum(rows), matrix.shape[1]), jnp.bfloat16)],
+        cost_estimate=CHEAP,
+        name="hidden_grads",
+    )(*strips, matrix)
 
 
 def lane_sums(block):
@@ -1122,22 +1209,22 @@
     ff_slices = slice_pieces(at, gate_weight, up_weight)
     token_ring.go()
     attn_swap.go()
-    hold((attn_swap,))
+    hold((attn_swap, token_ring))
+    token_ring.go()
     attn_swap.go()
     ff_slices, cosine, sine = hold((attn_swap, token_ring), ff_slices, cosine, sine)
     token_ring.go()
     attn_swap.go()
     hold((attn_swap,))
     attn_swap.go()
-    own = hold((token_ring,), attn_swap.result())
-    token_ring.go()
+    own = hold((), attn_swap.result())
     near, far = cross(own, 1), cross(own, 2)
     ff_swap, cotangent_ring = Swap(ff_slices, weight_rows), Gather(out_cotangent)
+    hold((token_ring, ff_swap, cotangent_ring))
+    token_ring.go()
     own, near, far = hold((token_ring, ff_swap), own, near, far)
-    token_ring.go()
-    both = cross(far, 1)
     ff_swap.go()
-    own, near, far, both = hold((token_ring,), own, near, far, both)
+    both = hold((), cross(far, 1))
 
     first_normed, attn_raw, query_rows, own, attn_matrix, gains = project(
         at_own, token_ring.strips(), (own, near, far, both), cosine, sine, query_cols, pad
@@ -1145,12 +1232,11 @@
     gain_one = gains[:4].reshape(1, model_width)
     gain_two = gains[4:8].reshape(1, model_width)
     head_gains = jnp.pad(gains[8, : 2 * HEAD_SIZE].reshape(2, HEAD_SIZE), ((0, 6), (0, 0)))
-    own = hold((ff_swap,), own)
     near, far = cross(own, 1), cross(own, 2)
+    hold((ff_swap,))
     ff_swap.go()
-    own, near, far = hold((ff_swap, cotangent_ring), own, near, far)
+    own, near, far = hold((), own, near, far)
     both = cross(far, 1)
-    ff_swap.go()
     kv = hold((ff_swap, cotangent_ring), own, far, near, both)
     ff_swap.go()
     cotangent_ring.go()
@@ -1162,11 +1248,13 @@
     def by_strips(groups):
         return dict(zip(STRIPS, split_groups(groups, local_rows)))
 
-    attended, ff_own = hold((cotangent_ring,), attended, ff_swap.result())
+    attended = hold((cotangent_ring, ff_swap), attended)
     branch_parts = [matmul(rows, output_rows).astype(narrow) for rows in by_groups(attended)]
     branch_ring = Scatter(by_strips(branch_parts))
     branch_ring.go()
     cotangent_ring.go()
+    ff_swap.go()
+    ff_own = hold((), ff_swap.result())
     ff_near, ff_far = cross(ff_own, 1), cross(ff_own, 2)
     hold((branch_ring, cotangent_ring))
     branch_ring.go()
@@ -1174,12 +1262,15 @@
     hold((branch_ring, cotangent_ring))
     branch_ring.go()
     cotangent_ring.go()
-    ff_near, ff_far = hold((branch_ring, cotangent_ring), ff_near, ff_far)
+    ff_near, ff_far, cotangent_strips, down_matrix = hold(
+        (branch_ring, cotangent_ring), ff_near, ff_far, cotangent_ring.strips(), down_matrix
+    )
     branch_ring.go()
     ff_both = cross(ff_far, 1)
-    cotangent_groups = grouped(cotangent_ring.strips())
-    hidden_grads = [matmul(rows, down_matrix, ALONG) for rows in cotangent_groups]
-    hidden_grads, ff_both = hold((branch_ring,), hidden_grads, ff_both)
+    hidden_grads = hidden_grads_of(cotangent_strips, down_matrix)
+    ff_own, ff_near, ff_far, hidden_grads, ff_both = hold(
+        (branch_ring,), ff_own, ff_near, ff_far, hidden_grads, ff_both
+    )
     tokens_wide = tokens.astype(wide)
     resid = tokens_wide + branch_ring.total()
     rho_two = inverse_rms(resid)
@@ -1225,14 +1316,19 @@
     resid_ring.go()
     hold((resid_ring,), parts[2], parts[6])
     resid_ring.go()
-    back_zero = hold((resid_ring,), back(0))
+    back_zero, second_groups, ff_gradient_groups = hold(
+        (resid_ring,), back(0), second_groups, ff_gradient_groups
+    )
     parts[0], parts[1], parts[7] = split(back_zero)
     resid_ring.go()
     ff_own, ff_far, ff_sent = hold(
         (resid_ring,), *weight_grads(at_own, second_groups, ff_gradient_groups, weight_rows)
     )
     resid_ring.go()
-    ff_own, ff_far = hold((resid_ring,), *scatter_cross(ff_own, ff_far, ff_sent))
+    ff_own, ff_far = scatter_cross(ff_own, ff_far, ff_sent)
+    ff_own, ff_far, hidden_groups, cotangent_strips = hold(
+        (resid_ring,), ff_own, ff_far, hidden_groups, cotangent_strips
+    )
     ff_far = cross(ff_far, 2)
     scaled = gain_two * resid_ring.total()
     resid_gradient = out_cotangent.astype(wide) + rho_two * (
@@ -1252,10 +1348,10 @@
 
     grad_ring.go()
     out_parts = [matmul(rows, down_matrix).astype(narrow) for rows in hidden_groups]
-    out_parts = hold((grad_ring,), *out_parts)
+    out_parts, hidden_groups = hold((grad_ring,), out_parts, hidden_groups)
     out_ring = Scatter(by_strips(out_parts))
     grad_ring.go()
-    down_gradient = row_grads(hidden_groups, cotangent_groups)
+    down_gradient = row_grads(hidden_groups, cotangent_strips)
     down_gradient = hold((grad_ring,), down_gradient)
     down_gradient = scatter_head(down_gradient)
     grad_ring.go()
@@ -1273,54 +1369,61 @@
     query_grads, kv_own, kv_far, kv_sent = attend_back(
         place, order, query_rows, attended_grads, attended, lse, kv
     )
-    query_grads, kv_own, kv_far, kv_sent = hold(
-        (out_ring, ff_swap), query_grads, kv_own, kv_far, kv_sent
-    )
-    kv_own, kv_far = hold((), *scatter_cross(kv_own, kv_far, kv_sent))
+    query_grads, kv_own, kv_far, kv_sent, grad_groups, attended = hold(
+        (out_ring, ff_swap), query_grads, kv_own, kv_far, kv_sent, grad_groups, attended
+    )
+    out_ring.go()
+    kv_own, kv_far = scatter_cross(kv_own, kv_far, kv_sent)
+    output_weight_gradient = row_grads([attended], grad_groups)
+    kv_own, kv_far, output_weight_gradient = hold(
+        (out_ring, ff_swap), kv_own, kv_far, output_weight_gradient
+    )
+    output_weight_gradient = scatter_head(output_weight_gradient)
     ff_swap.go()
-    out_ring.go()
-    kv_grads = add(kv_own, cross(kv_far, 2))
-    output_weight_gradient = row_grads([attended], grad_groups)
-    kv_grads, output_weight_gradient = hold((ff_swap,), kv_grads, output_weight_gradient)
-    output_weight_gradient = scatter_head(output_weight_gradient).astype(wide)
+    kv_grads = hold((ff_swap,), add(kv_own, cross(kv_far, 2)))
     ff_swap.go()
     attn_gradient, first_parts, gain_sums = project_back(
         query_grads, kv_grads, attn_raw, head_gains, cosine, sine, attn_matrix
     )
     attn_gradient, first_parts, gain_sums = hold(
-        (out_ring, ff_swap), attn_gradient, first_parts, gain_sums
+        (ff_swap,), attn_gradient, first_parts, gain_sums
     )
     token_ring = Scatter(by_strips(by_groups(first_parts)))
     token_ring.go()
     ff_swap.go()
     gain_sums = gain_sums + cross(gain_sums, 1)
+    gain_sums = gain_sums + cross(gain_sums, 2)
     attn_own, attn_far, attn_sent = weight_grads(
         at_own, [first_normed], [attn_gradient], weight_rows
     )
     attn_own, attn_far, attn_sent, gain_sums = hold(
-        (token_ring,), attn_own, attn_far, attn_sent, gain_sums
+        (token_ring, ff_swap), attn_own, attn_far, attn_sent, gain_sums
     )
     token_ring.go()
     attn_own, attn_far = hold((), *scatter_cross(attn_own, attn_far, attn_sent))
     attn_far = cross(attn_far, 2)
-    gain_sums = gain_sums + cross(gain_sums, 2)
-    gain_sums = hold((token_ring, ff_swap), gain_sums)
-    token_ring.go()
     gain_sums = gain_sums + mirror(gain_sums, 1)
     gate_weight_gradient, up_weight_gradient, ff_sums = widen(at, ff_swap, gate_weight, up_weight)
+    gate_weight_gradient, up_weight_gradient, ff_sums, gain_sums = hold(
+        (token_ring,), gate_weight_gradient, up_weight_gradient, ff_sums, gain_sums
+    )
+    token_ring.go()
+    gain_sums = gain_sums + mirror(gain_sums, 2)
+    feedforward_norm_gradient = jnp.sum(ff_sums, axis=1) / feedforward_norm.astype(wide)
     attn_swap = Swap(add(attn_own, attn_far), weight_rows)
-    gate_weight_gradient, up_weight_gradient, ff_sums, gain_sums = hold(
-        (token_ring, attn_swap), gate_weight_gradient, up_weight_gradient, ff_sums, gain_sums
-    )
-    feedforward_norm_gradient = jnp.sum(ff_sums, axis=1) / feedforward_norm.astype(wide)
+    feedforward_norm_gradient, gain_sums, down_gradient = hold(
+        (token_ring, attn_swap),
+        feedforward_norm_gradient, gain_sums, down_gradient.astype(wide),
+    )
     attn_swap.go()
     token_ring.go()
-    gain_sums = gain_sums + mirror(gain_sums, 2)
-    gain_sums = hold((token_ring, attn_swap, out_ring), gain_sums)
+    gain_sums = gain_sums + mirror(gain_sums, 4)
+    output_weight_gradient, gain_sums = hold(
+        (token_ring, attn_swap, out_ring), output_weight_gradient.astype(wide), gain_sums
+    )
     attn_swap.go()
     out_ring.go()
-    gain_sums = gain_sums + mirror(gain_sums, 4)
-    gain_sums = hold((attn_swap,), gain_sums)
+    hold((attn_swap,))
     attn_swap.go()
     hold((attn_swap,))
     attn_swap.go()
@@ -1349,7 +1452,7 @@
         feedforward_norm_gradient,
         gate_weight_gradient,
         up_weight_gradient,
-        down_gradient.astype(wide),
+        down_gradient,
     )
 
 

time: 647 us -> 666 us (1.029)
  Pallas kernels: 126 us -> 141 us
  waiting for transfers between devices: 238 us -> 249 us
  matrix products: 45.3 us -> 37.2 us
    ppermute x17, waiting for transfers between devices: 5.88 us -> 45.2 us  [cross(): return lax.ppermute(value, 'head', [(i, i ^ by) for i in range(4)])]
    ppermute x96, waiting for transfers between devices: 210 us -> 174 us  [hop(): lax.ppermute(value, 'blk', [(RING[i], RING[(i + by) % count]) for i in ra...]
    dot_general x24 -> x20, matrix products: 45.3 us -> 37.2 us  [matmul(): lax.dot_general(left, right, dims, preferred_element_type=jnp.float32)]
    pallas_call x2 -> x3, Pallas kernels: 13.1 us -> 21.2 us  [the longest x2 13.3 us: row_grads(): pl.pallas_call(lambda *refs: row_grads_kernel(*refs, lefts=len(lefts)), g...]
    ppermute x3, waiting for transfers between devices: 22.1 us -> 30 us  [mirror(): return lax.ppermute(value, 'blk', [(i, i ^ by) for i in range(len(RING))])]
  transfers between devices with their start and end apart: 120 -> 120, of which waited for: 62 -> 61; matrix products, arithmetic and copies ran while one was open for 18% -> 16% of each run, Pallas kernels for 20% -> 22%
where the time goes in v7:
time: 666 us; the launch traced here: 654 us
  waiting for transfers between devices  249 us (37%)
  Pallas kernels  141 us (21%)
  starting transfers between devices  117 us (18%)
  other arithmetic  66 us (10%)
  matrix products  37.2 us (6%)
  local copies, waits for them, and re-layouts  28 us (4%)
  between operations  15.8 us (2%)
    ppermute x96, waiting for transfers between devices, hop(): lax.ppermute(value, 'blk', [(RING[i], RING[(i + by) % count]) for i in ra...  174 us
    ppermute x96, starting transfers between devices, hop(): lax.ppermute(value, 'blk', [(RING[i], RING[(i + by) % count]) for i in ra...  102 us
    ppermute x17, waiting for transfers between devices, cross(): return lax.ppermute(value, 'head', [(i, i ^ by) for i in range(4)])  45.2 us
    dot_general x20, matrix products, matmul(): lax.dot_general(left, right, dims, preferred_element_type=jnp.float32)  37.2 us
    ppermute x3, waiting for transfers between devices, mirror(): return lax.ppermute(value, 'blk', [(i, i ^ by) for i in range(len(RING))])  30 us
    pallas_call x1, Pallas kernels, attend_back(): pl.pallas_call(lambda *refs: attend_back_kernel(*refs, groups=len(grads))...  26.9 us
    convert_element_type x18, other arithmetic, add(): (left.astype(jnp.float32) + right.astype(jnp.float32)).astype(left.dtype)  25.7 us
    pallas_call x2, Pallas kernels, weight_grads(): pl.pallas_call(lambda *refs: weight_grads_kernel(*refs, groups=len(lefts)...  23.2 us
  transfers between devices with their start and end apart: 120, of which 61 were waited for; matrix products, arithmetic and copies ran while one was open for 16% of the time, Pallas kernels for 22%

profile of v7, /device:TPU:0, one launch (start us, length us, event | category | flops | bytes accessed | tf_op | source)
XLA Modules:
  0.0 653.7 jit_solution(941999420161027181)
XLA Ops:
  19.5 10.5 %collective-permute-done.refs_1_ = bf16[280,512]{1,0:T(8,128)(2,1)S(1)} collective-permute-done((bf16[280,512]{1,0:T(8,128)(2,1)S(1)}, bf16[280,512]{1,0:T(8,128)(2,1)S(1)}, u32[]{:S(2)}, u32[]{:S(2)}) %collective-permute-start) | collective-permute-done | bytes 286752 | tf_op jit(solution)/shard_map/ppermute | solution.py:621
  40.2 8.4 %collective-permute-done.4.refs_3_ = bf16[200,512]{1,0:T(8,128)(2,1)S(1)} collective-permute-done((bf16[200,512]{1,0:T(8,128)(2,1)S(1)}, bf16[200,512]{1,0:T(8,128)(2,1)S(1)}, u32[]{:S(2)}, u32[]{:S(2)}) %collective-permute-start.4) | collective-permute-done | bytes 204832 | tf_op jit(solution)/shard_map/ppermute | solution.py:621
  53.7 8.8 %collective-permute-done.8.refs_6_ = bf16[128,2048]{1,0:T(8,128)(2,1)S(1)} collective-permute-done((bf16[128,2048]{1,0:T(8,128)(2,1)}, bf16[128,2048]{1,0:T(8,128)(2,1)S(1)}, u32[]{:S(2)}, u32[]{:S(2)}) %collective-permute-start.8) | collective-permute-done | bytes 524320 | tf_op jit(solution)/shard_map/ppermute | solution.py:621
  76.4 7.7 %collective-permute-done.11 = bf16[64,2048]{1,0:T(8,128)(2,1)S(1)} collective-permute-done((bf16[64,2048]{1,0:T(8,128)(2,1)S(1)}, bf16[64,2048]{1,0:T(8,128)(2,1)S(1)}, u32[]{:S(2)}, u32[]{:S(2)}) %collective-permute-start.11) | collective-permute-done | bytes 262176 | tf_op jit(solution)/shard_map/ppermute | solution.py:621
  93.9 14.4 %project.1 = (bf16[1024,2048]{1,0:T(8,128)(2,1)}, f32[1024,512]{1,0:T(8,128)}, bf16[1024,256]{1,0:T(8,128)(2,1)}, bf16[1024,256]{1,0:T(8,128)(2,1)}, bf16[2048,512]{1,0:T(8,128)(2,1)}, /*index=5*/f32[16,512]{1,0:T(8,128)}) custom-call(s32[9]{0:T(128)} %pad_add_fusion.refs_0_.at_ref, bf16[128,2048]{1,0:T(8,128)(2,1)} %bitcast.80, ...), custom_call_target="tpu_custom_call" | custom-call | flops 30000001024 | bytes 33554432 | tf_op jit(solution)/shard_map/project/pallas_call | solution.py:878
  110.5 12.5 %collective-permute-done.24.refs_1_.refs_10_ = bf16[1024,256]{1,0:T(8,128)(2,1)} collective-permute-done((bf16[1024,256]{1,0:T(8,128)(2,1)}, bf16[1024,256]{1,0:T(8,128)(2,1)}, u32[]{:S(2)}, u32[]{:S(2)}) %collective-permute-start.24) | collective-permute-done | bytes 524320 | tf_op jit(solution)/shard_map/ppermute | solution.py:625
  126.9 12.0 %collective-permute-done.20.refs_3_ = bf16[160,1536]{1,0:T(8,128)(2,1)S(1)} collective-permute-done((bf16[160,1536]{1,0:T(8,128)(2,1)}, bf16[160,1536]{1,0:T(8,128)(2,1)S(1)}, u32[]{:S(2)}, u32[]{:S(2)}) %collective-permute-start.20) | collective-permute-done | bytes 491552 | tf_op jit(solution)/shard_map/ppermute | solution.py:621
  144.8 19.1 %attend.1 = (bf16[1024,256]{1,0:T(8,128)(2,1)}, f32[8,8,256]{2,1,0:T(8,128)}) custom-call(s32[8]{0:T(128)} %get-tuple-element.581.place_ref.refs_0_, s32[32]{0:T(128)} %copy-done.90, bf16[1024,256]{1,0:T(8,128)(2,1)} %get-tuple-element.292.q_ref.refs_2_, bf16[1024,256]{1,0:T(8,128)(2,1)} %get-tuple-element.293.refs_0_.refs_9_, ...), custom_call_target="tpu_custom_call" | custom-call | flops 30000001024 | bytes 33554432 | tf_op jit(solution)/shard_map/attend/pallas_call | solution.py:484
  193.7 9.6 %collective-permute-done.40.refs_7_ = bf16[32,1536]{1,0:T(8,128)(2,1)S(1)} collective-permute-done((bf16[32,1536]{1,0:T(8,128)(2,1)S(1)}, bf16[32,1536]{1,0:T(8,128)(2,1)S(1)}, u32[]{:S(2)}, u32[]{:S(2)}) %collective-permute-start.40) | collective-permute-done | bytes 98336 | tf_op jit(solution)/shard_map/ppermute | solution.py:621
  234.0 12.6 %collective-permute-done.43.refs_2_ = bf16[512,1536]{1,0:T(8,128)(2,1)} collective-permute-done((bf16[512,1536]{1,0:T(8,128)(2,1)}, bf16[512,1536]{1,0:T(8,128)(2,1)}, u32[]{:S(2)}, u32[]{:S(2)}) %collective-permute-start.43) | collective-permute-done | bytes 1572896 | tf_op jit(solution)/shard_map/ppermute | solution.py:625
  249.2 7.9 %hidden_grads.1 = (f32[384,768]{1,0:T(8,128)}, f32[256,768]{1,0:T(8,128)}, f32[256,768]{1,0:T(8,128)}, f32[128,768]{1,0:T(8,128)}) custom-call(bf16[128,2048]{1,0:T(8,128)(2,1)} %bitcast.74, bf16[128,2048]{1,0:T(8,128)(2,1)} %copy-done.25, bf16[128,2048]{1,0:T(8,128)(2,1)} %copy-done.26, bf16[128,2048]{1,0:T(8,128)(2,1)} %collective-permute-done.32.refs_3_.refs_7_, ...), custom_call_target="tpu_custom_call" | custom-call | flops 1 | bytes 1 | tf_op jit(solution)/shard_map/hidden_grads/pallas_call | solution.py:1059
  265.7 8.5 %assemble.1 = bf16[8,4,64,1536]{3,2,1,0:T(8,128)(2,1)} custom-call(s32[9]{0:T(128)} %pad_add_fusion.refs_0_.at_ref, bf16[512,1536]{1,0:T(8,128)(2,1)} %stack.3.refs_0_, bf16[512,1536]{1,0:T(8,128)(2,1)} %collective-permute-done.42.refs_1_, bf16[512,1536]{1,0:T(8,128)(2,1)} %collective-permute-done.43.refs_2_, bf16[512,1536]{1,0:T(8,128)(2,1)} %collective-permute-done.48.refs_3_), custom_call_target="tpu_custom_call" | custom-call | flops 1 | bytes 1 | tf_op jit(solution)/shard_map/assemble/pallas_call | solution.py:790
  332.5 8.3 %collective-permute-done.60 = bf16[128,2048]{1,0:T(8,128)(2,1)S(1)} collective-permute-done((bf16[128,2048]{1,0:T(8,128)(2,1)S(1)}, bf16[128,2048]{1,0:T(8,128)(2,1)S(1)}, u32[]{:S(2)}, u32[]{:S(2)}) %collective-permute-start.60) | collective-permute-done | bytes 524320 | tf_op jit(solution)/shard_map/ppermute | solution.py:621
  344.9 14.3 %weight_grads.2 = (bf16[512,1536]{1,0:T(8,128)(2,1)}, bf16[512,1536]{1,0:T(8,128)(2,1)}, bf16[2,512,1536]{2,1,0:T(8,128)(2,1)}) custom-call(s32[9]{0:T(128)} %pad_add_fusion.refs_0_.at_ref, bf16[384,2048]{1,0:T(8,128)(2,1)} %pad_maximum_fusion.refs_1_, bf16[256,2048]{1,0:T(8,128)(2,1)} %copy-done.24, bf16[256,2048]{1,0:T(8,128)(2,1)} %copy-done.23, ...), custom_call_target="tpu_custom_call" | custom-call | flops 1 | bytes 1 | tf_op jit(solution)/shard_map/weight_grads/pallas_call | solution.py:975
  400.3 8.5 %row_grads.2 = bf16[768,2048]{1,0:T(8,128)(2,1)} custom-call(bf16[384,768]{1,0:T(8,128)(2,1)} %get-tuple-element.390.refs_0_, bf16[256,768]{1,0:T(8,128)(2,1)} %get-tuple-element.391.refs_1_, bf16[256,768]{1,0:T(8,128)(2,1)} %get-tuple-element.392.refs_2_, bf16[128,768]{1,0:T(8,128)(2,1)} %get-tuple-element.393.refs_3_, bf16[128,2048]{1,0:T(8,128)(2,1)} %bitcast.75, ...), custom_call_target="tpu_custom_call" | custom-call | flops 1 | bytes 1 | tf_op jit(solution)/shard_map/row_grads/pallas_call | solution.py:1022
  437.3 26.9 %attend_back.1 = (bf16[1024,256]{1,0:T(8,128)(2,1)}, bf16[1024,256]{1,0:T(8,128)(2,1)}, bf16[1024,256]{1,0:T(8,128)(2,1)}, bf16[2048,256]{1,0:T(8,128)(2,1)}) custom-call(s32[8]{0:T(128)} %get-tuple-element.581.place_ref.refs_0_, s32[32]{0:T(128)} %copy-done.90, bf16[1024,256]{1,0:T(8,128)(2,1)} %get-tuple-element.292.q_ref.refs_2_, ...), custom_call_target="tpu_custom_call" | custom-call | flops 30000001024 | bytes 33554432 | tf_op jit(solution)/shard_map/attend_back/pallas_call | solution.py:587
  476.7 7.6 %collective-permute-done.82 = bf16[128,2048]{1,0:T(8,128)(2,1)} collective-permute-done((bf16[128,2048]{1,0:T(8,128)(2,1)}, bf16[128,2048]{1,0:T(8,128)(2,1)}, u32[]{:S(2)}, u32[]{:S(2)}) %collective-permute-start.82) | collective-permute-done | bytes 524320 | tf_op jit(solution)/shard_map/ppermute | solution.py:621
  494.0 9.8 %collective-permute-done.84.refs_3_ = bf16[160,1536]{1,0:T(8,128)(2,1)S(1)} collective-permute-done((bf16[160,1536]{1,0:T(8,128)(2,1)S(1)}, bf16[160,1536]{1,0:T(8,128)(2,1)S(1)}, u32[]{:S(2)}, u32[]{:S(2)}) %collective-permute-start.84) | collective-permute-done | bytes 491552 | tf_op jit(solution)/shard_map/ppermute | solution.py:621
  504.9 9.4 %collective-permute-done.86 = bf16[1024,256]{1,0:T(8,128)(2,1)S(1)} collective-permute-done((bf16[1024,256]{1,0:T(8,128)(2,1)S(1)}, bf16[1024,256]{1,0:T(8,128)(2,1)S(1)}, u32[]{:S(2)}, u32[]{:S(2)}) %collective-permute-start.86) | collective-permute-done | bytes 524320 | tf_op jit(solution)/shard_map/ppermute | solution.py:625
  517.3 11.0 %project_back.1 = (bf16[1024,512]{1,0:T(8,128)(2,1)}, bf16[1024,2048]{1,0:T(8,128)(2,1)}, f32[8,128]{1,0:T(8,128)}) custom-call(bf16[1024,256]{1,0:T(8,128)(2,1)} %get-tuple-element.443.dq_ref, bf16[1024,256]{1,0:T(8,128)(2,1)} %add_convert_fusion.11.dkv_ref, f32[1024,512]{1,0:T(8,128)} %get-tuple-element.445.raw_ref, f32[8,128]{1,0:T(8,128)} %pad.9.head_gain_ref, ...), custom_call_target="tpu_custom_call" | custom-call | flops 30000001024 | bytes 33554432 | tf_op jit(solution)/shard_map/project_back/pallas_call | solution.py:930
  537.5 8.9 %weight_grads.3 = (bf16[512,512]{1,0:T(8,128)(2,1)}, bf16[512,512]{1,0:T(8,128)(2,1)}, bf16[2,512,512]{2,1,0:T(8,128)(2,1)}) custom-call(s32[9]{0:T(128)} %pad_add_fusion.refs_0_.at_ref, bf16[1024,2048]{1,0:T(8,128)(2,1)} %get-tuple-element.453.refs_1_, bf16[1024,512]{1,0:T(8,128)(2,1)} %get-tuple-element.454.refs_2_), custom_call_target="tpu_custom_call" | custom-call | flops 1 | bytes 1 | tf_op jit(solution)/shard_map/weight_grads/pallas_call | solution.py:975
  556.6 8.2 %collective-permute-done.97 = f32[8,128]{1,0:T(8,128)S(1)} collective-permute-done((f32[8,128]{1,0:T(8,128)S(1)}, f32[8,128]{1,0:T(8,128)S(1)}, u32[]{:S(2)}, u32[]{:S(2)}) %collective-permute-start.97) | collective-permute-done | bytes 4128 | tf_op jit(solution)/shard_map/ppermute | solution.py:629
  571.9 9.3 %collective-permute-done.102 = f32[8,128]{1,0:T(8,128)S(1)} collective-permute-done((f32[8,128]{1,0:T(8,128)S(1)}, f32[8,128]{1,0:T(8,128)S(1)}, u32[]{:S(2)}, u32[]{:S(2)}) %collective-permute-start.102) | collective-permute-done | bytes 4128 | tf_op jit(solution)/shard_map/ppermute | solution.py:629
  597.7 12.4 %collective-permute-done.107 = f32[8,128]{1,0:T(8,128)S(1)} collective-permute-done((f32[8,128]{1,0:T(8,128)S(1)}, f32[8,128]{1,0:T(8,128)S(1)}, u32[]{:S(2)}, u32[]{:S(2)}) %collective-permute-start.107) | collective-permute-done | bytes 4128 | tf_op jit(solution)/shard_map/ppermute | solution.py:629
  (593 shorter events, 371.0 us)
Async XLA Ops:
  7.2 158.4 %all-gather.3.cloned.1.call-start = ((), (), s32[]{:S(2)}) async-start(), calls=%async_computation.2 | async-start | bytes 1310720 | tf_op jit(solution)/shard_map/all_gather | solution.py:1122
  7.3 22.8 %collective-permute-start.2 = (bf16[128,2048]{1,0:T(8,128)(2,1)}, bf16[128,2048]{1,0:T(8,128)(2,1)S(1)}, u32[]{:S(2)}, u32[]{:S(2)}) collective-permute-start(bf16[128,2048]{1,0:T(8,128)(2,1)} %bitcast.78), channel_id=1, source_target_pairs={{0,4},{8,0},{16,8},{24,16},{28,24},{20,28},{12,20},{4,12},{1,5},{9... | collective-permute-start | bytes 1572872 | tf_op jit(solution)/shard_map/ppermute | solution.py:621
  90.3 143.6 %all-gather.5.cloned.1.call-start = ((), (), s32[]{:S(2)}) async-start(), calls=%async_computation.3 | async-start | bytes 3932160 | tf_op jit(solution)/shard_map/all_gather | solution.py:1122
  91.0 32.0 %collective-permute-start.18 = (bf16[224,1536]{1,0:T(8,128)(2,1)}, bf16[224,1536]{1,0:T(8,128)(2,1)S(1)}, u32[]{:S(2)}, u32[]{:S(2)}) collective-permute-start(bf16[224,1536]{1,0:T(8,128)(2,1)} %get-tuple-element.273), channel_id=1, source_target_pairs={{0,8},{8,16},{16,24},{24,28},{28,20},{20,12},{12,4},{4,0},{1,9},{9... | collective-permute-start | bytes 2064392 | tf_op jit(solution)/shard_map/ppermute | solution.py:621
  92.3 31.6 %collective-permute-start.19 = (bf16[224,1536]{1,0:T(8,128)(2,1)S(1)}, bf16[224,1536]{1,0:T(8,128)(2,1)S(1)}, u32[]{:S(2)}, u32[]{:S(2)}) collective-permute-start(bf16[224,1536]{1,0:T(8,128)(2,1)S(1)} %get-tuple-element.274), channel_id=1, source_target_pairs={{0,4},{8,0},{16,8},{24,16},{28,24},{20,28},{12,20},{4,12},{1,5},{9... | collective-permute-start | bytes 2064392 | tf_op jit(solution)/shard_map/ppermute | solution.py:621
  126.8 460.1 %reduce-scatter.3.cloned.1.call-start = ((), (), s32[]{:S(2)}) async-start(), calls=%async_computation.4 | async-start | bytes 3932160 | tf_op jit(solution)/shard_map/reduce_scatter | solution.py:1126
  140.6 24.9 %collective-permute-start.26 = (bf16[128,2048]{1,0:T(8,128)(2,1)S(1)}, bf16[128,2048]{1,0:T(8,128)(2,1)S(1)}, u32[]{:S(2)}, u32[]{:S(2)}) collective-permute-start(bf16[128,2048]{1,0:T(8,128)(2,1)S(1)} %bitcast.76), channel_id=1, source_target_pairs={{0,4},{8,0},{16,8},{24,16},{28,24},{20,28},{12,20},{4,12},{1,5},{9... | collective-permute-start | bytes 1572872 | tf_op jit(solution)/shard_map/ppermute | solution.py:621
  142.7 22.8 %collective-permute-start.27 = (bf16[128,2048]{1,0:T(8,128)(2,1)S(1)}, bf16[128,2048]{1,0:T(8,128)(2,1)S(1)}, u32[]{:S(2)}, u32[]{:S(2)}) collective-permute-start(bf16[128,2048]{1,0:T(8,128)(2,1)S(1)} %bitcast.77), channel_id=1, source_target_pairs={{0,8},{8,16},{16,24},{24,28},{28,20},{20,12},{12,4},{4,0},{1,9},{9... | collective-permute-start | bytes 1572872 | tf_op jit(solution)/shard_map/ppermute | solution.py:621
  142.7 21.2 %collective-permute-start.28 = (bf16[96,1536]{1,0:T(8,128)(2,1)}, bf16[96,1536]{1,0:T(8,128)(2,1)S(1)}, u32[]{:S(2)}, u32[]{:S(2)}) collective-permute-start(bf16[96,1536]{1,0:T(8,128)(2,1)} %slice.479), channel_id=1, source_target_pairs={{0,8},{8,16},{16,24},{24,28},{28,20},{20,12},{12,4},{4,0},{1,9},{9... | collective-permute-start | bytes 884744 | tf_op jit(solution)/shard_map/ppermute | solution.py:621
  188.2 21.2 %collective-permute-start.35 = (bf16[128,2048]{1,0:T(8,128)(2,1)}, bf16[128,2048]{1,0:T(8,128)(2,1)}, u32[]{:S(2)}, u32[]{:S(2)}) collective-permute-start(bf16[128,2048]{1,0:T(8,128)(2,1)} %pad_maximum_fusion.8), channel_id=1, source_target_pairs={{0,4},{8,0},{16,8},{24,16},{28,24},{20,28},{12,20},{4,12},{1,5},{9... | collective-permute-start | bytes 1572872 | tf_op jit(solution)/shard_map/ppermute | solution.py:621
  189.7 21.1 %collective-permute-start.34 = (bf16[128,2048]{1,0:T(8,128)(2,1)}, bf16[128,2048]{1,0:T(8,128)(2,1)}, u32[]{:S(2)}, u32[]{:S(2)}) collective-permute-start(bf16[128,2048]{1,0:T(8,128)(2,1)} %pad_maximum_fusion.7), channel_id=1, source_target_pairs={{0,8},{8,16},{16,24},{24,28},{28,20},{20,12},{12,4},{4,0},{1,9},{9... | collective-permute-start | bytes 1572872 | tf_op jit(solution)/shard_map/ppermute | solution.py:621
  192.3 21.1 %collective-permute-start.36 = (bf16[128,2048]{1,0:T(8,128)(2,1)}, bf16[128,2048]{1,0:T(8,128)(2,1)S(1)}, u32[]{:S(2)}, u32[]{:S(2)}) collective-permute-start(bf16[128,2048]{1,0:T(8,128)(2,1)} %collective-permute-done.32.refs_3_.refs_7_), channel_id=1, source_target_pairs={{0,4},{8,0},{16,8},{24,16},{28,24},{20,28},{12,20},{4,12},{1,5},{9... | collective-permute-start | bytes 1572872 | tf_op jit(solution)/shard_map/ppermute | solution.py:621
  209.5 24.5 %collective-permute-start.42 = (bf16[512,1536]{1,0:T(8,128)(2,1)}, bf16[512,1536]{1,0:T(8,128)(2,1)}, u32[]{:S(2)}, u32[]{:S(2)}) collective-permute-start(bf16[512,1536]{1,0:T(8,128)(2,1)} %stack.3.refs_0_), channel_id=1, source_target_pairs={{0,1},{1,0},{2,3},{3,2},{4,5},{5,4},{6,7},{7,6},{8,9},{9,8},{10,11... | collective-permute-start | bytes 4718600 | tf_op jit(solution)/shard_map/ppermute | solution.py:625
  209.5 37.1 %collective-permute-start.43 = (bf16[512,1536]{1,0:T(8,128)(2,1)}, bf16[512,1536]{1,0:T(8,128)(2,1)}, u32[]{:S(2)}, u32[]{:S(2)}) collective-permute-start(bf16[512,1536]{1,0:T(8,128)(2,1)} %stack.3.refs_0_), channel_id=1, source_target_pairs={{0,2},{1,3},{2,0},{3,1},{4,6},{5,7},{6,4},{7,5},{8,10},{9,11},{10,... | collective-permute-start | bytes 4718600 | tf_op jit(solution)/shard_map/ppermute | solution.py:625
  381.1 45.2 %collective-permute-start.68 = (bf16[512,1536]{1,0:T(8,128)(2,1)}, bf16[512,1536]{1,0:T(8,128)(2,1)}, u32[]{:S(2)}, u32[]{:S(2)}) collective-permute-start(bf16[512,1536]{1,0:T(8,128)(2,1)} %get-tuple-element.385), channel_id=1, source_target_pairs={{0,2},{1,3},{2,0},{3,1},{4,6},{5,7},{6,4},{7,5},{8,10},{9,11},{10,... | collective-permute-start | bytes 4718600 | tf_op jit(solution)/shard_map/ppermute | solution.py:625
  432.0 32.2 %collective-permute-start.76 = (bf16[128,2048]{1,0:T(8,128)(2,1)}, bf16[128,2048]{1,0:T(8,128)(2,1)}, u32[]{:S(2)}, u32[]{:S(2)}) collective-permute-start(bf16[128,2048]{1,0:T(8,128)(2,1)} %pad_maximum_fusion.13), channel_id=1, source_target_pairs={{0,4},{8,0},{16,8},{24,16},{28,24},{20,28},{12,20},{4,12},{1,5},{9... | collective-permute-start | bytes 1572872 | tf_op jit(solution)/shard_map/ppermute | solution.py:621
  433.5 30.7 %collective-permute-start.75 = (bf16[128,2048]{1,0:T(8,128)(2,1)}, bf16[128,2048]{1,0:T(8,128)(2,1)}, u32[]{:S(2)}, u32[]{:S(2)}) collective-permute-start(bf16[128,2048]{1,0:T(8,128)(2,1)} %pad_maximum_fusion.12), channel_id=1, source_target_pairs={{0,8},{8,16},{16,24},{24,28},{28,20},{20,12},{12,4},{4,0},{1,9},{9... | collective-permute-start | bytes 1572872 | tf_op jit(solution)/shard_map/ppermute | solution.py:621
  434.0 32.7 %collective-permute-start.77 = (bf16[224,1536]{1,0:T(8,128)(2,1)}, bf16[224,1536]{1,0:T(8,128)(2,1)S(1)}, u32[]{:S(2)}, u32[]{:S(2)}) collective-permute-start(bf16[224,1536]{1,0:T(8,128)(2,1)} %get-tuple-element.410), channel_id=1, source_target_pairs={{0,8},{8,16},{16,24},{24,28},{28,20},{20,12},{12,4},{4,0},{1,9},{9... | collective-permute-start | bytes 2064392 | tf_op jit(solution)/shard_map/ppermute | solution.py:621
  435.8 31.9 %collective-permute-start.78 = (bf16[224,1536]{1,0:T(8,128)(2,1)}, bf16[224,1536]{1,0:T(8,128)(2,1)}, u32[]{:S(2)}, u32[]{:S(2)}) collective-permute-start(bf16[224,1536]{1,0:T(8,128)(2,1)} %get-tuple-element.411), channel_id=1, source_target_pairs={{0,4},{8,0},{16,8},{24,16},{28,24},{20,28},{12,20},{4,12},{1,5},{9... | collective-permute-start | bytes 2064392 | tf_op jit(solution)/shard_map/ppermute | solution.py:621
  471.6 124.3 %reduce-scatter.5.cloned.1.call-start = ((), (), s32[]{:S(2)}) async-start(), calls=%async_computation.5 | async-start | bytes 1310720 | tf_op jit(solution)/shard_map/reduce_scatter | solution.py:1126
  489.7 24.6 %collective-permute-start.86 = (bf16[1024,256]{1,0:T(8,128)(2,1)S(1)}, bf16[1024,256]{1,0:T(8,128)(2,1)S(1)}, u32[]{:S(2)}, u32[]{:S(2)}) collective-permute-start(bf16[1024,256]{1,0:T(8,128)(2,1)S(1)} %get-tuple-element.440), channel_id=1, source_target_pairs={{0,2},{1,3},{2,0},{3,1},{4,6},{5,7},{6,4},{7,5},{8,10},{9,11},{10,... | collective-permute-start | bytes 1572872 | tf_op jit(solution)/shard_map/ppermute | solution.py:625
  589.5 21.7 %collective-permute-start.103 = (bf16[128,2048]{1,0:T(8,128)(2,1)}, bf16[128,2048]{1,0:T(8,128)(2,1)}, u32[]{:S(2)}, u32[]{:S(2)}) collective-permute-start(bf16[128,2048]{1,0:T(8,128)(2,1)} %get-tuple-element.475), channel_id=1, source_target_pairs={{0,8},{8,16},{16,24},{24,28},{28,20},{20,12},{12,4},{4,0},{1,9},{9... | collective-permute-start | bytes 1572872 | tf_op jit(solution)/shard_map/ppermute | solution.py:621
  611.2 33.3 %collective-permute-start.109 = (bf16[128,2048]{1,0:T(8,128)(2,1)}, bf16[128,2048]{1,0:T(8,128)(2,1)S(1)}, u32[]{:S(2)}, u32[]{:S(2)}) collective-permute-start(bf16[128,2048]{1,0:T(8,128)(2,1)} %get-tuple-element.484), channel_id=1, source_target_pairs={{0,4},{8,0},{16,8},{24,16},{28,24},{20,28},{12,20},{4,12},{1,5},{9... | collective-permute-start | bytes 1572872 | tf_op jit(solution)/shard_map/ppermute | solution.py:621
  611.4 33.1 %collective-permute-start.108 = (bf16[128,2048]{1,0:T(8,128)(2,1)}, bf16[128,2048]{1,0:T(8,128)(2,1)}, u32[]{:S(2)}, u32[]{:S(2)}) collective-permute-start(bf16[128,2048]{1,0:T(8,128)(2,1)} %get-tuple-element.483), channel_id=1, source_target_pairs={{0,8},{8,16},{16,24},{24,28},{28,20},{20,12},{12,4},{4,0},{1,9},{9... | collective-permute-start | bytes 1572872 | tf_op jit(solution)/shard_map/ppermute | solution.py:621
  (191 other events, 2230.3 us)
Sparse Core Ops, SparseCore 0:
  90.5 17.9 all-gather.2
  127.0 29.5 all-gather.4
  471.7 49.4 reduce-scatter.2
  552.5 24.4 reduce-scatter.4

commit v8 on v7

--- a/solution.py
+++ b/solution.py
@@ -428,15 +428,11 @@
 def sort_strips(order_ref, kv_refs, keys, values):
     per = kv_refs[0].shape[0] // STRIP
     for j, ref in enumerate(kv_refs):
-
-        def sort(i, carry, j=j, ref=ref):
+        for i in range(per):
             target = pl.multiple_of(order_ref[j * per + i] * STRIP, STRIP)
-            here = pl.ds(pl.multiple_of(i * STRIP, STRIP), STRIP)
+            here = slice(i * STRIP, (i + 1) * STRIP)
             keys[pl.ds(target, STRIP), :] = ref[here, :HEAD_SIZE]
             values[pl.ds(target, STRIP), :HEAD_SIZE] = ref[here, HEAD_SIZE:]
-            return carry
-
-        lax.fori_loop(0, per, sort, 0)
 
 
 def attend_kernel(place_ref, order_ref, q_ref, *refs):
@@ -559,19 +555,15 @@
         for j in range(4):
             target = (own_ref, far_ref, sent_ref, sent_ref)[j]
             base = per if j == 3 else 0
-
-            def spread(i, carry, j=j, target=target, base=base):
+            for i in range(per):
                 source = pl.multiple_of(order_ref[j * per + i] * STRIP, STRIP)
-                here = pl.ds(pl.multiple_of((base + i) * STRIP, STRIP), STRIP)
+                here = slice((base + i) * STRIP, (base + i + 1) * STRIP)
                 target[here, :HEAD_SIZE] = (
                     key_sums[pl.ds(source, STRIP), :] * (1.0 / LOG2E)
                 ).astype(jnp.bfloat16)
                 target[here, HEAD_SIZE:] = value_sums[pl.ds(source, STRIP), :].astype(
                     jnp.bfloat16
                 )
-                return carry
-
-            lax.fori_loop(0, per, spread, 0)
 
 
 def attend_back(place, order, queries, grads, attended, lse, kv):
@@ -625,10 +617,6 @@
     return lax.ppermute(value, "head", [(i, i ^ by) for i in range(4)])
 
 
-def mirror(value, by):
-    return lax.ppermute(value, "blk", [(i, i ^ by) for i in range(len(RING))])
-
-
 def add(left, right):
     return (left.astype(jnp.float32) + right.astype(jnp.float32)).astype(left.dtype)
 
@@ -812,44 +800,28 @@
     each = pieces[0].shape[0] // 8
     rows = matrix_ref.shape[0] // 32
     own = at_ref[8]
-    gains_ref[...] = jnp.zeros_like(gains_ref)
-
-    def place(s, carry):
-        piece_at = pl.multiple_of(s * each, 16)
+    gains = jnp.zeros(gains_ref.shape, jnp.float32)
+    for s in range(8):
         for j in range(4):
             first = pl.multiple_of((at_ref[s] * 4 + (own ^ j)) * rows, rows)
-            matrix_ref[pl.ds(first, rows), :] = pieces[j][pl.ds(piece_at, rows), :]
-            gains_ref[...] += pieces[j][
-                pl.ds(pl.multiple_of(piece_at + rows, 16), each - rows), :
-            ].astype(jnp.float32)
-        return carry
-
-    lax.fori_loop(0, 8, place, 0)
-    width = gains_ref.shape[1]
+            matrix_ref[pl.ds(first, rows), :] = pieces[j][s * each : s * each + rows, :]
+            gains += pieces[j][s * each + rows : (s + 1) * each, :].astype(jnp.float32)
+    gains_ref[...] = gains
+    width = gains.shape[1]
     first = 0
     for ref in token_refs:
-        normed_ref[first : first + ref.shape[0], :] = ref[...]
-        first += ref.shape[0]
-
-    def norm(index, carry):
-        here = pl.ds(pl.multiple_of(index * 32, 32), 32)
-        block = normed_ref[here, :].astype(jnp.float32)
+        block = ref[...].astype(jnp.float32)
         block = block * inverse_rms(block)
+        here = slice(first, first + ref.shape[0])
         for i in range(block.shape[1] // width):
             cols = slice(i * width, (i + 1) * width)
-            normed_ref[here, cols] = (block[:, cols] * gains_ref[i : i + 1, :]).astype(
-                jnp.bfloat16
-            )
-        return carry
-
-    lax.fori_loop(0, normed_ref.shape[0] // 32, norm, 0)
-    query_gain = gains_ref[8:9, :HEAD_SIZE]
-    key_gain = gains_ref[8:9, HEAD_SIZE : 2 * HEAD_SIZE]
+            normed_ref[here, cols] = (block[:, cols] * gains[i : i + 1]).astype(jnp.bfloat16)
+        first += ref.shape[0]
+    query_gain, key_gain = gains[8:9, :HEAD_SIZE], gains[8:9, HEAD_SIZE : 2 * HEAD_SIZE]
     query_cols = q_ref.shape[1]
     step = 256
-
-    def heads(index, carry):
-        here = pl.ds(pl.multiple_of(index * step, step), step)
+    for first in range(0, q_ref.shape[0], step):
+        here = slice(first, first + step)
         raw = jnp.dot(normed_ref[here, :], matrix_ref[...], preferred_element_type=jnp.float32)
         raw_ref[here, :] = raw
         cosine, sine = cos_ref[here, :], sin_ref[here, :]
@@ -863,9 +835,6 @@
                 part = spun(part * inverse_rms(part) * key_gain, cosine, sine)
                 kv_ref[here, :HEAD_SIZE] = part.astype(jnp.bfloat16)
         kv_ref[here, HEAD_SIZE:] = raw[:, query_cols + HEAD_SIZE :].astype(jnp.bfloat16)
-        return carry
-
-    lax.fori_loop(0, q_ref.shape[0] // step, heads, 0)
 
 
 def project(at, strips, pieces, cosine, sine, query_cols, pad):
@@ -899,9 +868,8 @@
     query_cols = dq_ref.shape[1]
     step = 256
     gain_ref[...] = jnp.zeros_like(gain_ref)
-
-    def block(index, carry):
-        here = pl.ds(pl.multiple_of(index * step, step), step)
+    for first in range(0, dq_ref.shape[0], step):
+        here = slice(first, first + step)
         cosine, sine = cos_ref[here, :], sin_ref[here, :]
         for col in range(0, query_cols + HEAD_SIZE, HEAD_SIZE):
             cols = slice(col, col + HEAD_SIZE)
@@ -919,9 +887,6 @@
         part_ref[here, :] = lax.dot_general(
             grad_ref[here, :], matrix_ref[...], ALONG, preferred_element_type=jnp.float32
         ).astype(jnp.bfloat16)
-        return carry
-
-    lax.fori_loop(0, dq_ref.shape[0] // step, block, 0)
 
 
 def project_back(query_grads, kv_grads, raw, head_gains, cosine, sine, matrix):
@@ -942,38 +907,38 @@
 
 
 def dots(lefts, rights, dims):
-    if len(lefts) == 1:
-        parts, first = [], 0
-        for right in rights:
-            parts.append(lefts[0][first : first + right.shape[0], :])
-            first += right.shape[0]
-    else:
-        parts = [left[...] for left in lefts]
     return sum(
-        lax.dot_general(part, right[...], dims, preferred_element_type=jnp.float32)
-        for part, right in zip(parts, rights)
-    )
-
-
-def weight_grads_kernel(at_ref, *refs, groups):
+        lax.dot_general(left[...], right[...], dims, preferred_element_type=jnp.float32)
+        for left, right in zip(lefts, rights)
+    )
+
+
+def weight_grads_kernel(at_ref, *refs, groups, rows):
     own_ref, far_ref, sent_ref, held = refs[-4:]
     own = at_ref[8]
     sums = dots(refs[:groups], refs[groups : 2 * groups], DOWN)
     held[...] = sums.astype(jnp.bfloat16).reshape(held.shape)
-    own_ref[...] = held[own]
-    far_ref[...] = held[own ^ 2]
-    sent_ref[0] = held[own ^ 1]
-    sent_ref[1] = held[own ^ 3]
-
-
-def weight_grads(at, lefts, rights, rows):
+    own_ref[:rows, :] = held[own]
+    far_ref[:rows, :] = held[own ^ 2]
+    sent_ref[0, :rows] = held[own ^ 1]
+    sent_ref[1, :rows] = held[own ^ 3]
+    if own_ref.shape[0] > rows:
+        pad = refs[2 * groups][...]
+        own_ref[rows:, :] = pad
+        far_ref[rows:, :] = pad
+        sent_ref[0, rows:] = pad
+        sent_ref[1, rows:] = pad
+
+
+def weight_grads(at, lefts, rights, rows, pad=None):
     count = at.shape[0] - 1
     cols = rights[0].shape[1]
-    total = sum(left.shape[0] for left in lefts)
-    part = pl.BlockSpec((rows, cols), lambda i, at: (i, 0))
-    shape = jax.ShapeDtypeStruct((count * rows, cols), jnp.bfloat16)
+    pads = [] if pad is None else [pad]
+    each = rows + sum(p.shape[0] for p in pads)
+    part = pl.BlockSpec((each, cols), lambda i, at: (i, 0))
+    shape = jax.ShapeDtypeStruct((count * each, cols), jnp.bfloat16)
     own, far, sent = pl.pallas_call(
-        lambda *refs: weight_grads_kernel(*refs, groups=len(lefts)),
+        lambda *refs: weight_grads_kernel(*refs, groups=len(lefts), rows=rows),
         grid_spec=pltpu.PrefetchScalarGridSpec(
             num_scalar_prefetch=1,
             grid=(count,),
@@ -981,17 +946,17 @@
                 pl.BlockSpec((left.shape[0], 4 * rows), lambda i, at: (0, at[i]))
                 for left in lefts
             ]
-            + [pl.BlockSpec(right.shape, lambda i, at: (0, 0)) for right in rights],
-            out_specs=[part, part, pl.BlockSpec((2, rows, cols), lambda i, at: (0, i, 0))],
+            + [pl.BlockSpec(right.shape, lambda i, at: (0, 0)) for right in (*rights, *pads)],
+            out_specs=[part, part, pl.BlockSpec((2, each, cols), lambda i, at: (0, i, 0))],
             scratch_shapes=[pltpu.VMEM((4, rows, cols), jnp.bfloat16)],
         ),
         out_shape=[
-            shape, shape, jax.ShapeDtypeStruct((2, count * rows, cols), jnp.bfloat16),
+            shape, shape, jax.ShapeDtypeStruct((2, count * each, cols), jnp.bfloat16),
         ],
         cost_estimate=CHEAP,
         name="weight_grads",
-    )(at, *lefts, *rights)
-    return own, far, sent.reshape(2 * count * rows, cols)
+    )(at, *lefts, *rights, *pads)
+    return own, far, sent.reshape(2 * count * each, cols)
 
 
 def row_grads_kernel(*refs, lefts):
@@ -1075,24 +1040,31 @@
 
 def widen(at, swap, *weights):
     rows, taken, count = weights[0].shape[0], [item[1:] for item in swap.taken], len(weights)
+    pad = swap.rows - rows
 
     def widen_kernel(at_ref, *refs):
         piece_refs, refs = refs[: len(taken)], refs[len(taken) :]
         grads, sums_ref = refs[count : 2 * count], refs[2 * count]
-        sums_ref[...] = jnp.zeros_like(sums_ref)
+        for ref in refs[2 * count :]:
+            ref[...] = jnp.zeros_like(ref)
         for ref, (start, size, spot, top) in zip(piece_refs, taken):
-            here = slice(top, top + size)
+            used = min(size, rows - top)
+            here = slice(top, top + used)
             first = 0
             for weight, grad in zip(refs[:count], grads):
                 width = weight.shape[1] // 8
                 there = columns(at_ref[spot], width)
-                block = ref[start : start + size, first : first + width].astype(jnp.float32)
+                block = ref[start : start + used, first : first + width].astype(jnp.float32)
                 grad[here, there] = block
                 sums_ref[here, :] += lane_sums(block * weight[here, there].astype(jnp.float32))
                 first += width
+            if used < size:
+                refs[-1][...] += ref[start + used : start + size, :].astype(jnp.float32)
 
     vmem = pl.BlockSpec(memory_space=pltpu.VMEM)
     shapes = [w.shape for w in weights] + [(rows, 128)]
+    if pad:
+        shapes.append((pad, swap.taken[0][0].shape[1]))
     return pl.pallas_call(
         widen_kernel,
         grid=(1,),
@@ -1209,22 +1181,23 @@
     ff_slices = slice_pieces(at, gate_weight, up_weight)
     token_ring.go()
     attn_swap.go()
-    hold((attn_swap, token_ring))
-    token_ring.go()
-    attn_swap.go()
-    ff_slices, cosine, sine = hold((attn_swap, token_ring), ff_slices, cosine, sine)
-    token_ring.go()
+    hold((attn_swap,))
     attn_swap.go()
     hold((attn_swap,))
     attn_swap.go()
-    own = hold((), attn_swap.result())
+    hold((attn_swap,))
+    attn_swap.go()
+    own = hold((token_ring,), attn_swap.result())
     near, far = cross(own, 1), cross(own, 2)
+    token_ring.go()
+    ff_slices, cosine, sine = hold((token_ring,), ff_slices, cosine, sine)
     ff_swap, cotangent_ring = Swap(ff_slices, weight_rows), Gather(out_cotangent)
-    hold((token_ring, ff_swap, cotangent_ring))
     token_ring.go()
-    own, near, far = hold((token_ring, ff_swap), own, near, far)
+    own, near, far = hold((token_ring,), own, near, far)
+    both = cross(far, 1)
+    token_ring.go()
+    own, near, far, both = hold((token_ring, ff_swap), own, near, far, both)
     ff_swap.go()
-    both = hold((), cross(far, 1))
 
     first_normed, attn_raw, query_rows, own, attn_matrix, gains = project(
         at_own, token_ring.strips(), (own, near, far, both), cosine, sine, query_cols, pad
@@ -1233,13 +1206,11 @@
     gain_two = gains[4:8].reshape(1, model_width)
     head_gains = jnp.pad(gains[8, : 2 * HEAD_SIZE].reshape(2, HEAD_SIZE), ((0, 6), (0, 0)))
     near, far = cross(own, 1), cross(own, 2)
-    hold((ff_swap,))
-    ff_swap.go()
-    own, near, far = hold((), own, near, far)
+    own, near, far = hold((ff_swap, cotangent_ring), own, near, far)
     both = cross(far, 1)
-    kv = hold((ff_swap, cotangent_ring), own, far, near, both)
     ff_swap.go()
     cotangent_ring.go()
+    kv = hold((), own, far, near, both)
     attended, lse = attend(place, order, query_rows, kv)
 
     def by_groups(rows):
@@ -1252,25 +1223,24 @@
     branch_parts = [matmul(rows, output_rows).astype(narrow) for rows in by_groups(attended)]
     branch_ring = Scatter(by_strips(branch_parts))
     branch_ring.go()
+    ff_swap.go()
     cotangent_ring.go()
+    hold((branch_ring, cotangent_ring, ff_swap))
+    branch_ring.go()
     ff_swap.go()
     ff_own = hold((), ff_swap.result())
     ff_near, ff_far = cross(ff_own, 1), cross(ff_own, 2)
-    hold((branch_ring, cotangent_ring))
-    branch_ring.go()
     cotangent_ring.go()
     hold((branch_ring, cotangent_ring))
     branch_ring.go()
     cotangent_ring.go()
-    ff_near, ff_far, cotangent_strips, down_matrix = hold(
-        (branch_ring, cotangent_ring), ff_near, ff_far, cotangent_ring.strips(), down_matrix
+    cotangent_strips, down_matrix = hold(
+        (branch_ring, cotangent_ring), cotangent_ring.strips(), down_matrix
     )
     branch_ring.go()
+    hidden_grads = hidden_grads_of(cotangent_strips, down_matrix)
+    hidden_grads, ff_near, ff_far = hold((branch_ring,), hidden_grads, ff_near, ff_far)
     ff_both = cross(ff_far, 1)
-    hidden_grads = hidden_grads_of(cotangent_strips, down_matrix)
-    ff_own, ff_near, ff_far, hidden_grads, ff_both = hold(
-        (branch_ring,), ff_own, ff_near, ff_far, hidden_grads, ff_both
-    )
     tokens_wide = tokens.astype(wide)
     resid = tokens_wide + branch_ring.total()
     rho_two = inverse_rms(resid)
@@ -1314,11 +1284,15 @@
     parts[3], parts[5] = split(hold((), back(2)))
     parts[2], parts[6] = split(hold((), back(1)))
     resid_ring.go()
-    hold((resid_ring,), parts[2], parts[6])
+    _, _, hidden_groups, cotangent_strips = hold(
+        (resid_ring,), parts[2], parts[6], hidden_groups, cotangent_strips
+    )
     resid_ring.go()
-    back_zero, second_groups, ff_gradient_groups = hold(
-        (resid_ring,), back(0), second_groups, ff_gradient_groups
-    )
+    down_gradient = row_grads(hidden_groups, cotangent_strips)
+    back_zero, down_gradient, second_groups, ff_gradient_groups = hold(
+        (resid_ring,), back(0), down_gradient, second_groups, ff_gradient_groups
+    )
+    down_gradient = scatter_head(down_gradient)
     parts[0], parts[1], parts[7] = split(back_zero)
     resid_ring.go()
     ff_own, ff_far, ff_sent = hold(
@@ -1326,9 +1300,7 @@
     )
     resid_ring.go()
     ff_own, ff_far = scatter_cross(ff_own, ff_far, ff_sent)
-    ff_own, ff_far, hidden_groups, cotangent_strips = hold(
-        (resid_ring,), ff_own, ff_far, hidden_groups, cotangent_strips
-    )
+    ff_own, ff_far, hidden_groups = hold((resid_ring,), ff_own, ff_far, hidden_groups)
     ff_far = cross(ff_far, 2)
     scaled = gain_two * resid_ring.total()
     resid_gradient = out_cotangent.astype(wide) + rho_two * (
@@ -1348,12 +1320,10 @@
 
     grad_ring.go()
     out_parts = [matmul(rows, down_matrix).astype(narrow) for rows in hidden_groups]
-    out_parts, hidden_groups = hold((grad_ring,), out_parts, hidden_groups)
+    out_parts = hold((grad_ring,), *out_parts)
     out_ring = Scatter(by_strips(out_parts))
     grad_ring.go()
-    down_gradient = row_grads(hidden_groups, cotangent_strips)
-    down_gradient = hold((grad_ring,), down_gradient)
-    down_gradient = scatter_head(down_gradient)
+    hold((grad_ring,))
     grad_ring.go()
     attention_back(0)
     hold((out_ring, grad_ring))
@@ -1378,49 +1348,46 @@
     kv_own, kv_far, output_weight_gradient = hold(
         (out_ring, ff_swap), kv_own, kv_far, output_weight_gradient
     )
-    output_weight_gradient = scatter_head(output_weight_gradient)
     ff_swap.go()
     kv_grads = hold((ff_swap,), add(kv_own, cross(kv_far, 2)))
     ff_swap.go()
     attn_gradient, first_parts, gain_sums = project_back(
         query_grads, kv_grads, attn_raw, head_gains, cosine, sine, attn_matrix
     )
-    attn_gradient, first_parts, gain_sums = hold(
-        (ff_swap,), attn_gradient, first_parts, gain_sums
+    gain_sums = jnp.pad(
+        gain_sums[:2].reshape(1, 2 * HEAD_SIZE).astype(narrow),
+        ((0, pad - 1), (0, attn_cols - 2 * HEAD_SIZE)),
+    )
+    attn_gradient, first_parts, gain_sums, output_weight_gradient = hold(
+        (ff_swap,), attn_gradient, first_parts, gain_sums, output_weight_gradient
     )
     token_ring = Scatter(by_strips(by_groups(first_parts)))
     token_ring.go()
     ff_swap.go()
-    gain_sums = gain_sums + cross(gain_sums, 1)
-    gain_sums = gain_sums + cross(gain_sums, 2)
     attn_own, attn_far, attn_sent = weight_grads(
-        at_own, [first_normed], [attn_gradient], weight_rows
-    )
-    attn_own, attn_far, attn_sent, gain_sums = hold(
-        (token_ring, ff_swap), attn_own, attn_far, attn_sent, gain_sums
+        at_own, [first_normed], [attn_gradient], weight_rows, gain_sums
+    )
+    attn_own, attn_far, attn_sent = hold(
+        (token_ring, ff_swap), attn_own, attn_far, attn_sent
     )
     token_ring.go()
     attn_own, attn_far = hold((), *scatter_cross(attn_own, attn_far, attn_sent))
     attn_far = cross(attn_far, 2)
-    gain_sums = gain_sums + mirror(gain_sums, 1)
     gate_weight_gradient, up_weight_gradient, ff_sums = widen(at, ff_swap, gate_weight, up_weight)
-    gate_weight_gradient, up_weight_gradient, ff_sums, gain_sums = hold(
-        (token_ring,), gate_weight_gradient, up_weight_gradient, ff_sums, gain_sums
+    gate_weight_gradient, up_weight_gradient, ff_sums = hold(
+        (token_ring,), gate_weight_gradient, up_weight_gradient, ff_sums
     )
     token_ring.go()
-    gain_sums = gain_sums + mirror(gain_sums, 2)
     feedforward_norm_gradient = jnp.sum(ff_sums, axis=1) / feedforward_norm.astype(wide)
-    attn_swap = Swap(add(attn_own, attn_far), weight_rows)
-    feedforward_norm_gradient, gain_sums, down_gradient = hold(
+    attn_swap = Swap(add(attn_own, attn_far), weight_rows + pad)
+    feedforward_norm_gradient, down_gradient, output_weight_gradient = hold(
         (token_ring, attn_swap),
-        feedforward_norm_gradient, gain_sums, down_gradient.astype(wide),
-    )
+        feedforward_norm_gradient, down_gradient.astype(wide), output_weight_gradient,
+    )
+    output_weight_gradient = scatter_head(output_weight_gradient).astype(wide)
     attn_swap.go()
     token_ring.go()
-    gain_sums = gain_sums + mirror(gain_sums, 4)
-    output_weight_gradient, gain_sums = hold(
-        (token_ring, attn_swap, out_ring), output_weight_gradient.astype(wide), gain_sums
-    )
+    hold((token_ring, attn_swap, out_ring))
     attn_swap.go()
     out_ring.go()
     hold((attn_swap,))
@@ -1428,10 +1395,11 @@
     hold((attn_swap,))
     attn_swap.go()
     layer_out = (resid + out_ring.total()).astype(narrow)
-    query_weight_gradient, key_weight_gradient, value_weight_gradient, norm_sums = widen(
+    query_weight_gradient, key_weight_gradient, value_weight_gradient, norm_sums, gain_sums = widen(
         at, attn_swap, query_weight, key_projection, value_projection
     )
     attention_norm_gradient = jnp.sum(norm_sums, axis=1) / attention_norm.astype(wide)
+    gain_sums = gain_sums[0, : 2 * HEAD_SIZE].reshape(2, HEAD_SIZE)
     gain_sums = lax.dynamic_slice_in_dim(gain_sums, number * small, small, 1)
     rho_one = inverse_rms(tokens_wide)
     unit_one = tokens_wide * rho_one

time: 666 us -> 659 us (0.989)
  Pallas kernels: 141 us -> 134 us
  starting transfers between devices: 117 us -> 110 us
    ppermute x96, waiting for transfers between devices: 174 us -> 224 us  [hop(): lax.ppermute(value, 'blk', [(RING[i], RING[(i + by) % count]) for i in ra...]
    ppermute x3 -> x0, waiting for transfers between devices: 30 us -> none  [mirror(): return lax.ppermute(value, 'blk', [(i, i ^ by) for i in range(len(RING))])]
    ppermute x17 -> x15, waiting for transfers between devices: 45.2 us -> 28.9 us  [cross(): return lax.ppermute(value, 'head', [(i, i ^ by) for i in range(4)])]
  transfers between devices with their start and end apart: 120 -> 115, of which waited for: 61 -> 59; matrix products, arithmetic and copies ran while one was open for 16% -> 17% of each run, Pallas kernels for 22% -> 19%
where the time goes in v8:
time: 659 us; the launch traced here: 648 us
  waiting for transfers between devices  253 us (38%)
  Pallas kernels  134 us (20%)
  starting transfers between devices  110 us (17%)
  other arithmetic  65.4 us (10%)
  matrix products  36.6 us (6%)
  local copies, waits for them, and re-layouts  33 us (5%)
  between operations  15.7 us (2%)
    ppermute x96, waiting for transfers between devices, hop(): lax.ppermute(value, 'blk', [(RING[i], RING[(i + by) % count]) for i in ra...  224 us
    ppermute x96, starting transfers between devices, hop(): lax.ppermute(value, 'blk', [(RING[i], RING[(i + by) % count]) for i in ra...  101 us
    dot_general x20, matrix products, matmul(): lax.dot_general(left, right, dims, preferred_element_type=jnp.float32)  36.6 us
    ppermute x15, waiting for transfers between devices, cross(): return lax.ppermute(value, 'head', [(i, i ^ by) for i in range(4)])  28.9 us
    convert_element_type x18, other arithmetic, add(): (left.astype(jnp.float32) + right.astype(jnp.float32)).astype(left.dtype)  27.1 us
    pallas_call x1, Pallas kernels, attend_back(): pl.pallas_call(lambda *refs: attend_back_kernel(*refs, groups=len(grads))...  26.1 us
    pallas_call x2, Pallas kernels, weight_grads(): pl.pallas_call(lambda *refs: weight_grads_kernel(*refs, groups=len(lefts)...  23.4 us
    pallas_call x1, Pallas kernels, attend(): pl.pallas_call(attend_kernel, grid_spec=pltpu.PrefetchScalarGridSpec(num_...  18.6 us
  transfers between devices with their start and end apart: 115, of which 59 were waited for; matrix products, arithmetic and copies ran while one was open for 17% of the time, Pallas kernels for 19%

profile of v8, /device:TPU:0, one launch (start us, length us, event | category | flops | bytes accessed | tf_op | source)
XLA Modules:
  0.0 648.1 jit_solution(6010311512249814960)
XLA Ops:
  18.8 11.2 %collective-permute-done.2.refs_1_ = bf16[280,512]{1,0:T(8,128)(2,1)S(1)} collective-permute-done((bf16[280,512]{1,0:T(8,128)(2,1)S(1)}, bf16[280,512]{1,0:T(8,128)(2,1)S(1)}, u32[]{:S(2)}, u32[]{:S(2)}) %collective-permute-start.2) | collective-permute-done | bytes 286752 | tf_op jit(solution)/shard_map/ppermute | solution.py:613
  64.2 13.4 %collective-permute-done.15.refs_11_ = bf16[640,512]{1,0:T(8,128)(2,1)} collective-permute-done((bf16[640,512]{1,0:T(8,128)(2,1)S(1)}, bf16[640,512]{1,0:T(8,128)(2,1)}, u32[]{:S(2)}, u32[]{:S(2)}) %collective-permute-start.15) | collective-permute-done | bytes 655392 | tf_op jit(solution)/shard_map/ppermute | solution.py:617
  88.4 9.9 %project.1 = (bf16[1024,2048]{1,0:T(8,128)(2,1)}, f32[1024,512]{1,0:T(8,128)}, bf16[1024,256]{1,0:T(8,128)(2,1)}, bf16[1024,256]{1,0:T(8,128)(2,1)}, bf16[2048,512]{1,0:T(8,128)(2,1)}, /*index=5*/f32[16,512]{1,0:T(8,128)}) custom-call(s32[9]{0:T(128)} %pad_add_fusion.refs_0_.at_ref, bf16[128,2048]{1,0:T(8,128)(2,1)} %bitcast.85, ...), custom_call_target="tpu_custom_call" | custom-call | flops 30000001024 | bytes 33554432 | tf_op jit(solution)/shard_map/project/pallas_call | solution.py:847
  104.2 9.6 %collective-permute-done.22.refs_1_.refs_10_ = bf16[1024,256]{1,0:T(8,128)(2,1)} collective-permute-done((bf16[1024,256]{1,0:T(8,128)(2,1)}, bf16[1024,256]{1,0:T(8,128)(2,1)}, u32[]{:S(2)}, u32[]{:S(2)}) %collective-permute-start.22) | collective-permute-done | bytes 524320 | tf_op jit(solution)/shard_map/ppermute | solution.py:617
  118.0 10.2 %collective-permute-done.25.refs_3_ = bf16[160,1536]{1,0:T(8,128)(2,1)} collective-permute-done((bf16[160,1536]{1,0:T(8,128)(2,1)}, bf16[160,1536]{1,0:T(8,128)(2,1)}, u32[]{:S(2)}, u32[]{:S(2)}) %collective-permute-start.25) | collective-permute-done | bytes 491552 | tf_op jit(solution)/shard_map/ppermute | solution.py:613
  131.7 18.6 %attend.1 = (bf16[1024,256]{1,0:T(8,128)(2,1)}, f32[8,8,256]{2,1,0:T(8,128)}) custom-call(s32[8]{0:T(128)} %get-tuple-element.571.place_ref.refs_0_, s32[32]{0:T(128)} %copy-done.81, bf16[1024,256]{1,0:T(8,128)(2,1)} %get-tuple-element.283.q_ref.refs_2_, bf16[1024,256]{1,0:T(8,128)(2,1)} %get-tuple-element.287.refs_0_.refs_9_, ...), custom_call_target="tpu_custom_call" | custom-call | flops 30000001024 | bytes 33554432 | tf_op jit(solution)/shard_map/attend/pallas_call | solution.py:480
  162.4 15.6 %collective-permute-done.32.refs_5_ = bf16[96,1536]{1,0:T(8,128)(2,1)S(1)} collective-permute-done((bf16[96,1536]{1,0:T(8,128)(2,1)}, bf16[96,1536]{1,0:T(8,128)(2,1)S(1)}, u32[]{:S(2)}, u32[]{:S(2)}) %collective-permute-start.32) | collective-permute-done | bytes 294944 | tf_op jit(solution)/shard_map/ppermute | solution.py:613
  183.6 9.3 %collective-permute-done.35 = bf16[128,2048]{1,0:T(8,128)(2,1)S(1)} collective-permute-done((bf16[128,2048]{1,0:T(8,128)(2,1)S(1)}, bf16[128,2048]{1,0:T(8,128)(2,1)S(1)}, u32[]{:S(2)}, u32[]{:S(2)}) %collective-permute-start.35) | collective-permute-done | bytes 524320 | tf_op jit(solution)/shard_map/ppermute | solution.py:613
  222.5 14.6 %collective-permute-done.40 = bf16[64,2048]{1,0:T(8,128)(2,1)S(1)} collective-permute-done((bf16[64,2048]{1,0:T(8,128)(2,1)S(1)}, bf16[64,2048]{1,0:T(8,128)(2,1)S(1)}, u32[]{:S(2)}, u32[]{:S(2)}) %collective-permute-start.40) | collective-permute-done | bytes 262176 | tf_op jit(solution)/shard_map/ppermute | solution.py:613
  242.8 7.9 %hidden_grads.1 = (f32[384,768]{1,0:T(8,128)}, f32[256,768]{1,0:T(8,128)}, f32[256,768]{1,0:T(8,128)}, f32[128,768]{1,0:T(8,128)}) custom-call(bf16[128,2048]{1,0:T(8,128)(2,1)} %bitcast.79, bf16[128,2048]{1,0:T(8,128)(2,1)} %copy-done.24, bf16[128,2048]{1,0:T(8,128)(2,1)} %collective-permute-done.24.refs_2_.refs_6_, bf16[128,2048]{1,0:T(8,128)(2,1)} %copy-done.25, ...), custom_call_target="tpu_custom_call" | custom-call | flops 1 | bytes 1 | tf_op jit(solution)/shard_map/hidden_grads/pallas_call | solution.py:1024
  259.1 12.3 %collective-permute-done.48 = bf16[128,2048]{1,0:T(8,128)(2,1)S(1)} collective-permute-done((bf16[128,2048]{1,0:T(8,128)(2,1)S(1)}, bf16[128,2048]{1,0:T(8,128)(2,1)S(1)}, u32[]{:S(2)}, u32[]{:S(2)}) %collective-permute-start.48) | collective-permute-done | bytes 524320 | tf_op jit(solution)/shard_map/ppermute | solution.py:613
  273.7 8.5 %assemble.1 = bf16[8,4,64,1536]{3,2,1,0:T(8,128)(2,1)} custom-call(s32[9]{0:T(128)} %pad_add_fusion.refs_0_.at_ref, bf16[512,1536]{1,0:T(8,128)(2,1)} %stack.3.refs_0_, bf16[512,1536]{1,0:T(8,128)(2,1)} %collective-permute-done.46.refs_1_, bf16[512,1536]{1,0:T(8,128)(2,1)} %collective-permute-done.47.refs_2_, bf16[512,1536]{1,0:T(8,128)(2,1)} %collective-permute-done.50.refs_3_), custom_call_target="tpu_custom_call" | custom-call | flops 1 | bytes 1 | tf_op jit(solution)/shard_map/assemble/pallas_call | solution.py:778
  340.0 8.5 %row_grads.2 = bf16[768,2048]{1,0:T(8,128)(2,1)} custom-call(bf16[384,768]{1,0:T(8,128)(2,1)} %get-tuple-element.382.refs_0_, bf16[256,768]{1,0:T(8,128)(2,1)} %get-tuple-element.383.refs_1_, bf16[256,768]{1,0:T(8,128)(2,1)} %get-tuple-element.384.refs_2_, bf16[128,768]{1,0:T(8,128)(2,1)} %get-tuple-element.385.refs_3_, bf16[128,2048]{1,0:T(8,128)(2,1)} %bitcast.80, ...), custom_call_target="tpu_custom_call" | custom-call | flops 1 | bytes 1 | tf_op jit(solution)/shard_map/row_grads/pallas_call | solution.py:987
  353.3 14.4 %weight_grads.2 = (bf16[512,1536]{1,0:T(8,128)(2,1)}, bf16[512,1536]{1,0:T(8,128)(2,1)}, bf16[2,512,1536]{2,1,0:T(8,128)(2,1)}) custom-call(s32[9]{0:T(128)} %pad_add_fusion.refs_0_.at_ref, bf16[384,2048]{1,0:T(8,128)(2,1)} %pad_maximum_fusion.refs_1_, bf16[256,2048]{1,0:T(8,128)(2,1)} %copy-done.23, bf16[256,2048]{1,0:T(8,128)(2,1)} %copy-done.22, ...), custom_call_target="tpu_custom_call" | custom-call | flops 1 | bytes 1 | tf_op jit(solution)/shard_map/weight_grads/pallas_call | solution.py:940
  376.4 7.5 %collective-permute-done.63 = bf16[128,2048]{1,0:T(8,128)(2,1)S(1)} collective-permute-done((bf16[128,2048]{1,0:T(8,128)(2,1)S(1)}, bf16[128,2048]{1,0:T(8,128)(2,1)S(1)}, u32[]{:S(2)}, u32[]{:S(2)}) %collective-permute-start.63) | collective-permute-done | bytes 524320 | tf_op jit(solution)/shard_map/ppermute | solution.py:613
  415.6 8.4 %collective-permute-done.71 = bf16[128,2048]{1,0:T(8,128)(2,1)S(1)} collective-permute-done((bf16[128,2048]{1,0:T(8,128)(2,1)S(1)}, bf16[128,2048]{1,0:T(8,128)(2,1)S(1)}, u32[]{:S(2)}, u32[]{:S(2)}) %collective-permute-start.71) | collective-permute-done | bytes 524320 | tf_op jit(solution)/shard_map/ppermute | solution.py:613
  439.6 26.1 %attend_back.1 = (bf16[1024,256]{1,0:T(8,128)(2,1)}, bf16[1024,256]{1,0:T(8,128)(2,1)}, bf16[1024,256]{1,0:T(8,128)(2,1)}, bf16[2048,256]{1,0:T(8,128)(2,1)}) custom-call(s32[8]{0:T(128)} %get-tuple-element.571.place_ref.refs_0_, s32[32]{0:T(128)} %copy-done.81, bf16[1024,256]{1,0:T(8,128)(2,1)} %get-tuple-element.283.q_ref.refs_2_, ...), custom_call_target="tpu_custom_call" | custom-call | flops 30000001024 | bytes 33554432 | tf_op jit(solution)/shard_map/attend_back/pallas_call | solution.py:579
  478.7 7.9 %collective-permute-done.82 = bf16[128,2048]{1,0:T(8,128)(2,1)S(1)} collective-permute-done((bf16[128,2048]{1,0:T(8,128)(2,1)}, bf16[128,2048]{1,0:T(8,128)(2,1)S(1)}, u32[]{:S(2)}, u32[]{:S(2)}) %collective-permute-start.82) | collective-permute-done | bytes 524320 | tf_op jit(solution)/shard_map/ppermute | solution.py:613
  497.1 9.8 %collective-permute-done.84.refs_3_ = bf16[160,1536]{1,0:T(8,128)(2,1)S(1)} collective-permute-done((bf16[160,1536]{1,0:T(8,128)(2,1)}, bf16[160,1536]{1,0:T(8,128)(2,1)S(1)}, u32[]{:S(2)}, u32[]{:S(2)}) %collective-permute-start.84) | collective-permute-done | bytes 491552 | tf_op jit(solution)/shard_map/ppermute | solution.py:613
  513.2 9.3 %project_back.1 = (bf16[1024,512]{1,0:T(8,128)(2,1)}, bf16[1024,2048]{1,0:T(8,128)(2,1)}, f32[8,128]{1,0:T(8,128)}) custom-call(bf16[1024,256]{1,0:T(8,128)(2,1)} %get-tuple-element.435.dq_ref, bf16[1024,256]{1,0:T(8,128)(2,1)} %add_convert_fusion.11.dkv_ref, f32[1024,512]{1,0:T(8,128)} %get-tuple-element.437.raw_ref, f32[8,128]{1,0:T(8,128)} %pad.13.head_gain_ref, ...), custom_call_target="tpu_custom_call" | custom-call | flops 30000001024 | bytes 33554432 | tf_op jit(solution)/shard_map/project_back/pallas_call | solution.py:895
  532.1 9.0 %weight_grads.3 = (bf16[640,512]{1,0:T(8,128)(2,1)}, bf16[640,512]{1,0:T(8,128)(2,1)}, bf16[2,640,512]{2,1,0:T(8,128)(2,1)}) custom-call(s32[9]{0:T(128)} %pad_add_fusion.refs_0_.at_ref, bf16[1024,2048]{1,0:T(8,128)(2,1)} %get-tuple-element.446.refs_1_, bf16[1024,512]{1,0:T(8,128)(2,1)} %get-tuple-element.447.refs_2_, bf16[16,512]{1,0:T(8,128)(2,1)} %pad.14.refs_3_), custom_call_target="tpu_custom_call" | custom-call | flops 1 | bytes 1 | tf_op jit(solution)/shard_map/weight_grads/pallas_call | solution.py:940
  566.5 8.2 %collective-permute-done.96 = bf16[128,2048]{1,0:T(8,128)(2,1)} collective-permute-done((bf16[128,2048]{1,0:T(8,128)(2,1)}, bf16[128,2048]{1,0:T(8,128)(2,1)}, u32[]{:S(2)}, u32[]{:S(2)}) %collective-permute-start.96) | collective-permute-done | bytes 524320 | tf_op jit(solution)/shard_map/ppermute | solution.py:613
  586.1 14.1 %collective-permute-done.101.refs_1_ = bf16[280,512]{1,0:T(8,128)(2,1)} collective-permute-done((bf16[280,512]{1,0:T(8,128)(2,1)}, bf16[280,512]{1,0:T(8,128)(2,1)}, u32[]{:S(2)}, u32[]{:S(2)}) %collective-permute-start.101) | collective-permute-done | bytes 286752 | tf_op jit(solution)/shard_map/ppermute | solution.py:613
  608.1 11.4 %collective-permute-done.105.refs_3_ = bf16[200,512]{1,0:T(8,128)(2,1)S(1)} collective-permute-done((bf16[200,512]{1,0:T(8,128)(2,1)S(1)}, bf16[200,512]{1,0:T(8,128)(2,1)S(1)}, u32[]{:S(2)}, u32[]{:S(2)}) %collective-permute-start.105) | collective-permute-done | bytes 204832 | tf_op jit(solution)/shard_map/ppermute | solution.py:613
  (560 shorter events, 356.8 us)
Async XLA Ops:
  7.2 143.1 %all-gather.3.cloned.1.call-start = ((), (), s32[]{:S(2)}) async-start(), calls=%async_computation.2 | async-start | bytes 1310720 | tf_op jit(solution)/shard_map/all_gather | solution.py:1094
  7.2 44.2 %collective-permute-start = (bf16[128,2048]{1,0:T(8,128)(2,1)}, bf16[128,2048]{1,0:T(8,128)(2,1)}, u32[]{:S(2)}, u32[]{:S(2)}) collective-permute-start(bf16[128,2048]{1,0:T(8,128)(2,1)} %bitcast.83), channel_id=1, source_target_pairs={{0,4},{8,0},{16,8},{24,16},{28,24},{20,28},{12,20},{4,12},{1,5},{9... | collective-permute-start | bytes 1572872 | tf_op jit(solution)/shard_map/ppermute | solution.py:613
  10.3 41.2 %collective-permute-start.1 = (bf16[128,2048]{1,0:T(8,128)(2,1)}, bf16[128,2048]{1,0:T(8,128)(2,1)}, u32[]{:S(2)}, u32[]{:S(2)}) collective-permute-start(bf16[128,2048]{1,0:T(8,128)(2,1)} %bitcast.84), channel_id=1, source_target_pairs={{0,8},{8,16},{16,24},{24,28},{28,20},{20,12},{12,4},{4,0},{1,9},{9... | collective-permute-start | bytes 1572872 | tf_op jit(solution)/shard_map/ppermute | solution.py:613
  63.5 176.6 %all-gather.5.cloned.1.call-start = ((), (), s32[]{:S(2)}) async-start(), calls=%async_computation.3 | async-start | bytes 3932160 | tf_op jit(solution)/shard_map/all_gather | solution.py:1094
  115.9 429.4 %reduce-scatter.3.cloned.1.call-start = ((), (), s32[]{:S(2)}) async-start(), calls=%async_computation.4 | async-start | bytes 3932160 | tf_op jit(solution)/shard_map/reduce_scatter | solution.py:1098
  115.9 34.4 %collective-permute-start.23 = (bf16[128,2048]{1,0:T(8,128)(2,1)S(1)}, bf16[128,2048]{1,0:T(8,128)(2,1)S(1)}, u32[]{:S(2)}, u32[]{:S(2)}) collective-permute-start(bf16[128,2048]{1,0:T(8,128)(2,1)S(1)} %bitcast.81), channel_id=1, source_target_pairs={{0,4},{8,0},{16,8},{24,16},{28,24},{20,28},{12,20},{4,12},{1,5},{9... | collective-permute-start | bytes 1572872 | tf_op jit(solution)/shard_map/ppermute | solution.py:613
  116.0 34.3 %collective-permute-start.24 = (bf16[128,2048]{1,0:T(8,128)(2,1)S(1)}, bf16[128,2048]{1,0:T(8,128)(2,1)}, u32[]{:S(2)}, u32[]{:S(2)}) collective-permute-start(bf16[128,2048]{1,0:T(8,128)(2,1)S(1)} %bitcast.82), channel_id=1, source_target_pairs={{0,8},{8,16},{16,24},{24,28},{28,20},{20,12},{12,4},{4,0},{1,9},{9... | collective-permute-start | bytes 1572872 | tf_op jit(solution)/shard_map/ppermute | solution.py:613
  154.8 23.2 %collective-permute-start.30 = (bf16[128,2048]{1,0:T(8,128)(2,1)S(1)}, bf16[128,2048]{1,0:T(8,128)(2,1)S(1)}, u32[]{:S(2)}, u32[]{:S(2)}) collective-permute-start(bf16[128,2048]{1,0:T(8,128)(2,1)S(1)} %collective-permute-done.23.refs_1_.refs_5_), channel_id=1, source_target_pairs={{0,4},{8,0},{16,8},{24,16},{28,24},{20,28},{12,20},{4,12},{1,5},{9... | collective-permute-start | bytes 1572872 | tf_op jit(solution)/shard_map/ppermute | solution.py:613
  155.0 23.0 %collective-permute-start.31 = (bf16[128,2048]{1,0:T(8,128)(2,1)}, bf16[128,2048]{1,0:T(8,128)(2,1)S(1)}, u32[]{:S(2)}, u32[]{:S(2)}) collective-permute-start(bf16[128,2048]{1,0:T(8,128)(2,1)} %collective-permute-done.24.refs_2_.refs_6_), channel_id=1, source_target_pairs={{0,8},{8,16},{16,24},{24,28},{28,20},{20,12},{12,4},{4,0},{1,9},{9... | collective-permute-start | bytes 1572872 | tf_op jit(solution)/shard_map/ppermute | solution.py:613
  156.9 21.1 %collective-permute-start.32 = (bf16[96,1536]{1,0:T(8,128)(2,1)}, bf16[96,1536]{1,0:T(8,128)(2,1)S(1)}, u32[]{:S(2)}, u32[]{:S(2)}) collective-permute-start(bf16[96,1536]{1,0:T(8,128)(2,1)} %slice.488), channel_id=1, source_target_pairs={{0,8},{8,16},{16,24},{24,28},{28,20},{20,12},{12,4},{4,0},{1,9},{9... | collective-permute-start | bytes 884744 | tf_op jit(solution)/shard_map/ppermute | solution.py:613
  180.3 21.3 %collective-permute-start.36 = (bf16[128,2048]{1,0:T(8,128)(2,1)S(1)}, bf16[128,2048]{1,0:T(8,128)(2,1)S(1)}, u32[]{:S(2)}, u32[]{:S(2)}) collective-permute-start(bf16[128,2048]{1,0:T(8,128)(2,1)S(1)} %collective-permute-done.30.refs_3_.refs_7_), channel_id=1, source_target_pairs={{0,4},{8,0},{16,8},{24,16},{28,24},{20,28},{12,20},{4,12},{1,5},{9... | collective-permute-start | bytes 1572872 | tf_op jit(solution)/shard_map/ppermute | solution.py:613
  182.0 21.5 %collective-permute-start.37 = (bf16[128,2048]{1,0:T(8,128)(2,1)S(1)}, bf16[128,2048]{1,0:T(8,128)(2,1)S(1)}, u32[]{:S(2)}, u32[]{:S(2)}) collective-permute-start(bf16[128,2048]{1,0:T(8,128)(2,1)S(1)} %collective-permute-done.31.refs_4_.refs_8_), channel_id=1, source_target_pairs={{0,8},{8,16},{16,24},{24,28},{28,20},{20,12},{12,4},{4,0},{1,9},{9... | collective-permute-start | bytes 1572872 | tf_op jit(solution)/shard_map/ppermute | solution.py:613
  215.4 38.6 %collective-permute-start.46 = (bf16[512,1536]{1,0:T(8,128)(2,1)}, bf16[512,1536]{1,0:T(8,128)(2,1)}, u32[]{:S(2)}, u32[]{:S(2)}) collective-permute-start(bf16[512,1536]{1,0:T(8,128)(2,1)} %stack.3.refs_0_), channel_id=1, source_target_pairs={{0,1},{1,0},{2,3},{3,2},{4,5},{5,4},{6,7},{7,6},{8,9},{9,8},{10,11... | collective-permute-start | bytes 4718600 | tf_op jit(solution)/shard_map/ppermute | solution.py:617
  215.4 38.6 %collective-permute-start.47 = (bf16[512,1536]{1,0:T(8,128)(2,1)}, bf16[512,1536]{1,0:T(8,128)(2,1)}, u32[]{:S(2)}, u32[]{:S(2)}) collective-permute-start(bf16[512,1536]{1,0:T(8,128)(2,1)} %stack.3.refs_0_), channel_id=1, source_target_pairs={{0,2},{1,3},{2,0},{3,1},{4,6},{5,7},{6,4},{7,5},{8,10},{9,11},{10,... | collective-permute-start | bytes 4718600 | tf_op jit(solution)/shard_map/ppermute | solution.py:617
  217.5 21.4 %collective-permute-start.39 = (bf16[128,2048]{1,0:T(8,128)(2,1)S(1)}, bf16[128,2048]{1,0:T(8,128)(2,1)S(1)}, u32[]{:S(2)}, u32[]{:S(2)}) collective-permute-start(bf16[128,2048]{1,0:T(8,128)(2,1)S(1)} %copy-done.53), channel_id=1, source_target_pairs={{0,4},{8,0},{16,8},{24,16},{28,24},{20,28},{12,20},{4,12},{1,5},{9... | collective-permute-start | bytes 1572872 | tf_op jit(solution)/shard_map/ppermute | solution.py:613
  388.0 41.5 %collective-permute-start.68 = (bf16[512,1536]{1,0:T(8,128)(2,1)S(1)}, bf16[512,1536]{1,0:T(8,128)(2,1)S(1)}, u32[]{:S(2)}, u32[]{:S(2)}) collective-permute-start(bf16[512,1536]{1,0:T(8,128)(2,1)S(1)} %get-tuple-element.389), channel_id=1, source_target_pairs={{0,2},{1,3},{2,0},{3,1},{4,6},{5,7},{6,4},{7,5},{8,10},{9,11},{10,... | collective-permute-start | bytes 4718600 | tf_op jit(solution)/shard_map/ppermute | solution.py:617
  434.2 31.5 %collective-permute-start.76 = (bf16[128,2048]{1,0:T(8,128)(2,1)}, bf16[128,2048]{1,0:T(8,128)(2,1)}, u32[]{:S(2)}, u32[]{:S(2)}) collective-permute-start(bf16[128,2048]{1,0:T(8,128)(2,1)} %pad_maximum_fusion.13), channel_id=1, source_target_pairs={{0,4},{8,0},{16,8},{24,16},{28,24},{20,28},{12,20},{4,12},{1,5},{9... | collective-permute-start | bytes 1572872 | tf_op jit(solution)/shard_map/ppermute | solution.py:613
  435.6 30.1 %collective-permute-start.75 = (bf16[128,2048]{1,0:T(8,128)(2,1)}, bf16[128,2048]{1,0:T(8,128)(2,1)}, u32[]{:S(2)}, u32[]{:S(2)}) collective-permute-start(bf16[128,2048]{1,0:T(8,128)(2,1)} %pad_maximum_fusion.12), channel_id=1, source_target_pairs={{0,8},{8,16},{16,24},{24,28},{28,20},{20,12},{12,4},{4,0},{1,9},{9... | collective-permute-start | bytes 1572872 | tf_op jit(solution)/shard_map/ppermute | solution.py:613
  436.2 32.1 %collective-permute-start.77 = (bf16[224,1536]{1,0:T(8,128)(2,1)}, bf16[224,1536]{1,0:T(8,128)(2,1)}, u32[]{:S(2)}, u32[]{:S(2)}) collective-permute-start(bf16[224,1536]{1,0:T(8,128)(2,1)} %get-tuple-element.402), channel_id=1, source_target_pairs={{0,8},{8,16},{16,24},{24,28},{28,20},{20,12},{12,4},{4,0},{1,9},{9... | collective-permute-start | bytes 2064392 | tf_op jit(solution)/shard_map/ppermute | solution.py:613
  438.0 32.2 %collective-permute-start.78 = (bf16[224,1536]{1,0:T(8,128)(2,1)}, bf16[224,1536]{1,0:T(8,128)(2,1)}, u32[]{:S(2)}, u32[]{:S(2)}) collective-permute-start(bf16[224,1536]{1,0:T(8,128)(2,1)} %get-tuple-element.403), channel_id=1, source_target_pairs={{0,4},{8,0},{16,8},{24,16},{28,24},{20,28},{12,20},{4,12},{1,5},{9... | collective-permute-start | bytes 2064392 | tf_op jit(solution)/shard_map/ppermute | solution.py:613
  494.4 144.9 %reduce-scatter.5.cloned.1.call-start = ((), (), s32[]{:S(2)}) async-start(), calls=%async_computation.5 | async-start | bytes 1310720 | tf_op jit(solution)/shard_map/reduce_scatter | solution.py:1098
  543.2 20.4 %collective-permute-start.97 = (bf16[1280,512]{1,0:T(8,128)(2,1)}, bf16[1280,512]{1,0:T(8,128)(2,1)}, u32[]{:S(2)}, u32[]{:S(2)}) collective-permute-start(bf16[1280,512]{1,0:T(8,128)(2,1)} %bitcast.8), channel_id=1, source_target_pairs={{0,1},{1,0},{2,3},{3,2},{4,5},{5,4},{6,7},{7,6},{8,9},{9,8},{10,11... | collective-permute-start | bytes 3932168 | tf_op jit(solution)/shard_map/ppermute | solution.py:617
  602.1 34.7 %collective-permute-start.104 = (bf16[128,2048]{1,0:T(8,128)(2,1)}, bf16[128,2048]{1,0:T(8,128)(2,1)}, u32[]{:S(2)}, u32[]{:S(2)}) collective-permute-start(bf16[128,2048]{1,0:T(8,128)(2,1)} %get-tuple-element.474), channel_id=1, source_target_pairs={{0,4},{8,0},{16,8},{24,16},{28,24},{20,28},{12,20},{4,12},{1,5},{9... | collective-permute-start | bytes 1572872 | tf_op jit(solution)/shard_map/ppermute | solution.py:613
  603.7 33.2 %collective-permute-start.103 = (bf16[128,2048]{1,0:T(8,128)(2,1)}, bf16[128,2048]{1,0:T(8,128)(2,1)}, u32[]{:S(2)}, u32[]{:S(2)}) collective-permute-start(bf16[128,2048]{1,0:T(8,128)(2,1)} %get-tuple-element.473), channel_id=1, source_target_pairs={{0,8},{8,16},{16,24},{24,28},{28,20},{20,12},{12,4},{4,0},{1,9},{9... | collective-permute-start | bytes 1572872 | tf_op jit(solution)/shard_map/ppermute | solution.py:613
  (175 other events, 1885.1 us)
Sparse Core Ops, SparseCore 0:
  63.6 18.8 all-gather.2
  116.0 29.8 all-gather.4
  494.5 36.8 reduce-scatter.2
  586.2 23.5 reduce-scatter.4

commit v9 on v8

--- a/solution.py
+++ b/solution.py
@@ -1205,12 +1205,15 @@
     gain_one = gains[:4].reshape(1, model_width)
     gain_two = gains[4:8].reshape(1, model_width)
     head_gains = jnp.pad(gains[8, : 2 * HEAD_SIZE].reshape(2, HEAD_SIZE), ((0, 6), (0, 0)))
+    own = hold((ff_swap,), own)
     near, far = cross(own, 1), cross(own, 2)
+    ff_swap.go()
     own, near, far = hold((ff_swap, cotangent_ring), own, near, far)
     both = cross(far, 1)
     ff_swap.go()
+    kv = hold((ff_swap, cotangent_ring), own, far, near, both)
+    ff_swap.go()
     cotangent_ring.go()
-    kv = hold((), own, far, near, both)
     attended, lse = attend(place, order, query_rows, kv)
 
     def by_groups(rows):
@@ -1223,24 +1226,22 @@
     branch_parts = [matmul(rows, output_rows).astype(narrow) for rows in by_groups(attended)]
     branch_ring = Scatter(by_strips(branch_parts))
     branch_ring.go()
-    ff_swap.go()
     cotangent_ring.go()
-    hold((branch_ring, cotangent_ring, ff_swap))
-    branch_ring.go()
-    ff_swap.go()
     ff_own = hold((), ff_swap.result())
     ff_near, ff_far = cross(ff_own, 1), cross(ff_own, 2)
+    hold((branch_ring, cotangent_ring))
+    branch_ring.go()
     cotangent_ring.go()
     hold((branch_ring, cotangent_ring))
     branch_ring.go()
     cotangent_ring.go()
-    cotangent_strips, down_matrix = hold(
-        (branch_ring, cotangent_ring), cotangent_ring.strips(), down_matrix
+    ff_near, ff_far, cotangent_strips, down_matrix = hold(
+        (branch_ring, cotangent_ring), ff_near, ff_far, cotangent_ring.strips(), down_matrix
     )
     branch_ring.go()
+    ff_both = cross(ff_far, 1)
     hidden_grads = hidden_grads_of(cotangent_strips, down_matrix)
-    hidden_grads, ff_near, ff_far = hold((branch_ring,), hidden_grads, ff_near, ff_far)
-    ff_both = cross(ff_far, 1)
+    hidden_grads, ff_both = hold((branch_ring,), hidden_grads, ff_both)
     tokens_wide = tokens.astype(wide)
     resid = tokens_wide + branch_ring.total()
     rho_two = inverse_rms(resid)
@@ -1371,27 +1372,28 @@
         (token_ring, ff_swap), attn_own, attn_far, attn_sent
     )
     token_ring.go()
-    attn_own, attn_far = hold((), *scatter_cross(attn_own, attn_far, attn_sent))
+    attn_own, attn_far = scatter_cross(attn_own, attn_far, attn_sent)
     attn_far = cross(attn_far, 2)
     gate_weight_gradient, up_weight_gradient, ff_sums = widen(at, ff_swap, gate_weight, up_weight)
-    gate_weight_gradient, up_weight_gradient, ff_sums = hold(
-        (token_ring,), gate_weight_gradient, up_weight_gradient, ff_sums
-    )
+    attn_swap = Swap(add(attn_own, attn_far), weight_rows + pad)
+    gate_weight_gradient, up_weight_gradient, ff_sums, output_weight_gradient = hold(
+        (token_ring, attn_swap),
+        gate_weight_gradient, up_weight_gradient, ff_sums, output_weight_gradient,
+    )
+    output_weight_gradient = scatter_head(output_weight_gradient)
+    attn_swap.go()
     token_ring.go()
     feedforward_norm_gradient = jnp.sum(ff_sums, axis=1) / feedforward_norm.astype(wide)
-    attn_swap = Swap(add(attn_own, attn_far), weight_rows + pad)
-    feedforward_norm_gradient, down_gradient, output_weight_gradient = hold(
-        (token_ring, attn_swap),
-        feedforward_norm_gradient, down_gradient.astype(wide), output_weight_gradient,
-    )
-    output_weight_gradient = scatter_head(output_weight_gradient).astype(wide)
+    feedforward_norm_gradient, down_gradient = hold(
+        (token_ring, attn_swap), feedforward_norm_gradient, down_gradient.astype(wide)
+    )
     attn_swap.go()
     token_ring.go()
-    hold((token_ring, attn_swap, out_ring))
+    output_weight_gradient = hold(
+        (token_ring, attn_swap, out_ring), output_weight_gradient.astype(wide)
+    )
     attn_swap.go()
     out_ring.go()
-    hold((attn_swap,))
-    attn_swap.go()
     hold((attn_swap,))
     attn_swap.go()
     layer_out = (resid + out_ring.total()).astype(narrow)

time: 659 us -> 631 us (0.958)
  waiting for transfers between devices: 253 us -> 225 us
    ppermute x96, waiting for transfers between devices: 224 us -> 202 us  [hop(): lax.ppermute(value, 'blk', [(RING[i], RING[(i + by) % count]) for i in ra...]
  transfers between devices with their start and end apart: 115 -> 115, of which waited for: 59 -> 61; matrix products, arithmetic and copies ran while one was open for 17% -> 17% of each run, Pallas kernels for 19% -> 22%
where the time goes in v9:
time: 631 us; the launch traced here: 621 us
  waiting for transfers between devices  225 us (36%)
  Pallas kernels  136 us (22%)
  starting transfers between devices  109 us (17%)
  other arithmetic  68.4 us (11%)
  matrix products  36.6 us (6%)
  local copies, waits for them, and re-layouts  30.3 us (5%)
  between operations  15.6 us (2%)
    ppermute x96, waiting for transfers between devices, hop(): lax.ppermute(value, 'blk', [(RING[i], RING[(i + by) % count]) for i in ra...  202 us
    ppermute x96, starting transfers between devices, hop(): lax.ppermute(value, 'blk', [(RING[i], RING[(i + by) % count]) for i in ra...  102 us
    dot_general x20, matrix products, matmul(): lax.dot_general(left, right, dims, preferred_element_type=jnp.float32)  36.6 us
    pallas_call x1, Pallas kernels, attend_back(): pl.pallas_call(lambda *refs: attend_back_kernel(*refs, groups=len(grads))...  27.7 us
    convert_element_type x18, other arithmetic, add(): (left.astype(jnp.float32) + right.astype(jnp.float32)).astype(left.dtype)  26.2 us
    pallas_call x2, Pallas kernels, weight_grads(): pl.pallas_call(lambda *refs: weight_grads_kernel(*refs, groups=len(lefts)...  23.3 us
    ppermute x15, waiting for transfers between devices, cross(): return lax.ppermute(value, 'head', [(i, i ^ by) for i in range(4)])  23.2 us
    pallas_call x1, Pallas kernels, attend(): pl.pallas_call(attend_kernel, grid_spec=pltpu.PrefetchScalarGridSpec(num_...  19.8 us
  transfers between devices with their start and end apart: 115, of which 61 were waited for; matrix products, arithmetic and copies ran while one was open for 17% of the time, Pallas kernels for 22%

profile of v9, /device:TPU:0, one launch (start us, length us, event | category | flops | bytes accessed | tf_op | source)
XLA Modules:
  0.0 620.9 jit_solution(10621897267989682961)
XLA Ops:
  18.8 11.2 %collective-permute-done.2.refs_1_ = bf16[280,512]{1,0:T(8,128)(2,1)S(1)} collective-permute-done((bf16[280,512]{1,0:T(8,128)(2,1)S(1)}, bf16[280,512]{1,0:T(8,128)(2,1)S(1)}, u32[]{:S(2)}, u32[]{:S(2)}) %collective-permute-start.2) | collective-permute-done | bytes 286752 | tf_op jit(solution)/shard_map/ppermute | solution.py:613
  64.1 13.4 %collective-permute-done.15.refs_11_ = bf16[640,512]{1,0:T(8,128)(2,1)} collective-permute-done((bf16[640,512]{1,0:T(8,128)(2,1)S(1)}, bf16[640,512]{1,0:T(8,128)(2,1)}, u32[]{:S(2)}, u32[]{:S(2)}) %collective-permute-start.15) | collective-permute-done | bytes 655392 | tf_op jit(solution)/shard_map/ppermute | solution.py:617
  88.3 9.9 %project.1 = (bf16[1024,2048]{1,0:T(8,128)(2,1)}, f32[1024,512]{1,0:T(8,128)}, bf16[1024,256]{1,0:T(8,128)(2,1)}, bf16[1024,256]{1,0:T(8,128)(2,1)}, bf16[2048,512]{1,0:T(8,128)(2,1)}, /*index=5*/f32[16,512]{1,0:T(8,128)}) custom-call(s32[9]{0:T(128)} %pad_add_fusion.refs_0_.at_ref, bf16[128,2048]{1,0:T(8,128)(2,1)} %bitcast.87, ...), custom_call_target="tpu_custom_call" | custom-call | flops 30000001024 | bytes 33554432 | tf_op jit(solution)/shard_map/project/pallas_call | solution.py:847
  108.1 11.3 %collective-permute-done.21.refs_3_ = bf16[160,1536]{1,0:T(8,128)(2,1)S(1)} collective-permute-done((bf16[160,1536]{1,0:T(8,128)(2,1)S(1)}, bf16[160,1536]{1,0:T(8,128)(2,1)S(1)}, u32[]{:S(2)}, u32[]{:S(2)}) %collective-permute-start.21) | collective-permute-done | bytes 491552 | tf_op jit(solution)/shard_map/ppermute | solution.py:613
  123.8 7.3 %collective-permute-done.25.refs_5_ = bf16[96,1536]{1,0:T(8,128)(2,1)S(1)} collective-permute-done((bf16[96,1536]{1,0:T(8,128)(2,1)S(1)}, bf16[96,1536]{1,0:T(8,128)(2,1)S(1)}, u32[]{:S(2)}, u32[]{:S(2)}) %collective-permute-start.25) | collective-permute-done | bytes 294944 | tf_op jit(solution)/shard_map/ppermute | solution.py:613
  137.5 19.8 %attend.1 = (bf16[1024,256]{1,0:T(8,128)(2,1)}, f32[8,8,256]{2,1,0:T(8,128)}) custom-call(s32[8]{0:T(128)} %get-tuple-element.575.place_ref.refs_0_, s32[32]{0:T(128)} %copy-done.85, bf16[1024,256]{1,0:T(8,128)(2,1)} %get-tuple-element.296.q_ref.refs_2_, bf16[1024,256]{1,0:T(8,128)(2,1)} %get-tuple-element.297.refs_0_.refs_9_, ...), custom_call_target="tpu_custom_call" | custom-call | flops 30000001024 | bytes 33554432 | tf_op jit(solution)/shard_map/attend/pallas_call | solution.py:480
  171.8 5.7 collective-permute-done.34.refs_3_.refs_7_
  194.1 6.4 %collective-permute-done.38.refs_5_.refs_9_ = bf16[128,2048]{1,0:T(8,128)(2,1)S(1)} collective-permute-done((bf16[128,2048]{1,0:T(8,128)(2,1)}, bf16[128,2048]{1,0:T(8,128)(2,1)S(1)}, u32[]{:S(2)}, u32[]{:S(2)}) %collective-permute-start.38) | collective-permute-done | bytes 524320 | tf_op jit(solution)/shard_map/ppermute | solution.py:613
  212.0 7.0 %collective-permute-done.44 = bf16[64,2048]{1,0:T(8,128)(2,1)S(1)} collective-permute-done((bf16[64,2048]{1,0:T(8,128)(2,1)S(1)}, bf16[64,2048]{1,0:T(8,128)(2,1)S(1)}, u32[]{:S(2)}, u32[]{:S(2)}) %collective-permute-start.44) | collective-permute-done | bytes 262176 | tf_op jit(solution)/shard_map/ppermute | solution.py:613
  226.0 7.9 %hidden_grads.1 = (f32[384,768]{1,0:T(8,128)}, f32[256,768]{1,0:T(8,128)}, f32[256,768]{1,0:T(8,128)}, f32[128,768]{1,0:T(8,128)}) custom-call(bf16[128,2048]{1,0:T(8,128)(2,1)} %bitcast.81, bf16[128,2048]{1,0:T(8,128)(2,1)} %copy-done.23, bf16[128,2048]{1,0:T(8,128)(2,1)} %collective-permute-done.29.refs_2_.refs_6_, ...), custom_call_target="tpu_custom_call" | custom-call | flops 1 | bytes 1 | tf_op jit(solution)/shard_map/hidden_grads/pallas_call | solution.py:1024
  243.0 8.5 %assemble.1 = bf16[8,4,64,1536]{3,2,1,0:T(8,128)(2,1)} custom-call(s32[9]{0:T(128)} %pad_add_fusion.refs_0_.at_ref, bf16[512,1536]{1,0:T(8,128)(2,1)} %stack.3.refs_0_, bf16[512,1536]{1,0:T(8,128)(2,1)} %collective-permute-done.42.refs_1_, bf16[512,1536]{1,0:T(8,128)(2,1)} %collective-permute-done.43.refs_2_, bf16[512,1536]{1,0:T(8,128)(2,1)} %collective-permute-done.48.refs_3_), custom_call_target="tpu_custom_call" | custom-call | flops 1 | bytes 1 | tf_op jit(solution)/shard_map/assemble/pallas_call | solution.py:778
  309.4 8.5 %row_grads.2 = bf16[768,2048]{1,0:T(8,128)(2,1)} custom-call(bf16[384,768]{1,0:T(8,128)(2,1)} %get-tuple-element.389.refs_0_, bf16[256,768]{1,0:T(8,128)(2,1)} %get-tuple-element.390.refs_1_, bf16[256,768]{1,0:T(8,128)(2,1)} %get-tuple-element.391.refs_2_, bf16[128,768]{1,0:T(8,128)(2,1)} %get-tuple-element.392.refs_3_, bf16[128,2048]{1,0:T(8,128)(2,1)} %bitcast.82, ...), custom_call_target="tpu_custom_call" | custom-call | flops 1 | bytes 1 | tf_op jit(solution)/shard_map/row_grads/pallas_call | solution.py:987
  323.1 14.4 %weight_grads.2 = (bf16[512,1536]{1,0:T(8,128)(2,1)}, bf16[512,1536]{1,0:T(8,128)(2,1)}, bf16[2,512,1536]{2,1,0:T(8,128)(2,1)}) custom-call(s32[9]{0:T(128)} %pad_add_fusion.refs_0_.at_ref, bf16[384,2048]{1,0:T(8,128)(2,1)} %pad_maximum_fusion.refs_1_, bf16[256,2048]{1,0:T(8,128)(2,1)} %copy-done.22, bf16[256,2048]{1,0:T(8,128)(2,1)} %copy-done.21, ...), custom_call_target="tpu_custom_call" | custom-call | flops 1 | bytes 1 | tf_op jit(solution)/shard_map/weight_grads/pallas_call | solution.py:940
  346.2 7.8 %collective-permute-done.63 = bf16[128,2048]{1,0:T(8,128)(2,1)S(1)} collective-permute-done((bf16[128,2048]{1,0:T(8,128)(2,1)S(1)}, bf16[128,2048]{1,0:T(8,128)(2,1)S(1)}, u32[]{:S(2)}, u32[]{:S(2)}) %collective-permute-start.63) | collective-permute-done | bytes 524320 | tf_op jit(solution)/shard_map/ppermute | solution.py:613
  375.1 7.9 %collective-permute-done.69 = bf16[128,2048]{1,0:T(8,128)(2,1)S(1)} collective-permute-done((bf16[128,2048]{1,0:T(8,128)(2,1)S(1)}, bf16[128,2048]{1,0:T(8,128)(2,1)S(1)}, u32[]{:S(2)}, u32[]{:S(2)}) %collective-permute-start.69) | collective-permute-done | bytes 524320 | tf_op jit(solution)/shard_map/ppermute | solution.py:613
  387.3 8.8 %collective-permute-done.71 = bf16[128,2048]{1,0:T(8,128)(2,1)S(1)} collective-permute-done((bf16[128,2048]{1,0:T(8,128)(2,1)S(1)}, bf16[128,2048]{1,0:T(8,128)(2,1)S(1)}, u32[]{:S(2)}, u32[]{:S(2)}) %collective-permute-start.71) | collective-permute-done | bytes 524320 | tf_op jit(solution)/shard_map/ppermute | solution.py:613
  411.8 27.7 %attend_back.1 = (bf16[1024,256]{1,0:T(8,128)(2,1)}, bf16[1024,256]{1,0:T(8,128)(2,1)}, bf16[1024,256]{1,0:T(8,128)(2,1)}, bf16[2048,256]{1,0:T(8,128)(2,1)}) custom-call(s32[8]{0:T(128)} %get-tuple-element.575.place_ref.refs_0_, s32[32]{0:T(128)} %copy-done.85, bf16[1024,256]{1,0:T(8,128)(2,1)} %get-tuple-element.296.q_ref.refs_2_, ...), custom_call_target="tpu_custom_call" | custom-call | flops 30000001024 | bytes 33554432 | tf_op jit(solution)/shard_map/attend_back/pallas_call | solution.py:579
  452.4 7.9 %collective-permute-done.82 = bf16[128,2048]{1,0:T(8,128)(2,1)S(1)} collective-permute-done((bf16[128,2048]{1,0:T(8,128)(2,1)}, bf16[128,2048]{1,0:T(8,128)(2,1)S(1)}, u32[]{:S(2)}, u32[]{:S(2)}) %collective-permute-start.82) | collective-permute-done | bytes 524320 | tf_op jit(solution)/shard_map/ppermute | solution.py:613
  469.5 10.0 %collective-permute-done.84.refs_3_ = bf16[160,1536]{1,0:T(8,128)(2,1)S(1)} collective-permute-done((bf16[160,1536]{1,0:T(8,128)(2,1)}, bf16[160,1536]{1,0:T(8,128)(2,1)S(1)}, u32[]{:S(2)}, u32[]{:S(2)}) %collective-permute-start.84) | collective-permute-done | bytes 491552 | tf_op jit(solution)/shard_map/ppermute | solution.py:613
  486.0 9.5 %project_back.1 = (bf16[1024,512]{1,0:T(8,128)(2,1)}, bf16[1024,2048]{1,0:T(8,128)(2,1)}, f32[8,128]{1,0:T(8,128)}) custom-call(bf16[1024,256]{1,0:T(8,128)(2,1)} %get-tuple-element.442.dq_ref, bf16[1024,256]{1,0:T(8,128)(2,1)} %add_convert_fusion.11.dkv_ref, f32[1024,512]{1,0:T(8,128)} %get-tuple-element.444.raw_ref, f32[8,128]{1,0:T(8,128)} %pad.13.head_gain_ref, ...), custom_call_target="tpu_custom_call" | custom-call | flops 30000001024 | bytes 33554432 | tf_op jit(solution)/shard_map/project_back/pallas_call | solution.py:895
  503.7 9.0 %weight_grads.3 = (bf16[640,512]{1,0:T(8,128)(2,1)}, bf16[640,512]{1,0:T(8,128)(2,1)}, bf16[2,640,512]{2,1,0:T(8,128)(2,1)}) custom-call(s32[9]{0:T(128)} %pad_add_fusion.refs_0_.at_ref, bf16[1024,2048]{1,0:T(8,128)(2,1)} %get-tuple-element.453.refs_1_, bf16[1024,512]{1,0:T(8,128)(2,1)} %get-tuple-element.454.refs_2_, bf16[16,512]{1,0:T(8,128)(2,1)} %pad.14.refs_3_), custom_call_target="tpu_custom_call" | custom-call | flops 1 | bytes 1 | tf_op jit(solution)/shard_map/weight_grads/pallas_call | solution.py:940
  546.6 13.4 %collective-permute-done.99.refs_1_ = bf16[280,512]{1,0:T(8,128)(2,1)S(1)} collective-permute-done((bf16[280,512]{1,0:T(8,128)(2,1)}, bf16[280,512]{1,0:T(8,128)(2,1)S(1)}, u32[]{:S(2)}, u32[]{:S(2)}) %collective-permute-start.99) | collective-permute-done | bytes 286752 | tf_op jit(solution)/shard_map/ppermute | solution.py:613
  570.2 10.9 %collective-permute-done.103.refs_3_ = bf16[200,512]{1,0:T(8,128)(2,1)S(1)} collective-permute-done((bf16[200,512]{1,0:T(8,128)(2,1)}, bf16[200,512]{1,0:T(8,128)(2,1)S(1)}, u32[]{:S(2)}, u32[]{:S(2)}) %collective-permute-start.103) | collective-permute-done | bytes 204832 | tf_op jit(solution)/shard_map/ppermute | solution.py:613
  590.0 9.2 %collective-permute-done.107.refs_5_ = bf16[120,512]{1,0:T(8,128)(2,1)S(1)} collective-permute-done((bf16[120,512]{1,0:T(8,128)(2,1)}, bf16[120,512]{1,0:T(8,128)(2,1)S(1)}, u32[]{:S(2)}, u32[]{:S(2)}) %collective-permute-start.107) | collective-permute-done | bytes 122912 | tf_op jit(solution)/shard_map/ppermute | solution.py:613
  (573 shorter events, 352.0 us)
Async XLA Ops:
  7.2 150.8 %all-gather.3.cloned.1.call-start = ((), (), s32[]{:S(2)}) async-start(), calls=%async_computation.2 | async-start | bytes 1310720 | tf_op jit(solution)/shard_map/all_gather | solution.py:1094
  7.2 44.2 %collective-permute-start = (bf16[128,2048]{1,0:T(8,128)(2,1)}, bf16[128,2048]{1,0:T(8,128)(2,1)}, u32[]{:S(2)}, u32[]{:S(2)}) collective-permute-start(bf16[128,2048]{1,0:T(8,128)(2,1)} %bitcast.85), channel_id=1, source_target_pairs={{0,4},{8,0},{16,8},{24,16},{28,24},{20,28},{12,20},{4,12},{1,5},{9... | collective-permute-start | bytes 1572872 | tf_op jit(solution)/shard_map/ppermute | solution.py:613
  10.3 41.1 %collective-permute-start.1 = (bf16[128,2048]{1,0:T(8,128)(2,1)}, bf16[128,2048]{1,0:T(8,128)(2,1)}, u32[]{:S(2)}, u32[]{:S(2)}) collective-permute-start(bf16[128,2048]{1,0:T(8,128)(2,1)} %bitcast.86), channel_id=1, source_target_pairs={{0,8},{8,16},{16,24},{24,28},{28,20},{20,12},{12,4},{4,0},{1,9},{9... | collective-permute-start | bytes 1572872 | tf_op jit(solution)/shard_map/ppermute | solution.py:613
  58.2 19.3 %collective-permute-start.15 = (bf16[640,512]{1,0:T(8,128)(2,1)S(1)}, bf16[640,512]{1,0:T(8,128)(2,1)}, u32[]{:S(2)}, u32[]{:S(2)}) collective-permute-start(bf16[640,512]{1,0:T(8,128)(2,1)S(1)} %copy-done.45), channel_id=1, source_target_pairs={{0,2},{1,3},{2,0},{3,1},{4,6},{5,7},{6,4},{7,5},{8,10},{9,11},{10,... | collective-permute-start | bytes 1966088 | tf_op jit(solution)/shard_map/ppermute | solution.py:617
  63.5 157.0 %all-gather.5.cloned.1.call-start = ((), (), s32[]{:S(2)}) async-start(), calls=%async_computation.3 | async-start | bytes 3932160 | tf_op jit(solution)/shard_map/all_gather | solution.py:1094
  123.8 419.7 %reduce-scatter.3.cloned.1.call-start = ((), (), s32[]{:S(2)}) async-start(), calls=%async_computation.4 | async-start | bytes 3932160 | tf_op jit(solution)/shard_map/reduce_scatter | solution.py:1098
  133.2 24.2 %collective-permute-start.28 = (bf16[128,2048]{1,0:T(8,128)(2,1)S(1)}, bf16[128,2048]{1,0:T(8,128)(2,1)S(1)}, u32[]{:S(2)}, u32[]{:S(2)}) collective-permute-start(bf16[128,2048]{1,0:T(8,128)(2,1)S(1)} %bitcast.83), channel_id=1, source_target_pairs={{0,4},{8,0},{16,8},{24,16},{28,24},{20,28},{12,20},{4,12},{1,5},{9... | collective-permute-start | bytes 1572872 | tf_op jit(solution)/shard_map/ppermute | solution.py:613
  133.8 23.5 %collective-permute-start.29 = (bf16[128,2048]{1,0:T(8,128)(2,1)S(1)}, bf16[128,2048]{1,0:T(8,128)(2,1)}, u32[]{:S(2)}, u32[]{:S(2)}) collective-permute-start(bf16[128,2048]{1,0:T(8,128)(2,1)S(1)} %bitcast.84), channel_id=1, source_target_pairs={{0,8},{8,16},{16,24},{24,28},{28,20},{20,12},{12,4},{4,0},{1,9},{9... | collective-permute-start | bytes 1572872 | tf_op jit(solution)/shard_map/ppermute | solution.py:613
  135.3 22.0 %collective-permute-start.30 = (bf16[32,1536]{1,0:T(8,128)(2,1)S(1)}, bf16[32,1536]{1,0:T(8,128)(2,1)S(1)}, u32[]{:S(2)}, u32[]{:S(2)}) collective-permute-start(bf16[32,1536]{1,0:T(8,128)(2,1)S(1)} %slice.490), channel_id=1, source_target_pairs={{0,8},{8,16},{16,24},{24,28},{28,20},{20,12},{12,4},{4,0},{1,9},{9... | collective-permute-start | bytes 294920 | tf_op jit(solution)/shard_map/ppermute | solution.py:613
  136.3 21.0 %collective-permute-start.31 = (bf16[32,1536]{1,0:T(8,128)(2,1)S(1)}, bf16[32,1536]{1,0:T(8,128)(2,1)S(1)}, u32[]{:S(2)}, u32[]{:S(2)}) collective-permute-start(bf16[32,1536]{1,0:T(8,128)(2,1)S(1)} %slice.491), channel_id=1, source_target_pairs={{0,4},{8,0},{16,8},{24,16},{28,24},{20,28},{12,20},{4,12},{1,5},{9... | collective-permute-start | bytes 294920 | tf_op jit(solution)/shard_map/ppermute | solution.py:613
  183.3 37.1 %collective-permute-start.42 = (bf16[512,1536]{1,0:T(8,128)(2,1)}, bf16[512,1536]{1,0:T(8,128)(2,1)}, u32[]{:S(2)}, u32[]{:S(2)}) collective-permute-start(bf16[512,1536]{1,0:T(8,128)(2,1)} %stack.3.refs_0_), channel_id=1, source_target_pairs={{0,1},{1,0},{2,3},{3,2},{4,5},{5,4},{6,7},{7,6},{8,9},{9,8},{10,11... | collective-permute-start | bytes 4718600 | tf_op jit(solution)/shard_map/ppermute | solution.py:617
  192.0 31.3 %collective-permute-start.43 = (bf16[512,1536]{1,0:T(8,128)(2,1)}, bf16[512,1536]{1,0:T(8,128)(2,1)}, u32[]{:S(2)}, u32[]{:S(2)}) collective-permute-start(bf16[512,1536]{1,0:T(8,128)(2,1)} %stack.3.refs_0_), channel_id=1, source_target_pairs={{0,2},{1,3},{2,0},{3,1},{4,6},{5,7},{6,4},{7,5},{8,10},{9,11},{10,... | collective-permute-start | bytes 4718600 | tf_op jit(solution)/shard_map/ppermute | solution.py:617
  357.6 44.0 %collective-permute-start.68 = (bf16[512,1536]{1,0:T(8,128)(2,1)S(1)}, bf16[512,1536]{1,0:T(8,128)(2,1)S(1)}, u32[]{:S(2)}, u32[]{:S(2)}) collective-permute-start(bf16[512,1536]{1,0:T(8,128)(2,1)S(1)} %get-tuple-element.396), channel_id=1, source_target_pairs={{0,2},{1,3},{2,0},{3,1},{4,6},{5,7},{6,4},{7,5},{8,10},{9,11},{10,... | collective-permute-start | bytes 4718600 | tf_op jit(solution)/shard_map/ppermute | solution.py:617
  406.4 33.2 %collective-permute-start.76 = (bf16[128,2048]{1,0:T(8,128)(2,1)}, bf16[128,2048]{1,0:T(8,128)(2,1)}, u32[]{:S(2)}, u32[]{:S(2)}) collective-permute-start(bf16[128,2048]{1,0:T(8,128)(2,1)} %pad_maximum_fusion.13), channel_id=1, source_target_pairs={{0,4},{8,0},{16,8},{24,16},{28,24},{20,28},{12,20},{4,12},{1,5},{9... | collective-permute-start | bytes 1572872 | tf_op jit(solution)/shard_map/ppermute | solution.py:613
  407.8 31.7 %collective-permute-start.75 = (bf16[128,2048]{1,0:T(8,128)(2,1)}, bf16[128,2048]{1,0:T(8,128)(2,1)}, u32[]{:S(2)}, u32[]{:S(2)}) collective-permute-start(bf16[128,2048]{1,0:T(8,128)(2,1)} %pad_maximum_fusion.12), channel_id=1, source_target_pairs={{0,8},{8,16},{16,24},{24,28},{28,20},{20,12},{12,4},{4,0},{1,9},{9... | collective-permute-start | bytes 1572872 | tf_op jit(solution)/shard_map/ppermute | solution.py:613
  408.4 33.8 %collective-permute-start.77 = (bf16[224,1536]{1,0:T(8,128)(2,1)}, bf16[224,1536]{1,0:T(8,128)(2,1)}, u32[]{:S(2)}, u32[]{:S(2)}) collective-permute-start(bf16[224,1536]{1,0:T(8,128)(2,1)} %get-tuple-element.409), channel_id=1, source_target_pairs={{0,8},{8,16},{16,24},{24,28},{28,20},{20,12},{12,4},{4,0},{1,9},{9... | collective-permute-start | bytes 2064392 | tf_op jit(solution)/shard_map/ppermute | solution.py:613
  409.7 34.2 %collective-permute-start.78 = (bf16[224,1536]{1,0:T(8,128)(2,1)}, bf16[224,1536]{1,0:T(8,128)(2,1)}, u32[]{:S(2)}, u32[]{:S(2)}) collective-permute-start(bf16[224,1536]{1,0:T(8,128)(2,1)} %get-tuple-element.410), channel_id=1, source_target_pairs={{0,4},{8,0},{16,8},{24,16},{28,24},{20,28},{12,20},{4,12},{1,5},{9... | collective-permute-start | bytes 2064392 | tf_op jit(solution)/shard_map/ppermute | solution.py:613
  469.5 113.0 %reduce-scatter.5.cloned.1.call-start = ((), (), s32[]{:S(2)}) async-start(), calls=%async_computation.5 | async-start | bytes 1310720 | tf_op jit(solution)/shard_map/reduce_scatter | solution.py:1098
  539.3 22.1 %collective-permute-start.98 = (bf16[128,2048]{1,0:T(8,128)(2,1)}, bf16[128,2048]{1,0:T(8,128)(2,1)}, u32[]{:S(2)}, u32[]{:S(2)}) collective-permute-start(bf16[128,2048]{1,0:T(8,128)(2,1)} %get-tuple-element.469), channel_id=1, source_target_pairs={{0,4},{8,0},{16,8},{24,16},{28,24},{20,28},{12,20},{4,12},{1,5},{9... | collective-permute-start | bytes 1572872 | tf_op jit(solution)/shard_map/ppermute | solution.py:613
  540.7 20.7 %collective-permute-start.97 = (bf16[128,2048]{1,0:T(8,128)(2,1)}, bf16[128,2048]{1,0:T(8,128)(2,1)}, u32[]{:S(2)}, u32[]{:S(2)}) collective-permute-start(bf16[128,2048]{1,0:T(8,128)(2,1)} %get-tuple-element.468), channel_id=1, source_target_pairs={{0,8},{8,16},{16,24},{24,28},{28,20},{20,12},{12,4},{4,0},{1,9},{9... | collective-permute-start | bytes 1572872 | tf_op jit(solution)/shard_map/ppermute | solution.py:613
  564.4 19.9 %collective-permute-start.101 = (bf16[128,2048]{1,0:T(8,128)(2,1)}, bf16[128,2048]{1,0:T(8,128)(2,1)S(1)}, u32[]{:S(2)}, u32[]{:S(2)}) collective-permute-start(bf16[128,2048]{1,0:T(8,128)(2,1)} %get-tuple-element.474), channel_id=1, source_target_pairs={{0,8},{8,16},{16,24},{24,28},{28,20},{20,12},{12,4},{4,0},{1,9},{9... | collective-permute-start | bytes 1572872 | tf_op jit(solution)/shard_map/ppermute | solution.py:613
  565.1 19.1 %collective-permute-start.102 = (bf16[128,2048]{1,0:T(8,128)(2,1)}, bf16[128,2048]{1,0:T(8,128)(2,1)}, u32[]{:S(2)}, u32[]{:S(2)}) collective-permute-start(bf16[128,2048]{1,0:T(8,128)(2,1)} %get-tuple-element.475), channel_id=1, source_target_pairs={{0,4},{8,0},{16,8},{24,16},{28,24},{20,28},{12,20},{4,12},{1,5},{9... | collective-permute-start | bytes 1572872 | tf_op jit(solution)/shard_map/ppermute | solution.py:613
  584.3 27.2 %collective-permute-start.106 = (bf16[128,2048]{1,0:T(8,128)(2,1)}, bf16[128,2048]{1,0:T(8,128)(2,1)}, u32[]{:S(2)}, u32[]{:S(2)}) collective-permute-start(bf16[128,2048]{1,0:T(8,128)(2,1)} %get-tuple-element.482), channel_id=1, source_target_pairs={{0,4},{8,0},{16,8},{24,16},{28,24},{20,28},{12,20},{4,12},{1,5},{9... | collective-permute-start | bytes 1572872 | tf_op jit(solution)/shard_map/ppermute | solution.py:613
  585.3 26.2 %collective-permute-start.105 = (bf16[128,2048]{1,0:T(8,128)(2,1)}, bf16[128,2048]{1,0:T(8,128)(2,1)}, u32[]{:S(2)}, u32[]{:S(2)}) collective-permute-start(bf16[128,2048]{1,0:T(8,128)(2,1)} %get-tuple-element.481), channel_id=1, source_target_pairs={{0,8},{8,16},{16,24},{24,28},{28,20},{20,12},{12,4},{4,0},{1,9},{9... | collective-permute-start | bytes 1572872 | tf_op jit(solution)/shard_map/ppermute | solution.py:613
  (181 other events, 1859.5 us)
Sparse Core Ops, SparseCore 0:
  63.6 18.8 all-gather.2
  123.9 26.3 all-gather.4
  469.6 36.8 reduce-scatter.2
  539.5 23.7 reduce-scatter.4

commit v10 on v9

--- a/solution.py
+++ b/solution.py
@@ -675,18 +675,23 @@
         self.taken = [(pieces, 0, rows, 0, 0)]
         self.state = (pieces[rows:cut], pieces[cut:])
 
-    def go(self):
+    def go(self, late=False):
         self.step += 1
         rows, step = self.rows, self.step
         right, left = hop(self.state[0], 1), hop(self.state[1], -1)
         if step < 4:
             self.taken.append((right, 0, rows, 8 - step, 0))
             self.taken.append((left, left.shape[0] - rows, rows, step, 0))
-            self.state = right[rows:], left[:-rows]
+            self.state = right, left
+            if not late:
+                self.trim()
         else:
             self.taken.append((right, 0, rows // 2, 4, 0))
             self.taken.append((left, 0, rows // 2, 4, rows // 2))
             self.state = right, left
+
+    def trim(self):
+        self.state = self.state[0][self.rows :], self.state[1][: -self.rows]
 
     def operands(self):
         return [item[0] for item in self.taken]
@@ -1071,7 +1076,7 @@
         in_specs=[pl.BlockSpec(memory_space=pltpu.SMEM), *swap.specs()] + [vmem] * count,
         out_specs=[vmem] * len(shapes),
         out_shape=[jax.ShapeDtypeStruct(shape, jnp.float32) for shape in shapes],
-        cost_estimate=CHEAP,
+        cost_estimate=LONG,
         name="widen",
     )(at, *swap.operands(), *weights)
 
@@ -1181,7 +1186,7 @@
     ff_slices = slice_pieces(at, gate_weight, up_weight)
     token_ring.go()
     attn_swap.go()
-    hold((attn_swap,))
+    ff_slices, cosine, sine = hold((attn_swap,), ff_slices, cosine, sine)
     attn_swap.go()
     hold((attn_swap,))
     attn_swap.go()
@@ -1190,14 +1195,15 @@
     own = hold((token_ring,), attn_swap.result())
     near, far = cross(own, 1), cross(own, 2)
     token_ring.go()
-    ff_slices, cosine, sine = hold((token_ring,), ff_slices, cosine, sine)
     ff_swap, cotangent_ring = Swap(ff_slices, weight_rows), Gather(out_cotangent)
+    hold((token_ring, ff_swap, cotangent_ring))
     token_ring.go()
     own, near, far = hold((token_ring,), own, near, far)
     both = cross(far, 1)
     token_ring.go()
-    own, near, far, both = hold((token_ring, ff_swap), own, near, far, both)
+    own, near, far, both = hold((token_ring, ff_swap, cotangent_ring), own, near, far, both)
     ff_swap.go()
+    cotangent_ring.go()
 
     first_normed, attn_raw, query_rows, own, attn_matrix, gains = project(
         at_own, token_ring.strips(), (own, near, far, both), cosine, sine, query_cols, pad
@@ -1205,14 +1211,11 @@
     gain_one = gains[:4].reshape(1, model_width)
     gain_two = gains[4:8].reshape(1, model_width)
     head_gains = jnp.pad(gains[8, : 2 * HEAD_SIZE].reshape(2, HEAD_SIZE), ((0, 6), (0, 0)))
-    own = hold((ff_swap,), own)
     near, far = cross(own, 1), cross(own, 2)
-    ff_swap.go()
     own, near, far = hold((ff_swap, cotangent_ring), own, near, far)
     both = cross(far, 1)
-    ff_swap.go()
     kv = hold((ff_swap, cotangent_ring), own, far, near, both)
-    ff_swap.go()
+    ff_swap.go(late=True)
     cotangent_ring.go()
     attended, lse = attend(place, order, query_rows, kv)
 
@@ -1226,22 +1229,23 @@
     branch_parts = [matmul(rows, output_rows).astype(narrow) for rows in by_groups(attended)]
     branch_ring = Scatter(by_strips(branch_parts))
     branch_ring.go()
+    ff_swap.trim()
+    ff_swap.go()
+    hold((branch_ring, ff_swap))
+    branch_ring.go()
+    ff_swap.go()
     cotangent_ring.go()
-    ff_own = hold((), ff_swap.result())
+    ff_own = hold((branch_ring, cotangent_ring), ff_swap.result())
     ff_near, ff_far = cross(ff_own, 1), cross(ff_own, 2)
-    hold((branch_ring, cotangent_ring))
     branch_ring.go()
     cotangent_ring.go()
-    hold((branch_ring, cotangent_ring))
+    cotangent_strips, down_matrix = hold(
+        (branch_ring, cotangent_ring), cotangent_ring.strips(), down_matrix
+    )
     branch_ring.go()
-    cotangent_ring.go()
-    ff_near, ff_far, cotangent_strips, down_matrix = hold(
-        (branch_ring, cotangent_ring), ff_near, ff_far, cotangent_ring.strips(), down_matrix
-    )
-    branch_ring.go()
+    hidden_grads = hidden_grads_of(cotangent_strips, down_matrix)
+    hidden_grads, ff_near, ff_far = hold((branch_ring,), hidden_grads, ff_near, ff_far)
     ff_both = cross(ff_far, 1)
-    hidden_grads = hidden_grads_of(cotangent_strips, down_matrix)
-    hidden_grads, ff_both = hold((branch_ring,), hidden_grads, ff_both)
     tokens_wide = tokens.astype(wide)
     resid = tokens_wide + branch_ring.total()
     rho_two = inverse_rms(resid)
@@ -1335,7 +1339,7 @@
     ff_swap = Swap(add(ff_own, ff_far), weight_rows)
     hold((grad_ring, ff_swap, out_ring))
     out_ring.go()
-    ff_swap.go()
+    ff_swap.go(late=True)
     attention_back(3)
     query_grads, kv_own, kv_far, kv_sent = attend_back(
         place, order, query_rows, attended_grads, attended, lse, kv
@@ -1344,6 +1348,7 @@
         (out_ring, ff_swap), query_grads, kv_own, kv_far, kv_sent, grad_groups, attended
     )
     out_ring.go()
+    ff_swap.trim()
     kv_own, kv_far = scatter_cross(kv_own, kv_far, kv_sent)
     output_weight_gradient = row_grads([attended], grad_groups)
     kv_own, kv_far, output_weight_gradient = hold(
@@ -1360,25 +1365,27 @@
         ((0, pad - 1), (0, attn_cols - 2 * HEAD_SIZE)),
     )
     attn_gradient, first_parts, gain_sums, output_weight_gradient = hold(
-        (ff_swap,), attn_gradient, first_parts, gain_sums, output_weight_gradient
+        (ff_swap, out_ring), attn_gradient, first_parts, gain_sums, output_weight_gradient
     )
     token_ring = Scatter(by_strips(by_groups(first_parts)))
     token_ring.go()
     ff_swap.go()
+    out_ring.go()
     attn_own, attn_far, attn_sent = weight_grads(
         at_own, [first_normed], [attn_gradient], weight_rows, gain_sums
     )
     attn_own, attn_far, attn_sent = hold(
-        (token_ring, ff_swap), attn_own, attn_far, attn_sent
+        (token_ring, ff_swap, out_ring), attn_own, attn_far, attn_sent
     )
     token_ring.go()
     attn_own, attn_far = scatter_cross(attn_own, attn_far, attn_sent)
     attn_far = cross(attn_far, 2)
+    layer_out = (resid + out_ring.total()).astype(narrow)
     gate_weight_gradient, up_weight_gradient, ff_sums = widen(at, ff_swap, gate_weight, up_weight)
     attn_swap = Swap(add(attn_own, attn_far), weight_rows + pad)
-    gate_weight_gradient, up_weight_gradient, ff_sums, output_weight_gradient = hold(
+    gate_weight_gradient, up_weight_gradient, ff_sums, output_weight_gradient, layer_out = hold(
         (token_ring, attn_swap),
-        gate_weight_gradient, up_weight_gradient, ff_sums, output_weight_gradient,
+        gate_weight_gradient, up_weight_gradient, ff_sums, output_weight_gradient, layer_out,
     )
     output_weight_gradient = scatter_head(output_weight_gradient)
     attn_swap.go()
@@ -1390,13 +1397,11 @@
     attn_swap.go()
     token_ring.go()
     output_weight_gradient = hold(
-        (token_ring, attn_swap, out_ring), output_weight_gradient.astype(wide)
+        (token_ring, attn_swap), output_weight_gradient.astype(wide)
     )
     attn_swap.go()
-    out_ring.go()
     hold((attn_swap,))
     attn_swap.go()
-    layer_out = (resid + out_ring.total()).astype(narrow)
     query_weight_gradient, key_weight_gradient, value_weight_gradient, norm_sums, gain_sums = widen(
         at, attn_swap, query_weight, key_projection, value_projection
     )

time: 631 us -> 632 us (level)
  waiting for transfers between devices: 225 us -> 232 us
    ppermute x96, waiting for transfers between devices: 202 us -> 215 us  [hop(): lax.ppermute(value, 'blk', [(RING[i], RING[(i + by) % count]) for i in ra...]
    ppermute x15, waiting for transfers between devices: 23.2 us -> 16.7 us  [cross(): return lax.ppermute(value, 'head', [(i, i ^ by) for i in range(4)])]
  transfers between devices with their start and end apart: 115 -> 115, of which waited for: 61 -> 64; matrix products, arithmetic and copies ran while one was open for 17% -> 17% of each run, Pallas kernels for 22% -> 20%
where the time goes in v10:
time: 632 us; the launch traced here: 620 us
  waiting for transfers between devices  232 us (37%)
  Pallas kernels  134 us (21%)
  starting transfers between devices  110 us (17%)
  other arithmetic  64 us (10%)
  matrix products  37.1 us (6%)
  local copies, waits for them, and re-layouts  27.5 us (4%)
  between operations  15.7 us (2%)
    ppermute x96, waiting for transfers between devices, hop(): lax.ppermute(value, 'blk', [(RING[i], RING[(i + by) % count]) for i in ra...  215 us
    ppermute x96, starting transfers between devices, hop(): lax.ppermute(value, 'blk', [(RING[i], RING[(i + by) % count]) for i in ra...  101 us
    dot_general x20, matrix products, matmul(): lax.dot_general(left, right, dims, preferred_element_type=jnp.float32)  37.1 us
    pallas_call x1, Pallas kernels, attend_back(): pl.pallas_call(lambda *refs: attend_back_kernel(*refs, groups=len(grads))...  25.7 us
    convert_element_type x18, other arithmetic, add(): (left.astype(jnp.float32) + right.astype(jnp.float32)).astype(left.dtype)  23.9 us
    pallas_call x2, Pallas kernels, weight_grads(): pl.pallas_call(lambda *refs: weight_grads_kernel(*refs, groups=len(lefts)...  23.5 us
    pallas_call x1, Pallas kernels, attend(): pl.pallas_call(attend_kernel, grid_spec=pltpu.PrefetchScalarGridSpec(num_...  18.7 us
    ppermute x15, waiting for transfers between devices, cross(): return lax.ppermute(value, 'head', [(i, i ^ by) for i in range(4)])  16.7 us
  transfers between devices with their start and end apart: 115, of which 64 were waited for; matrix products, arithmetic and copies ran while one was open for 17% of the time, Pallas kernels for 20%

profile of v10, /device:TPU:0, one launch (start us, length us, event | category | flops | bytes accessed | tf_op | source)
XLA Modules:
  0.0 620.2 jit_solution(15156351365136076143)
XLA Ops:
  56.2 6.5 %collective-permute-done.10.refs_4_ = bf16[128,2048]{1,0:T(8,128)(2,1)S(1)} collective-permute-done((bf16[128,2048]{1,0:T(8,128)(2,1)}, bf16[128,2048]{1,0:T(8,128)(2,1)S(1)}, u32[]{:S(2)}, u32[]{:S(2)}) %collective-permute-start.10) | collective-permute-done | bytes 524320 | tf_op jit(solution)/shard_map/ppermute | solution.py:613
  65.4 5.6 collective-permute-done.15.refs_11_
  88.9 9.9 %project.1 = (bf16[1024,2048]{1,0:T(8,128)(2,1)}, f32[1024,512]{1,0:T(8,128)}, bf16[1024,256]{1,0:T(8,128)(2,1)}, bf16[1024,256]{1,0:T(8,128)(2,1)}, bf16[2048,512]{1,0:T(8,128)(2,1)}, /*index=5*/f32[16,512]{1,0:T(8,128)}) custom-call(s32[9]{0:T(128)} %pad_add_fusion.refs_0_.at_ref, bf16[128,2048]{1,0:T(8,128)(2,1)} %bitcast.84, ...), custom_call_target="tpu_custom_call" | custom-call | flops 30000001024 | bytes 33554432 | tf_op jit(solution)/shard_map/project/pallas_call | solution.py:852
  107.2 6.2 collective-permute-done.21.refs_1_.refs_5_
  122.6 18.7 %attend.1 = (bf16[1024,256]{1,0:T(8,128)(2,1)}, f32[8,8,256]{2,1,0:T(8,128)}) custom-call(s32[8]{0:T(128)} %get-tuple-element.591.place_ref.refs_0_, s32[32]{0:T(128)} %copy-done.91, bf16[1024,256]{1,0:T(8,128)(2,1)} %get-tuple-element.307.q_ref.refs_2_, bf16[1024,256]{1,0:T(8,128)(2,1)} %get-tuple-element.308.refs_0_.refs_9_, ...), custom_call_target="tpu_custom_call" | custom-call | flops 30000001024 | bytes 33554432 | tf_op jit(solution)/shard_map/attend/pallas_call | solution.py:480
  166.1 13.7 %collective-permute-done.38.refs_7_ = bf16[32,1536]{1,0:T(8,128)(2,1)S(1)} collective-permute-done((bf16[32,1536]{1,0:T(8,128)(2,1)S(1)}, bf16[32,1536]{1,0:T(8,128)(2,1)S(1)}, u32[]{:S(2)}, u32[]{:S(2)}) %collective-permute-start.38) | collective-permute-done | bytes 98336 | tf_op jit(solution)/shard_map/ppermute | solution.py:613
  204.2 11.6 %collective-permute-done.42 = bf16[64,2048]{1,0:T(8,128)(2,1)S(1)} collective-permute-done((bf16[64,2048]{1,0:T(8,128)(2,1)S(1)}, bf16[64,2048]{1,0:T(8,128)(2,1)S(1)}, u32[]{:S(2)}, u32[]{:S(2)}) %collective-permute-start.42) | collective-permute-done | bytes 262176 | tf_op jit(solution)/shard_map/ppermute | solution.py:613
  221.9 8.0 %hidden_grads.1 = (f32[384,768]{1,0:T(8,128)}, f32[256,768]{1,0:T(8,128)}, f32[256,768]{1,0:T(8,128)}, f32[128,768]{1,0:T(8,128)}) custom-call(bf16[128,2048]{1,0:T(8,128)(2,1)} %bitcast.78, bf16[128,2048]{1,0:T(8,128)(2,1)} %copy-done.24, bf16[128,2048]{1,0:T(8,128)(2,1)} %copy-done.25, bf16[128,2048]{1,0:T(8,128)(2,1)} %collective-permute-done.26.refs_3_.refs_7_, ...), custom_call_target="tpu_custom_call" | custom-call | flops 1 | bytes 1 | tf_op jit(solution)/shard_map/hidden_grads/pallas_call | solution.py:1029
  238.3 12.3 %collective-permute-done.48 = bf16[128,2048]{1,0:T(8,128)(2,1)S(1)} collective-permute-done((bf16[128,2048]{1,0:T(8,128)(2,1)S(1)}, bf16[128,2048]{1,0:T(8,128)(2,1)S(1)}, u32[]{:S(2)}, u32[]{:S(2)}) %collective-permute-start.48) | collective-permute-done | bytes 524320 | tf_op jit(solution)/shard_map/ppermute | solution.py:613
  252.7 8.5 %assemble.1 = bf16[8,4,64,1536]{3,2,1,0:T(8,128)(2,1)} custom-call(s32[9]{0:T(128)} %pad_add_fusion.refs_0_.at_ref, bf16[512,1536]{1,0:T(8,128)(2,1)} %stack.3.refs_0_, bf16[512,1536]{1,0:T(8,128)(2,1)} %collective-permute-done.46.refs_1_, bf16[512,1536]{1,0:T(8,128)(2,1)} %collective-permute-done.47.refs_2_, bf16[512,1536]{1,0:T(8,128)(2,1)} %collective-permute-done.50.refs_3_), custom_call_target="tpu_custom_call" | custom-call | flops 1 | bytes 1 | tf_op jit(solution)/shard_map/assemble/pallas_call | solution.py:783
  263.2 4.8 fusion.29
  319.4 8.6 %row_grads.2 = bf16[768,2048]{1,0:T(8,128)(2,1)} custom-call(bf16[384,768]{1,0:T(8,128)(2,1)} %get-tuple-element.402.refs_0_, bf16[256,768]{1,0:T(8,128)(2,1)} %get-tuple-element.403.refs_1_, bf16[256,768]{1,0:T(8,128)(2,1)} %get-tuple-element.404.refs_2_, bf16[128,768]{1,0:T(8,128)(2,1)} %get-tuple-element.405.refs_3_, bf16[128,2048]{1,0:T(8,128)(2,1)} %bitcast.79, ...), custom_call_target="tpu_custom_call" | custom-call | flops 1 | bytes 1 | tf_op jit(solution)/shard_map/row_grads/pallas_call | solution.py:992
  332.7 14.3 %weight_grads.2 = (bf16[512,1536]{1,0:T(8,128)(2,1)}, bf16[512,1536]{1,0:T(8,128)(2,1)}, bf16[2,512,1536]{2,1,0:T(8,128)(2,1)}) custom-call(s32[9]{0:T(128)} %pad_add_fusion.refs_0_.at_ref, bf16[384,2048]{1,0:T(8,128)(2,1)} %pad_maximum_fusion.refs_1_, bf16[256,2048]{1,0:T(8,128)(2,1)} %copy-done.22, bf16[256,2048]{1,0:T(8,128)(2,1)} %copy-done.21, ...), custom_call_target="tpu_custom_call" | custom-call | flops 1 | bytes 1 | tf_op jit(solution)/shard_map/weight_grads/pallas_call | solution.py:945
  355.7 7.5 %collective-permute-done.63 = bf16[128,2048]{1,0:T(8,128)(2,1)S(1)} collective-permute-done((bf16[128,2048]{1,0:T(8,128)(2,1)S(1)}, bf16[128,2048]{1,0:T(8,128)(2,1)S(1)}, u32[]{:S(2)}, u32[]{:S(2)}) %collective-permute-start.63) | collective-permute-done | bytes 524320 | tf_op jit(solution)/shard_map/ppermute | solution.py:613
  384.6 7.4 %collective-permute-done.69 = bf16[128,2048]{1,0:T(8,128)(2,1)S(1)} collective-permute-done((bf16[128,2048]{1,0:T(8,128)(2,1)S(1)}, bf16[128,2048]{1,0:T(8,128)(2,1)S(1)}, u32[]{:S(2)}, u32[]{:S(2)}) %collective-permute-start.69) | collective-permute-done | bytes 524320 | tf_op jit(solution)/shard_map/ppermute | solution.py:613
  395.5 8.8 %collective-permute-done.71 = bf16[128,2048]{1,0:T(8,128)(2,1)S(1)} collective-permute-done((bf16[128,2048]{1,0:T(8,128)(2,1)S(1)}, bf16[128,2048]{1,0:T(8,128)(2,1)S(1)}, u32[]{:S(2)}, u32[]{:S(2)}) %collective-permute-start.71) | collective-permute-done | bytes 524320 | tf_op jit(solution)/shard_map/ppermute | solution.py:613
  420.9 25.7 %attend_back.1 = (bf16[1024,256]{1,0:T(8,128)(2,1)}, bf16[1024,256]{1,0:T(8,128)(2,1)}, bf16[1024,256]{1,0:T(8,128)(2,1)}, bf16[2048,256]{1,0:T(8,128)(2,1)}) custom-call(s32[8]{0:T(128)} %get-tuple-element.591.place_ref.refs_0_, s32[32]{0:T(128)} %copy-done.91, bf16[1024,256]{1,0:T(8,128)(2,1)} %get-tuple-element.307.q_ref.refs_2_, ...), custom_call_target="tpu_custom_call" | custom-call | flops 30000001024 | bytes 33554432 | tf_op jit(solution)/shard_map/attend_back/pallas_call | solution.py:579
  472.9 9.9 %collective-permute-done.84.refs_3_ = bf16[160,1536]{1,0:T(8,128)(2,1)S(1)} collective-permute-done((bf16[160,1536]{1,0:T(8,128)(2,1)}, bf16[160,1536]{1,0:T(8,128)(2,1)S(1)}, u32[]{:S(2)}, u32[]{:S(2)}) %collective-permute-start.84) | collective-permute-done | bytes 491552 | tf_op jit(solution)/shard_map/ppermute | solution.py:613
  488.2 9.9 %project_back.1 = (bf16[1024,512]{1,0:T(8,128)(2,1)}, bf16[1024,2048]{1,0:T(8,128)(2,1)}, f32[8,128]{1,0:T(8,128)}) custom-call(bf16[1024,256]{1,0:T(8,128)(2,1)} %get-tuple-element.457.dq_ref, bf16[1024,256]{1,0:T(8,128)(2,1)} %add_convert_fusion.11.dkv_ref, f32[1024,512]{1,0:T(8,128)} %get-tuple-element.459.raw_ref, f32[8,128]{1,0:T(8,128)} %pad.13.head_gain_ref, ...), custom_call_target="tpu_custom_call" | custom-call | flops 30000001024 | bytes 33554432 | tf_op jit(solution)/shard_map/project_back/pallas_call | solution.py:900
  507.8 9.1 %weight_grads.3 = (bf16[640,512]{1,0:T(8,128)(2,1)}, bf16[640,512]{1,0:T(8,128)(2,1)}, bf16[2,640,512]{2,1,0:T(8,128)(2,1)}) custom-call(s32[9]{0:T(128)} %pad_add_fusion.refs_0_.at_ref, bf16[1024,2048]{1,0:T(8,128)(2,1)} %get-tuple-element.470.refs_1_, bf16[1024,512]{1,0:T(8,128)(2,1)} %get-tuple-element.471.refs_2_, bf16[16,512]{1,0:T(8,128)(2,1)} %pad.14.refs_3_), custom_call_target="tpu_custom_call" | custom-call | flops 1 | bytes 1 | tf_op jit(solution)/shard_map/weight_grads/pallas_call | solution.py:945
  521.4 4.9 collective-permute-done.94
  536.6 9.3 %collective-permute-done.96 = bf16[128,2048]{1,0:T(8,128)(2,1)S(1)} collective-permute-done((bf16[128,2048]{1,0:T(8,128)(2,1)}, bf16[128,2048]{1,0:T(8,128)(2,1)S(1)}, u32[]{:S(2)}, u32[]{:S(2)}) %collective-permute-start.96) | collective-permute-done | bytes 524320 | tf_op jit(solution)/shard_map/ppermute | solution.py:613
  558.1 12.3 %collective-permute-done.101.refs_1_ = bf16[280,512]{1,0:T(8,128)(2,1)} collective-permute-done((bf16[280,512]{1,0:T(8,128)(2,1)S(1)}, bf16[280,512]{1,0:T(8,128)(2,1)}, u32[]{:S(2)}, u32[]{:S(2)}) %collective-permute-start.101) | collective-permute-done | bytes 286752 | tf_op jit(solution)/shard_map/ppermute | solution.py:613
  581.0 11.1 %collective-permute-done.105.refs_3_ = bf16[200,512]{1,0:T(8,128)(2,1)S(1)} collective-permute-done((bf16[200,512]{1,0:T(8,128)(2,1)S(1)}, bf16[200,512]{1,0:T(8,128)(2,1)S(1)}, u32[]{:S(2)}, u32[]{:S(2)}) %collective-permute-start.105) | collective-permute-done | bytes 204832 | tf_op jit(solution)/shard_map/ppermute | solution.py:613
  (580 shorter events, 360.0 us)
Async XLA Ops:
  7.2 137.0 %all-gather.3.cloned.1.call-start = ((), (), s32[]{:S(2)}) async-start(), calls=%async_computation.2 | async-start | bytes 1310720 | tf_op jit(solution)/shard_map/all_gather | solution.py:1099
  7.3 44.2 %collective-permute-start = (bf16[128,2048]{1,0:T(8,128)(2,1)}, bf16[128,2048]{1,0:T(8,128)(2,1)}, u32[]{:S(2)}, u32[]{:S(2)}) collective-permute-start(bf16[128,2048]{1,0:T(8,128)(2,1)} %bitcast.82), channel_id=1, source_target_pairs={{0,4},{8,0},{16,8},{24,16},{28,24},{20,28},{12,20},{4,12},{1,5},{9... | collective-permute-start | bytes 1572872 | tf_op jit(solution)/shard_map/ppermute | solution.py:613
  10.3 41.2 %collective-permute-start.1 = (bf16[128,2048]{1,0:T(8,128)(2,1)}, bf16[128,2048]{1,0:T(8,128)(2,1)}, u32[]{:S(2)}, u32[]{:S(2)}) collective-permute-start(bf16[128,2048]{1,0:T(8,128)(2,1)} %bitcast.83), channel_id=1, source_target_pairs={{0,8},{8,16},{16,24},{24,28},{28,20},{20,12},{12,4},{4,0},{1,9},{9... | collective-permute-start | bytes 1572872 | tf_op jit(solution)/shard_map/ppermute | solution.py:613
  75.1 144.1 %all-gather.5.cloned.1.call-start = ((), (), s32[]{:S(2)}) async-start(), calls=%async_computation.3 | async-start | bytes 3932160 | tf_op jit(solution)/shard_map/all_gather | solution.py:1099
  86.8 26.6 %collective-permute-start.21 = (bf16[128,2048]{1,0:T(8,128)(2,1)S(1)}, bf16[128,2048]{1,0:T(8,128)(2,1)S(1)}, u32[]{:S(2)}, u32[]{:S(2)}) collective-permute-start(bf16[128,2048]{1,0:T(8,128)(2,1)S(1)} %bitcast.80), channel_id=1, source_target_pairs={{0,4},{8,0},{16,8},{24,16},{28,24},{20,28},{12,20},{4,12},{1,5},{9... | collective-permute-start | bytes 1572872 | tf_op jit(solution)/shard_map/ppermute | solution.py:613
  88.5 24.9 %collective-permute-start.22 = (bf16[128,2048]{1,0:T(8,128)(2,1)S(1)}, bf16[128,2048]{1,0:T(8,128)(2,1)S(1)}, u32[]{:S(2)}, u32[]{:S(2)}) collective-permute-start(bf16[128,2048]{1,0:T(8,128)(2,1)S(1)} %bitcast.81), channel_id=1, source_target_pairs={{0,8},{8,16},{16,24},{24,28},{28,20},{20,12},{12,4},{4,0},{1,9},{9... | collective-permute-start | bytes 1572872 | tf_op jit(solution)/shard_map/ppermute | solution.py:613
  116.4 438.5 %reduce-scatter.3.cloned.1.call-start = ((), (), s32[]{:S(2)}) async-start(), calls=%async_computation.4 | async-start | bytes 3932160 | tf_op jit(solution)/shard_map/reduce_scatter | solution.py:1103
  118.5 25.7 %collective-permute-start.26 = (bf16[128,2048]{1,0:T(8,128)(2,1)S(1)}, bf16[128,2048]{1,0:T(8,128)(2,1)}, u32[]{:S(2)}, u32[]{:S(2)}) collective-permute-start(bf16[128,2048]{1,0:T(8,128)(2,1)S(1)} %collective-permute-done.21.refs_1_.refs_5_), channel_id=1, source_target_pairs={{0,4},{8,0},{16,8},{24,16},{28,24},{20,28},{12,20},{4,12},{1,5},{9... | collective-permute-start | bytes 1572872 | tf_op jit(solution)/shard_map/ppermute | solution.py:613
  120.0 24.2 %collective-permute-start.27 = (bf16[128,2048]{1,0:T(8,128)(2,1)S(1)}, bf16[128,2048]{1,0:T(8,128)(2,1)}, u32[]{:S(2)}, u32[]{:S(2)}) collective-permute-start(bf16[128,2048]{1,0:T(8,128)(2,1)S(1)} %collective-permute-done.22.refs_2_.refs_6_), channel_id=1, source_target_pairs={{0,8},{8,16},{16,24},{24,28},{28,20},{20,12},{12,4},{4,0},{1,9},{9... | collective-permute-start | bytes 1572872 | tf_op jit(solution)/shard_map/ppermute | solution.py:613
  120.5 23.7 %collective-permute-start.28 = (bf16[160,1536]{1,0:T(8,128)(2,1)S(1)}, bf16[160,1536]{1,0:T(8,128)(2,1)S(1)}, u32[]{:S(2)}, u32[]{:S(2)}) collective-permute-start(bf16[160,1536]{1,0:T(8,128)(2,1)S(1)} %slice.486), channel_id=1, source_target_pairs={{0,8},{8,16},{16,24},{24,28},{28,20},{20,12},{12,4},{4,0},{1,9},{9... | collective-permute-start | bytes 1474568 | tf_op jit(solution)/shard_map/ppermute | solution.py:613
  120.6 23.6 %collective-permute-start.29 = (bf16[160,1536]{1,0:T(8,128)(2,1)}, bf16[160,1536]{1,0:T(8,128)(2,1)S(1)}, u32[]{:S(2)}, u32[]{:S(2)}) collective-permute-start(bf16[160,1536]{1,0:T(8,128)(2,1)} %slice.487), channel_id=1, source_target_pairs={{0,4},{8,0},{16,8},{24,16},{28,24},{20,28},{12,20},{4,12},{1,5},{9... | collective-permute-start | bytes 1474568 | tf_op jit(solution)/shard_map/ppermute | solution.py:613
  161.1 29.2 %collective-permute-start.35 = (bf16[128,2048]{1,0:T(8,128)(2,1)}, bf16[128,2048]{1,0:T(8,128)(2,1)}, u32[]{:S(2)}, u32[]{:S(2)}) collective-permute-start(bf16[128,2048]{1,0:T(8,128)(2,1)} %pad_maximum_fusion.8), channel_id=1, source_target_pairs={{0,4},{8,0},{16,8},{24,16},{28,24},{20,28},{12,20},{4,12},{1,5},{9... | collective-permute-start | bytes 1572872 | tf_op jit(solution)/shard_map/ppermute | solution.py:613
  162.7 27.7 %collective-permute-start.34 = (bf16[128,2048]{1,0:T(8,128)(2,1)}, bf16[128,2048]{1,0:T(8,128)(2,1)}, u32[]{:S(2)}, u32[]{:S(2)}) collective-permute-start(bf16[128,2048]{1,0:T(8,128)(2,1)} %pad_maximum_fusion.7), channel_id=1, source_target_pairs={{0,8},{8,16},{16,24},{24,28},{28,20},{20,12},{12,4},{4,0},{1,9},{9... | collective-permute-start | bytes 1572872 | tf_op jit(solution)/shard_map/ppermute | solution.py:613
  164.0 28.3 %collective-permute-start.36 = (bf16[128,2048]{1,0:T(8,128)(2,1)}, bf16[128,2048]{1,0:T(8,128)(2,1)S(1)}, u32[]{:S(2)}, u32[]{:S(2)}) collective-permute-start(bf16[128,2048]{1,0:T(8,128)(2,1)} %collective-permute-done.26.refs_3_.refs_7_), channel_id=1, source_target_pairs={{0,4},{8,0},{16,8},{24,16},{28,24},{20,28},{12,20},{4,12},{1,5},{9... | collective-permute-start | bytes 1572872 | tf_op jit(solution)/shard_map/ppermute | solution.py:613
  165.2 27.2 %collective-permute-start.37 = (bf16[128,2048]{1,0:T(8,128)(2,1)}, bf16[128,2048]{1,0:T(8,128)(2,1)}, u32[]{:S(2)}, u32[]{:S(2)}) collective-permute-start(bf16[128,2048]{1,0:T(8,128)(2,1)} %collective-permute-done.27.refs_4_.refs_8_), channel_id=1, source_target_pairs={{0,8},{8,16},{16,24},{24,28},{28,20},{20,12},{12,4},{4,0},{1,9},{9... | collective-permute-start | bytes 1572872 | tf_op jit(solution)/shard_map/ppermute | solution.py:613
  194.4 39.2 %collective-permute-start.46 = (bf16[512,1536]{1,0:T(8,128)(2,1)S(1)}, bf16[512,1536]{1,0:T(8,128)(2,1)}, u32[]{:S(2)}, u32[]{:S(2)}) collective-permute-start(bf16[512,1536]{1,0:T(8,128)(2,1)S(1)} %copy-done.6), channel_id=1, source_target_pairs={{0,1},{1,0},{2,3},{3,2},{4,5},{5,4},{6,7},{7,6},{8,9},{9,8},{10,11... | collective-permute-start | bytes 4718600 | tf_op jit(solution)/shard_map/ppermute | solution.py:617
  194.4 39.2 %collective-permute-start.47 = (bf16[512,1536]{1,0:T(8,128)(2,1)S(1)}, bf16[512,1536]{1,0:T(8,128)(2,1)}, u32[]{:S(2)}, u32[]{:S(2)}) collective-permute-start(bf16[512,1536]{1,0:T(8,128)(2,1)S(1)} %copy-done.6), channel_id=1, source_target_pairs={{0,2},{1,3},{2,0},{3,1},{4,6},{5,7},{6,4},{7,5},{8,10},{9,11},{10,... | collective-permute-start | bytes 4718600 | tf_op jit(solution)/shard_map/ppermute | solution.py:617
  367.2 42.9 %collective-permute-start.68 = (bf16[512,1536]{1,0:T(8,128)(2,1)S(1)}, bf16[512,1536]{1,0:T(8,128)(2,1)S(1)}, u32[]{:S(2)}, u32[]{:S(2)}) collective-permute-start(bf16[512,1536]{1,0:T(8,128)(2,1)S(1)} %get-tuple-element.409), channel_id=1, source_target_pairs={{0,2},{1,3},{2,0},{3,1},{4,6},{5,7},{6,4},{7,5},{8,10},{9,11},{10,... | collective-permute-start | bytes 4718600 | tf_op jit(solution)/shard_map/ppermute | solution.py:617
  414.8 31.8 %collective-permute-start.76 = (bf16[128,2048]{1,0:T(8,128)(2,1)}, bf16[128,2048]{1,0:T(8,128)(2,1)}, u32[]{:S(2)}, u32[]{:S(2)}) collective-permute-start(bf16[128,2048]{1,0:T(8,128)(2,1)} %pad_maximum_fusion.13), channel_id=1, source_target_pairs={{0,4},{8,0},{16,8},{24,16},{28,24},{20,28},{12,20},{4,12},{1,5},{9... | collective-permute-start | bytes 1572872 | tf_op jit(solution)/shard_map/ppermute | solution.py:613
  414.9 31.7 %collective-permute-start.75 = (bf16[128,2048]{1,0:T(8,128)(2,1)S(1)}, bf16[128,2048]{1,0:T(8,128)(2,1)}, u32[]{:S(2)}, u32[]{:S(2)}) collective-permute-start(bf16[128,2048]{1,0:T(8,128)(2,1)S(1)} %pad_maximum_fusion.12), channel_id=1, source_target_pairs={{0,8},{8,16},{16,24},{24,28},{28,20},{20,12},{12,4},{4,0},{1,9},{9... | collective-permute-start | bytes 1572872 | tf_op jit(solution)/shard_map/ppermute | solution.py:613
  416.9 32.3 %collective-permute-start.77 = (bf16[224,1536]{1,0:T(8,128)(2,1)}, bf16[224,1536]{1,0:T(8,128)(2,1)}, u32[]{:S(2)}, u32[]{:S(2)}) collective-permute-start(bf16[224,1536]{1,0:T(8,128)(2,1)} %get-tuple-element.422), channel_id=1, source_target_pairs={{0,8},{8,16},{16,24},{24,28},{28,20},{20,12},{12,4},{4,0},{1,9},{9... | collective-permute-start | bytes 2064392 | tf_op jit(solution)/shard_map/ppermute | solution.py:613
  419.0 30.2 %collective-permute-start.78 = (bf16[224,1536]{1,0:T(8,128)(2,1)}, bf16[224,1536]{1,0:T(8,128)(2,1)}, u32[]{:S(2)}, u32[]{:S(2)}) collective-permute-start(bf16[224,1536]{1,0:T(8,128)(2,1)} %get-tuple-element.423), channel_id=1, source_target_pairs={{0,4},{8,0},{16,8},{24,16},{28,24},{20,28},{12,20},{4,12},{1,5},{9... | collective-permute-start | bytes 2064392 | tf_op jit(solution)/shard_map/ppermute | solution.py:613
  472.9 120.9 %reduce-scatter.5.cloned.1.call-start = ((), (), s32[]{:S(2)}) async-start(), calls=%async_computation.5 | async-start | bytes 1310720 | tf_op jit(solution)/shard_map/reduce_scatter | solution.py:1103
  551.6 21.6 %collective-permute-start.99 = (bf16[128,2048]{1,0:T(8,128)(2,1)S(1)}, bf16[128,2048]{1,0:T(8,128)(2,1)}, u32[]{:S(2)}, u32[]{:S(2)}) collective-permute-start(bf16[128,2048]{1,0:T(8,128)(2,1)S(1)} %get-tuple-element.488), channel_id=1, source_target_pairs={{0,8},{8,16},{16,24},{24,28},{28,20},{20,12},{12,4},{4,0},{1,9},{9... | collective-permute-start | bytes 1572872 | tf_op jit(solution)/shard_map/ppermute | solution.py:613
  (185 other events, 1948.8 us)
Sparse Core Ops, SparseCore 0:
  75.3 18.8 all-gather.2
  116.5 29.3 all-gather.4
  473.0 37.2 reduce-scatter.2
  551.0 22.7 reduce-scatter.4

commit v11 on v10

--- a/solution.py
+++ b/solution.py
@@ -634,14 +634,15 @@
             self.got[self.step], self.got[8 - self.step] = self.state
         else:
             half = left.shape[0] // 2
-            self.got[4] = jnp.concatenate([hop(left[:half], -1), hop(right[half:], 1)], axis=0)
-            self.state = (self.got[4],)
+            self.state = hop(left[:half], -1), hop(right[half:], 1)
 
     def strips(self):
-        return [self.got[s] for s in STRIPS]
+        return [self.got[s] for s in STRIPS[:-1]] + list(self.state)
 
     def group(self, index):
         first, last = GROUPS[index]
+        if index == 3:
+            return jnp.concatenate(self.state, axis=0)
         return jnp.concatenate([self.got[s] for s in STRIPS[first:last]], axis=0)
 
 
@@ -670,25 +671,22 @@
 
 class Swap:
     def __init__(self, pieces, rows):
-        cut = 4 * rows + rows // 2
         self.rows, self.step = rows, 0
         self.taken = [(pieces, 0, rows, 0, 0)]
-        self.state = (pieces[rows:cut], pieces[cut:])
+        self.across = pieces[4 * rows : 5 * rows]
+        self.state = (pieces[rows : 4 * rows], pieces[5 * rows :])
 
     def go(self, late=False):
         self.step += 1
         rows, step = self.rows, self.step
         right, left = hop(self.state[0], 1), hop(self.state[1], -1)
-        if step < 4:
-            self.taken.append((right, 0, rows, 8 - step, 0))
-            self.taken.append((left, left.shape[0] - rows, rows, step, 0))
-            self.state = right, left
-            if not late:
-                self.trim()
-        else:
-            self.taken.append((right, 0, rows // 2, 4, 0))
-            self.taken.append((left, 0, rows // 2, 4, rows // 2))
-            self.state = right, left
+        self.taken.append((right, 0, rows, 8 - step, 0))
+        self.taken.append((left, left.shape[0] - rows, rows, step, 0))
+        self.state = right, left
+        if step == 1:
+            self.taken.append((hop(self.across, 4), 0, rows, 4, 0))
+        if step < 3 and not late:
+            self.trim()
 
     def trim(self):
         self.state = self.state[0][self.rows :], self.state[1][: -self.rows]
@@ -1190,8 +1188,6 @@
     attn_swap.go()
     hold((attn_swap,))
     attn_swap.go()
-    hold((attn_swap,))
-    attn_swap.go()
     own = hold((token_ring,), attn_swap.result())
     near, far = cross(own, 1), cross(own, 2)
     token_ring.go()
@@ -1231,21 +1227,21 @@
     branch_ring.go()
     ff_swap.trim()
     ff_swap.go()
-    hold((branch_ring, ff_swap))
-    branch_ring.go()
-    ff_swap.go()
-    cotangent_ring.go()
-    ff_own = hold((branch_ring, cotangent_ring), ff_swap.result())
+    ff_own = hold((branch_ring,), ff_swap.result())
     ff_near, ff_far = cross(ff_own, 1), cross(ff_own, 2)
     branch_ring.go()
     cotangent_ring.go()
-    cotangent_strips, down_matrix = hold(
-        (branch_ring, cotangent_ring), cotangent_ring.strips(), down_matrix
-    )
+    hold((branch_ring, cotangent_ring))
+    branch_ring.go()
+    cotangent_ring.go()
+    ff_near, ff_far, down_matrix = hold(
+        (branch_ring, cotangent_ring), ff_near, ff_far, down_matrix
+    )
+    cotangent_strips = hold((), cotangent_ring.strips())
     branch_ring.go()
     hidden_grads = hidden_grads_of(cotangent_strips, down_matrix)
-    hidden_grads, ff_near, ff_far = hold((branch_ring,), hidden_grads, ff_near, ff_far)
     ff_both = cross(ff_far, 1)
+    hidden_grads, ff_both = hold((branch_ring,), hidden_grads, ff_both)
     tokens_wide = tokens.astype(wide)
     resid = tokens_wide + branch_ring.total()
     rho_two = inverse_rms(resid)
@@ -1369,13 +1365,12 @@
     )
     token_ring = Scatter(by_strips(by_groups(first_parts)))
     token_ring.go()
-    ff_swap.go()
     out_ring.go()
     attn_own, attn_far, attn_sent = weight_grads(
         at_own, [first_normed], [attn_gradient], weight_rows, gain_sums
     )
     attn_own, attn_far, attn_sent = hold(
-        (token_ring, ff_swap, out_ring), attn_own, attn_far, attn_sent
+        (token_ring, out_ring), attn_own, attn_far, attn_sent
     )
     token_ring.go()
     attn_own, attn_far = scatter_cross(attn_own, attn_far, attn_sent)
@@ -1399,8 +1394,6 @@
     output_weight_gradient = hold(
         (token_ring, attn_swap), output_weight_gradient.astype(wide)
     )
-    attn_swap.go()
-    hold((attn_swap,))
     attn_swap.go()
     query_weight_gradient, key_weight_gradient, value_weight_gradient, norm_sums, gain_sums = widen(
         at, attn_swap, query_weight, key_projection, value_projection

time: 632 us -> 611 us (0.967)
  waiting for transfers between devices: 232 us -> 200 us
  starting transfers between devices: 110 us -> 123 us
    ppermute x96 -> x92, waiting for transfers between devices: 215 us -> 187 us  [hop(): lax.ppermute(value, 'blk', [(RING[i], RING[(i + by) % count]) for i in ra...]
    ppermute x96 -> x92, starting transfers between devices: 101 us -> 108 us  [hop(): lax.ppermute(value, 'blk', [(RING[i], RING[(i + by) % count]) for i in ra...]
  transfers between devices with their start and end apart: 115 -> 111, of which waited for: 64 -> 57; matrix products, arithmetic and copies ran while one was open for 17% -> 17% of each run, Pallas kernels for 20% -> 21%
where the time goes in v11:
time: 611 us; the launch traced here: 599 us
  waiting for transfers between devices  200 us (33%)
  Pallas kernels  130 us (21%)
  starting transfers between devices  123 us (20%)
  other arithmetic  62.2 us (10%)
  matrix products  36.4 us (6%)
  local copies, waits for them, and re-layouts  32.2 us (5%)
  between operations  15.6 us (3%)
    ppermute x92, waiting for transfers between devices, hop(): lax.ppermute(value, 'blk', [(RING[i], RING[(i + by) % count]) for i in ra...  187 us
    ppermute x92, starting transfers between devices, hop(): lax.ppermute(value, 'blk', [(RING[i], RING[(i + by) % count]) for i in ra...  108 us
    dot_general x20, matrix products, matmul(): lax.dot_general(left, right, dims, preferred_element_type=jnp.float32)  36.4 us
    pallas_call x1, Pallas kernels, attend_back(): pl.pallas_call(lambda *refs: attend_back_kernel(*refs, groups=len(grads))...  24.1 us
    convert_element_type x18, other arithmetic, add(): (left.astype(jnp.float32) + right.astype(jnp.float32)).astype(left.dtype)  23.5 us
    pallas_call x2, Pallas kernels, weight_grads(): pl.pallas_call(lambda *refs: weight_grads_kernel(*refs, groups=len(lefts)...  23.4 us
    pallas_call x1, Pallas kernels, attend(): pl.pallas_call(attend_kernel, grid_spec=pltpu.PrefetchScalarGridSpec(num_...  17.7 us
    ppermute x15, starting transfers between devices, cross(): return lax.ppermute(value, 'head', [(i, i ^ by) for i in range(4)])  14.7 us
  transfers between devices with their start and end apart: 111, of which 57 were waited for; matrix products, arithmetic and copies ran while one was open for 17% of the time, Pallas kernels for 21%

profile of v11, /device:TPU:0, one launch (start us, length us, event | category | flops | bytes accessed | tf_op | source)
XLA Modules:
  0.0 599.1 jit_solution(17227558105884193766)
XLA Ops:
  50.7 6.3 %collective-permute-done.9.refs_4_ = bf16[128,2048]{1,0:T(8,128)(2,1)S(1)} collective-permute-done((bf16[128,2048]{1,0:T(8,128)(2,1)}, bf16[128,2048]{1,0:T(8,128)(2,1)S(1)}, u32[]{:S(2)}, u32[]{:S(2)}) %collective-permute-start.9) | collective-permute-done | bytes 524320 | tf_op jit(solution)/shard_map/ppermute | solution.py:613
  72.7 5.9 collective-permute-done.15.refs_8_
  83.7 9.9 %project.1 = (bf16[1024,2048]{1,0:T(8,128)(2,1)}, f32[1024,512]{1,0:T(8,128)}, bf16[1024,256]{1,0:T(8,128)(2,1)}, bf16[1024,256]{1,0:T(8,128)(2,1)}, bf16[2048,512]{1,0:T(8,128)(2,1)}, /*index=5*/f32[16,512]{1,0:T(8,128)}) custom-call(s32[9]{0:T(128)} %pad_add_fusion.refs_0_.at_ref, bf16[128,2048]{1,0:T(8,128)(2,1)} %bitcast.86, ...), custom_call_target="tpu_custom_call" | custom-call | flops 30000001024 | bytes 33554432 | tf_op jit(solution)/shard_map/project/pallas_call | solution.py:850
  114.4 17.7 %attend.1 = (bf16[1024,256]{1,0:T(8,128)(2,1)}, f32[8,8,256]{2,1,0:T(8,128)}) custom-call(s32[8]{0:T(128)} %get-tuple-element.605.place_ref.refs_0_, s32[32]{0:T(128)} %copy-done.88, bf16[1024,256]{1,0:T(8,128)(2,1)} %get-tuple-element.314.q_ref.refs_2_, bf16[1024,256]{1,0:T(8,128)(2,1)} %get-tuple-element.315.refs_0_.refs_9_, ...), custom_call_target="tpu_custom_call" | custom-call | flops 30000001024 | bytes 33554432 | tf_op jit(solution)/shard_map/attend/pallas_call | solution.py:480
  149.2 7.1 %collective-permute-done.32.refs_6_ = bf16[64,1536]{1,0:T(8,128)(2,1)} collective-permute-done((bf16[64,1536]{1,0:T(8,128)(2,1)S(1)}, bf16[64,1536]{1,0:T(8,128)(2,1)}, u32[]{:S(2)}, u32[]{:S(2)}) %collective-permute-start.32) | collective-permute-done | bytes 196640 | tf_op jit(solution)/shard_map/ppermute | solution.py:613
  165.0 10.7 %collective-permute-done.35 = bf16[128,2048]{1,0:T(8,128)(2,1)S(1)} collective-permute-done((bf16[128,2048]{1,0:T(8,128)(2,1)S(1)}, bf16[128,2048]{1,0:T(8,128)(2,1)S(1)}, u32[]{:S(2)}, u32[]{:S(2)}) %collective-permute-start.35) | collective-permute-done | bytes 524320 | tf_op jit(solution)/shard_map/ppermute | solution.py:613
  178.3 6.5 %collective-permute-done.36.refs_5_.refs_9_ = bf16[128,2048]{1,0:T(8,128)(2,1)S(1)} collective-permute-done((bf16[128,2048]{1,0:T(8,128)(2,1)S(1)}, bf16[128,2048]{1,0:T(8,128)(2,1)S(1)}, u32[]{:S(2)}, u32[]{:S(2)}) %collective-permute-start.36) | collective-permute-done | bytes 524320 | tf_op jit(solution)/shard_map/ppermute | solution.py:613
  190.9 9.2 %collective-permute-done.39 = bf16[128,2048]{1,0:T(8,128)(2,1)S(1)} collective-permute-done((bf16[128,2048]{1,0:T(8,128)(2,1)S(1)}, bf16[128,2048]{1,0:T(8,128)(2,1)S(1)}, u32[]{:S(2)}, u32[]{:S(2)}) %collective-permute-start.39) | collective-permute-done | bytes 524320 | tf_op jit(solution)/shard_map/ppermute | solution.py:613
  210.5 7.9 %hidden_grads.1 = (f32[384,768]{1,0:T(8,128)}, f32[256,768]{1,0:T(8,128)}, f32[256,768]{1,0:T(8,128)}, f32[128,768]{1,0:T(8,128)}) custom-call(bf16[128,2048]{1,0:T(8,128)(2,1)} %bitcast.80, bf16[128,2048]{1,0:T(8,128)(2,1)} %copy-done.25, bf16[128,2048]{1,0:T(8,128)(2,1)} %copy-done.26, bf16[128,2048]{1,0:T(8,128)(2,1)} %copy-done.27, ...), custom_call_target="tpu_custom_call" | custom-call | flops 1 | bytes 1 | tf_op jit(solution)/shard_map/hidden_grads/pallas_call | solution.py:1027
  228.2 8.5 %assemble.1 = bf16[8,4,64,1536]{3,2,1,0:T(8,128)(2,1)} custom-call(s32[9]{0:T(128)} %pad_add_fusion.refs_0_.at_ref, bf16[512,1536]{1,0:T(8,128)(2,1)} %stack.3.refs_0_, bf16[512,1536]{1,0:T(8,128)(2,1)} %collective-permute-done.42.refs_1_, bf16[512,1536]{1,0:T(8,128)(2,1)} %collective-permute-done.43.refs_2_, bf16[512,1536]{1,0:T(8,128)(2,1)} %collective-permute-done.46.refs_3_), custom_call_target="tpu_custom_call" | custom-call | flops 1 | bytes 1 | tf_op jit(solution)/shard_map/assemble/pallas_call | solution.py:781
  281.6 6.2 %collective-permute-done.56 = bf16[64,2048]{1,0:T(8,128)(2,1)S(1)} collective-permute-done((bf16[64,2048]{1,0:T(8,128)(2,1)S(1)}, bf16[64,2048]{1,0:T(8,128)(2,1)S(1)}, u32[]{:S(2)}, u32[]{:S(2)}) %collective-permute-start.56) | collective-permute-done | bytes 262176 | tf_op jit(solution)/shard_map/ppermute | solution.py:613
  295.5 8.5 %row_grads.2 = bf16[768,2048]{1,0:T(8,128)(2,1)} custom-call(bf16[384,768]{1,0:T(8,128)(2,1)} %get-tuple-element.414.refs_0_, bf16[256,768]{1,0:T(8,128)(2,1)} %get-tuple-element.415.refs_1_, bf16[256,768]{1,0:T(8,128)(2,1)} %get-tuple-element.416.refs_2_, bf16[128,768]{1,0:T(8,128)(2,1)} %get-tuple-element.417.refs_3_, bf16[128,2048]{1,0:T(8,128)(2,1)} %bitcast.81, ...), custom_call_target="tpu_custom_call" | custom-call | flops 1 | bytes 1 | tf_op jit(solution)/shard_map/row_grads/pallas_call | solution.py:990
  308.7 14.4 %weight_grads.2 = (bf16[512,1536]{1,0:T(8,128)(2,1)}, bf16[512,1536]{1,0:T(8,128)(2,1)}, bf16[2,512,1536]{2,1,0:T(8,128)(2,1)}) custom-call(s32[9]{0:T(128)} %pad_add_fusion.refs_0_.at_ref, bf16[384,2048]{1,0:T(8,128)(2,1)} %pad_maximum_fusion.refs_1_, bf16[256,2048]{1,0:T(8,128)(2,1)} %copy-done.23, bf16[256,2048]{1,0:T(8,128)(2,1)} %copy-done.22, ...), custom_call_target="tpu_custom_call" | custom-call | flops 1 | bytes 1 | tf_op jit(solution)/shard_map/weight_grads/pallas_call | solution.py:943
  331.7 7.5 %collective-permute-done.61 = bf16[128,2048]{1,0:T(8,128)(2,1)S(1)} collective-permute-done((bf16[128,2048]{1,0:T(8,128)(2,1)S(1)}, bf16[128,2048]{1,0:T(8,128)(2,1)S(1)}, u32[]{:S(2)}, u32[]{:S(2)}) %collective-permute-start.61) | collective-permute-done | bytes 524320 | tf_op jit(solution)/shard_map/ppermute | solution.py:613
  361.4 7.6 %collective-permute-done.66 = bf16[128,2048]{1,0:T(8,128)(2,1)S(1)} collective-permute-done((bf16[128,2048]{1,0:T(8,128)(2,1)S(1)}, bf16[128,2048]{1,0:T(8,128)(2,1)S(1)}, u32[]{:S(2)}, u32[]{:S(2)}) %collective-permute-start.66) | collective-permute-done | bytes 524320 | tf_op jit(solution)/shard_map/ppermute | solution.py:613
  372.7 8.8 %collective-permute-done.68 = bf16[128,2048]{1,0:T(8,128)(2,1)S(1)} collective-permute-done((bf16[128,2048]{1,0:T(8,128)(2,1)S(1)}, bf16[128,2048]{1,0:T(8,128)(2,1)S(1)}, u32[]{:S(2)}, u32[]{:S(2)}) %collective-permute-start.68) | collective-permute-done | bytes 524320 | tf_op jit(solution)/shard_map/ppermute | solution.py:613
  400.5 24.1 %attend_back.1 = (bf16[1024,256]{1,0:T(8,128)(2,1)}, bf16[1024,256]{1,0:T(8,128)(2,1)}, bf16[1024,256]{1,0:T(8,128)(2,1)}, bf16[2048,256]{1,0:T(8,128)(2,1)}) custom-call(s32[8]{0:T(128)} %get-tuple-element.605.place_ref.refs_0_, s32[32]{0:T(128)} %copy-done.88, bf16[1024,256]{1,0:T(8,128)(2,1)} %get-tuple-element.314.q_ref.refs_2_, ...), custom_call_target="tpu_custom_call" | custom-call | flops 30000001024 | bytes 33554432 | tf_op jit(solution)/shard_map/attend_back/pallas_call | solution.py:579
  447.0 6.9 %collective-permute-start.84 = (bf16[1024,256]{1,0:T(8,128)(2,1)}, bf16[1024,256]{1,0:T(8,128)(2,1)S(1)}, u32[]{:S(2)}, u32[]{:S(2)}) collective-permute-start(bf16[1024,256]{1,0:T(8,128)(2,1)} %get-tuple-element.470), channel_id=1, source_target_pairs={{0,2},{1,3},{2,0},{3,1},{4,6},{5,7},{6,4},{7,5},{8,10},{9,11},{10,... | collective-permute-start | bytes 1572872 | tf_op jit(solution)/shard_map/ppermute | solution.py:617
  457.3 6.9 %collective-permute-done.82.refs_4_ = bf16[128,1536]{1,0:T(8,128)(2,1)S(1)} collective-permute-done((bf16[128,1536]{1,0:T(8,128)(2,1)}, bf16[128,1536]{1,0:T(8,128)(2,1)S(1)}, u32[]{:S(2)}, u32[]{:S(2)}) %collective-permute-start.82) | collective-permute-done | bytes 393248 | tf_op jit(solution)/shard_map/ppermute | solution.py:613
  469.0 9.3 %project_back.1 = (bf16[1024,512]{1,0:T(8,128)(2,1)}, bf16[1024,2048]{1,0:T(8,128)(2,1)}, f32[8,128]{1,0:T(8,128)}) custom-call(bf16[1024,256]{1,0:T(8,128)(2,1)} %get-tuple-element.475.dq_ref, bf16[1024,256]{1,0:T(8,128)(2,1)} %add_convert_fusion.11.dkv_ref, f32[1024,512]{1,0:T(8,128)} %get-tuple-element.477.raw_ref, f32[8,128]{1,0:T(8,128)} %pad.13.head_gain_ref, ...), custom_call_target="tpu_custom_call" | custom-call | flops 30000001024 | bytes 33554432 | tf_op jit(solution)/shard_map/project_back/pallas_call | solution.py:898
  491.0 9.0 %weight_grads.3 = (bf16[640,512]{1,0:T(8,128)(2,1)}, bf16[640,512]{1,0:T(8,128)(2,1)}, bf16[2,640,512]{2,1,0:T(8,128)(2,1)}) custom-call(s32[9]{0:T(128)} %pad_add_fusion.refs_0_.at_ref, bf16[1024,2048]{1,0:T(8,128)(2,1)} %get-tuple-element.486.refs_1_, bf16[1024,512]{1,0:T(8,128)(2,1)} %get-tuple-element.487.refs_2_, bf16[16,512]{1,0:T(8,128)(2,1)} %pad.14.refs_3_), custom_call_target="tpu_custom_call" | custom-call | flops 1 | bytes 1 | tf_op jit(solution)/shard_map/weight_grads/pallas_call | solution.py:943
  518.4 8.8 %collective-permute-done.92 = bf16[128,2048]{1,0:T(8,128)(2,1)S(1)} collective-permute-done((bf16[128,2048]{1,0:T(8,128)(2,1)}, bf16[128,2048]{1,0:T(8,128)(2,1)S(1)}, u32[]{:S(2)}, u32[]{:S(2)}) %collective-permute-start.92) | collective-permute-done | bytes 524320 | tf_op jit(solution)/shard_map/ppermute | solution.py:613
  539.7 12.9 %collective-permute-done.98.refs_1_ = bf16[240,512]{1,0:T(8,128)(2,1)} collective-permute-done((bf16[240,512]{1,0:T(8,128)(2,1)S(1)}, bf16[240,512]{1,0:T(8,128)(2,1)}, u32[]{:S(2)}, u32[]{:S(2)}) %collective-permute-start.98) | collective-permute-done | bytes 245792 | tf_op jit(solution)/shard_map/ppermute | solution.py:613
  564.3 10.1 %collective-permute-done.102.refs_4_ = bf16[160,512]{1,0:T(8,128)(2,1)S(1)} collective-permute-done((bf16[160,512]{1,0:T(8,128)(2,1)S(1)}, bf16[160,512]{1,0:T(8,128)(2,1)S(1)}, u32[]{:S(2)}, u32[]{:S(2)}) %collective-permute-start.102) | collective-permute-done | bytes 163872 | tf_op jit(solution)/shard_map/ppermute | solution.py:613
  (564 shorter events, 352.7 us)
Async XLA Ops:
  7.2 130.7 %all-gather.3.cloned.1.call-start = ((), (), s32[]{:S(2)}) async-start(), calls=%async_computation.2 | async-start | bytes 1310720 | tf_op jit(solution)/shard_map/all_gather | solution.py:1097
  7.3 38.7 %collective-permute-start = (bf16[128,2048]{1,0:T(8,128)(2,1)}, bf16[128,2048]{1,0:T(8,128)(2,1)}, u32[]{:S(2)}, u32[]{:S(2)}) collective-permute-start(bf16[128,2048]{1,0:T(8,128)(2,1)} %bitcast.84), channel_id=1, source_target_pairs={{0,4},{8,0},{16,8},{24,16},{28,24},{20,28},{12,20},{4,12},{1,5},{9... | collective-permute-start | bytes 1572872 | tf_op jit(solution)/shard_map/ppermute | solution.py:613
  10.3 35.7 %collective-permute-start.1 = (bf16[128,2048]{1,0:T(8,128)(2,1)}, bf16[128,2048]{1,0:T(8,128)(2,1)}, u32[]{:S(2)}, u32[]{:S(2)}) collective-permute-start(bf16[128,2048]{1,0:T(8,128)(2,1)} %bitcast.85), channel_id=1, source_target_pairs={{0,8},{8,16},{16,24},{24,28},{28,20},{20,12},{12,4},{4,0},{1,9},{9... | collective-permute-start | bytes 1572872 | tf_op jit(solution)/shard_map/ppermute | solution.py:613
  72.0 131.5 %all-gather.5.cloned.1.call-start = ((), (), s32[]{:S(2)}) async-start(), calls=%async_computation.3 | async-start | bytes 3932160 | tf_op jit(solution)/shard_map/all_gather | solution.py:1097
  81.7 24.5 %collective-permute-start.20 = (bf16[128,2048]{1,0:T(8,128)(2,1)S(1)}, bf16[128,2048]{1,0:T(8,128)(2,1)S(1)}, u32[]{:S(2)}, u32[]{:S(2)}) collective-permute-start(bf16[128,2048]{1,0:T(8,128)(2,1)S(1)} %bitcast.82), channel_id=1, source_target_pairs={{0,4},{8,0},{16,8},{24,16},{28,24},{20,28},{12,20},{4,12},{1,5},{9... | collective-permute-start | bytes 1572872 | tf_op jit(solution)/shard_map/ppermute | solution.py:613
  82.9 23.3 %collective-permute-start.21 = (bf16[128,2048]{1,0:T(8,128)(2,1)S(1)}, bf16[128,2048]{1,0:T(8,128)(2,1)S(1)}, u32[]{:S(2)}, u32[]{:S(2)}) collective-permute-start(bf16[128,2048]{1,0:T(8,128)(2,1)S(1)} %bitcast.83), channel_id=1, source_target_pairs={{0,8},{8,16},{16,24},{24,28},{28,20},{20,12},{12,4},{4,0},{1,9},{9... | collective-permute-start | bytes 1572872 | tf_op jit(solution)/shard_map/ppermute | solution.py:613
  108.3 428.2 %reduce-scatter.3.cloned.1.call-start = ((), (), s32[]{:S(2)}) async-start(), calls=%async_computation.4 | async-start | bytes 3932160 | tf_op jit(solution)/shard_map/reduce_scatter | solution.py:1101
  109.0 40.2 %collective-permute-start.31 = (bf16[64,1536]{1,0:T(8,128)(2,1)}, bf16[64,1536]{1,0:T(8,128)(2,1)}, u32[]{:S(2)}, u32[]{:S(2)}) collective-permute-start(bf16[64,1536]{1,0:T(8,128)(2,1)} %slice.383), channel_id=1, source_target_pairs={{0,28},{8,20},{16,12},{24,4},{28,0},{20,8},{12,16},{4,24},{1,29},{... | collective-permute-start | bytes 589832 | tf_op jit(solution)/shard_map/ppermute | solution.py:613
  110.4 27.5 %collective-permute-start.25 = (bf16[128,2048]{1,0:T(8,128)(2,1)S(1)}, bf16[128,2048]{1,0:T(8,128)(2,1)S(1)}, u32[]{:S(2)}, u32[]{:S(2)}) collective-permute-start(bf16[128,2048]{1,0:T(8,128)(2,1)S(1)} %collective-permute-done.20.refs_1_.refs_5_), channel_id=1, source_target_pairs={{0,4},{8,0},{16,8},{24,16},{28,24},{20,28},{12,20},{4,12},{1,5},{9... | collective-permute-start | bytes 1572872 | tf_op jit(solution)/shard_map/ppermute | solution.py:613
  111.6 26.4 %collective-permute-start.26 = (bf16[128,2048]{1,0:T(8,128)(2,1)S(1)}, bf16[128,2048]{1,0:T(8,128)(2,1)S(1)}, u32[]{:S(2)}, u32[]{:S(2)}) collective-permute-start(bf16[128,2048]{1,0:T(8,128)(2,1)S(1)} %collective-permute-done.21.refs_2_.refs_6_), channel_id=1, source_target_pairs={{0,8},{8,16},{16,24},{24,28},{28,20},{20,12},{12,4},{4,0},{1,9},{9... | collective-permute-start | bytes 1572872 | tf_op jit(solution)/shard_map/ppermute | solution.py:613
  112.4 25.5 %collective-permute-start.27 = (bf16[128,1536]{1,0:T(8,128)(2,1)}, bf16[128,1536]{1,0:T(8,128)(2,1)S(1)}, u32[]{:S(2)}, u32[]{:S(2)}) collective-permute-start(bf16[128,1536]{1,0:T(8,128)(2,1)} %slice.469), channel_id=1, source_target_pairs={{0,8},{8,16},{16,24},{24,28},{28,20},{20,12},{12,4},{4,0},{1,9},{9... | collective-permute-start | bytes 1179656 | tf_op jit(solution)/shard_map/ppermute | solution.py:613
  113.1 24.7 %collective-permute-start.28 = (bf16[128,1536]{1,0:T(8,128)(2,1)}, bf16[128,1536]{1,0:T(8,128)(2,1)S(1)}, u32[]{:S(2)}, u32[]{:S(2)}) collective-permute-start(bf16[128,1536]{1,0:T(8,128)(2,1)} %slice.470), channel_id=1, source_target_pairs={{0,4},{8,0},{16,8},{24,16},{28,24},{20,28},{12,20},{4,12},{1,5},{9... | collective-permute-start | bytes 1179656 | tf_op jit(solution)/shard_map/ppermute | solution.py:613
  163.0 21.8 %collective-permute-start.36 = (bf16[128,2048]{1,0:T(8,128)(2,1)S(1)}, bf16[128,2048]{1,0:T(8,128)(2,1)S(1)}, u32[]{:S(2)}, u32[]{:S(2)}) collective-permute-start(bf16[128,2048]{1,0:T(8,128)(2,1)S(1)} %copy-done.28), channel_id=1, source_target_pairs={{0,4},{8,0},{16,8},{24,16},{28,24},{20,28},{12,20},{4,12},{1,5},{9... | collective-permute-start | bytes 1572872 | tf_op jit(solution)/shard_map/ppermute | solution.py:613
  164.7 21.3 %collective-permute-start.37 = (bf16[128,2048]{1,0:T(8,128)(2,1)S(1)}, bf16[128,2048]{1,0:T(8,128)(2,1)S(1)}, u32[]{:S(2)}, u32[]{:S(2)}) collective-permute-start(bf16[128,2048]{1,0:T(8,128)(2,1)S(1)} %copy-done.30), channel_id=1, source_target_pairs={{0,8},{8,16},{16,24},{24,28},{28,20},{20,12},{12,4},{4,0},{1,9},{9... | collective-permute-start | bytes 1572872 | tf_op jit(solution)/shard_map/ppermute | solution.py:613
  165.0 41.5 %collective-permute-start.42 = (bf16[512,1536]{1,0:T(8,128)(2,1)S(1)}, bf16[512,1536]{1,0:T(8,128)(2,1)}, u32[]{:S(2)}, u32[]{:S(2)}) collective-permute-start(bf16[512,1536]{1,0:T(8,128)(2,1)S(1)} %copy-done.5), channel_id=1, source_target_pairs={{0,1},{1,0},{2,3},{3,2},{4,5},{5,4},{6,7},{7,6},{8,9},{9,8},{10,11... | collective-permute-start | bytes 4718600 | tf_op jit(solution)/shard_map/ppermute | solution.py:617
  175.7 32.2 %collective-permute-start.43 = (bf16[512,1536]{1,0:T(8,128)(2,1)S(1)}, bf16[512,1536]{1,0:T(8,128)(2,1)}, u32[]{:S(2)}, u32[]{:S(2)}) collective-permute-start(bf16[512,1536]{1,0:T(8,128)(2,1)S(1)} %copy-done.5), channel_id=1, source_target_pairs={{0,2},{1,3},{2,0},{3,1},{4,6},{5,7},{6,4},{7,5},{8,10},{9,11},{10,... | collective-permute-start | bytes 4718600 | tf_op jit(solution)/shard_map/ppermute | solution.py:617
  348.9 35.1 %collective-permute-start.72 = (bf16[512,1536]{1,0:T(8,128)(2,1)S(1)}, bf16[512,1536]{1,0:T(8,128)(2,1)S(1)}, u32[]{:S(2)}, u32[]{:S(2)}) collective-permute-start(bf16[512,1536]{1,0:T(8,128)(2,1)S(1)} %get-tuple-element.434), channel_id=1, source_target_pairs={{0,2},{1,3},{2,0},{3,1},{4,6},{5,7},{6,4},{7,5},{8,10},{9,11},{10,... | collective-permute-start | bytes 4718600 | tf_op jit(solution)/shard_map/ppermute | solution.py:617
  395.3 29.3 %collective-permute-start.76 = (bf16[128,2048]{1,0:T(8,128)(2,1)}, bf16[128,2048]{1,0:T(8,128)(2,1)}, u32[]{:S(2)}, u32[]{:S(2)}) collective-permute-start(bf16[128,2048]{1,0:T(8,128)(2,1)} %pad_maximum_fusion.12), channel_id=1, source_target_pairs={{0,4},{8,0},{16,8},{24,16},{28,24},{20,28},{12,20},{4,12},{1,5},{9... | collective-permute-start | bytes 1572872 | tf_op jit(solution)/shard_map/ppermute | solution.py:613
  396.8 27.8 %collective-permute-start.75 = (bf16[128,2048]{1,0:T(8,128)(2,1)S(1)}, bf16[128,2048]{1,0:T(8,128)(2,1)}, u32[]{:S(2)}, u32[]{:S(2)}) collective-permute-start(bf16[128,2048]{1,0:T(8,128)(2,1)S(1)} %pad_maximum_fusion.11), channel_id=1, source_target_pairs={{0,8},{8,16},{16,24},{24,28},{28,20},{20,12},{12,4},{4,0},{1,9},{9... | collective-permute-start | bytes 1572872 | tf_op jit(solution)/shard_map/ppermute | solution.py:613
  397.3 29.9 %collective-permute-start.77 = (bf16[192,1536]{1,0:T(8,128)(2,1)}, bf16[192,1536]{1,0:T(8,128)(2,1)}, u32[]{:S(2)}, u32[]{:S(2)}) collective-permute-start(bf16[192,1536]{1,0:T(8,128)(2,1)} %get-tuple-element.440), channel_id=1, source_target_pairs={{0,8},{8,16},{16,24},{24,28},{28,20},{20,12},{12,4},{4,0},{1,9},{9... | collective-permute-start | bytes 1769480 | tf_op jit(solution)/shard_map/ppermute | solution.py:613
  398.7 28.5 %collective-permute-start.78 = (bf16[192,1536]{1,0:T(8,128)(2,1)}, bf16[192,1536]{1,0:T(8,128)(2,1)}, u32[]{:S(2)}, u32[]{:S(2)}) collective-permute-start(bf16[192,1536]{1,0:T(8,128)(2,1)} %get-tuple-element.441), channel_id=1, source_target_pairs={{0,4},{8,0},{16,8},{24,16},{28,24},{20,28},{12,20},{4,12},{1,5},{9... | collective-permute-start | bytes 1769480 | tf_op jit(solution)/shard_map/ppermute | solution.py:613
  457.3 118.5 %reduce-scatter.5.cloned.1.call-start = ((), (), s32[]{:S(2)}) async-start(), calls=%async_computation.5 | async-start | bytes 1310720 | tf_op jit(solution)/shard_map/reduce_scatter | solution.py:1101
  531.9 23.3 %collective-permute-start.97 = (bf16[128,2048]{1,0:T(8,128)(2,1)S(1)}, bf16[128,2048]{1,0:T(8,128)(2,1)S(1)}, u32[]{:S(2)}, u32[]{:S(2)}) collective-permute-start(bf16[128,2048]{1,0:T(8,128)(2,1)S(1)} %get-tuple-element.505), channel_id=1, source_target_pairs={{0,4},{8,0},{16,8},{24,16},{28,24},{20,28},{12,20},{4,12},{1,5},{9... | collective-permute-start | bytes 1572872 | tf_op jit(solution)/shard_map/ppermute | solution.py:613
  561.9 22.3 %collective-permute-start.104 = (bf16[80,512]{1,0:T(8,128)(2,1)S(1)}, bf16[80,512]{1,0:T(8,128)(2,1)S(1)}, u32[]{:S(2)}, u32[]{:S(2)}) collective-permute-start(bf16[80,512]{1,0:T(8,128)(2,1)S(1)} %slice.515), channel_id=1, source_target_pairs={{0,28},{8,20},{16,12},{24,4},{28,0},{20,8},{12,16},{4,24},{1,29},{... | collective-permute-start | bytes 245768 | tf_op jit(solution)/shard_map/ppermute | solution.py:613
  (180 other events, 1893.1 us)
Sparse Core Ops, SparseCore 0:
  72.1 15.4 all-gather.2
  108.4 26.5 all-gather.4
  457.4 36.7 reduce-scatter.2
  532.0 24.9 reduce-scatter.4

commit v12 on v11

--- a/solution.py
+++ b/solution.py
@@ -683,10 +683,13 @@
         self.taken.append((right, 0, rows, 8 - step, 0))
         self.taken.append((left, left.shape[0] - rows, rows, step, 0))
         self.state = right, left
-        if step == 1:
-            self.taken.append((hop(self.across, 4), 0, rows, 4, 0))
+        if step == 1 and not late:
+            self.opposite(hop(self.across, 4))
         if step < 3 and not late:
             self.trim()
+
+    def opposite(self, piece):
+        self.taken.append((piece, 0, self.rows, 4, 0))
 
     def trim(self):
         self.state = self.state[0][self.rows :], self.state[1][: -self.rows]
@@ -1340,8 +1343,9 @@
     query_grads, kv_own, kv_far, kv_sent = attend_back(
         place, order, query_rows, attended_grads, attended, lse, kv
     )
-    query_grads, kv_own, kv_far, kv_sent, grad_groups, attended = hold(
-        (out_ring, ff_swap), query_grads, kv_own, kv_far, kv_sent, grad_groups, attended
+    query_grads, kv_own, kv_far, kv_sent, grad_groups, attended, down_gradient = hold(
+        (out_ring, ff_swap),
+        query_grads, kv_own, kv_far, kv_sent, grad_groups, attended, down_gradient,
     )
     out_ring.go()
     ff_swap.trim()
@@ -1351,7 +1355,10 @@
         (out_ring, ff_swap), kv_own, kv_far, output_weight_gradient
     )
     ff_swap.go()
-    kv_grads = hold((ff_swap,), add(kv_own, cross(kv_far, 2)))
+    kv_grads, ff_opposite = hold(
+        (ff_swap,), add(kv_own, cross(kv_far, 2)), hop(ff_swap.across, 4)
+    )
+    ff_swap.opposite(ff_opposite)
     ff_swap.go()
     attn_gradient, first_parts, gain_sums = project_back(
         query_grads, kv_grads, attn_raw, head_gains, cosine, sine, attn_matrix
@@ -1376,23 +1383,24 @@
     attn_own, attn_far = scatter_cross(attn_own, attn_far, attn_sent)
     attn_far = cross(attn_far, 2)
     layer_out = (resid + out_ring.total()).astype(narrow)
-    gate_weight_gradient, up_weight_gradient, ff_sums = widen(at, ff_swap, gate_weight, up_weight)
     attn_swap = Swap(add(attn_own, attn_far), weight_rows + pad)
-    gate_weight_gradient, up_weight_gradient, ff_sums, output_weight_gradient, layer_out = hold(
-        (token_ring, attn_swap),
-        gate_weight_gradient, up_weight_gradient, ff_sums, output_weight_gradient, layer_out,
+    output_weight_gradient, layer_out, gate_weight, up_weight = hold(
+        (token_ring, attn_swap), output_weight_gradient, layer_out, gate_weight, up_weight
     )
     output_weight_gradient = scatter_head(output_weight_gradient)
     attn_swap.go()
     token_ring.go()
+    gate_weight_gradient, up_weight_gradient, ff_sums = widen(at, ff_swap, gate_weight, up_weight)
+    gate_weight_gradient, up_weight_gradient, ff_sums = hold(
+        (token_ring, attn_swap), gate_weight_gradient, up_weight_gradient, ff_sums
+    )
     feedforward_norm_gradient = jnp.sum(ff_sums, axis=1) / feedforward_norm.astype(wide)
-    feedforward_norm_gradient, down_gradient = hold(
-        (token_ring, attn_swap), feedforward_norm_gradient, down_gradient.astype(wide)
-    )
+    down_gradient = down_gradient.astype(wide)
     attn_swap.go()
     token_ring.go()
-    output_weight_gradient = hold(
-        (token_ring, attn_swap), output_weight_gradient.astype(wide)
+    output_weight_gradient, down_gradient, feedforward_norm_gradient = hold(
+        (token_ring, attn_swap),
+        output_weight_gradient.astype(wide), down_gradient, feedforward_norm_gradient,
     )
     attn_swap.go()
     query_weight_gradient, key_weight_gradient, value_weight_gradient, norm_sums, gain_sums = widen(

time: 611 us -> 602 us (0.985)
    ppermute x15, waiting for transfers between devices: 13.3 us -> 27.3 us  [cross(): return lax.ppermute(value, 'head', [(i, i ^ by) for i in range(4)])]
    ppermute x92, waiting for transfers between devices: 187 us -> 173 us  [hop(): lax.ppermute(value, 'blk', [(RING[i], RING[(i + by) % count]) for i in ra...]
  transfers between devices with their start and end apart: 111 -> 111, of which waited for: 57 -> 57; matrix products, arithmetic and copies ran while one was open for 17% -> 16% of each run, Pallas kernels for 21% -> 22%
where the time goes in v12:
time: 602 us; the launch traced here: 592 us
  waiting for transfers between devices  201 us (33%)
  Pallas kernels  133 us (22%)
  starting transfers between devices  120 us (20%)
  other arithmetic  60.5 us (10%)
  matrix products  36.3 us (6%)
  local copies, waits for them, and re-layouts  27.2 us (5%)
  between operations  15.7 us (3%)
    ppermute x92, waiting for transfers between devices, hop(): lax.ppermute(value, 'blk', [(RING[i], RING[(i + by) % count]) for i in ra...  173 us
    ppermute x92, starting transfers between devices, hop(): lax.ppermute(value, 'blk', [(RING[i], RING[(i + by) % count]) for i in ra...  109 us
    dot_general x20, matrix products, matmul(): lax.dot_general(left, right, dims, preferred_element_type=jnp.float32)  36.3 us
    ppermute x15, waiting for transfers between devices, cross(): return lax.ppermute(value, 'head', [(i, i ^ by) for i in range(4)])  27.3 us
    pallas_call x1, Pallas kernels, attend_back(): pl.pallas_call(lambda *refs: attend_back_kernel(*refs, groups=len(grads))...  25.6 us
    convert_element_type x18, other arithmetic, add(): (left.astype(jnp.float32) + right.astype(jnp.float32)).astype(left.dtype)  24.6 us
    pallas_call x2, Pallas kernels, weight_grads(): pl.pallas_call(lambda *refs: weight_grads_kernel(*refs, groups=len(lefts)...  23.3 us
    pallas_call x1, Pallas kernels, attend(): pl.pallas_call(attend_kernel, grid_spec=pltpu.PrefetchScalarGridSpec(num_...  18.6 us
  transfers between devices with their start and end apart: 111, of which 57 were waited for; matrix products, arithmetic and copies ran while one was open for 16% of the time, Pallas kernels for 22%

profile of v12, /device:TPU:0, one launch (start us, length us, event | category | flops | bytes accessed | tf_op | source)
XLA Modules:
  0.0 592.5 jit_solution(15431590380582541231)
XLA Ops:
  50.7 6.4 %collective-permute-done.9.refs_4_ = bf16[128,2048]{1,0:T(8,128)(2,1)S(1)} collective-permute-done((bf16[128,2048]{1,0:T(8,128)(2,1)}, bf16[128,2048]{1,0:T(8,128)(2,1)S(1)}, u32[]{:S(2)}, u32[]{:S(2)}) %collective-permute-start.9) | collective-permute-done | bytes 524320 | tf_op jit(solution)/shard_map/ppermute | solution.py:613
  72.7 5.9 collective-permute-done.15.refs_8_
  83.7 9.9 %project.1 = (bf16[1024,2048]{1,0:T(8,128)(2,1)}, f32[1024,512]{1,0:T(8,128)}, bf16[1024,256]{1,0:T(8,128)(2,1)}, bf16[1024,256]{1,0:T(8,128)(2,1)}, bf16[2048,512]{1,0:T(8,128)(2,1)}, /*index=5*/f32[16,512]{1,0:T(8,128)}) custom-call(s32[9]{0:T(128)} %pad_add_fusion.refs_0_.at_ref, bf16[128,2048]{1,0:T(8,128)(2,1)} %bitcast.86, ...), custom_call_target="tpu_custom_call" | custom-call | flops 30000001024 | bytes 33554432 | tf_op jit(solution)/shard_map/project/pallas_call | solution.py:853
  101.2 5.0 collective-permute-done.20.refs_1_.refs_5_
  114.5 18.6 %attend.1 = (bf16[1024,256]{1,0:T(8,128)(2,1)}, f32[8,8,256]{2,1,0:T(8,128)}) custom-call(s32[8]{0:T(128)} %get-tuple-element.613.place_ref.refs_0_, s32[32]{0:T(128)} %copy-done.89, bf16[1024,256]{1,0:T(8,128)(2,1)} %get-tuple-element.318.q_ref.refs_2_, bf16[1024,256]{1,0:T(8,128)(2,1)} %get-tuple-element.319.refs_0_.refs_9_, ...), custom_call_target="tpu_custom_call" | custom-call | flops 30000001024 | bytes 33554432 | tf_op jit(solution)/shard_map/attend/pallas_call | solution.py:480
  149.2 7.2 %collective-permute-done.32.refs_6_ = bf16[64,1536]{1,0:T(8,128)(2,1)} collective-permute-done((bf16[64,1536]{1,0:T(8,128)(2,1)S(1)}, bf16[64,1536]{1,0:T(8,128)(2,1)}, u32[]{:S(2)}, u32[]{:S(2)}) %collective-permute-start.32) | collective-permute-done | bytes 196640 | tf_op jit(solution)/shard_map/ppermute | solution.py:613
  165.1 10.7 %collective-permute-done.35 = bf16[128,2048]{1,0:T(8,128)(2,1)S(1)} collective-permute-done((bf16[128,2048]{1,0:T(8,128)(2,1)S(1)}, bf16[128,2048]{1,0:T(8,128)(2,1)S(1)}, u32[]{:S(2)}, u32[]{:S(2)}) %collective-permute-start.35) | collective-permute-done | bytes 524320 | tf_op jit(solution)/shard_map/ppermute | solution.py:613
  178.3 6.6 %collective-permute-done.36.refs_5_.refs_9_ = bf16[128,2048]{1,0:T(8,128)(2,1)S(1)} collective-permute-done((bf16[128,2048]{1,0:T(8,128)(2,1)S(1)}, bf16[128,2048]{1,0:T(8,128)(2,1)S(1)}, u32[]{:S(2)}, u32[]{:S(2)}) %collective-permute-start.36) | collective-permute-done | bytes 524320 | tf_op jit(solution)/shard_map/ppermute | solution.py:613
  191.0 9.2 %collective-permute-done.39 = bf16[128,2048]{1,0:T(8,128)(2,1)S(1)} collective-permute-done((bf16[128,2048]{1,0:T(8,128)(2,1)S(1)}, bf16[128,2048]{1,0:T(8,128)(2,1)S(1)}, u32[]{:S(2)}, u32[]{:S(2)}) %collective-permute-start.39) | collective-permute-done | bytes 524320 | tf_op jit(solution)/shard_map/ppermute | solution.py:613
  210.6 7.9 %hidden_grads.1 = (f32[384,768]{1,0:T(8,128)}, f32[256,768]{1,0:T(8,128)}, f32[256,768]{1,0:T(8,128)}, f32[128,768]{1,0:T(8,128)}) custom-call(bf16[128,2048]{1,0:T(8,128)(2,1)} %bitcast.80, bf16[128,2048]{1,0:T(8,128)(2,1)} %copy-done.25, bf16[128,2048]{1,0:T(8,128)(2,1)} %copy-done.26, bf16[128,2048]{1,0:T(8,128)(2,1)} %copy-done.27, ...), custom_call_target="tpu_custom_call" | custom-call | flops 1 | bytes 1 | tf_op jit(solution)/shard_map/hidden_grads/pallas_call | solution.py:1030
  228.2 8.5 %assemble.1 = bf16[8,4,64,1536]{3,2,1,0:T(8,128)(2,1)} custom-call(s32[9]{0:T(128)} %pad_add_fusion.refs_0_.at_ref, bf16[512,1536]{1,0:T(8,128)(2,1)} %stack.3.refs_0_, bf16[512,1536]{1,0:T(8,128)(2,1)} %collective-permute-done.42.refs_1_, bf16[512,1536]{1,0:T(8,128)(2,1)} %collective-permute-done.43.refs_2_, bf16[512,1536]{1,0:T(8,128)(2,1)} %collective-permute-done.46.refs_3_), custom_call_target="tpu_custom_call" | custom-call | flops 1 | bytes 1 | tf_op jit(solution)/shard_map/assemble/pallas_call | solution.py:784
  281.5 6.1 %collective-permute-done.56 = bf16[64,2048]{1,0:T(8,128)(2,1)S(1)} collective-permute-done((bf16[64,2048]{1,0:T(8,128)(2,1)S(1)}, bf16[64,2048]{1,0:T(8,128)(2,1)S(1)}, u32[]{:S(2)}, u32[]{:S(2)}) %collective-permute-start.56) | collective-permute-done | bytes 262176 | tf_op jit(solution)/shard_map/ppermute | solution.py:613
  295.3 8.6 %row_grads.2 = bf16[768,2048]{1,0:T(8,128)(2,1)} custom-call(bf16[384,768]{1,0:T(8,128)(2,1)} %get-tuple-element.418.refs_0_, bf16[256,768]{1,0:T(8,128)(2,1)} %get-tuple-element.419.refs_1_, bf16[256,768]{1,0:T(8,128)(2,1)} %get-tuple-element.420.refs_2_, bf16[128,768]{1,0:T(8,128)(2,1)} %get-tuple-element.421.refs_3_, bf16[128,2048]{1,0:T(8,128)(2,1)} %bitcast.81, ...), custom_call_target="tpu_custom_call" | custom-call | flops 1 | bytes 1 | tf_op jit(solution)/shard_map/row_grads/pallas_call | solution.py:993
  308.5 14.3 %weight_grads.2 = (bf16[512,1536]{1,0:T(8,128)(2,1)}, bf16[512,1536]{1,0:T(8,128)(2,1)}, bf16[2,512,1536]{2,1,0:T(8,128)(2,1)}) custom-call(s32[9]{0:T(128)} %pad_add_fusion.refs_0_.at_ref, bf16[384,2048]{1,0:T(8,128)(2,1)} %pad_maximum_fusion.refs_1_, bf16[256,2048]{1,0:T(8,128)(2,1)} %copy-done.23, bf16[256,2048]{1,0:T(8,128)(2,1)} %copy-done.22, ...), custom_call_target="tpu_custom_call" | custom-call | flops 1 | bytes 1 | tf_op jit(solution)/shard_map/weight_grads/pallas_call | solution.py:946
  362.2 7.7 %collective-permute-done.66 = bf16[128,2048]{1,0:T(8,128)(2,1)S(1)} collective-permute-done((bf16[128,2048]{1,0:T(8,128)(2,1)S(1)}, bf16[128,2048]{1,0:T(8,128)(2,1)S(1)}, u32[]{:S(2)}, u32[]{:S(2)}) %collective-permute-start.66) | collective-permute-done | bytes 524320 | tf_op jit(solution)/shard_map/ppermute | solution.py:613
  373.8 8.5 %collective-permute-done.68 = bf16[128,2048]{1,0:T(8,128)(2,1)S(1)} collective-permute-done((bf16[128,2048]{1,0:T(8,128)(2,1)S(1)}, bf16[128,2048]{1,0:T(8,128)(2,1)S(1)}, u32[]{:S(2)}, u32[]{:S(2)}) %collective-permute-start.68) | collective-permute-done | bytes 524320 | tf_op jit(solution)/shard_map/ppermute | solution.py:613
  386.6 9.9 %collective-permute-done.72 = bf16[512,1536]{1,0:T(8,128)(2,1)S(1)} collective-permute-done((bf16[512,1536]{1,0:T(8,128)(2,1)S(1)}, bf16[512,1536]{1,0:T(8,128)(2,1)S(1)}, u32[]{:S(2)}, u32[]{:S(2)}) %collective-permute-start.72) | collective-permute-done | bytes 1572896 | tf_op jit(solution)/shard_map/ppermute | solution.py:617
  405.6 25.6 %attend_back.1 = (bf16[1024,256]{1,0:T(8,128)(2,1)}, bf16[1024,256]{1,0:T(8,128)(2,1)}, bf16[1024,256]{1,0:T(8,128)(2,1)}, bf16[2048,256]{1,0:T(8,128)(2,1)}) custom-call(s32[8]{0:T(128)} %get-tuple-element.613.place_ref.refs_0_, s32[32]{0:T(128)} %copy-done.89, bf16[1024,256]{1,0:T(8,128)(2,1)} %get-tuple-element.318.q_ref.refs_2_, ...), custom_call_target="tpu_custom_call" | custom-call | flops 30000001024 | bytes 33554432 | tf_op jit(solution)/shard_map/attend_back/pallas_call | solution.py:579
  441.8 5.5 collective-permute-done.80
  474.6 9.3 %project_back.1 = (bf16[1024,512]{1,0:T(8,128)(2,1)}, bf16[1024,2048]{1,0:T(8,128)(2,1)}, f32[8,128]{1,0:T(8,128)}) custom-call(bf16[1024,256]{1,0:T(8,128)(2,1)} %get-tuple-element.480.dq_ref, bf16[1024,256]{1,0:T(8,128)(2,1)} %add_convert_fusion.11.dkv_ref, f32[1024,512]{1,0:T(8,128)} %get-tuple-element.482.raw_ref, f32[8,128]{1,0:T(8,128)} %pad.13.head_gain_ref, ...), custom_call_target="tpu_custom_call" | custom-call | flops 30000001024 | bytes 33554432 | tf_op jit(solution)/shard_map/project_back/pallas_call | solution.py:901
  492.0 9.0 %weight_grads.3 = (bf16[640,512]{1,0:T(8,128)(2,1)}, bf16[640,512]{1,0:T(8,128)(2,1)}, bf16[2,640,512]{2,1,0:T(8,128)(2,1)}) custom-call(s32[9]{0:T(128)} %pad_add_fusion.refs_0_.at_ref, bf16[1024,2048]{1,0:T(8,128)(2,1)} %get-tuple-element.491.refs_1_, bf16[1024,512]{1,0:T(8,128)(2,1)} %get-tuple-element.492.refs_2_, bf16[16,512]{1,0:T(8,128)(2,1)} %pad.14.refs_3_), custom_call_target="tpu_custom_call" | custom-call | flops 1 | bytes 1 | tf_op jit(solution)/shard_map/weight_grads/pallas_call | solution.py:946
  512.0 8.0 %collective-permute-done.93 = bf16[128,2048]{1,0:T(8,128)(2,1)S(1)} collective-permute-done((bf16[128,2048]{1,0:T(8,128)(2,1)S(1)}, bf16[128,2048]{1,0:T(8,128)(2,1)S(1)}, u32[]{:S(2)}, u32[]{:S(2)}) %collective-permute-start.93) | collective-permute-done | bytes 524320 | tf_op jit(solution)/shard_map/ppermute | solution.py:613
  534.2 11.5 %collective-permute-done.98.refs_1_ = bf16[240,512]{1,0:T(8,128)(2,1)S(1)} collective-permute-done((bf16[240,512]{1,0:T(8,128)(2,1)S(1)}, bf16[240,512]{1,0:T(8,128)(2,1)S(1)}, u32[]{:S(2)}, u32[]{:S(2)}) %collective-permute-start.98) | collective-permute-done | bytes 245792 | tf_op jit(solution)/shard_map/ppermute | solution.py:613
  560.0 8.0 %collective-permute-done.102.refs_4_ = bf16[160,512]{1,0:T(8,128)(2,1)S(1)} collective-permute-done((bf16[160,512]{1,0:T(8,128)(2,1)S(1)}, bf16[160,512]{1,0:T(8,128)(2,1)S(1)}, u32[]{:S(2)}, u32[]{:S(2)}) %collective-permute-start.102) | collective-permute-done | bytes 163872 | tf_op jit(solution)/shard_map/ppermute | solution.py:613
  (566 shorter events, 349.0 us)
Async XLA Ops:
  7.2 130.8 %all-gather.3.cloned.1.call-start = ((), (), s32[]{:S(2)}) async-start(), calls=%async_computation.2 | async-start | bytes 1310720 | tf_op jit(solution)/shard_map/all_gather | solution.py:1100
  7.3 38.8 %collective-permute-start = (bf16[128,2048]{1,0:T(8,128)(2,1)}, bf16[128,2048]{1,0:T(8,128)(2,1)}, u32[]{:S(2)}, u32[]{:S(2)}) collective-permute-start(bf16[128,2048]{1,0:T(8,128)(2,1)} %bitcast.84), channel_id=1, source_target_pairs={{0,4},{8,0},{16,8},{24,16},{28,24},{20,28},{12,20},{4,12},{1,5},{9... | collective-permute-start | bytes 1572872 | tf_op jit(solution)/shard_map/ppermute | solution.py:613
  10.3 35.7 %collective-permute-start.1 = (bf16[128,2048]{1,0:T(8,128)(2,1)}, bf16[128,2048]{1,0:T(8,128)(2,1)}, u32[]{:S(2)}, u32[]{:S(2)}) collective-permute-start(bf16[128,2048]{1,0:T(8,128)(2,1)} %bitcast.85), channel_id=1, source_target_pairs={{0,8},{8,16},{16,24},{24,28},{28,20},{20,12},{12,4},{4,0},{1,9},{9... | collective-permute-start | bytes 1572872 | tf_op jit(solution)/shard_map/ppermute | solution.py:613
  72.0 131.6 %all-gather.5.cloned.1.call-start = ((), (), s32[]{:S(2)}) async-start(), calls=%async_computation.3 | async-start | bytes 3932160 | tf_op jit(solution)/shard_map/all_gather | solution.py:1100
  81.7 24.5 %collective-permute-start.20 = (bf16[128,2048]{1,0:T(8,128)(2,1)S(1)}, bf16[128,2048]{1,0:T(8,128)(2,1)S(1)}, u32[]{:S(2)}, u32[]{:S(2)}) collective-permute-start(bf16[128,2048]{1,0:T(8,128)(2,1)S(1)} %bitcast.82), channel_id=1, source_target_pairs={{0,4},{8,0},{16,8},{24,16},{28,24},{20,28},{12,20},{4,12},{1,5},{9... | collective-permute-start | bytes 1572872 | tf_op jit(solution)/shard_map/ppermute | solution.py:613
  82.9 23.3 %collective-permute-start.21 = (bf16[128,2048]{1,0:T(8,128)(2,1)S(1)}, bf16[128,2048]{1,0:T(8,128)(2,1)S(1)}, u32[]{:S(2)}, u32[]{:S(2)}) collective-permute-start(bf16[128,2048]{1,0:T(8,128)(2,1)S(1)} %bitcast.83), channel_id=1, source_target_pairs={{0,8},{8,16},{16,24},{24,28},{28,20},{20,12},{12,4},{4,0},{1,9},{9... | collective-permute-start | bytes 1572872 | tf_op jit(solution)/shard_map/ppermute | solution.py:613
  108.3 324.5 %reduce-scatter.3.cloned.1.call-start = ((), (), s32[]{:S(2)}) async-start(), calls=%async_computation.4 | async-start | bytes 3932160 | tf_op jit(solution)/shard_map/reduce_scatter | solution.py:1104
  109.0 40.2 %collective-permute-start.31 = (bf16[64,1536]{1,0:T(8,128)(2,1)}, bf16[64,1536]{1,0:T(8,128)(2,1)}, u32[]{:S(2)}, u32[]{:S(2)}) collective-permute-start(bf16[64,1536]{1,0:T(8,128)(2,1)} %slice.383), channel_id=1, source_target_pairs={{0,28},{8,20},{16,12},{24,4},{28,0},{20,8},{12,16},{4,24},{1,29},{... | collective-permute-start | bytes 589832 | tf_op jit(solution)/shard_map/ppermute | solution.py:613
  110.4 27.5 %collective-permute-start.25 = (bf16[128,2048]{1,0:T(8,128)(2,1)S(1)}, bf16[128,2048]{1,0:T(8,128)(2,1)S(1)}, u32[]{:S(2)}, u32[]{:S(2)}) collective-permute-start(bf16[128,2048]{1,0:T(8,128)(2,1)S(1)} %collective-permute-done.20.refs_1_.refs_5_), channel_id=1, source_target_pairs={{0,4},{8,0},{16,8},{24,16},{28,24},{20,28},{12,20},{4,12},{1,5},{9... | collective-permute-start | bytes 1572872 | tf_op jit(solution)/shard_map/ppermute | solution.py:613
  111.6 26.4 %collective-permute-start.26 = (bf16[128,2048]{1,0:T(8,128)(2,1)S(1)}, bf16[128,2048]{1,0:T(8,128)(2,1)S(1)}, u32[]{:S(2)}, u32[]{:S(2)}) collective-permute-start(bf16[128,2048]{1,0:T(8,128)(2,1)S(1)} %collective-permute-done.21.refs_2_.refs_6_), channel_id=1, source_target_pairs={{0,8},{8,16},{16,24},{24,28},{28,20},{20,12},{12,4},{4,0},{1,9},{9... | collective-permute-start | bytes 1572872 | tf_op jit(solution)/shard_map/ppermute | solution.py:613
  112.4 25.5 %collective-permute-start.27 = (bf16[128,1536]{1,0:T(8,128)(2,1)}, bf16[128,1536]{1,0:T(8,128)(2,1)S(1)}, u32[]{:S(2)}, u32[]{:S(2)}) collective-permute-start(bf16[128,1536]{1,0:T(8,128)(2,1)} %slice.469), channel_id=1, source_target_pairs={{0,8},{8,16},{16,24},{24,28},{28,20},{20,12},{12,4},{4,0},{1,9},{9... | collective-permute-start | bytes 1179656 | tf_op jit(solution)/shard_map/ppermute | solution.py:613
  113.2 24.7 %collective-permute-start.28 = (bf16[128,1536]{1,0:T(8,128)(2,1)}, bf16[128,1536]{1,0:T(8,128)(2,1)S(1)}, u32[]{:S(2)}, u32[]{:S(2)}) collective-permute-start(bf16[128,1536]{1,0:T(8,128)(2,1)} %slice.470), channel_id=1, source_target_pairs={{0,4},{8,0},{16,8},{24,16},{28,24},{20,28},{12,20},{4,12},{1,5},{9... | collective-permute-start | bytes 1179656 | tf_op jit(solution)/shard_map/ppermute | solution.py:613
  163.0 21.8 %collective-permute-start.36 = (bf16[128,2048]{1,0:T(8,128)(2,1)S(1)}, bf16[128,2048]{1,0:T(8,128)(2,1)S(1)}, u32[]{:S(2)}, u32[]{:S(2)}) collective-permute-start(bf16[128,2048]{1,0:T(8,128)(2,1)S(1)} %copy-done.28), channel_id=1, source_target_pairs={{0,4},{8,0},{16,8},{24,16},{28,24},{20,28},{12,20},{4,12},{1,5},{9... | collective-permute-start | bytes 1572872 | tf_op jit(solution)/shard_map/ppermute | solution.py:613
  164.8 21.3 %collective-permute-start.37 = (bf16[128,2048]{1,0:T(8,128)(2,1)S(1)}, bf16[128,2048]{1,0:T(8,128)(2,1)S(1)}, u32[]{:S(2)}, u32[]{:S(2)}) collective-permute-start(bf16[128,2048]{1,0:T(8,128)(2,1)S(1)} %copy-done.30), channel_id=1, source_target_pairs={{0,8},{8,16},{16,24},{24,28},{28,20},{20,12},{12,4},{4,0},{1,9},{9... | collective-permute-start | bytes 1572872 | tf_op jit(solution)/shard_map/ppermute | solution.py:613
  165.1 41.5 %collective-permute-start.42 = (bf16[512,1536]{1,0:T(8,128)(2,1)S(1)}, bf16[512,1536]{1,0:T(8,128)(2,1)}, u32[]{:S(2)}, u32[]{:S(2)}) collective-permute-start(bf16[512,1536]{1,0:T(8,128)(2,1)S(1)} %copy-done.5), channel_id=1, source_target_pairs={{0,1},{1,0},{2,3},{3,2},{4,5},{5,4},{6,7},{7,6},{8,9},{9,8},{10,11... | collective-permute-start | bytes 4718600 | tf_op jit(solution)/shard_map/ppermute | solution.py:617
  175.8 32.2 %collective-permute-start.43 = (bf16[512,1536]{1,0:T(8,128)(2,1)S(1)}, bf16[512,1536]{1,0:T(8,128)(2,1)}, u32[]{:S(2)}, u32[]{:S(2)}) collective-permute-start(bf16[512,1536]{1,0:T(8,128)(2,1)S(1)} %copy-done.5), channel_id=1, source_target_pairs={{0,2},{1,3},{2,0},{3,1},{4,6},{5,7},{6,4},{7,5},{8,10},{9,11},{10,... | collective-permute-start | bytes 4718600 | tf_op jit(solution)/shard_map/ppermute | solution.py:617
  325.7 242.4 %reduce-scatter.5.cloned.1.call-start = ((), (), s32[]{:S(2)}) async-start(), calls=%async_computation.5 | async-start | bytes 1310720 | tf_op jit(solution)/shard_map/reduce_scatter | solution.py:1104
  349.6 46.9 %collective-permute-start.72 = (bf16[512,1536]{1,0:T(8,128)(2,1)S(1)}, bf16[512,1536]{1,0:T(8,128)(2,1)S(1)}, u32[]{:S(2)}, u32[]{:S(2)}) collective-permute-start(bf16[512,1536]{1,0:T(8,128)(2,1)S(1)} %get-tuple-element.438), channel_id=1, source_target_pairs={{0,2},{1,3},{2,0},{3,1},{4,6},{5,7},{6,4},{7,5},{8,10},{9,11},{10,... | collective-permute-start | bytes 4718600 | tf_op jit(solution)/shard_map/ppermute | solution.py:617
  400.4 30.8 %collective-permute-start.76 = (bf16[128,2048]{1,0:T(8,128)(2,1)}, bf16[128,2048]{1,0:T(8,128)(2,1)}, u32[]{:S(2)}, u32[]{:S(2)}) collective-permute-start(bf16[128,2048]{1,0:T(8,128)(2,1)} %pad_maximum_fusion.12), channel_id=1, source_target_pairs={{0,4},{8,0},{16,8},{24,16},{28,24},{20,28},{12,20},{4,12},{1,5},{9... | collective-permute-start | bytes 1572872 | tf_op jit(solution)/shard_map/ppermute | solution.py:613
  401.8 29.4 %collective-permute-start.75 = (bf16[128,2048]{1,0:T(8,128)(2,1)S(1)}, bf16[128,2048]{1,0:T(8,128)(2,1)}, u32[]{:S(2)}, u32[]{:S(2)}) collective-permute-start(bf16[128,2048]{1,0:T(8,128)(2,1)S(1)} %pad_maximum_fusion.11), channel_id=1, source_target_pairs={{0,8},{8,16},{16,24},{24,28},{28,20},{20,12},{12,4},{4,0},{1,9},{9... | collective-permute-start | bytes 1572872 | tf_op jit(solution)/shard_map/ppermute | solution.py:613
  402.4 30.4 %collective-permute-start.77 = (bf16[192,1536]{1,0:T(8,128)(2,1)}, bf16[192,1536]{1,0:T(8,128)(2,1)}, u32[]{:S(2)}, u32[]{:S(2)}) collective-permute-start(bf16[192,1536]{1,0:T(8,128)(2,1)} %get-tuple-element.444), channel_id=1, source_target_pairs={{0,8},{8,16},{16,24},{24,28},{28,20},{20,12},{12,4},{4,0},{1,9},{9... | collective-permute-start | bytes 1769480 | tf_op jit(solution)/shard_map/ppermute | solution.py:613
  403.9 29.0 %collective-permute-start.78 = (bf16[192,1536]{1,0:T(8,128)(2,1)}, bf16[192,1536]{1,0:T(8,128)(2,1)}, u32[]{:S(2)}, u32[]{:S(2)}) collective-permute-start(bf16[192,1536]{1,0:T(8,128)(2,1)} %get-tuple-element.445), channel_id=1, source_target_pairs={{0,4},{8,0},{16,8},{24,16},{28,24},{20,28},{12,20},{4,12},{1,5},{9... | collective-permute-start | bytes 1769480 | tf_op jit(solution)/shard_map/ppermute | solution.py:613
  526.0 21.7 %collective-permute-start.97 = (bf16[128,2048]{1,0:T(8,128)(2,1)S(1)}, bf16[128,2048]{1,0:T(8,128)(2,1)S(1)}, u32[]{:S(2)}, u32[]{:S(2)}) collective-permute-start(bf16[128,2048]{1,0:T(8,128)(2,1)S(1)} %get-tuple-element.507), channel_id=1, source_target_pairs={{0,4},{8,0},{16,8},{24,16},{28,24},{20,28},{12,20},{4,12},{1,5},{9... | collective-permute-start | bytes 1572872 | tf_op jit(solution)/shard_map/ppermute | solution.py:613
  553.9 23.7 %collective-permute-start.104 = (bf16[80,512]{1,0:T(8,128)(2,1)S(1)}, bf16[80,512]{1,0:T(8,128)(2,1)S(1)}, u32[]{:S(2)}, u32[]{:S(2)}) collective-permute-start(bf16[80,512]{1,0:T(8,128)(2,1)S(1)} %slice.515), channel_id=1, source_target_pairs={{0,28},{8,20},{16,12},{24,4},{28,0},{20,8},{12,16},{4,24},{1,29},{... | collective-permute-start | bytes 245768 | tf_op jit(solution)/shard_map/ppermute | solution.py:613
  (181 other events, 1878.6 us)
Sparse Core Ops, SparseCore 0:
  72.2 15.4 all-gather.2
  108.4 26.5 all-gather.4
  325.8 49.6 reduce-scatter.2
  530.2 24.2 reduce-scatter.4

commit v13 on v12

--- a/solution.py
+++ b/solution.py
@@ -1288,15 +1288,11 @@
     parts[3], parts[5] = split(hold((), back(2)))
     parts[2], parts[6] = split(hold((), back(1)))
     resid_ring.go()
-    _, _, hidden_groups, cotangent_strips = hold(
-        (resid_ring,), parts[2], parts[6], hidden_groups, cotangent_strips
-    )
+    hold((resid_ring,), parts[2], parts[6])
     resid_ring.go()
-    down_gradient = row_grads(hidden_groups, cotangent_strips)
-    back_zero, down_gradient, second_groups, ff_gradient_groups = hold(
-        (resid_ring,), back(0), down_gradient, second_groups, ff_gradient_groups
-    )
-    down_gradient = scatter_head(down_gradient)
+    back_zero, second_groups, ff_gradient_groups = hold(
+        (resid_ring,), back(0), second_groups, ff_gradient_groups
+    )
     parts[0], parts[1], parts[7] = split(back_zero)
     resid_ring.go()
     ff_own, ff_far, ff_sent = hold(
@@ -1327,10 +1323,11 @@
     out_parts = hold((grad_ring,), *out_parts)
     out_ring = Scatter(by_strips(out_parts))
     grad_ring.go()
-    hold((grad_ring,))
+    hidden_groups, cotangent_strips = hold((grad_ring,), hidden_groups, cotangent_strips)
     grad_ring.go()
     attention_back(0)
-    hold((out_ring, grad_ring))
+    down_gradient = hold((out_ring, grad_ring), row_grads(hidden_groups, cotangent_strips))
+    down_gradient = scatter_head(down_gradient)
     out_ring.go()
     grad_ring.go()
     attention_back(1)
@@ -1343,16 +1340,15 @@
     query_grads, kv_own, kv_far, kv_sent = attend_back(
         place, order, query_rows, attended_grads, attended, lse, kv
     )
-    query_grads, kv_own, kv_far, kv_sent, grad_groups, attended, down_gradient = hold(
-        (out_ring, ff_swap),
-        query_grads, kv_own, kv_far, kv_sent, grad_groups, attended, down_gradient,
+    query_grads, kv_own, kv_far, kv_sent, grad_groups, attended = hold(
+        (out_ring, ff_swap), query_grads, kv_own, kv_far, kv_sent, grad_groups, attended
     )
     out_ring.go()
     ff_swap.trim()
     kv_own, kv_far = scatter_cross(kv_own, kv_far, kv_sent)
     output_weight_gradient = row_grads([attended], grad_groups)
-    kv_own, kv_far, output_weight_gradient = hold(
-        (out_ring, ff_swap), kv_own, kv_far, output_weight_gradient
+    kv_own, kv_far, output_weight_gradient, down_gradient = hold(
+        (out_ring, ff_swap), kv_own, kv_far, output_weight_gradient, down_gradient
     )
     ff_swap.go()
     kv_grads, ff_opposite = hold(

time: 602 us -> 611 us (1.015)
  local copies, waits for them, and re-layouts: 27.2 us -> 40.6 us
  waiting for transfers between devices: 201 us -> 190 us
    ppermute x15, waiting for transfers between devices: 27.3 us -> 18.4 us  [cross(): return lax.ppermute(value, 'head', [(i, i ^ by) for i in range(4)])]
  transfers between devices with their start and end apart: 111 -> 111, of which waited for: 57 -> 60; matrix products, arithmetic and copies ran while one was open for 16% -> 19% of each run, Pallas kernels for 22% -> 23%
where the time goes in v13:
time: 611 us; the launch traced here: 601 us
  waiting for transfers between devices  190 us (31%)
  Pallas kernels  139 us (23%)
  starting transfers between devices  118 us (19%)
  other arithmetic  62.3 us (10%)
  local copies, waits for them, and re-layouts  40.6 us (7%)
  matrix products  35.4 us (6%)
  between operations  15.6 us (3%)
    ppermute x92, waiting for transfers between devices, hop(): lax.ppermute(value, 'blk', [(RING[i], RING[(i + by) % count]) for i in ra...  172 us
    ppermute x92, starting transfers between devices, hop(): lax.ppermute(value, 'blk', [(RING[i], RING[(i + by) % count]) for i in ra...  109 us
    dot_general x20, matrix products, matmul(): lax.dot_general(left, right, dims, preferred_element_type=jnp.float32)  35.4 us
    pallas_call x1, Pallas kernels, attend_back(): pl.pallas_call(lambda *refs: attend_back_kernel(*refs, groups=len(grads))...  29.5 us
    convert_element_type x18, other arithmetic, add(): (left.astype(jnp.float32) + right.astype(jnp.float32)).astype(left.dtype)  27.8 us
    pallas_call x2, Pallas kernels, weight_grads(): pl.pallas_call(lambda *refs: weight_grads_kernel(*refs, groups=len(lefts)...  23.3 us
    pallas_call x1, Pallas kernels, attend(): pl.pallas_call(attend_kernel, grid_spec=pltpu.PrefetchScalarGridSpec(num_...  21.5 us
    ppermute x15, waiting for transfers between devices, cross(): return lax.ppermute(value, 'head', [(i, i ^ by) for i in range(4)])  18.4 us
  transfers between devices with their start and end apart: 111, of which 60 were waited for; matrix products, arithmetic and copies ran while one was open for 19% of the time, Pallas kernels for 23%

profile of v13, /device:TPU:0, one launch (start us, length us, event | category | flops | bytes accessed | tf_op | source)
XLA Modules:
  0.0 601.2 jit_solution(5838079450061708985)
XLA Ops:
  50.7 6.3 %collective-permute-done.9.refs_4_ = bf16[128,2048]{1,0:T(8,128)(2,1)S(1)} collective-permute-done((bf16[128,2048]{1,0:T(8,128)(2,1)}, bf16[128,2048]{1,0:T(8,128)(2,1)S(1)}, u32[]{:S(2)}, u32[]{:S(2)}) %collective-permute-start.9) | collective-permute-done | bytes 524320 | tf_op jit(solution)/shard_map/ppermute | solution.py:613
  72.7 5.8 collective-permute-done.15.refs_8_
  83.7 9.9 %project.1 = (bf16[1024,2048]{1,0:T(8,128)(2,1)}, f32[1024,512]{1,0:T(8,128)}, bf16[1024,256]{1,0:T(8,128)(2,1)}, bf16[1024,256]{1,0:T(8,128)(2,1)}, bf16[2048,512]{1,0:T(8,128)(2,1)}, /*index=5*/f32[16,512]{1,0:T(8,128)}) custom-call(s32[9]{0:T(128)} %pad_add_fusion.refs_0_.at_ref, bf16[128,2048]{1,0:T(8,128)(2,1)} %bitcast.86, ...), custom_call_target="tpu_custom_call" | custom-call | flops 30000001024 | bytes 33554432 | tf_op jit(solution)/shard_map/project/pallas_call | solution.py:853
  101.2 5.0 collective-permute-done.20.refs_1_.refs_5_
  114.5 21.5 %attend.1 = (bf16[1024,256]{1,0:T(8,128)(2,1)}, f32[8,8,256]{2,1,0:T(8,128)}) custom-call(s32[8]{0:T(128)} %get-tuple-element.613.place_ref.refs_0_, s32[32]{0:T(128)} %copy-done.94, bf16[1024,256]{1,0:T(8,128)(2,1)} %get-tuple-element.318.q_ref.refs_2_, bf16[1024,256]{1,0:T(8,128)(2,1)} %get-tuple-element.319.refs_0_.refs_9_, ...), custom_call_target="tpu_custom_call" | custom-call | flops 30000001024 | bytes 33554432 | tf_op jit(solution)/shard_map/attend/pallas_call | solution.py:480
  149.2 7.2 %collective-permute-done.32.refs_6_ = bf16[64,1536]{1,0:T(8,128)(2,1)} collective-permute-done((bf16[64,1536]{1,0:T(8,128)(2,1)S(1)}, bf16[64,1536]{1,0:T(8,128)(2,1)}, u32[]{:S(2)}, u32[]{:S(2)}) %collective-permute-start.32) | collective-permute-done | bytes 196640 | tf_op jit(solution)/shard_map/ppermute | solution.py:613
  165.1 10.7 %collective-permute-done.35 = bf16[128,2048]{1,0:T(8,128)(2,1)S(1)} collective-permute-done((bf16[128,2048]{1,0:T(8,128)(2,1)S(1)}, bf16[128,2048]{1,0:T(8,128)(2,1)S(1)}, u32[]{:S(2)}, u32[]{:S(2)}) %collective-permute-start.35) | collective-permute-done | bytes 524320 | tf_op jit(solution)/shard_map/ppermute | solution.py:613
  178.3 6.6 %collective-permute-done.36.refs_5_.refs_9_ = bf16[128,2048]{1,0:T(8,128)(2,1)S(1)} collective-permute-done((bf16[128,2048]{1,0:T(8,128)(2,1)S(1)}, bf16[128,2048]{1,0:T(8,128)(2,1)S(1)}, u32[]{:S(2)}, u32[]{:S(2)}) %collective-permute-start.36) | collective-permute-done | bytes 524320 | tf_op jit(solution)/shard_map/ppermute | solution.py:613
  191.0 9.2 %collective-permute-done.39 = bf16[128,2048]{1,0:T(8,128)(2,1)S(1)} collective-permute-done((bf16[128,2048]{1,0:T(8,128)(2,1)S(1)}, bf16[128,2048]{1,0:T(8,128)(2,1)S(1)}, u32[]{:S(2)}, u32[]{:S(2)}) %collective-permute-start.39) | collective-permute-done | bytes 524320 | tf_op jit(solution)/shard_map/ppermute | solution.py:613
  210.6 7.9 %hidden_grads.1 = (f32[384,768]{1,0:T(8,128)}, f32[256,768]{1,0:T(8,128)}, f32[256,768]{1,0:T(8,128)}, f32[128,768]{1,0:T(8,128)}) custom-call(bf16[128,2048]{1,0:T(8,128)(2,1)} %bitcast.80, bf16[128,2048]{1,0:T(8,128)(2,1)} %copy-done.25, bf16[128,2048]{1,0:T(8,128)(2,1)} %copy-done.26, bf16[128,2048]{1,0:T(8,128)(2,1)} %copy-done.27, ...), custom_call_target="tpu_custom_call" | custom-call | flops 1 | bytes 1 | tf_op jit(solution)/shard_map/hidden_grads/pallas_call | solution.py:1030
  228.2 8.6 %assemble.1 = bf16[8,4,64,1536]{3,2,1,0:T(8,128)(2,1)} custom-call(s32[9]{0:T(128)} %pad_add_fusion.refs_0_.at_ref, bf16[512,1536]{1,0:T(8,128)(2,1)} %stack.3.refs_0_, bf16[512,1536]{1,0:T(8,128)(2,1)} %collective-permute-done.42.refs_1_, bf16[512,1536]{1,0:T(8,128)(2,1)} %collective-permute-done.43.refs_2_, bf16[512,1536]{1,0:T(8,128)(2,1)} %collective-permute-done.46.refs_3_), custom_call_target="tpu_custom_call" | custom-call | flops 1 | bytes 1 | tf_op jit(solution)/shard_map/assemble/pallas_call | solution.py:784
  281.5 7.1 %collective-permute-done.56 = bf16[64,2048]{1,0:T(8,128)(2,1)S(1)} collective-permute-done((bf16[64,2048]{1,0:T(8,128)(2,1)S(1)}, bf16[64,2048]{1,0:T(8,128)(2,1)S(1)}, u32[]{:S(2)}, u32[]{:S(2)}) %collective-permute-start.56) | collective-permute-done | bytes 262176 | tf_op jit(solution)/shard_map/ppermute | solution.py:613
  293.9 7.3 %collective-permute-done.58 = bf16[128,2048]{1,0:T(8,128)(2,1)S(1)} collective-permute-done((bf16[128,2048]{1,0:T(8,128)(2,1)S(1)}, bf16[128,2048]{1,0:T(8,128)(2,1)S(1)}, u32[]{:S(2)}, u32[]{:S(2)}) %collective-permute-start.58) | collective-permute-done | bytes 524320 | tf_op jit(solution)/shard_map/ppermute | solution.py:613
  307.4 14.4 %weight_grads.2 = (bf16[512,1536]{1,0:T(8,128)(2,1)}, bf16[512,1536]{1,0:T(8,128)(2,1)}, bf16[2,512,1536]{2,1,0:T(8,128)(2,1)}) custom-call(s32[9]{0:T(128)} %pad_add_fusion.refs_0_.at_ref, bf16[384,2048]{1,0:T(8,128)(2,1)} %pad_maximum_fusion.refs_1_, bf16[256,2048]{1,0:T(8,128)(2,1)} %copy-done.23, bf16[256,2048]{1,0:T(8,128)(2,1)} %copy-done.22, ...), custom_call_target="tpu_custom_call" | custom-call | flops 1 | bytes 1 | tf_op jit(solution)/shard_map/weight_grads/pallas_call | solution.py:946
  332.3 5.8 collective-permute-done.61
  361.0 6.9 %collective-permute-done.66 = bf16[128,2048]{1,0:T(8,128)(2,1)} collective-permute-done((bf16[128,2048]{1,0:T(8,128)(2,1)S(1)}, bf16[128,2048]{1,0:T(8,128)(2,1)}, u32[]{:S(2)}, u32[]{:S(2)}) %collective-permute-start.66) | collective-permute-done | bytes 524320 | tf_op jit(solution)/shard_map/ppermute | solution.py:613
  371.2 8.5 %row_grads.2 = bf16[768,2048]{1,0:T(8,128)(2,1)} custom-call(bf16[384,768]{1,0:T(8,128)(2,1)} %get-tuple-element.418.refs_0_, bf16[256,768]{1,0:T(8,128)(2,1)} %get-tuple-element.419.refs_1_, bf16[256,768]{1,0:T(8,128)(2,1)} %get-tuple-element.420.refs_2_, bf16[128,768]{1,0:T(8,128)(2,1)} %get-tuple-element.421.refs_3_, bf16[128,2048]{1,0:T(8,128)(2,1)} %bitcast.81, ...), custom_call_target="tpu_custom_call" | custom-call | flops 1 | bytes 1 | tf_op jit(solution)/shard_map/row_grads/pallas_call | solution.py:993
  410.2 29.5 %attend_back.1 = (bf16[1024,256]{1,0:T(8,128)(2,1)}, bf16[1024,256]{1,0:T(8,128)(2,1)}, bf16[1024,256]{1,0:T(8,128)(2,1)}, bf16[2048,256]{1,0:T(8,128)(2,1)}) custom-call(s32[8]{0:T(128)} %get-tuple-element.613.place_ref.refs_0_, s32[32]{0:T(128)} %copy-done.94, bf16[1024,256]{1,0:T(8,128)(2,1)} %get-tuple-element.318.q_ref.refs_2_, ...), custom_call_target="tpu_custom_call" | custom-call | flops 30000001024 | bytes 33554432 | tf_op jit(solution)/shard_map/attend_back/pallas_call | solution.py:579
  468.2 5.1 collective-permute-done.82.refs_3_
  483.0 9.3 %project_back.1 = (bf16[1024,512]{1,0:T(8,128)(2,1)}, bf16[1024,2048]{1,0:T(8,128)(2,1)}, f32[8,128]{1,0:T(8,128)}) custom-call(bf16[1024,256]{1,0:T(8,128)(2,1)} %get-tuple-element.480.dq_ref, bf16[1024,256]{1,0:T(8,128)(2,1)} %add_convert_fusion.11.dkv_ref, f32[1024,512]{1,0:T(8,128)} %get-tuple-element.482.raw_ref, f32[8,128]{1,0:T(8,128)} %pad.13.head_gain_ref, ...), custom_call_target="tpu_custom_call" | custom-call | flops 30000001024 | bytes 33554432 | tf_op jit(solution)/shard_map/project_back/pallas_call | solution.py:901
  500.5 9.0 %weight_grads.3 = (bf16[640,512]{1,0:T(8,128)(2,1)}, bf16[640,512]{1,0:T(8,128)(2,1)}, bf16[2,640,512]{2,1,0:T(8,128)(2,1)}) custom-call(s32[9]{0:T(128)} %pad_add_fusion.refs_0_.at_ref, bf16[1024,2048]{1,0:T(8,128)(2,1)} %get-tuple-element.491.refs_1_, bf16[1024,512]{1,0:T(8,128)(2,1)} %get-tuple-element.492.refs_2_, bf16[16,512]{1,0:T(8,128)(2,1)} %pad.14.refs_3_), custom_call_target="tpu_custom_call" | custom-call | flops 1 | bytes 1 | tf_op jit(solution)/shard_map/weight_grads/pallas_call | solution.py:946
  521.6 7.1 %collective-permute-done.93 = bf16[128,2048]{1,0:T(8,128)(2,1)S(1)} collective-permute-done((bf16[128,2048]{1,0:T(8,128)(2,1)S(1)}, bf16[128,2048]{1,0:T(8,128)(2,1)S(1)}, u32[]{:S(2)}, u32[]{:S(2)}) %collective-permute-start.93) | collective-permute-done | bytes 524320 | tf_op jit(solution)/shard_map/ppermute | solution.py:613
  542.9 11.0 %collective-permute-done.98.refs_1_ = bf16[240,512]{1,0:T(8,128)(2,1)S(1)} collective-permute-done((bf16[240,512]{1,0:T(8,128)(2,1)S(1)}, bf16[240,512]{1,0:T(8,128)(2,1)S(1)}, u32[]{:S(2)}, u32[]{:S(2)}) %collective-permute-start.98) | collective-permute-done | bytes 245792 | tf_op jit(solution)/shard_map/ppermute | solution.py:613
  568.8 6.8 %collective-permute-done.102.refs_4_ = bf16[160,512]{1,0:T(8,128)(2,1)S(1)} collective-permute-done((bf16[160,512]{1,0:T(8,128)(2,1)S(1)}, bf16[160,512]{1,0:T(8,128)(2,1)S(1)}, u32[]{:S(2)}, u32[]{:S(2)}) %collective-permute-start.102) | collective-permute-done | bytes 163872 | tf_op jit(solution)/shard_map/ppermute | solution.py:613
  (576 shorter events, 359.0 us)
Async XLA Ops:
  7.2 130.8 %all-gather.3.cloned.1.call-start = ((), (), s32[]{:S(2)}) async-start(), calls=%async_computation.2 | async-start | bytes 1310720 | tf_op jit(solution)/shard_map/all_gather | solution.py:1100
  7.3 38.7 %collective-permute-start = (bf16[128,2048]{1,0:T(8,128)(2,1)}, bf16[128,2048]{1,0:T(8,128)(2,1)}, u32[]{:S(2)}, u32[]{:S(2)}) collective-permute-start(bf16[128,2048]{1,0:T(8,128)(2,1)} %bitcast.84), channel_id=1, source_target_pairs={{0,4},{8,0},{16,8},{24,16},{28,24},{20,28},{12,20},{4,12},{1,5},{9... | collective-permute-start | bytes 1572872 | tf_op jit(solution)/shard_map/ppermute | solution.py:613
  10.3 35.7 %collective-permute-start.1 = (bf16[128,2048]{1,0:T(8,128)(2,1)}, bf16[128,2048]{1,0:T(8,128)(2,1)}, u32[]{:S(2)}, u32[]{:S(2)}) collective-permute-start(bf16[128,2048]{1,0:T(8,128)(2,1)} %bitcast.85), channel_id=1, source_target_pairs={{0,8},{8,16},{16,24},{24,28},{28,20},{20,12},{12,4},{4,0},{1,9},{9... | collective-permute-start | bytes 1572872 | tf_op jit(solution)/shard_map/ppermute | solution.py:613
  72.0 131.6 %all-gather.5.cloned.1.call-start = ((), (), s32[]{:S(2)}) async-start(), calls=%async_computation.3 | async-start | bytes 3932160 | tf_op jit(solution)/shard_map/all_gather | solution.py:1100
  81.7 24.5 %collective-permute-start.20 = (bf16[128,2048]{1,0:T(8,128)(2,1)S(1)}, bf16[128,2048]{1,0:T(8,128)(2,1)S(1)}, u32[]{:S(2)}, u32[]{:S(2)}) collective-permute-start(bf16[128,2048]{1,0:T(8,128)(2,1)S(1)} %bitcast.82), channel_id=1, source_target_pairs={{0,4},{8,0},{16,8},{24,16},{28,24},{20,28},{12,20},{4,12},{1,5},{9... | collective-permute-start | bytes 1572872 | tf_op jit(solution)/shard_map/ppermute | solution.py:613
  82.9 23.3 %collective-permute-start.21 = (bf16[128,2048]{1,0:T(8,128)(2,1)S(1)}, bf16[128,2048]{1,0:T(8,128)(2,1)S(1)}, u32[]{:S(2)}, u32[]{:S(2)}) collective-permute-start(bf16[128,2048]{1,0:T(8,128)(2,1)S(1)} %bitcast.83), channel_id=1, source_target_pairs={{0,8},{8,16},{16,24},{24,28},{28,20},{20,12},{12,4},{4,0},{1,9},{9... | collective-permute-start | bytes 1572872 | tf_op jit(solution)/shard_map/ppermute | solution.py:613
  108.3 354.0 %reduce-scatter.3.cloned.1.call-start = ((), (), s32[]{:S(2)}) async-start(), calls=%async_computation.4 | async-start | bytes 3932160 | tf_op jit(solution)/shard_map/reduce_scatter | solution.py:1104
  109.1 40.2 %collective-permute-start.31 = (bf16[64,1536]{1,0:T(8,128)(2,1)}, bf16[64,1536]{1,0:T(8,128)(2,1)}, u32[]{:S(2)}, u32[]{:S(2)}) collective-permute-start(bf16[64,1536]{1,0:T(8,128)(2,1)} %slice.383), channel_id=1, source_target_pairs={{0,28},{8,20},{16,12},{24,4},{28,0},{20,8},{12,16},{4,24},{1,29},{... | collective-permute-start | bytes 589832 | tf_op jit(solution)/shard_map/ppermute | solution.py:613
  110.4 27.5 %collective-permute-start.25 = (bf16[128,2048]{1,0:T(8,128)(2,1)S(1)}, bf16[128,2048]{1,0:T(8,128)(2,1)S(1)}, u32[]{:S(2)}, u32[]{:S(2)}) collective-permute-start(bf16[128,2048]{1,0:T(8,128)(2,1)S(1)} %collective-permute-done.20.refs_1_.refs_5_), channel_id=1, source_target_pairs={{0,4},{8,0},{16,8},{24,16},{28,24},{20,28},{12,20},{4,12},{1,5},{9... | collective-permute-start | bytes 1572872 | tf_op jit(solution)/shard_map/ppermute | solution.py:613
  111.6 26.4 %collective-permute-start.26 = (bf16[128,2048]{1,0:T(8,128)(2,1)S(1)}, bf16[128,2048]{1,0:T(8,128)(2,1)S(1)}, u32[]{:S(2)}, u32[]{:S(2)}) collective-permute-start(bf16[128,2048]{1,0:T(8,128)(2,1)S(1)} %collective-permute-done.21.refs_2_.refs_6_), channel_id=1, source_target_pairs={{0,8},{8,16},{16,24},{24,28},{28,20},{20,12},{12,4},{4,0},{1,9},{9... | collective-permute-start | bytes 1572872 | tf_op jit(solution)/shard_map/ppermute | solution.py:613
  112.4 25.5 %collective-permute-start.27 = (bf16[128,1536]{1,0:T(8,128)(2,1)}, bf16[128,1536]{1,0:T(8,128)(2,1)S(1)}, u32[]{:S(2)}, u32[]{:S(2)}) collective-permute-start(bf16[128,1536]{1,0:T(8,128)(2,1)} %slice.469), channel_id=1, source_target_pairs={{0,8},{8,16},{16,24},{24,28},{28,20},{20,12},{12,4},{4,0},{1,9},{9... | collective-permute-start | bytes 1179656 | tf_op jit(solution)/shard_map/ppermute | solution.py:613
  113.2 24.7 %collective-permute-start.28 = (bf16[128,1536]{1,0:T(8,128)(2,1)}, bf16[128,1536]{1,0:T(8,128)(2,1)S(1)}, u32[]{:S(2)}, u32[]{:S(2)}) collective-permute-start(bf16[128,1536]{1,0:T(8,128)(2,1)} %slice.470), channel_id=1, source_target_pairs={{0,4},{8,0},{16,8},{24,16},{28,24},{20,28},{12,20},{4,12},{1,5},{9... | collective-permute-start | bytes 1179656 | tf_op jit(solution)/shard_map/ppermute | solution.py:613
  163.0 21.8 %collective-permute-start.36 = (bf16[128,2048]{1,0:T(8,128)(2,1)S(1)}, bf16[128,2048]{1,0:T(8,128)(2,1)S(1)}, u32[]{:S(2)}, u32[]{:S(2)}) collective-permute-start(bf16[128,2048]{1,0:T(8,128)(2,1)S(1)} %copy-done.28), channel_id=1, source_target_pairs={{0,4},{8,0},{16,8},{24,16},{28,24},{20,28},{12,20},{4,12},{1,5},{9... | collective-permute-start | bytes 1572872 | tf_op jit(solution)/shard_map/ppermute | solution.py:613
  164.8 21.3 %collective-permute-start.37 = (bf16[128,2048]{1,0:T(8,128)(2,1)S(1)}, bf16[128,2048]{1,0:T(8,128)(2,1)S(1)}, u32[]{:S(2)}, u32[]{:S(2)}) collective-permute-start(bf16[128,2048]{1,0:T(8,128)(2,1)S(1)} %copy-done.30), channel_id=1, source_target_pairs={{0,8},{8,16},{16,24},{24,28},{28,20},{20,12},{12,4},{4,0},{1,9},{9... | collective-permute-start | bytes 1572872 | tf_op jit(solution)/shard_map/ppermute | solution.py:613
  165.1 41.5 %collective-permute-start.42 = (bf16[512,1536]{1,0:T(8,128)(2,1)S(1)}, bf16[512,1536]{1,0:T(8,128)(2,1)}, u32[]{:S(2)}, u32[]{:S(2)}) collective-permute-start(bf16[512,1536]{1,0:T(8,128)(2,1)S(1)} %copy-done.5), channel_id=1, source_target_pairs={{0,1},{1,0},{2,3},{3,2},{4,5},{5,4},{6,7},{7,6},{8,9},{9,8},{10,11... | collective-permute-start | bytes 4718600 | tf_op jit(solution)/shard_map/ppermute | solution.py:617
  175.8 32.2 %collective-permute-start.43 = (bf16[512,1536]{1,0:T(8,128)(2,1)S(1)}, bf16[512,1536]{1,0:T(8,128)(2,1)}, u32[]{:S(2)}, u32[]{:S(2)}) collective-permute-start(bf16[512,1536]{1,0:T(8,128)(2,1)S(1)} %copy-done.5), channel_id=1, source_target_pairs={{0,2},{1,3},{2,0},{3,1},{4,6},{5,7},{6,4},{7,5},{8,10},{9,11},{10,... | collective-permute-start | bytes 4718600 | tf_op jit(solution)/shard_map/ppermute | solution.py:617
  346.1 41.2 %collective-permute-start.72 = (bf16[512,1536]{1,0:T(8,128)(2,1)}, bf16[512,1536]{1,0:T(8,128)(2,1)}, u32[]{:S(2)}, u32[]{:S(2)}) collective-permute-start(bf16[512,1536]{1,0:T(8,128)(2,1)} %get-tuple-element.438), channel_id=1, source_target_pairs={{0,2},{1,3},{2,0},{3,1},{4,6},{5,7},{6,4},{7,5},{8,10},{9,11},{10,... | collective-permute-start | bytes 4718600 | tf_op jit(solution)/shard_map/ppermute | solution.py:617
  394.7 181.6 %reduce-scatter.5.cloned.1.call-start = ((), (), s32[]{:S(2)}) async-start(), calls=%async_computation.5 | async-start | bytes 1310720 | tf_op jit(solution)/shard_map/reduce_scatter | solution.py:1104
  403.1 36.6 %collective-permute-start.76 = (bf16[128,2048]{1,0:T(8,128)(2,1)}, bf16[128,2048]{1,0:T(8,128)(2,1)}, u32[]{:S(2)}, u32[]{:S(2)}) collective-permute-start(bf16[128,2048]{1,0:T(8,128)(2,1)} %pad_maximum_fusion.12), channel_id=1, source_target_pairs={{0,4},{8,0},{16,8},{24,16},{28,24},{20,28},{12,20},{4,12},{1,5},{9... | collective-permute-start | bytes 1572872 | tf_op jit(solution)/shard_map/ppermute | solution.py:613
  404.7 35.0 %collective-permute-start.75 = (bf16[128,2048]{1,0:T(8,128)(2,1)S(1)}, bf16[128,2048]{1,0:T(8,128)(2,1)}, u32[]{:S(2)}, u32[]{:S(2)}) collective-permute-start(bf16[128,2048]{1,0:T(8,128)(2,1)S(1)} %pad_maximum_fusion.11), channel_id=1, source_target_pairs={{0,8},{8,16},{16,24},{24,28},{28,20},{20,12},{12,4},{4,0},{1,9},{9... | collective-permute-start | bytes 1572872 | tf_op jit(solution)/shard_map/ppermute | solution.py:613
  405.1 37.2 %collective-permute-start.77 = (bf16[192,1536]{1,0:T(8,128)(2,1)}, bf16[192,1536]{1,0:T(8,128)(2,1)}, u32[]{:S(2)}, u32[]{:S(2)}) collective-permute-start(bf16[192,1536]{1,0:T(8,128)(2,1)} %get-tuple-element.444), channel_id=1, source_target_pairs={{0,8},{8,16},{16,24},{24,28},{28,20},{20,12},{12,4},{4,0},{1,9},{9... | collective-permute-start | bytes 1769480 | tf_op jit(solution)/shard_map/ppermute | solution.py:613
  405.5 36.8 %collective-permute-start.78 = (bf16[192,1536]{1,0:T(8,128)(2,1)}, bf16[192,1536]{1,0:T(8,128)(2,1)}, u32[]{:S(2)}, u32[]{:S(2)}) collective-permute-start(bf16[192,1536]{1,0:T(8,128)(2,1)} %get-tuple-element.445), channel_id=1, source_target_pairs={{0,4},{8,0},{16,8},{24,16},{28,24},{20,28},{12,20},{4,12},{1,5},{9... | collective-permute-start | bytes 1769480 | tf_op jit(solution)/shard_map/ppermute | solution.py:613
  534.8 21.3 %collective-permute-start.97 = (bf16[128,2048]{1,0:T(8,128)(2,1)S(1)}, bf16[128,2048]{1,0:T(8,128)(2,1)S(1)}, u32[]{:S(2)}, u32[]{:S(2)}) collective-permute-start(bf16[128,2048]{1,0:T(8,128)(2,1)S(1)} %get-tuple-element.507), channel_id=1, source_target_pairs={{0,4},{8,0},{16,8},{24,16},{28,24},{20,28},{12,20},{4,12},{1,5},{9... | collective-permute-start | bytes 1572872 | tf_op jit(solution)/shard_map/ppermute | solution.py:613
  562.3 24.0 %collective-permute-start.104 = (bf16[80,512]{1,0:T(8,128)(2,1)S(1)}, bf16[80,512]{1,0:T(8,128)(2,1)S(1)}, u32[]{:S(2)}, u32[]{:S(2)}) collective-permute-start(bf16[80,512]{1,0:T(8,128)(2,1)S(1)} %slice.515), channel_id=1, source_target_pairs={{0,28},{8,20},{16,12},{24,4},{28,0},{20,8},{12,16},{4,24},{1,29},{... | collective-permute-start | bytes 245768 | tf_op jit(solution)/shard_map/ppermute | solution.py:613
  (186 other events, 1903.3 us)
Sparse Core Ops, SparseCore 0:
  72.1 15.4 all-gather.2
  108.4 26.6 all-gather.4
  394.8 38.3 reduce-scatter.2
  539.0 24.5 reduce-scatter.4
